TPU v7x, 32 devices: a whole 2x2x4 slice. The times are simulated.
32 devices in a mesh: lat: 8 (over z, y), lon: 4 (over x, core).
Axes of the slice: x: 2, y: 2, z: 4, core: 2. Of those that a mesh axis runs over, the one named last changes fastest.
Arguments:
- field: bfloat16 [32, 256, 3600], P(None, 'lat', 'lon'), may hold values from -6 to 6
- offsets: int32 [9, 2], replicated, may hold values from -2 to 2, as said below
- conv_weight: float32 [32, 9], replicated, may hold values from -2 to 2
- legendre: bfloat16 [64, 64, 128], P(('lat', 'lon')), may hold values from -5 to 5
- quad_weight: float32 [128], replicated, may hold values from 0.5 to 2
- band_limit: int32 [128], replicated, may hold values from 1 to 64, as said below
- mix_weight: bfloat16 [2, 64, 32, 32], replicated, may hold values from -0.125 to 0.125
Outputs:
- block_out: bfloat16 [32, 256, 3600], P(None, 'lat', 'lon')
Inputs may be any that keep to these rules, and one draw needn't show every extreme that they name: `offsets`: every offset lies within two rows and two columns; the taps include a row offset of +2, one of -2, a column offset of +2 and one of -2. `band_limit`: rows near the poles keep few orders; the rows nearest the equator keep all 64 orders.
All inputs are finite; a program needn't handle non-finite values.
Results may differ from a plain program's by a relative error of at most 0.01.
Values may be sent and summed in bfloat16 or wider, within the bound.
No kernel may reach another device: no remote copies, remote signals or barrier semaphores. Data moves between devices by JAX's collectives and lax.ppermute only.
A program may use at most 128 MiB of HBM per device.

v0:
```python
import math

import jax
import jax.numpy as jnp
from jax import lax
from jax.sharding import PartitionSpec as P

KTAPS = 9
M_DEV = 2


def padded(cells, sides, width, closed):
    for axis, dim in sides:
        count = lax.axis_size(axis)
        ends = count if closed else count - 1
        head = lax.slice_in_dim(cells, 0, width, axis=dim)
        tail = lax.slice_in_dim(cells, cells.shape[dim] - width, cells.shape[dim], axis=dim)
        cells = jnp.concatenate(
            [
                lax.ppermute(tail, axis, [(i, (i + 1) % count) for i in range(ends)]),
                cells,
                lax.ppermute(head, axis, [((i + 1) % count, i) for i in range(ends)]),
            ],
            axis=dim,
        )
    return cells


def wave_table(orders, points, period, inverse_form):
    angles = (orders[:, None] * points[None, :] % period).astype(jnp.float32) * (
        2.0 * math.pi / period
    )
    factor = jnp.full(orders.shape, 1.0 / math.sqrt(period), jnp.float32)
    if inverse_form:
        factor = jnp.where(orders == 0, 1.0, 2.0).astype(jnp.float32) * factor
    stacked = jnp.stack(
        [factor[:, None] * jnp.cos(angles), -factor[:, None] * jnp.sin(angles)], axis=1
    )
    return stacked.astype(jnp.bfloat16)


def per_device(field, offsets, conv_weight, legendre, quad_weight, band_limit, mix_weight):
    channels, lat_rows, lon_cols = field.shape
    lon_count = lax.axis_size("lon")
    lat_count = lax.axis_size("lat")
    total_lon = lon_cols * lon_count
    total_lat = lat_rows * lat_count
    half_rows = total_lat // 2
    orders_all = M_DEV * lat_count * lon_count
    quarter = orders_all // lon_count
    lon_points = lax.axis_index("lon") * lon_cols + lax.iota(jnp.int32, lon_cols)
    rimmed = padded(field, (("lat", 1),), 2, False)
    rimmed = padded(rimmed, (("lon", 2),), 2, True)
    running = jnp.zeros(field.shape, jnp.float32)
    for tap_index in range(KTAPS):
        window = lax.dynamic_slice(
            rimmed,
            (jnp.int32(0), 2 + offsets[tap_index, 0], 2 + offsets[tap_index, 1]),
            field.shape,
        )
        running = running + conv_weight[:, tap_index][:, None, None] * window.astype(jnp.float32)
    conv_out = running.astype(jnp.bfloat16)
    flattened = conv_out.reshape(channels * lat_rows, lon_cols)
    positions = lax.iota(jnp.int32, quarter * lax.axis_size("lon"))
    block_ids = positions // quarter
    remainder = positions % quarter
    wave_rows = wave_table(
        (remainder // M_DEV * lon_count + block_ids) * M_DEV + remainder % M_DEV,
        lon_points,
        total_lon,
        False,
    ).reshape(quarter * lax.axis_size("lon") * 2, lon_cols)
    summand = lax.dot_general(
        wave_rows, flattened, (((1,), (1,)), ((), ())), preferred_element_type=jnp.float32
    )
    spectrum_part = lax.psum_scatter(
        summand.reshape(quarter * lax.axis_size("lon"), 2, channels, lat_rows),
        "lon",
        scatter_dimension=0,
        tiled=True,
    ).astype(jnp.bfloat16)
    spectrum = lax.all_to_all(spectrum_part, "lat", split_axis=0, concat_axis=3, tiled=True)
    mine = (lax.axis_index("lat") * lon_count + lax.axis_index("lon")) * M_DEV + lax.iota(
        jnp.int32, M_DEV
    )
    north_part = spectrum[..., :half_rows].astype(jnp.float32)
    south_part = jnp.flip(spectrum[..., half_rows:], axis=3).astype(jnp.float32)
    kept_mask = (mine[:, None] < band_limit[None, :]).astype(jnp.float32)
    weight_q = quad_weight[None, :] * kept_mask * (1.0 / math.sqrt(half_rows))
    even_terms = (weight_q[:, None, None, :] * (north_part + south_part)).astype(jnp.bfloat16)
    odd_terms = (weight_q[:, None, None, :] * (north_part - south_part)).astype(jnp.bfloat16)
    paired = legendre.reshape(M_DEV, orders_all // 2, 2, half_rows)
    mix_pairs = mix_weight.reshape(2, orders_all // 2, 2, channels, channels)
    even_sum = jnp.zeros((M_DEV, 2, channels, half_rows), jnp.float32)
    odd_sum = jnp.zeros((M_DEV, 2, channels, half_rows), jnp.float32)
    for parity in range(2):
        same_parity = ((parity + mine) % 2 == 0)[:, None, None, None]
        operand = jnp.where(same_parity, even_terms, odd_terms)
        degree_plane = paired[:, :, parity]
        coeffs = jnp.einsum(
            "mui,mpci->mupc", degree_plane, operand, preferred_element_type=jnp.float32
        )
        degrees = 2 * lax.iota(jnp.int32, orders_all // 2) + parity
        triangle = (degrees[None, :] >= mine[:, None]).astype(jnp.float32)
        coeffs = (coeffs * triangle[:, :, None, None]).astype(jnp.bfloat16)
        with_real = jnp.einsum(
            "mupc,ucd->mupd", coeffs, mix_pairs[0, :, parity], preferred_element_type=jnp.float32
        )
        with_imag = jnp.einsum(
            "mupc,ucd->mupd", coeffs, mix_pairs[1, :, parity], preferred_element_type=jnp.float32
        )
        mixed = jnp.stack(
            [with_real[:, :, 0] - with_imag[:, :, 1], with_real[:, :, 1] + with_imag[:, :, 0]],
            axis=2,
        ).astype(jnp.bfloat16)
        returned = jnp.einsum(
            "mui,mupc->mpci", degree_plane, mixed, preferred_element_type=jnp.float32
        )
        even_sum = even_sum + jnp.where(same_parity, returned, 0.0)
        odd_sum = odd_sum + jnp.where(same_parity, 0.0, returned)
    north_out = (even_sum + odd_sum) * kept_mask[:, None, None, :]
    south_out = (even_sum - odd_sum) * kept_mask[:, None, None, :]
    grid_spectrum = jnp.concatenate([north_out, jnp.flip(south_out, axis=3)], axis=3).astype(
        jnp.bfloat16
    )
    pooled = lax.all_gather(grid_spectrum, "lon", axis=0, tiled=True)
    full_rows = lax.all_to_all(pooled, "lat", split_axis=3, concat_axis=0, tiled=True)
    wave_rows = wave_table(lax.iota(jnp.int32, orders_all), lon_points, total_lon, True).reshape(
        orders_all * 2, lon_cols
    )
    spectral_rows = full_rows.reshape(orders_all * 2, channels * lat_rows)
    synthesis = lax.dot_general(
        spectral_rows, wave_rows, (((0,), (0,)), ((), ())), preferred_element_type=jnp.float32
    )
    synthesis = synthesis.reshape(channels, lat_rows, lon_cols)
    return (conv_out.astype(jnp.float32) + jax.nn.gelu(synthesis, approximate=True)).astype(
        jnp.bfloat16
    )


def solution(mesh):
    placed = (P(None, "lat", "lon"), P(), P(), P(("lat", "lon"), None, None), P(), P(), P())
    return jax.shard_map(
        per_device, mesh=mesh, in_specs=placed, out_specs=P(None, "lat", "lon"), check_vma=False
    )
```

profile of v0, /device:TPU:0, one launch (start us, length us, event | category | flops | bytes accessed | tf_op | source)
XLA Modules:
  0.0 162.7 jit_solution(18433023728416947227)
XLA Ops:
  6.5 1.6 fusion.59
  8.1 4.9 %collective-permute-start = (bf16[32,2,900]{2,1,0:T(2,128)(2,1)S(1)}, bf16[32,2,900]{2,1,0:T(2,128)(2,1)S(1)}, u32[]{:S(2)}, u32[]{:S(2)}) collective-permute-start(bf16[32,2,900]{2,1,0:T(2,128)(2,1)S(1)} %get-tuple-element.7), channel_id=1, source_target_pairs={{0,4},{4,8},{8,12},{12,16},{16,20},{20,24},{24,28},{1,5},{5,9},{9,... | collective-permute-start | bytes 345608 | tf_op jit(solution)/shard_map/ppermute | solution.py:20
  13.0 1.3 collective-permute-start.1
  14.3 2.0 %fusion.61 = (s32[1,1]{0,1:T(1,128)}, s32[1,1]{0,1:T(1,128)}, s32[1,1]{0,1:T(1,128)}, s32[1,1]{0,1:T(1,128)}, s32[1,1]{0,1:T(1,128)}, /*index=5*/s32[1,1]{0,1:T(...) fusion(s32[9,2]{0,1:T(2,128)} %param.8), kind=kLoop, calls=%fused_computation.133 | loop fusion | bytes 144 | tf_op jit(solution)/shard_map/slice | solution.py:58
  31.2 3.2 %multiply_convert_fusion.1 = (bf16[64,1,900]{2,0,1:T(8,128)(2,1)S(1)}, bf16[64,1,900]{2,0,1:T(8,128)(2,1)}, bf16[64,1,900]{2,0,1:T(8,128)(2,1)}, bf16[64,1,900]{2,0,1:T(8,128)(2,1)}) fusion(f32[64]{0:T(128)S(1)} %get-tuple-element.54, s32[900]{0:T(1024)S(1)} %iota_add_fusion, f32[64]{0:T(128)S(1)} %get-tuple-element.55, s32[64]{0:T(128)S(1)} %fusion.49), kind=kLoop, calls=%fused_computation.44 | loop fusion | flops 1497600 | bytes 465168 | tf_op jit(solution)/shard_map/convert
  34.4 1.0 slice_bitcast_fusion.16
  35.4 0.0 collective-permute-done
  35.4 0.0 collective-permute-done.1
  35.4 2.0 %pad_maximum_fusion.3 = (bf16[32,36,2]{2,1,0:T(8,128)(2,1)}, bf16[32,36,2]{2,1,0:T(8,128)(2,1)S(1)}) fusion(bf16[32,2,900]{2,1,0:T(2,128)(2,1)S(1)} %collective-permute-done.1, bf16[32,32,900]{2,1,0:T(8,128)(2,1)} %param.7, bf16[32,2,900]{2,1,0:T(2,128)(2,1)S(1)} %collective-permute-done), kind=kLoop, calls=%fused_computation.28 | loop fusion | flops 27648 | bytes 2082816 | tf_op jit(solution)/shard_map/slice | solution.py:17
  37.4 0.0 collective-permute-start.2
  37.4 1.7 %collective-permute-start.3 = (bf16[32,36,2]{2,1,0:T(8,128)(2,1)S(1)}, bf16[32,36,2]{2,1,0:T(8,128)(2,1)S(1)}, u32[]{:S(2)}, u32[]{:S(2)}) collective-permute-start(bf16[32,36,2]{2,1,0:T(8,128)(2,1)S(1)} %get-tuple-element.6), channel_id=1, source_target_pairs={{1,0},{2,1},{3,2},{0,3},{5,4},{6,5},{7,6},{4,7},{9,8},{10,9},{11,1... | collective-permute-start | bytes 13832 | tf_op jit(solution)/shard_map/ppermute | solution.py:22
  47.0 0.0 collective-permute-done.3
  47.1 3.3 %pad_maximum_fusion = bf16[32,36,904]{2,1,0:T(8,128)(2,1)S(1)} fusion(bf16[32,36,2]{2,1,0:T(8,128)(2,1)S(1)} %collective-permute-done.3, bf16[32,2,900]{2,1,0:T(2,128)(2,1)S(1)} %collective-permute-done.1, bf16[32,32,900]{2,1,0:T(8,128)(2,1)S(1)} %copy-done, bf16[32,2,900]{2,1,0:T(2,128)(2,1)S(1)} %collective-permute-done, ...), kind=kLoop, calls=%fused_computation.11 | loop fusion | flops 10414080 | bytes 4165632 | tf_op jit(solution)/shard_map/concatenate | solution.py:18
  50.3 20.3 %add_convert_fusion = bf16[32,32,900]{2,1,0:T(8,128)(2,1)S(1)} fusion(bf16[32,36,904]{2,1,0:T(8,128)(2,1)S(1)} %pad_maximum_fusion, s32[]{:T(128)S(6)} %select_n.189, s32[]{:T(128)S(6)} %select_n.190, f32[32]{0:T(128)S(1)} %get-tuple-element.22, s32[]{:T(128)S(6)} %select_n.187, s32[]{:T(128)S(6)} %select_n.188, f32[32]{0:T(128)S(1)} %get-tuple-element.23, ...), kind=kLoop, calls=%fused_computation.10 | loop fusion | flops 24883200 | bytes 18433224 | tf_op jit(solution)/shard_map/convert_element_type | solution.py:62
  70.7 0.0 copy-start.1
  70.7 0.0 copy-start.8
  70.7 0.0 copy-start.9
  70.8 0.0 copy-start.5
  70.8 3.1 %fusion.9 = f32[64,2,32,32]{3,0,2,1:T(8,128)} fusion(bf16[32,32,900]{2,1,0:T(8,128)(2,1)S(1)} %add_convert_fusion, bf16[64,1,900]{2,0,1:T(8,128)(2,1)S(1)} %copy-done.3, bf16[64,1,900]{2,0,1:T(8,128)(2,1)S(1)} %copy-done.4), kind=kOutput, calls=%fused_computation.12 | convolution fusion | flops 236390400 | bytes 2597888 | tf_op jit(solution)/shard_map/dot_general | solution.py:73
  73.9 0.0 reduce-scatter.2.cloned.1.call-update
  73.9 0.1 fusion.48
  74.0 0.1 compare_convert_fusion.2
  74.1 0.7 fusion.60
  74.7 33.1 %reduce-scatter.2.cloned.1.call-done = f32[16,2,32,32]{3,0,2,1:T(8,128)} async-done(((f32[64,2,32,32]{3,0,2,1:T(8,128)}), f32[16,2,32,32]{3,0,2,1:T(8,128)}) %reduce-scatter.2.cloned.1.call-update) | async-done | bytes 131088 | tf_op jit(solution)/shard_map/reduce_scatter | solution.py:76
  107.9 1.1 convert_element_type.141
  109.0 0.1 copy.33
  109.1 0.9 reshape.571
  110.0 5.5 %all-to-all-start = ((bf16[8,2,2048]{2,1,0:T(2,128)(2,1)}), bf16[8,2,2048]{2,1,0:T(2,128)(2,1)S(1)}, u32[]{:S(2)}, u32[]{:S(2)}) async-start(bf16[8,2,2048]{2,1,0:T(2,128)(2,1)} %reshape.571), calls=%async_computation.1 | async-start | bytes 131072 | tf_op jit(solution)/shard_map/all_to_all | solution.py:82
  115.5 0.1 compare_convert_fusion
  115.5 2.5 %copy.36 = bf16[2,64,32,32]{3,2,1,0:T(8,128)(2,1)S(1)} copy(bf16[2,64,32,32]{1,3,2,0:T(8,128)(2,1)} %param.13) | data formatting | bytes 524288 | tf_op args[6]
  118.1 0.5 fusion.52
  118.6 3.8 %all-to-all-done = bf16[8,2,2048]{2,1,0:T(2,128)(2,1)S(1)} async-done(((bf16[8,2,2048]{2,1,0:T(2,128)(2,1)}), bf16[8,2,2048]{2,1,0:T(2,128)(2,1)S(1)}, u32[]{:S(2)}, u32[]{:S(2)}) %all-to-all-start) | async-done | bytes 65568 | tf_op jit(solution)/shard_map/all_to_all | solution.py:82
  122.4 0.2 reshape.572
  122.6 0.2 copy.83
  122.7 0.2 all_to_all.27
  122.9 0.1 rev.8
  123.0 0.2 fusion.13
  123.3 0.1 copy.44
  123.4 0.2 convolution_bitcast_fusion.1
  123.6 0.2 convolution_bitcast_fusion
  123.8 0.8 fusion.14
  124.6 0.1 copy.38
  124.7 0.2 convolution_bitcast_fusion.2
  124.9 0.2 convolution_bitcast_fusion.3
  125.1 0.1 fusion.35
  125.2 0.1 pad_maximum_fusion.6
  125.3 0.2 fusion.38
  125.5 0.1 fusion.33
  125.5 0.1 pad_maximum_fusion.7
  125.7 1.0 subtract_multiply_fusion
  126.6 0.1 multiply_convert_fusion.4
  126.7 0.1 rev.9
  126.9 5.8 %all_gather.3 = bf16[8,2,32,256]{3,2,1,0:T(8,128)(2,1)S(1)} all-gather(bf16[2,2,32,256]{3,2,1,0:T(8,128)(2,1)S(1)} %pad_maximum_fusion.5), channel_id=1, replica_groups=mesh['lat'=8,'lon'=4] {'lon'}, dimensions={0}, use_global_device_ids=true | all-gather | bytes 327680 | tf_op jit(solution)/shard_map/all_gather | solution.py:126
  132.6 0.9 copy.48
  133.6 1.6 %reshape.573 = bf16[8,2,8192]{2,1,0:T(2,128)(2,1)} reshape(bf16[256,8,2,32]{3,2,1,0:T(2,128)(2,1)S(1)} %bitcast.150) | data formatting | bytes 524288
  135.2 3.4 %all-to-all-start.1 = ((bf16[8,2,8192]{2,1,0:T(2,128)(2,1)}), bf16[8,2,8192]{2,1,0:T(2,128)(2,1)S(1)}, u32[]{:S(2)}, u32[]{:S(2)}) async-start(bf16[8,2,8192]{2,1,0:T(2,128)(2,1)} %reshape.573), calls=%async_computation.2 | async-start | bytes 524288 | tf_op jit(solution)/shard_map/all_to_all | solution.py:127
  138.7 0.3 copy.51
  139.0 0.2 convert_element_type.154
  139.2 9.1 %all-to-all-done.1 = bf16[8,2,8192]{2,1,0:T(2,128)(2,1)S(1)} async-done(((bf16[8,2,8192]{2,1,0:T(2,128)(2,1)}), bf16[8,2,8192]{2,1,0:T(2,128)(2,1)S(1)}, u32[]{:S(2)}, u32[]{:S(2)}) %all-to-all-start.1) | async-done | bytes 262176 | tf_op jit(solution)/shard_map/all_to_all | solution.py:127
  148.3 0.5 reshape.574
  148.8 1.2 copy.49
  150.0 1.1 reshape.561
  151.1 0.2 copy.50
  151.3 4.6 %fusion.8 = bf16[32,32,900]{2,1,0:T(8,128)(2,1)} fusion(bf16[32,32,900]{2,1,0:T(8,128)(2,1)} %copy-done.1, bf16[32,32,128]{2,1,0:T(8,128)(2,1)S(1)} %bitcast.160, bf16[128,900]{1,0:T(8,128)(2,1)S(1)} %convert_element_type.154), kind=kOutput, calls=%fused_computation.9 | convolution fusion | flops 246067200 | bytes 4178944 | tf_op jit(solution)/shard_map/dot_general | solution.py:132
  (32 shorter events, 0.1 us)
Async XLA Ops:
  6.5 40.5 %copy-start = (bf16[32,32,900]{2,1,0:T(8,128)(2,1)S(1)}, bf16[32,32,900]{2,1,0:T(8,128)(2,1)}, u32[]{:S(2)}) copy-start(bf16[32,32,900]{2,1,0:T(8,128)(2,1)} %param.7) | copy-start | bytes 5529604
  6.5 101.4 %reduce-scatter.2.cloned.1.call-start = ((), (), s32[]{:S(2)}) async-start(), calls=%async_computation.3 | async-start | bytes 2621440 | tf_op jit(solution)/shard_map/reduce_scatter | solution.py:76
  8.1 27.3 %collective-permute-start = (bf16[32,2,900]{2,1,0:T(2,128)(2,1)S(1)}, bf16[32,2,900]{2,1,0:T(2,128)(2,1)S(1)}, u32[]{:S(2)}, u32[]{:S(2)}) collective-permute-start(bf16[32,2,900]{2,1,0:T(2,128)(2,1)S(1)} %get-tuple-element.7), channel_id=1, source_target_pairs={{0,4},{4,8},{8,12},{12,16},{16,20},{20,24},{24,28},{1,5},{5,9},{9,... | collective-permute-start | bytes 345608 | tf_op jit(solution)/shard_map/ppermute | solution.py:20
  13.0 22.4 %collective-permute-start.1 = (bf16[32,2,900]{2,1,0:T(2,128)(2,1)S(1)}, bf16[32,2,900]{2,1,0:T(2,128)(2,1)S(1)}, u32[]{:S(2)}, u32[]{:S(2)}) collective-permute-start(bf16[32,2,900]{2,1,0:T(2,128)(2,1)S(1)} %get-tuple-element.8), channel_id=1, source_target_pairs={{4,0},{8,4},{12,8},{16,12},{20,16},{24,20},{28,24},{5,1},{9,5},{13... | collective-permute-start | bytes 345608 | tf_op jit(solution)/shard_map/ppermute | solution.py:22
  37.4 9.6 %collective-permute-start.2 = (bf16[32,36,2]{2,1,0:T(8,128)(2,1)}, bf16[32,36,2]{2,1,0:T(8,128)(2,1)S(1)}, u32[]{:S(2)}, u32[]{:S(2)}) collective-permute-start(bf16[32,36,2]{2,1,0:T(8,128)(2,1)} %get-tuple-element.5), channel_id=1, source_target_pairs={{0,1},{1,2},{2,3},{3,0},{4,5},{5,6},{6,7},{7,4},{8,9},{9,10},{10,1... | collective-permute-start | bytes 13832 | tf_op jit(solution)/shard_map/ppermute | solution.py:20
  37.4 9.6 %collective-permute-start.3 = (bf16[32,36,2]{2,1,0:T(8,128)(2,1)S(1)}, bf16[32,36,2]{2,1,0:T(8,128)(2,1)S(1)}, u32[]{:S(2)}, u32[]{:S(2)}) collective-permute-start(bf16[32,36,2]{2,1,0:T(8,128)(2,1)S(1)} %get-tuple-element.6), channel_id=1, source_target_pairs={{1,0},{2,1},{3,2},{0,3},{5,4},{6,5},{7,6},{4,7},{9,8},{10,9},{11,1... | collective-permute-start | bytes 13832 | tf_op jit(solution)/shard_map/ppermute | solution.py:22
  50.3 20.4 %copy-start.3 = (bf16[64,1,900]{2,0,1:T(8,128)(2,1)S(1)}, bf16[64,1,900]{2,0,1:T(8,128)(2,1)}, u32[]{:S(2)}) copy-start(bf16[64,1,900]{2,0,1:T(8,128)(2,1)} %get-tuple-element.28) | copy-start | bytes 345604
  50.3 20.4 %copy-start.4 = (bf16[64,1,900]{2,0,1:T(8,128)(2,1)S(1)}, bf16[64,1,900]{2,0,1:T(8,128)(2,1)}, u32[]{:S(2)}) copy-start(bf16[64,1,900]{2,0,1:T(8,128)(2,1)} %get-tuple-element.29) | copy-start | bytes 345604
  70.7 47.4 %copy-start.1 = (bf16[32,32,900]{2,1,0:T(8,128)(2,1)}, bf16[32,32,900]{2,1,0:T(8,128)(2,1)S(1)}, u32[]{:S(2)}) copy-start(bf16[32,32,900]{2,1,0:T(8,128)(2,1)S(1)} %add_convert_fusion) | copy-start | bytes 5529604
  70.7 3.2 %copy-start.8 = (s32[128]{0:T(128)S(1)}, s32[128]{0:T(128)}, u32[]{:S(2)}) copy-start(s32[128]{0:T(128)} %param.12) | copy-start | bytes 1540
  70.7 3.2 %copy-start.9 = (f32[128]{0:T(128)S(1)}, f32[128]{0:T(128)}, u32[]{:S(2)}) copy-start(f32[128]{0:T(128)} %param.11) | copy-start | bytes 1540
  70.8 3.3 %copy-start.5 = (bf16[2,64,128]{2,1,0:T(8,128)(2,1)S(1)}, bf16[2,64,128]{2,1,0:T(8,128)(2,1)}, u32[]{:S(2)}) copy-start(bf16[2,64,128]{2,1,0:T(8,128)(2,1)} %param.10) | copy-start | bytes 98308
  109.0 14.0 %copy-start.7 = (bf16[2,32,1,128]{3,2,1,0:T(2,128)(2,1)S(1)}, bf16[2,32,1,128]{3,2,1,0:T(2,128)(2,1)}, u32[]{:S(2)}) copy-start(bf16[2,32,1,128]{3,2,1,0:T(2,128)(2,1)} %get-tuple-element.14) | copy-start | bytes 49156
  109.1 14.7 %copy-start.6 = (bf16[2,32,1,128]{3,2,1,0:T(2,128)(2,1)S(1)}, bf16[2,32,1,128]{3,2,1,0:T(2,128)(2,1)}, u32[]{:S(2)}) copy-start(bf16[2,32,1,128]{3,2,1,0:T(2,128)(2,1)} %get-tuple-element.13) | copy-start | bytes 49156
  110.0 12.4 %all-to-all-start = ((bf16[8,2,2048]{2,1,0:T(2,128)(2,1)}), bf16[8,2,2048]{2,1,0:T(2,128)(2,1)S(1)}, u32[]{:S(2)}, u32[]{:S(2)}) async-start(bf16[8,2,2048]{2,1,0:T(2,128)(2,1)} %reshape.571), calls=%async_computation.1 | async-start | bytes 131072 | tf_op jit(solution)/shard_map/all_to_all | solution.py:82
  118.6 4.7 %copy-start.11 = (pred[2]{0:T(512)(128)(4,1)}, pred[2]{0:T(512)(128)(4,1)S(1)}, u32[]{:S(2)}) copy-start(pred[2]{0:T(512)(128)(4,1)S(1)} %get-tuple-element.53) | copy-start | bytes 10
  118.6 7.0 %copy-start.10 = (pred[2]{0:T(512)(128)(4,1)S(1)}, pred[2]{0:T(512)(128)(4,1)}, u32[]{:S(2)}) copy-start(pred[2]{0:T(512)(128)(4,1)} %get-tuple-element.52) | copy-start | bytes 10
  123.4 3.3 %copy-start.12 = (pred[2]{0:T(512)(128)(4,1)S(1)}, pred[2]{0:T(512)(128)(4,1)}, u32[]{:S(2)}) copy-start(pred[2]{0:T(512)(128)(4,1)} %copy-done.11) | copy-start | bytes 10
  124.9 13.8 %copy-start.2 = (bf16[64,1,900]{2,0,1:T(8,128)(2,1)S(1)}, bf16[64,1,900]{2,0,1:T(8,128)(2,1)}, u32[]{:S(2)}) copy-start(bf16[64,1,900]{2,0,1:T(8,128)(2,1)} %get-tuple-element.27) | copy-start | bytes 345604
  135.2 13.1 %all-to-all-start.1 = ((bf16[8,2,8192]{2,1,0:T(2,128)(2,1)}), bf16[8,2,8192]{2,1,0:T(2,128)(2,1)S(1)}, u32[]{:S(2)}, u32[]{:S(2)}) async-start(bf16[8,2,8192]{2,1,0:T(2,128)(2,1)} %reshape.573), calls=%async_computation.2 | async-start | bytes 524288 | tf_op jit(solution)/shard_map/all_to_all | solution.py:127
Sparse Core Ops, SparseCore 0:
  74.0 33.8 reduce-scatter.1
where the time goes:
time: 164 us; the launch traced here: 163 us
  waiting for transfers between devices  46.1 us (28%)
  between operations  36.5 us (22%)
  other arithmetic  31.2 us (19%)
  starting transfers between devices  16.8 us (10%)
  local copies, waits for them, and re-layouts  15.7 us (10%)
  matrix products  10.7 us (7%)
  blocking collectives  5.79 us (4%)
    reduce_scatter x1, waiting for transfers between devices, per_device(): lax.psum_scatter(summand.reshape(quarter * lax.axis_size('lon'), 2, chann...  33.1 us
    convert_element_type x1, other arithmetic, per_device(): conv_out = running.astype(jnp.bfloat16)  20.3 us
    all_to_all x1, waiting for transfers between devices, per_device(): lax.all_to_all(pooled, 'lat', split_axis=3, concat_axis=0, tiled=True)  9.14 us
    unnamed x31, local copies, waits for them, and re-layouts  5.8 us
    all_gather x1, blocking collectives, per_device(): pooled = lax.all_gather(grid_spectrum, 'lon', axis=0, tiled=True)  5.79 us
    all_to_all x1, starting transfers between devices, per_device(): lax.all_to_all(spectrum_part, 'lat', split_axis=0, concat_axis=3, tiled=T...  5.5 us
    ppermute x2, starting transfers between devices, padded(): lax.ppermute(tail, axis, [(i, (i + 1) % count) for i in range(ends)])  4.88 us
    dot_general x1, matrix products, per_device(): lax.dot_general(spectral_rows, wave_rows, (((0,), (0,)), ((), ())), prefe...  4.64 us
  transfers between devices with their start and end apart: 7, of which 3 were waited for; matrix products, arithmetic and copies ran while one was open for 7% of the time, Pallas kernels for 0%

commit v1 on v0

v1 whole, which is shorter than its diff:
```python
import math

import jax
import jax.numpy as jnp
from jax import lax
from jax.sharding import PartitionSpec as P

KTAPS = 9
BOTH = ("lat", "lon")


def padded(cells, sides, width, closed):
    for axis, dim in sides:
        count = lax.axis_size(axis)
        ends = count if closed else count - 1
        head = lax.slice_in_dim(cells, 0, width, axis=dim)
        tail = lax.slice_in_dim(cells, cells.shape[dim] - width, cells.shape[dim], axis=dim)
        cells = jnp.concatenate(
            [
                lax.ppermute(tail, axis, [(i, (i + 1) % count) for i in range(ends)]),
                cells,
                lax.ppermute(head, axis, [((i + 1) % count, i) for i in range(ends)]),
            ],
            axis=dim,
        )
    return cells


def wave_table(orders, points, period, inverse_form):
    angles = (orders[:, None] * points[None, :] % period).astype(jnp.float32) * (
        2.0 * math.pi / period
    )
    factor = jnp.full(orders.shape, 1.0 / math.sqrt(period), jnp.float32)
    if inverse_form:
        factor = jnp.where(orders == 0, 1.0, 2.0).astype(jnp.float32) * factor
    stacked = jnp.stack(
        [factor[:, None] * jnp.cos(angles), -factor[:, None] * jnp.sin(angles)], axis=1
    )
    return stacked.astype(jnp.bfloat16)


def per_device(field, offsets, conv_weight, legendre, quad_weight, band_limit, mix_weight):
    channels, lat_rows, lon_cols = field.shape
    m_dev = legendre.shape[0]
    lon_count = lax.axis_size("lon")
    lat_count = lax.axis_size("lat")
    n_dev = lon_count * lat_count
    total_lon = lon_cols * lon_count
    total_lat = lat_rows * lat_count
    half_rows = total_lat // 2
    orders_all = m_dev * n_dev
    lon_points = lax.axis_index("lon") * lon_cols + lax.iota(jnp.int32, lon_cols)
    me = lax.axis_index("lat") * lon_count + lax.axis_index("lon")
    mine = me * m_dev + lax.iota(jnp.int32, m_dev)

    forward_rows = wave_table(
        lax.iota(jnp.int32, orders_all), lon_points, total_lon, False
    ).reshape(orders_all * 2, lon_cols)
    flat_field = field.reshape(channels * lat_rows, lon_cols)
    partial = lax.dot_general(
        forward_rows, flat_field, (((1,), (1,)), ((), ())), preferred_element_type=jnp.float32
    ).reshape(n_dev, m_dev, 2, channels, lat_rows)
    gathered = lax.all_to_all(partial, BOTH, 0, 0, tiled=True)
    summed = gathered.reshape(lat_count, lon_count, m_dev, 2, channels, lat_rows).sum(axis=1)
    raw_spec = jnp.transpose(summed, (1, 2, 3, 0, 4)).reshape(m_dev, 2, channels, total_lat)

    rim = jnp.pad(raw_spec, ((0, 0), (0, 0), (0, 0), (2, 2)))
    spec_acc = jnp.zeros(raw_spec.shape, jnp.float32)
    for tap_index in range(KTAPS):
        window = lax.dynamic_slice_in_dim(rim, 2 + offsets[tap_index, 0], total_lat, axis=3)
        turn = ((mine * offsets[tap_index, 1]) % total_lon).astype(jnp.float32) * (
            2.0 * math.pi / total_lon
        )
        cos_t = jnp.cos(turn)[:, None, None]
        sin_t = jnp.sin(turn)[:, None, None]
        real_part = cos_t * window[:, 0] - sin_t * window[:, 1]
        imag_part = sin_t * window[:, 0] + cos_t * window[:, 1]
        tap_w = conv_weight[:, tap_index][None, None, :, None]
        spec_acc = spec_acc + tap_w * jnp.stack([real_part, imag_part], axis=1)
    spectrum = spec_acc.astype(jnp.bfloat16)

    north_part = spectrum[..., :half_rows].astype(jnp.float32)
    south_part = jnp.flip(spectrum[..., half_rows:], axis=3).astype(jnp.float32)
    kept_mask = (mine[:, None] < band_limit[None, :]).astype(jnp.float32)
    weight_q = quad_weight[None, :] * kept_mask * (1.0 / math.sqrt(half_rows))
    even_terms = (weight_q[:, None, None, :] * (north_part + south_part)).astype(jnp.bfloat16)
    odd_terms = (weight_q[:, None, None, :] * (north_part - south_part)).astype(jnp.bfloat16)
    paired = legendre.reshape(m_dev, orders_all // 2, 2, half_rows)
    mix_pairs = mix_weight.reshape(2, orders_all // 2, 2, channels, channels)
    even_sum = jnp.zeros((m_dev, 2, channels, half_rows), jnp.float32)
    odd_sum = jnp.zeros((m_dev, 2, channels, half_rows), jnp.float32)
    for parity in range(2):
        same_parity = ((parity + mine) % 2 == 0)[:, None, None, None]
        operand = jnp.where(same_parity, even_terms, odd_terms)
        degree_plane = paired[:, :, parity]
        coeffs = jnp.einsum(
            "mui,mpci->mupc", degree_plane, operand, preferred_element_type=jnp.float32
        )
        degrees = 2 * lax.iota(jnp.int32, orders_all // 2) + parity
        triangle = (degrees[None, :] >= mine[:, None]).astype(jnp.float32)
        coeffs = (coeffs * triangle[:, :, None, None]).astype(jnp.bfloat16)
        with_real = jnp.einsum(
            "mupc,ucd->mupd", coeffs, mix_pairs[0, :, parity], preferred_element_type=jnp.float32
        )
        with_imag = jnp.einsum(
            "mupc,ucd->mupd", coeffs, mix_pairs[1, :, parity], preferred_element_type=jnp.float32
        )
        mixed = jnp.stack(
            [with_real[:, :, 0] - with_imag[:, :, 1], with_real[:, :, 1] + with_imag[:, :, 0]],
            axis=2,
        ).astype(jnp.bfloat16)
        returned = jnp.einsum(
            "mui,mupc->mpci", degree_plane, mixed, preferred_element_type=jnp.float32
        )
        even_sum = even_sum + jnp.where(same_parity, returned, 0.0)
        odd_sum = odd_sum + jnp.where(same_parity, 0.0, returned)
    north_out = (even_sum + odd_sum) * kept_mask[:, None, None, :]
    south_out = (even_sum - odd_sum) * kept_mask[:, None, None, :]
    grid_spectrum = jnp.concatenate([north_out, jnp.flip(south_out, axis=3)], axis=3).astype(
        jnp.bfloat16
    )

    by_group = jnp.transpose(
        grid_spectrum.reshape(m_dev, 2, channels, lat_count, lat_rows), (3, 0, 1, 2, 4)
    )
    outgoing = jnp.broadcast_to(
        by_group[:, None], (lat_count, lon_count, m_dev, 2, channels, lat_rows)
    ).reshape(n_dev, m_dev, 2, channels, lat_rows)
    full_rows = lax.all_to_all(outgoing, BOTH, 0, 0, tiled=True)
    spectral_rows = full_rows.reshape(orders_all * 2, channels * lat_rows)
    inverse_rows = wave_table(
        lax.iota(jnp.int32, orders_all), lon_points, total_lon, True
    ).reshape(orders_all * 2, lon_cols)
    synthesis = lax.dot_general(
        spectral_rows, inverse_rows, (((0,), (0,)), ((), ())), preferred_element_type=jnp.float32
    ).reshape(channels, lat_rows, lon_cols)

    rimmed = padded(field, (("lat", 1),), 2, False)
    rimmed = padded(rimmed, (("lon", 2),), 2, True)
    running = jnp.zeros(field.shape, jnp.float32)
    for tap_index in range(KTAPS):
        window = lax.dynamic_slice(
            rimmed,
            (jnp.int32(0), 2 + offsets[tap_index, 0], 2 + offsets[tap_index, 1]),
            field.shape,
        )
        running = running + conv_weight[:, tap_index][:, None, None] * window.astype(jnp.float32)
    conv_out = running.astype(jnp.bfloat16)
    return (conv_out.astype(jnp.float32) + jax.nn.gelu(synthesis, approximate=True)).astype(
        jnp.bfloat16
    )


def solution(mesh):
    placed = (P(None, "lat", "lon"), P(), P(), P(BOTH, None, None), P(), P(), P())
    return jax.shard_map(
        per_device, mesh=mesh, in_specs=placed, out_specs=P(None, "lat", "lon"), check_vma=False
    )
```

time: 164 us -> 137 us (0.84)
  waiting for transfers between devices: 46.1 us -> 0.02 us
  matrix products: 10.7 us -> 33.4 us
  between operations: 36.5 us -> 28.3 us
  blocking collectives: 5.79 us -> 0 us
  local copies, waits for them, and re-layouts: 15.7 us -> 20.3 us
  starting transfers between devices: 16.8 us -> 20.9 us
    reduce_scatter x1 -> x0, waiting for transfers between devices: 33.1 us -> none  [per_device(): lax.psum_scatter(summand.reshape(quarter * lax.axis_size('lon'), 2, chann...]
    convert_element_type x2 -> x1, other arithmetic: 21.4 us -> 0.84 us  [per_device(): spectrum = spec_acc.astype(jnp.bfloat16)]
    dot_general x2, matrix products: 7.73 us -> 26 us  [the longest x1 22.7 us: per_device(): lax.dot_general(spectral_rows, inverse_rows, (((0,), (0,)), ((), ())), pr...]
    all_to_all x2, waiting for transfers between devices: 12.9 us -> 0.01 us  [the longest x1 0.01 us: per_device(): gathered = lax.all_to_all(partial, BOTH, 0, 0, tiled=True)]
    sin x0 -> x9, other arithmetic: none -> 11.4 us  [per_device(): sin_t = jnp.sin(turn)[:, None, None]]
    all_gather x1 -> x0, blocking collectives: 5.79 us -> none  [per_device(): pooled = lax.all_gather(grid_spectrum, 'lon', axis=0, tiled=True)]
    all_to_all x2, starting transfers between devices: 8.91 us -> 14 us  [the longest x1 7.32 us: per_device(): gathered = lax.all_to_all(partial, BOTH, 0, 0, tiled=True)]
    unnamed x31 -> x39, local copies, waits for them, and re-layouts: 5.8 us -> 9.92 us
  transfers between devices with their start and end apart: 7 -> 6, of which waited for: 3 -> 0; matrix products, arithmetic and copies ran while one was open for 7% -> 38% of each run, Pallas kernels for 0% -> 0%
where the time goes in v1:
time: 137 us; the launch traced here: 136 us
  matrix products  33.4 us (24%)
  other arithmetic  32.7 us (24%)
  between operations  28.3 us (21%)
  starting transfers between devices  20.9 us (15%)
  local copies, waits for them, and re-layouts  20.3 us (15%)
    dot_general x1, matrix products, per_device(): lax.dot_general(spectral_rows, inverse_rows, (((0,), (0,)), ((), ())), pr...  22.7 us
    sin x9, other arithmetic, per_device(): sin_t = jnp.sin(turn)[:, None, None]  11.4 us
    unnamed x39, local copies, waits for them, and re-layouts  9.92 us
    all_to_all x1, starting transfers between devices, per_device(): gathered = lax.all_to_all(partial, BOTH, 0, 0, tiled=True)  7.32 us
    all_to_all x1, starting transfers between devices, per_device(): full_rows = lax.all_to_all(outgoing, BOTH, 0, 0, tiled=True)  6.71 us
    concatenate x1, other arithmetic, padded(): jnp.concatenate([lax.ppermute(tail, axis, [(i, (i + 1) % count) for i in...  5.3 us
    another operation x5, other arithmetic  4.86 us
    ppermute x2, starting transfers between devices, padded(): lax.ppermute(tail, axis, [(i, (i + 1) % count) for i in range(ends)])  3.92 us
  transfers between devices with their start and end apart: 6, of which 0 were waited for; matrix products, arithmetic and copies ran while one was open for 38% of the time, Pallas kernels for 0%

profile of v1, /device:TPU:0, one launch (start us, length us, event | category | flops | bytes accessed | tf_op | source)
XLA Modules:
  0.0 135.6 jit_solution(7839105453023283452)
XLA Ops:
  0.0 1.3 multiply_convert_fusion.3
  1.3 3.3 %fusion.9 = f32[32,2,2,32,32]{4,0,3,2,1:T(8,128)S(1)} fusion(bf16[32,32,900]{2,1,0:T(8,128)(2,1)} %param.7, bf16[32,2,1,900]{3,0,2,1:T(8,128)(2,1)S(1)} %get-tuple-element.55, bf16[32,2,1,900]{3,0,2,1:T(8,128)(2,1)S(1)} %get-tuple-element.54), kind=kOutput, calls=%fused_computation.12 | convolution fusion | flops 236390400 | bytes 2597888 | tf_op jit(solution)/shard_map/dot_general | solution.py:60
  4.6 2.5 %copy.66 = f32[32,2,2,32,32]{4,3,2,1,0:T(8,128)} copy(f32[32,2,2,32,32]{4,0,3,2,1:T(8,128)S(1)} %fusion.9) | data formatting | bytes 1048576 | tf_op jit(solution)/shard_map/dot_general | solution.py:60
  7.2 3.3 %reshape.616 = f32[32,1,4096]{2,1,0:T(1,128)} reshape(f32[32,2,2,32,32]{4,3,2,1,0:T(8,128)} %copy.66) | data formatting | bytes 1048576
  10.5 7.3 %all-to-all-start = ((f32[32,1,4096]{2,1,0:T(1,128)}), f32[32,1,4096]{2,1,0:T(1,128)S(1)}, u32[]{:S(2)}, u32[]{:S(2)}) async-start(f32[32,1,4096]{2,1,0:T(1,128)} %reshape.616), calls=%async_computation | async-start | bytes 1048576 | tf_op jit(solution)/shard_map/all_to_all | solution.py:63
  17.8 0.9 fusion.104
  18.7 3.7 %collective-permute-start = (bf16[32,2,900]{2,1,0:T(2,128)(2,1)}, bf16[32,2,900]{2,1,0:T(2,128)(2,1)S(1)}, u32[]{:S(2)}, u32[]{:S(2)}) collective-permute-start(bf16[32,2,900]{2,1,0:T(2,128)(2,1)} %get-tuple-element.7), channel_id=1, source_target_pairs={{0,4},{4,8},{8,12},{12,16},{16,20},{20,24},{24,28},{1,5},{5,9},{9,... | collective-permute-start | bytes 345608 | tf_op jit(solution)/shard_map/ppermute | solution.py:20
  22.4 1.5 %collective-permute-start.1 = (bf16[32,2,900]{2,1,0:T(2,128)(2,1)}, bf16[32,2,900]{2,1,0:T(2,128)(2,1)S(1)}, u32[]{:S(2)}, u32[]{:S(2)}) collective-permute-start(bf16[32,2,900]{2,1,0:T(2,128)(2,1)} %get-tuple-element.8), channel_id=1, source_target_pairs={{4,0},{8,4},{12,8},{16,12},{20,16},{24,20},{28,24},{5,1},{9,5},{13... | collective-permute-start | bytes 345608 | tf_op jit(solution)/shard_map/ppermute | solution.py:22
  23.9 0.7 fusion.106
  35.4 0.6 fusion.61
  36.0 1.3 fusion.102
  37.2 1.3 fusion.86
  38.6 1.3 fusion.100
  39.9 1.3 fusion.88
  41.2 1.2 fusion.96
  42.3 1.2 fusion.98
  43.6 1.3 fusion.90
  44.8 1.2 fusion.92
  46.1 0.6 fusion.60
  46.8 2.4 %copy.69 = bf16[2,64,32,32]{3,2,1,0:T(8,128)(2,1)} copy(bf16[2,64,32,32]{1,3,2,0:T(8,128)(2,1)S(1)} %copy-done.2) | data formatting | bytes 524288 | tf_op args[6]
  49.1 1.3 fusion.94
  50.5 0.6 compare_convert_fusion.2
  51.1 0.6 slice_bitcast_fusion.16
  51.7 0.7 fusion.105
  52.4 1.8 %multiply_convert_fusion.1 = (bf16[64,1,900]{2,0,1:T(8,128)(2,1)}, bf16[64,1,900]{2,0,1:T(8,128)(2,1)}) fusion(s32[900]{0:T(1024)S(1)} %iota_add_fusion, f32[64]{0:T(128)S(1)} %get-tuple-element.82, f32[64]{0:T(128)S(1)} %get-tuple-element.83), kind=kLoop, calls=%fused_computation.64 | loop fusion | flops 748800 | bytes 234512 | tf_op jit(solution)/shard_map/convert
  54.2 0.5 broadcast.1032
  54.7 1.9 %reduce = f32[32,4096]{1,0:T(8,128)S(1)} reduce(f32[32,1,4096]{2,1,0:T(1,128)S(1)} %all-to-all-done, f32[]{:T(128)} %broadcast.1032), dimensions={1}, to_apply=%all_to_all.6.reduce_sub_computation | reduce | bytes 1048580 | tf_op jit(solution)/shard_map/all_to_all | solution.py:63
  56.6 2.0 %reshape.617 = f32[32,2,2,32,32]{4,3,2,1,0:T(8,128)} reshape(f32[32,4096]{1,0:T(8,128)S(1)} %reduce) | data formatting | bytes 1048576
  58.6 1.9 %bitcast_reduce_fusion = f32[8,2,2,32,32]{4,3,2,1,0:T(8,128)S(1)} fusion(f32[32,2,2,32,32]{4,3,2,1,0:T(8,128)} %reshape.617), kind=kLoop, calls=%fused_computation.14 | loop fusion | flops 98304 | bytes 655360 | tf_op jit(solution)/shard_map/reduce_sum | solution.py:64
  60.5 0.3 copy.67
  60.8 0.2 reshape.602
  61.0 1.1 multiply_subtract_fusion
  62.1 1.0 multiply_subtract_fusion.1
  63.1 1.0 multiply_subtract_fusion.2
  64.1 0.8 fusion.39
  65.1 1.0 fusion.13
  66.1 0.7 copy.77
  66.8 1.0 convolution_bitcast_fusion.1
  67.7 1.6 %convolution_bitcast_fusion = f32[2,32,2,32]{3,2,0,1:T(2,128)} fusion(bf16[2,32,2,32]{3,2,0,1:T(2,128)(2,1)} %copy.77, bf16[2,32,2,32,32]{4,3,2,1,0:T(8,128)(2,1)S(1)} %bitcast.160), kind=kOutput, calls=%fused_computation.15 | convolution fusion | flops 262144 | bytes 286720 | tf_op jit(solution)/shard_map/mupc,ucd->mupd/dot_general | solution.py:105
  69.3 1.6 %fusion.14 = bf16[2,32,2,32]{1,3,2,0:T(8,128)(2,1)} fusion(f32[2,32]{1,0:T(2,128)} %get-tuple-element.76, pred[2]{0:T(512)(128)(4,1)} %get-tuple-element.80, bf16[2,32,1,128]{3,2,1,0:T(2,128)(2,1)} %get-tuple-element.43, bf16[2,2,32,128]{3,2,1,0:T(8,128)(2,1)} %copy-done.7, f32[2,128]{1,0:T(2,128)} %fusion.60, bf16[2,2,32,256]{3,2,1,0:T(8,128)(2,1)S(1)} %fusion.39), kind=kOutput, calls=%fused_computation.24 | convolution fusion | flops 1204224 | bytes 91394 | tf_op jit(solution)/shard_map/mui,mpci->mupc/dot_general | solution.py:96
  70.9 0.8 copy.71
  71.7 0.2 convolution_bitcast_fusion.2
  71.9 0.2 convolution_bitcast_fusion.3
  72.2 0.1 pad_maximum_fusion.5
  72.3 1.0 fusion.50
  73.2 1.0 fusion.45
  74.3 1.0 subtract_multiply_fusion
  75.3 0.8 multiply_convert_fusion.4
  76.1 0.1 concatenate.19
  76.3 0.1 concatenate.20
  76.4 0.2 maximum_bitcast_fusion.2
  76.6 0.2 broadcast_in_dim.52
  76.9 1.7 %reshape.618 = bf16[32,2,2048]{2,1,0:T(2,128)(2,1)} reshape(bf16[32,2,2,32,32]{4,3,2,1,0:T(8,128)(2,1)S(1)} %bitcast.156) | data formatting | bytes 524288
  78.6 6.7 %all-to-all-start.1 = ((bf16[32,2,2048]{2,1,0:T(2,128)(2,1)}), bf16[32,2,2048]{2,1,0:T(2,128)(2,1)S(1)}, u32[]{:S(2)}, u32[]{:S(2)}) async-start(bf16[32,2,2048]{2,1,0:T(2,128)(2,1)} %reshape.618), calls=%async_computation.1 | async-start | bytes 524288 | tf_op jit(solution)/shard_map/all_to_all | solution.py:129
  85.3 1.1 pad_maximum_fusion.3
  86.4 0.3 collective-permute-start.2
  86.7 1.5 %collective-permute-start.3 = (bf16[32,36,2]{2,1,0:T(8,128)(2,1)}, bf16[32,36,2]{2,1,0:T(8,128)(2,1)}, u32[]{:S(2)}, u32[]{:S(2)}) collective-permute-start(bf16[32,36,2]{2,1,0:T(8,128)(2,1)} %get-tuple-element.6), channel_id=1, source_target_pairs={{1,0},{2,1},{3,2},{0,3},{5,4},{6,5},{7,6},{4,7},{9,8},{10,9},{11,1... | collective-permute-start | bytes 13832 | tf_op jit(solution)/shard_map/ppermute | solution.py:22
  105.2 0.3 copy.83
  105.5 0.2 convert_element_type.257
  105.7 5.3 %pad_maximum_fusion = bf16[32,36,904]{2,1,0:T(8,128)(2,1)} fusion(bf16[32,36,2]{2,1,0:T(8,128)(2,1)} %collective-permute-done.3, bf16[32,2,900]{2,1,0:T(2,128)(2,1)S(1)} %collective-permute-done.1, bf16[32,32,900]{2,1,0:T(8,128)(2,1)S(1)} %copy-done, bf16[32,2,900]{2,1,0:T(2,128)(2,1)S(1)} %collective-permute-done, bf16[32,36,2]{2,1,0:T(8,128)(2,1)} %collective-permute-done.2), kind=kLoop, calls=%fused_computation.11 | loop fusion | flops 10414080 | bytes 4165632 | tf_op jit(solution)/shard_map/concatenate | solution.py:18
  111.1 0.5 reshape.619
  111.6 1.1 reshape.606
  112.7 0.2 copy.82
  112.9 22.7 %fusion.8 = bf16[32,32,900]{2,1,0:T(8,128)(2,1)} fusion(bf16[32,36,904]{2,1,0:T(8,128)(2,1)} %pad_maximum_fusion, s32[]{:T(128)S(6)} %select_n.282, s32[]{:T(128)S(6)} %select_n.283, f32[32]{0:T(128)S(1)} %copy-done.13, s32[]{:T(128)S(6)} %select_n.280, s32[]{:T(128)S(6)} %select_n.281, f32[32]{0:T(128)S(1)} %copy-done.14, s32[]{:T(128)S(6)} %select_n.278, ...), kind=kOutput, calls=%fused_computation.9 | convolution fusion | flops 270950400 | bytes 18925768 | tf_op jit(solution)/shard_map/dot_general | solution.py:134
  (53 shorter events, 0.6 us)
Async XLA Ops:
  7.1 10.6 %copy-start = (bf16[32,32,900]{2,1,0:T(8,128)(2,1)S(1)}, bf16[32,32,900]{2,1,0:T(8,128)(2,1)}, u32[]{:S(2)}) copy-start(bf16[32,32,900]{2,1,0:T(8,128)(2,1)} %param.7) | copy-start | bytes 5529604
  7.1 16.7 %copy-start.6 = (s32[9,2]{0,1:T(2,128)S(1)}, s32[9,2]{0,1:T(2,128)}, u32[]{:S(2)}) copy-start(s32[9,2]{0,1:T(2,128)} %param.8) | copy-start | bytes 220
  7.1 38.9 %copy-start.15 = (s32[128]{0:T(128)S(1)}, s32[128]{0:T(128)}, u32[]{:S(2)}) copy-start(s32[128]{0:T(128)} %param.12) | copy-start | bytes 1540
  7.1 39.0 %copy-start.16 = (f32[128]{0:T(128)S(1)}, f32[128]{0:T(128)}, u32[]{:S(2)}) copy-start(f32[128]{0:T(128)} %param.11) | copy-start | bytes 1540
  7.1 39.6 %copy-start.2 = (bf16[2,64,32,32]{1,3,2,0:T(8,128)(2,1)S(1)}, bf16[2,64,32,32]{1,3,2,0:T(8,128)(2,1)}, u32[]{:S(2)}) copy-start(bf16[2,64,32,32]{1,3,2,0:T(8,128)(2,1)} %param.13) | copy-start | bytes 786436
  7.2 44.0 %copy-start.8 = (f32[32,9]{0,1:T(8,128)S(1)}, f32[32,9]{0,1:T(8,128)}, u32[]{:S(2)}) copy-start(f32[32,9]{0,1:T(8,128)} %param.9) | copy-start | bytes 3460
  7.2 44.6 %copy-start.5 = (bf16[2,64,128]{2,1,0:T(8,128)(2,1)S(1)}, bf16[2,64,128]{2,1,0:T(8,128)(2,1)}, u32[]{:S(2)}) copy-start(bf16[2,64,128]{2,1,0:T(8,128)(2,1)} %param.10) | copy-start | bytes 98308
  10.5 43.7 %all-to-all-start = ((f32[32,1,4096]{2,1,0:T(1,128)}), f32[32,1,4096]{2,1,0:T(1,128)S(1)}, u32[]{:S(2)}, u32[]{:S(2)}) async-start(f32[32,1,4096]{2,1,0:T(1,128)} %reshape.616), calls=%async_computation | async-start | bytes 1048576 | tf_op jit(solution)/shard_map/all_to_all | solution.py:63
  18.7 66.6 %collective-permute-start = (bf16[32,2,900]{2,1,0:T(2,128)(2,1)}, bf16[32,2,900]{2,1,0:T(2,128)(2,1)S(1)}, u32[]{:S(2)}, u32[]{:S(2)}) collective-permute-start(bf16[32,2,900]{2,1,0:T(2,128)(2,1)} %get-tuple-element.7), channel_id=1, source_target_pairs={{0,4},{4,8},{8,12},{12,16},{16,20},{20,24},{24,28},{1,5},{5,9},{9,... | collective-permute-start | bytes 345608 | tf_op jit(solution)/shard_map/ppermute | solution.py:20
  22.4 63.0 %collective-permute-start.1 = (bf16[32,2,900]{2,1,0:T(2,128)(2,1)}, bf16[32,2,900]{2,1,0:T(2,128)(2,1)S(1)}, u32[]{:S(2)}, u32[]{:S(2)}) collective-permute-start(bf16[32,2,900]{2,1,0:T(2,128)(2,1)} %get-tuple-element.8), channel_id=1, source_target_pairs={{4,0},{8,4},{12,8},{16,12},{20,16},{24,20},{28,24},{5,1},{9,5},{13... | collective-permute-start | bytes 345608 | tf_op jit(solution)/shard_map/ppermute | solution.py:22
  61.0 5.7 %copy-start.1 = (bf16[2,64,32,32]{3,2,1,0:T(8,128)(2,1)S(1)}, bf16[2,64,32,32]{3,2,1,0:T(8,128)(2,1)}, u32[]{:S(2)}) copy-start(bf16[2,64,32,32]{3,2,1,0:T(8,128)(2,1)} %copy.69) | copy-start | bytes 786436
  65.1 1.7 %copy-start.7 = (bf16[2,2,32,128]{3,2,1,0:T(8,128)(2,1)}, bf16[2,2,32,128]{3,2,1,0:T(8,128)(2,1)S(1)}, u32[]{:S(2)}) copy-start(bf16[2,2,32,128]{3,2,1,0:T(8,128)(2,1)S(1)} %rev.8) | copy-start | bytes 98308
  76.9 11.3 %copy-start.3 = (bf16[64,1,900]{2,0,1:T(8,128)(2,1)S(1)}, bf16[64,1,900]{2,0,1:T(8,128)(2,1)}, u32[]{:S(2)}) copy-start(bf16[64,1,900]{2,0,1:T(8,128)(2,1)} %get-tuple-element.56) | copy-start | bytes 345604
  78.6 9.6 %copy-start.4 = (bf16[64,1,900]{2,0,1:T(8,128)(2,1)S(1)}, bf16[64,1,900]{2,0,1:T(8,128)(2,1)}, u32[]{:S(2)}) copy-start(bf16[64,1,900]{2,0,1:T(8,128)(2,1)} %get-tuple-element.57) | copy-start | bytes 345604
  78.6 32.4 %all-to-all-start.1 = ((bf16[32,2,2048]{2,1,0:T(2,128)(2,1)}), bf16[32,2,2048]{2,1,0:T(2,128)(2,1)S(1)}, u32[]{:S(2)}, u32[]{:S(2)}) async-start(bf16[32,2,2048]{2,1,0:T(2,128)(2,1)} %reshape.618), calls=%async_computation.1 | async-start | bytes 524288 | tf_op jit(solution)/shard_map/all_to_all | solution.py:129
  86.4 19.3 %collective-permute-start.2 = (bf16[32,36,2]{2,1,0:T(8,128)(2,1)}, bf16[32,36,2]{2,1,0:T(8,128)(2,1)}, u32[]{:S(2)}, u32[]{:S(2)}) collective-permute-start(bf16[32,36,2]{2,1,0:T(8,128)(2,1)} %get-tuple-element.5), channel_id=1, source_target_pairs={{0,1},{1,2},{2,3},{3,0},{4,5},{5,6},{6,7},{7,4},{8,9},{9,10},{10,1... | collective-permute-start | bytes 13832 | tf_op jit(solution)/shard_map/ppermute | solution.py:20
  86.7 19.0 %collective-permute-start.3 = (bf16[32,36,2]{2,1,0:T(8,128)(2,1)}, bf16[32,36,2]{2,1,0:T(8,128)(2,1)}, u32[]{:S(2)}, u32[]{:S(2)}) collective-permute-start(bf16[32,36,2]{2,1,0:T(8,128)(2,1)} %get-tuple-element.6), channel_id=1, source_target_pairs={{1,0},{2,1},{3,2},{0,3},{5,4},{6,5},{7,6},{4,7},{9,8},{10,9},{11,1... | collective-permute-start | bytes 13832 | tf_op jit(solution)/shard_map/ppermute | solution.py:22
  111.0 1.8 %copy-start.9 = (f32[32]{0:T(128)S(1)}, f32[32]{0:T(128)}, u32[]{:S(2)}) copy-start(f32[32]{0:T(128)} %get-tuple-element.48) | copy-start | bytes 388
  111.0 1.8 %copy-start.10 = (f32[32]{0:T(128)S(1)}, f32[32]{0:T(128)}, u32[]{:S(2)}) copy-start(f32[32]{0:T(128)} %get-tuple-element.49) | copy-start | bytes 388
  111.0 1.8 %copy-start.11 = (f32[32]{0:T(128)S(1)}, f32[32]{0:T(128)}, u32[]{:S(2)}) copy-start(f32[32]{0:T(128)} %get-tuple-element.50) | copy-start | bytes 388
  111.0 1.9 %copy-start.12 = (f32[32]{0:T(128)S(1)}, f32[32]{0:T(128)}, u32[]{:S(2)}) copy-start(f32[32]{0:T(128)} %get-tuple-element.51) | copy-start | bytes 388
  111.0 1.9 %copy-start.13 = (f32[32]{0:T(128)S(1)}, f32[32]{0:T(128)}, u32[]{:S(2)}) copy-start(f32[32]{0:T(128)} %get-tuple-element.52) | copy-start | bytes 388
  111.0 1.9 %copy-start.14 = (f32[32]{0:T(128)S(1)}, f32[32]{0:T(128)}, u32[]{:S(2)}) copy-start(f32[32]{0:T(128)} %get-tuple-element.53) | copy-start | bytes 388

commit v2 on v1

--- a/solution.py
+++ b/solution.py
@@ -4,26 +4,11 @@
 import jax.numpy as jnp
 from jax import lax
 from jax.sharding import PartitionSpec as P
+from jax.experimental import pallas as pl
+from jax.experimental.pallas import tpu as pltpu
 
 KTAPS = 9
 BOTH = ("lat", "lon")
-
-
-def padded(cells, sides, width, closed):
-    for axis, dim in sides:
-        count = lax.axis_size(axis)
-        ends = count if closed else count - 1
-        head = lax.slice_in_dim(cells, 0, width, axis=dim)
-        tail = lax.slice_in_dim(cells, cells.shape[dim] - width, cells.shape[dim], axis=dim)
-        cells = jnp.concatenate(
-            [
-                lax.ppermute(tail, axis, [(i, (i + 1) % count) for i in range(ends)]),
-                cells,
-                lax.ppermute(head, axis, [((i + 1) % count, i) for i in range(ends)]),
-            ],
-            axis=dim,
-        )
-    return cells
 
 
 def wave_table(orders, points, period, inverse_form):
@@ -65,14 +50,16 @@
     raw_spec = jnp.transpose(summed, (1, 2, 3, 0, 4)).reshape(m_dev, 2, channels, total_lat)
 
     rim = jnp.pad(raw_spec, ((0, 0), (0, 0), (0, 0), (2, 2)))
+    turns = ((mine[None, :] * offsets[:, 1:2]) % total_lon).astype(jnp.float32) * (
+        2.0 * math.pi / total_lon
+    )
+    cos_all = jnp.cos(turns)
+    sin_all = jnp.sin(turns)
     spec_acc = jnp.zeros(raw_spec.shape, jnp.float32)
     for tap_index in range(KTAPS):
         window = lax.dynamic_slice_in_dim(rim, 2 + offsets[tap_index, 0], total_lat, axis=3)
-        turn = ((mine * offsets[tap_index, 1]) % total_lon).astype(jnp.float32) * (
-            2.0 * math.pi / total_lon
-        )
-        cos_t = jnp.cos(turn)[:, None, None]
-        sin_t = jnp.sin(turn)[:, None, None]
+        cos_t = cos_all[tap_index][:, None, None]
+        sin_t = sin_all[tap_index][:, None, None]
         real_part = cos_t * window[:, 0] - sin_t * window[:, 1]
         imag_part = sin_t * window[:, 0] + cos_t * window[:, 1]
         tap_w = conv_weight[:, tap_index][None, None, :, None]
@@ -135,20 +122,68 @@
         spectral_rows, inverse_rows, (((0,), (0,)), ((), ())), preferred_element_type=jnp.float32
     ).reshape(channels, lat_rows, lon_cols)
 
-    rimmed = padded(field, (("lat", 1),), 2, False)
-    rimmed = padded(rimmed, (("lon", 2),), 2, True)
-    running = jnp.zeros(field.shape, jnp.float32)
-    for tap_index in range(KTAPS):
-        window = lax.dynamic_slice(
-            rimmed,
-            (jnp.int32(0), 2 + offsets[tap_index, 0], 2 + offsets[tap_index, 1]),
-            field.shape,
-        )
-        running = running + conv_weight[:, tap_index][:, None, None] * window.astype(jnp.float32)
-    conv_out = running.astype(jnp.bfloat16)
-    return (conv_out.astype(jnp.float32) + jax.nn.gelu(synthesis, approximate=True)).astype(
-        jnp.bfloat16
+    rim_rows = lat_rows + 8
+    rim_cols = ((lon_cols + 4 + 127) // 128) * 128
+    lat_n = lax.axis_size("lat")
+    south = lax.ppermute(
+        field[:, :2], "lat", [((i + 1), i) for i in range(lat_n - 1)]
     )
+    north = lax.ppermute(
+        field[:, lat_rows - 2 :], "lat", [(i, (i + 1)) for i in range(lat_n - 1)]
+    )
+    rows_ext = jnp.concatenate(
+        [field, south, jnp.zeros((channels, 4, lon_cols), field.dtype), north], axis=1
+    )
+    east = lax.ppermute(
+        rows_ext[:, :, :2], "lon", [((i + 1) % lon_count, i) for i in range(lon_count)]
+    )
+    west = lax.ppermute(
+        rows_ext[:, :, lon_cols - 2 :], "lon", [(i, (i + 1) % lon_count) for i in range(lon_count)]
+    )
+    rim = jnp.concatenate(
+        [
+            rows_ext,
+            east,
+            jnp.zeros((channels, rim_rows, rim_cols - lon_cols - 4), field.dtype),
+            west,
+        ],
+        axis=2,
+    )
+    return finish(offsets, conv_weight, rim, synthesis)
+
+
+def finish(offsets, conv_weight, rim, synthesis):
+    channels, lat_rows, lon_cols = synthesis.shape
+    rim_rows, rim_cols = rim.shape[1], rim.shape[2]
+    block_c = 8
+
+    def body(offs_ref, w_ref, rim_ref, syn_ref, out_ref):
+        blk = pl.program_id(0)
+        for c in range(block_c):
+            x = rim_ref[c].astype(jnp.float32)
+            acc = jnp.zeros((rim_rows, rim_cols), jnp.float32)
+            for k in range(KTAPS):
+                dr = offs_ref[k, 0]
+                dc = offs_ref[k, 1]
+                y = pltpu.roll(x, lax.rem(rim_rows - dr, rim_rows), 0)
+                y = pltpu.roll(y, lax.rem(rim_cols - dc, rim_cols), 1)
+                acc = acc + w_ref[blk * block_c + c, k] * y
+            conv = acc[:lat_rows, :lon_cols].astype(jnp.bfloat16).astype(jnp.float32)
+            out_ref[c] = (conv + jax.nn.gelu(syn_ref[c], approximate=True)).astype(jnp.bfloat16)
+
+    return pl.pallas_call(
+        body,
+        grid_spec=pltpu.PrefetchScalarGridSpec(
+            num_scalar_prefetch=2,
+            grid=(channels // block_c,),
+            in_specs=[
+                pl.BlockSpec((block_c, rim_rows, rim_cols), lambda b, o, w: (b, 0, 0)),
+                pl.BlockSpec((block_c, lat_rows, lon_cols), lambda b, o, w: (b, 0, 0)),
+            ],
+            out_specs=pl.BlockSpec((block_c, lat_rows, lon_cols), lambda b, o, w: (b, 0, 0)),
+        ),
+        out_shape=jax.ShapeDtypeStruct((channels, lat_rows, lon_cols), jnp.bfloat16),
+    )(offsets, conv_weight, rim, synthesis)
 
 
 def solution(mesh):

time: 137 us -> 119 us (0.87)
  Pallas kernels: 0 us -> 23.4 us
  matrix products: 33.4 us -> 13.4 us
  between operations: 28.3 us -> 11.6 us
  other arithmetic: 32.7 us -> 22.3 us
  local copies, waits for them, and re-layouts: 20.3 us -> 23.6 us
  waiting for transfers between devices: 0.02 us -> 3.01 us
    pallas_call x0 -> x1, Pallas kernels: none -> 23.4 us  [finish(): pl.pallas_call(body, grid_spec=pltpu.PrefetchScalarGridSpec(num_scalar_pr...]
    dot_general x1, matrix products: 22.7 us -> 2.66 us  [per_device(): lax.dot_general(spectral_rows, inverse_rows, (((0,), (0,)), ((), ())), pr...]
    sin x9 -> x0, other arithmetic: 11.4 us -> none  [per_device(): sin_t = jnp.sin(turn)[:, None, None]]
    all_to_all x1, waiting for transfers between devices: 0.01 us -> 2.99 us  [per_device(): full_rows = lax.all_to_all(outgoing, BOTH, 0, 0, tiled=True)]
    ppermute x4, starting transfers between devices: 6.89 us -> 8.98 us  [the longest x1 6.18 us: per_device(): lax.ppermute(field[:, lat_rows - 2:], 'lat', [(i, i + 1) for i in range(l...]
    all_to_all x1, starting transfers between devices: 7.32 us -> 5.6 us  [per_device(): gathered = lax.all_to_all(partial, BOTH, 0, 0, tiled=True)]
    unnamed x39 -> x29, local copies, waits for them, and re-layouts: 9.92 us -> 11.2 us
  transfers between devices with their start and end apart: 6 -> 6, of which waited for: 0 -> 1; matrix products, arithmetic and copies ran while one was open for 38% -> 45% of each run, Pallas kernels for 0% -> 0%
where the time goes in v2:
time: 119 us; the launch traced here: 118 us
  local copies, waits for them, and re-layouts  23.6 us (20%)
  Pallas kernels  23.4 us (20%)
  other arithmetic  22.3 us (19%)
  starting transfers between devices  20.6 us (17%)
  matrix products  13.4 us (11%)
  between operations  11.6 us (10%)
  waiting for transfers between devices  3.01 us (3%)
    pallas_call x1, Pallas kernels, finish(): pl.pallas_call(body, grid_spec=pltpu.PrefetchScalarGridSpec(num_scalar_pr...  23.4 us
    unnamed x29, local copies, waits for them, and re-layouts  11.2 us
    ppermute x1, starting transfers between devices, per_device(): lax.ppermute(field[:, lat_rows - 2:], 'lat', [(i, i + 1) for i in range(l...  6.18 us
    all_to_all x1, starting transfers between devices, per_device(): full_rows = lax.all_to_all(outgoing, BOTH, 0, 0, tiled=True)  6.03 us
    all_to_all x1, starting transfers between devices, per_device(): gathered = lax.all_to_all(partial, BOTH, 0, 0, tiled=True)  5.6 us
    another operation x5, other arithmetic  4.83 us
    concatenate x1, other arithmetic, per_device(): jnp.concatenate([rows_ext, east, jnp.zeros((channels, rim_rows, rim_cols...  4.47 us
    dot_general x1, matrix products, per_device(): lax.dot_general(forward_rows, flat_field, (((1,), (1,)), ((), ())), prefe...  3.32 us
  transfers between devices with their start and end apart: 6, of which 1 were waited for; matrix products, arithmetic and copies ran while one was open for 45% of the time, Pallas kernels for 0%

profile of v2, /device:TPU:0, one launch (start us, length us, event | category | flops | bytes accessed | tf_op | source)
XLA Modules:
  0.0 117.9 jit_solution(3535368309576633865)
XLA Ops:
  0.0 2.1 %fusion.64 = (bf16[32,2,900]{2,1,0:T(2,128)(2,1)}, bf16[32,2,900]{2,1,0:T(2,128)(2,1)S(1)}) fusion(bf16[32,32,900]{2,1,0:T(8,128)(2,1)} %param.7), kind=kLoop, calls=%fused_computation.192 | loop fusion | bytes 460800 | tf_op jit(solution)/shard_map/slice | solution.py:129
  2.1 1.3 %collective-permute-start = (bf16[32,2,900]{2,1,0:T(2,128)(2,1)}, bf16[32,2,900]{2,1,0:T(2,128)(2,1)S(1)}, u32[]{:S(2)}, u32[]{:S(2)}) collective-permute-start(bf16[32,2,900]{2,1,0:T(2,128)(2,1)} %get-tuple-element.7), channel_id=1, source_target_pairs={{4,0},{8,4},{12,8},{16,12},{20,16},{24,20},{28,24},{5,1},{9,5},{13... | collective-permute-start | bytes 345608 | tf_op jit(solution)/shard_map/ppermute | solution.py:128
  3.4 6.2 %collective-permute-start.1 = (bf16[32,2,900]{2,1,0:T(2,128)(2,1)S(1)}, bf16[32,2,900]{2,1,0:T(2,128)(2,1)}, u32[]{:S(2)}, u32[]{:S(2)}) collective-permute-start(bf16[32,2,900]{2,1,0:T(2,128)(2,1)S(1)} %get-tuple-element.8), channel_id=1, source_target_pairs={{0,4},{4,8},{8,12},{12,16},{16,20},{20,24},{24,28},{1,5},{5,9},{9,... | collective-permute-start | bytes 345608 | tf_op jit(solution)/shard_map/ppermute | solution.py:131
  9.5 1.3 %multiply_convert_fusion.3 = (bf16[32,2,1,900]{3,0,2,1:T(8,128)(2,1)S(1)}, bf16[32,2,1,900]{3,0,2,1:T(8,128)(2,1)S(1)}) fusion(s32[900]{0:T(1024)S(1)} %iota_add_fusion, s32[32,2]{0,1:T(2,128)S(1)} %multiply_add_fusion.9), kind=kLoop, calls=%fused_computation.59 | loop fusion | flops 748800 | bytes 234256 | tf_op jit(solution)/shard_map/convert.10
  10.8 3.3 %fusion = f32[32,2,2,32,32]{4,0,3,2,1:T(8,128)S(1)} fusion(bf16[32,32,900]{2,1,0:T(8,128)(2,1)} %param.7, bf16[32,2,1,900]{3,0,2,1:T(8,128)(2,1)S(1)} %get-tuple-element.73, bf16[32,2,1,900]{3,0,2,1:T(8,128)(2,1)S(1)} %get-tuple-element.72), kind=kOutput, calls=%fused_computation.1 | convolution fusion | flops 236390400 | bytes 2597888 | tf_op jit(solution)/shard_map/dot_general | solution.py:45
  14.1 2.5 %copy.74 = f32[32,2,2,32,32]{4,3,2,1,0:T(8,128)} copy(f32[32,2,2,32,32]{4,0,3,2,1:T(8,128)S(1)} %fusion) | data formatting | bytes 1048576 | tf_op jit(solution)/shard_map/dot_general | solution.py:45
  16.7 3.3 %reshape.474 = f32[32,1,4096]{2,1,0:T(1,128)} reshape(f32[32,2,2,32,32]{4,3,2,1,0:T(8,128)} %copy.74) | data formatting | bytes 1048576
  20.0 5.6 %all-to-all-start = ((f32[32,1,4096]{2,1,0:T(1,128)}), f32[32,1,4096]{2,1,0:T(1,128)S(1)}, u32[]{:S(2)}, u32[]{:S(2)}) async-start(f32[32,1,4096]{2,1,0:T(1,128)} %reshape.474), calls=%async_computation | async-start | bytes 1048576 | tf_op jit(solution)/shard_map/all_to_all | solution.py:48
  25.6 0.7 fusion.66
  26.4 0.7 fusion.56
  27.1 0.6 slice_bitcast_fusion.35
  29.0 0.1 fusion.50
  29.2 0.7 compare_convert_fusion.2
  29.8 0.7 slice_bitcast_fusion.8
  30.5 0.7 fusion.65
  31.2 1.8 %multiply_convert_fusion.1 = (bf16[64,1,900]{2,0,1:T(8,128)(2,1)}, bf16[64,1,900]{2,0,1:T(8,128)(2,1)}) fusion(s32[900]{0:T(1024)S(1)} %iota_add_fusion, f32[64]{0:T(128)S(1)} %get-tuple-element.93, f32[64]{0:T(128)S(1)} %get-tuple-element.94), kind=kLoop, calls=%fused_computation.54 | loop fusion | flops 748800 | bytes 234512 | tf_op jit(solution)/shard_map/convert
  42.8 2.3 %copy.77 = bf16[2,64,32,32]{3,2,1,0:T(8,128)(2,1)} copy(bf16[2,64,32,32]{1,3,2,0:T(8,128)(2,1)S(1)} %copy-done.2) | data formatting | bytes 524288 | tf_op args[6]
  45.2 0.6 fusion.57
  45.8 1.9 %pad_maximum_fusion.4 = (bf16[32,40,2]{2,1,0:T(8,128)(2,1)}, bf16[32,40,2]{2,1,0:T(8,128)(2,1)}) fusion(bf16[32,2,900]{2,1,0:T(2,128)(2,1)} %collective-permute-done.1, bf16[32,4,900]{2,1,0:T(4,128)(2,1)S(1)} %broadcast_in_dim.84, bf16[32,2,900]{2,1,0:T(2,128)(2,1)S(1)} %collective-permute-done, bf16[32,32,900]{2,1,0:T(8,128)(2,1)S(1)} %copy-done), kind=kLoop, calls=%fused_computation.37 | loop fusion | flops 40960 | bytes 2314240 | tf_op jit(solution)/shard_map/slice | solution.py:138
  47.7 1.5 %collective-permute-start.2 = (bf16[32,40,2]{2,1,0:T(8,128)(2,1)}, bf16[32,40,2]{2,1,0:T(8,128)(2,1)}, u32[]{:S(2)}, u32[]{:S(2)}) collective-permute-start(bf16[32,40,2]{2,1,0:T(8,128)(2,1)} %get-tuple-element.5), channel_id=1, source_target_pairs={{1,0},{2,1},{3,2},{0,3},{5,4},{6,5},{7,6},{4,7},{9,8},{10,9},{11,1... | collective-permute-start | bytes 15368 | tf_op jit(solution)/shard_map/ppermute | solution.py:137
  49.2 0.5 broadcast.510
  49.7 1.9 %reduce = f32[32,4096]{1,0:T(8,128)S(1)} reduce(f32[32,1,4096]{2,1,0:T(1,128)S(1)} %all-to-all-done, f32[]{:T(128)} %broadcast.510), dimensions={1}, to_apply=%all_to_all.6.reduce_sub_computation | reduce | bytes 1048580 | tf_op jit(solution)/shard_map/all_to_all | solution.py:48
  51.6 2.0 %reshape.475 = f32[32,2,2,32,32]{4,3,2,1,0:T(8,128)} reshape(f32[32,4096]{1,0:T(8,128)S(1)} %reduce) | data formatting | bytes 1048576
  53.6 1.9 %bitcast_reduce_fusion = f32[8,2,2,32,32]{4,3,2,1,0:T(8,128)S(1)} fusion(f32[32,2,2,32,32]{4,3,2,1,0:T(8,128)} %reshape.475), kind=kLoop, calls=%fused_computation.3 | loop fusion | flops 98304 | bytes 655360 | tf_op jit(solution)/shard_map/reduce_sum | solution.py:49
  55.5 0.3 copy.75
  55.9 0.2 reshape.460
  56.1 1.1 multiply_subtract_fusion.1
  57.2 1.0 multiply_subtract_fusion
  58.1 1.0 multiply_subtract_fusion.2
  59.1 0.9 fusion.28
  60.0 0.1 rev.8
  60.1 1.0 fusion.5
  61.1 0.7 copy.79
  61.8 1.0 convolution_bitcast_fusion.2
  62.7 1.6 %convolution_bitcast_fusion.3 = f32[2,32,2,32]{3,2,0,1:T(2,128)} fusion(bf16[2,32,2,32]{3,2,0,1:T(2,128)(2,1)} %copy.79, bf16[2,32,2,32,32]{4,3,2,1,0:T(8,128)(2,1)S(1)} %bitcast.179), kind=kOutput, calls=%fused_computation.8 | convolution fusion | flops 262144 | bytes 286720 | tf_op jit(solution)/shard_map/mupc,ucd->mupd/dot_general | solution.py:89
  64.3 1.6 %fusion.4 = bf16[2,32,2,32]{1,3,2,0:T(8,128)(2,1)} fusion(f32[2,32]{1,0:T(2,128)} %get-tuple-element.88, pred[2]{0:T(512)(128)(4,1)} %get-tuple-element.92, bf16[2,32,1,128]{3,2,1,0:T(2,128)(2,1)} %get-tuple-element.44, bf16[2,2,32,128]{3,2,1,0:T(8,128)(2,1)} %copy-done.6, f32[2,128]{1,0:T(2,128)} %fusion.56, bf16[2,2,32,256]{3,2,1,0:T(8,128)(2,1)S(1)} %fusion.28), kind=kOutput, calls=%fused_computation.12 | convolution fusion | flops 1204224 | bytes 91394 | tf_op jit(solution)/shard_map/mui,mpci->mupc/dot_general | solution.py:83
  65.9 0.8 copy.85
  66.8 0.2 convolution_bitcast_fusion
  67.0 0.2 convolution_bitcast_fusion.1
  67.1 1.0 fusion.36
  68.2 0.1 pad_maximum_fusion.6
  68.3 1.0 fusion.39
  69.3 0.1 pad_maximum_fusion.7
  69.4 1.0 subtract_multiply_fusion
  70.4 0.7 multiply_convert_fusion.4
  71.1 0.1 rev.9
  71.2 0.1 concatenate.20
  71.3 0.1 concatenate.19
  71.4 0.2 maximum_bitcast_fusion.2
  71.7 0.2 broadcast_in_dim.89
  71.9 1.7 %reshape.476 = bf16[32,2,2048]{2,1,0:T(2,128)(2,1)} reshape(bf16[32,2,2,32,32]{4,3,2,1,0:T(8,128)(2,1)S(1)} %bitcast.174) | data formatting | bytes 524288
  73.6 6.0 %all-to-all-start.1 = ((bf16[32,2,2048]{2,1,0:T(2,128)(2,1)}), bf16[32,2,2048]{2,1,0:T(2,128)(2,1)S(1)}, u32[]{:S(2)}, u32[]{:S(2)}) async-start(bf16[32,2,2048]{2,1,0:T(2,128)(2,1)} %reshape.476), calls=%async_computation.1 | async-start | bytes 524288 | tf_op jit(solution)/shard_map/all_to_all | solution.py:116
  79.7 1.0 pad_maximum_fusion.5
  80.7 0.7 copy.93.offs_ref
  81.4 0.7 copy.94.w_ref
  82.0 0.3 copy.91
  82.3 0.2 convert_element_type.115
  82.6 4.5 %pad_maximum_fusion.rim_ref = bf16[32,40,1024]{2,1,0:T(8,128)(2,1)} fusion(bf16[32,40,2]{2,1,0:T(8,128)(2,1)} %collective-permute-done.3, bf16[32,40,2]{2,1,0:T(8,128)(2,1)} %collective-permute-done.2, bf16[32,2,900]{2,1,0:T(2,128)(2,1)} %collective-permute-done.1, bf16[32,4,900]{2,1,0:T(4,128)(2,1)S(1)} %broadcast_in_dim.84, ...), kind=kLoop, calls=%fused_computation | loop fusion | flops 18350080 | bytes 4937728 | tf_op jit(solution)/shard_map/concatenate | solution.py:143
  87.1 3.0 %all-to-all-done.1 = bf16[32,2,2048]{2,1,0:T(2,128)(2,1)S(1)} async-done(((bf16[32,2,2048]{2,1,0:T(2,128)(2,1)}), bf16[32,2,2048]{2,1,0:T(2,128)(2,1)S(1)}, u32[]{:S(2)}, u32[]{:S(2)}) %all-to-all-start.1) | async-done | bytes 262176 | tf_op jit(solution)/shard_map/all_to_all | solution.py:116
  90.1 0.5 reshape.477
  90.6 1.1 reshape.464
  91.7 0.2 copy.90
  91.8 2.7 %fusion.12.syn_ref = f32[32,32,900]{2,1,0:T(8,128)} fusion(bf16[32,32,128]{2,1,0:T(8,128)(2,1)S(1)} %bitcast.176, bf16[128,900]{1,0:T(8,128)(2,1)S(1)} %convert_element_type.115), kind=kOutput, calls=%fused_computation.51 | convolution fusion | flops 235929600 | bytes 4178944 | tf_op jit(solution)/shard_map/dot_general | solution.py:121
  94.5 23.4 %shard_map.73 = bf16[32,32,900]{2,1,0:T(8,128)(2,1)} custom-call(s32[9,2]{1,0:T(8,128)} %copy.93.offs_ref, f32[32,9]{1,0:T(8,128)} %copy.94.w_ref, bf16[32,40,1024]{2,1,0:T(8,128)(2,1)} %pad_maximum_fusion.rim_ref, f32[32,32,900]{2,1,0:T(8,128)} %fusion.12.syn_ref), custom_call_target="tpu_custom_call" | custom-call | tf_op jit(solution)/shard_map/pallas_call | solution.py:174
  (41 shorter events, 0.4 us)
Async XLA Ops:
  2.1 43.6 %collective-permute-start = (bf16[32,2,900]{2,1,0:T(2,128)(2,1)}, bf16[32,2,900]{2,1,0:T(2,128)(2,1)S(1)}, u32[]{:S(2)}, u32[]{:S(2)}) collective-permute-start(bf16[32,2,900]{2,1,0:T(2,128)(2,1)} %get-tuple-element.7), channel_id=1, source_target_pairs={{4,0},{8,4},{12,8},{16,12},{20,16},{24,20},{28,24},{5,1},{9,5},{13... | collective-permute-start | bytes 345608 | tf_op jit(solution)/shard_map/ppermute | solution.py:128
  3.4 42.4 %collective-permute-start.1 = (bf16[32,2,900]{2,1,0:T(2,128)(2,1)S(1)}, bf16[32,2,900]{2,1,0:T(2,128)(2,1)}, u32[]{:S(2)}, u32[]{:S(2)}) collective-permute-start(bf16[32,2,900]{2,1,0:T(2,128)(2,1)S(1)} %get-tuple-element.8), channel_id=1, source_target_pairs={{0,4},{4,8},{8,12},{12,16},{16,20},{20,24},{24,28},{1,5},{5,9},{9,... | collective-permute-start | bytes 345608 | tf_op jit(solution)/shard_map/ppermute | solution.py:131
  16.7 8.9 %copy-start.7 = (s32[9,2]{0,1:T(2,128)S(1)}, s32[9,2]{0,1:T(2,128)}, u32[]{:S(2)}) copy-start(s32[9,2]{0,1:T(2,128)} %param.8) | copy-start | bytes 220
  16.7 9.7 %copy-start.9 = (s32[128]{0:T(128)S(1)}, s32[128]{0:T(128)}, u32[]{:S(2)}) copy-start(s32[128]{0:T(128)} %param.12) | copy-start | bytes 1540
  16.7 9.7 %copy-start.10 = (f32[128]{0:T(128)S(1)}, f32[128]{0:T(128)}, u32[]{:S(2)}) copy-start(f32[128]{0:T(128)} %param.11) | copy-start | bytes 1540
  16.7 10.4 %copy-start.8 = (f32[32,9]{0,1:T(8,128)S(1)}, f32[32,9]{0,1:T(8,128)}, u32[]{:S(2)}) copy-start(f32[32,9]{0,1:T(8,128)} %param.9) | copy-start | bytes 3460
  16.7 13.8 %copy-start.5 = (bf16[2,64,128]{2,1,0:T(8,128)(2,1)S(1)}, bf16[2,64,128]{2,1,0:T(8,128)(2,1)}, u32[]{:S(2)}) copy-start(bf16[2,64,128]{2,1,0:T(8,128)(2,1)} %param.10) | copy-start | bytes 98308
  16.7 26.1 %copy-start.2 = (bf16[2,64,32,32]{1,3,2,0:T(8,128)(2,1)S(1)}, bf16[2,64,32,32]{1,3,2,0:T(8,128)(2,1)}, u32[]{:S(2)}) copy-start(bf16[2,64,32,32]{1,3,2,0:T(8,128)(2,1)} %param.13) | copy-start | bytes 786436
  16.7 29.1 %copy-start = (bf16[32,32,900]{2,1,0:T(8,128)(2,1)S(1)}, bf16[32,32,900]{2,1,0:T(8,128)(2,1)}, u32[]{:S(2)}) copy-start(bf16[32,32,900]{2,1,0:T(8,128)(2,1)} %param.7) | copy-start | bytes 5529604
  20.0 29.2 %all-to-all-start = ((f32[32,1,4096]{2,1,0:T(1,128)}), f32[32,1,4096]{2,1,0:T(1,128)S(1)}, u32[]{:S(2)}, u32[]{:S(2)}) async-start(f32[32,1,4096]{2,1,0:T(1,128)} %reshape.474), calls=%async_computation | async-start | bytes 1048576 | tf_op jit(solution)/shard_map/all_to_all | solution.py:48
  45.7 7.9 %copy-start.3 = (bf16[32,2,900]{2,1,0:T(2,128)(2,1)}, bf16[32,2,900]{2,1,0:T(2,128)(2,1)S(1)}, u32[]{:S(2)}) copy-start(bf16[32,2,900]{2,1,0:T(2,128)(2,1)S(1)} %collective-permute-done) | copy-start | bytes 345604
  47.7 34.9 %collective-permute-start.2 = (bf16[32,40,2]{2,1,0:T(8,128)(2,1)}, bf16[32,40,2]{2,1,0:T(8,128)(2,1)}, u32[]{:S(2)}, u32[]{:S(2)}) collective-permute-start(bf16[32,40,2]{2,1,0:T(8,128)(2,1)} %get-tuple-element.5), channel_id=1, source_target_pairs={{1,0},{2,1},{3,2},{0,3},{5,4},{6,5},{7,6},{4,7},{9,8},{10,9},{11,1... | collective-permute-start | bytes 15368 | tf_op jit(solution)/shard_map/ppermute | solution.py:137
  49.2 33.4 %collective-permute-start.3 = (bf16[32,40,2]{2,1,0:T(8,128)(2,1)}, bf16[32,40,2]{2,1,0:T(8,128)(2,1)}, u32[]{:S(2)}, u32[]{:S(2)}) collective-permute-start(bf16[32,40,2]{2,1,0:T(8,128)(2,1)} %get-tuple-element.6), channel_id=1, source_target_pairs={{0,1},{1,2},{2,3},{3,0},{4,5},{5,6},{6,7},{7,4},{8,9},{9,10},{10,1... | collective-permute-start | bytes 15368 | tf_op jit(solution)/shard_map/ppermute | solution.py:140
  56.0 5.7 %copy-start.1 = (bf16[2,64,32,32]{3,2,1,0:T(8,128)(2,1)S(1)}, bf16[2,64,32,32]{3,2,1,0:T(8,128)(2,1)}, u32[]{:S(2)}) copy-start(bf16[2,64,32,32]{3,2,1,0:T(8,128)(2,1)} %copy.77) | copy-start | bytes 786436
  60.1 1.7 %copy-start.6 = (bf16[2,2,32,128]{3,2,1,0:T(8,128)(2,1)}, bf16[2,2,32,128]{3,2,1,0:T(8,128)(2,1)S(1)}, u32[]{:S(2)}) copy-start(bf16[2,2,32,128]{3,2,1,0:T(8,128)(2,1)S(1)} %rev.8) | copy-start | bytes 98308
  71.6 11.0 %copy-start.4 = (bf16[32,2,900]{2,1,0:T(2,128)(2,1)S(1)}, bf16[32,2,900]{2,1,0:T(2,128)(2,1)}, u32[]{:S(2)}) copy-start(bf16[32,2,900]{2,1,0:T(2,128)(2,1)} %copy-done.3) | copy-start | bytes 345604
  73.6 16.4 %all-to-all-start.1 = ((bf16[32,2,2048]{2,1,0:T(2,128)(2,1)}), bf16[32,2,2048]{2,1,0:T(2,128)(2,1)S(1)}, u32[]{:S(2)}, u32[]{:S(2)}) async-start(bf16[32,2,2048]{2,1,0:T(2,128)(2,1)} %reshape.476), calls=%async_computation.1 | async-start | bytes 524288 | tf_op jit(solution)/shard_map/all_to_all | solution.py:116

commit v3 on v2

--- a/solution.py
+++ b/solution.py
@@ -122,7 +122,6 @@
         spectral_rows, inverse_rows, (((0,), (0,)), ((), ())), preferred_element_type=jnp.float32
     ).reshape(channels, lat_rows, lon_cols)
 
-    rim_rows = lat_rows + 8
     rim_cols = ((lon_cols + 4 + 127) // 128) * 128
     lat_n = lax.axis_size("lat")
     south = lax.ppermute(
@@ -132,8 +131,9 @@
         field[:, lat_rows - 2 :], "lat", [(i, (i + 1)) for i in range(lat_n - 1)]
     )
     rows_ext = jnp.concatenate(
-        [field, south, jnp.zeros((channels, 4, lon_cols), field.dtype), north], axis=1
+        [north, field, south, jnp.zeros((channels, 4, lon_cols), field.dtype)], axis=1
     )
+    rim_rows = rows_ext.shape[1]
     east = lax.ppermute(
         rows_ext[:, :, :2], "lon", [((i + 1) % lon_count, i) for i in range(lon_count)]
     )
@@ -149,15 +149,17 @@
         ],
         axis=2,
     )
-    return finish(offsets, conv_weight, rim, synthesis)
+    conv_out = depthwise_conv(offsets, conv_weight, rim, lat_rows, lon_cols)
+    return (conv_out.astype(jnp.float32) + jax.nn.gelu(synthesis, approximate=True)).astype(
+        jnp.bfloat16
+    )
 
 
-def finish(offsets, conv_weight, rim, synthesis):
-    channels, lat_rows, lon_cols = synthesis.shape
-    rim_rows, rim_cols = rim.shape[1], rim.shape[2]
+def depthwise_conv(offsets, conv_weight, rim, lat_rows, lon_cols):
+    channels, rim_rows, rim_cols = rim.shape
     block_c = 8
 
-    def body(offs_ref, w_ref, rim_ref, syn_ref, out_ref):
+    def body(offs_ref, w_ref, rim_ref, out_ref):
         blk = pl.program_id(0)
         for c in range(block_c):
             x = rim_ref[c].astype(jnp.float32)
@@ -165,25 +167,26 @@
             for k in range(KTAPS):
                 dr = offs_ref[k, 0]
                 dc = offs_ref[k, 1]
-                y = pltpu.roll(x, lax.rem(rim_rows - dr, rim_rows), 0)
+                y = pltpu.roll(x, lax.rem(rim_rows - dr - 2, rim_rows), 0)
                 y = pltpu.roll(y, lax.rem(rim_cols - dc, rim_cols), 1)
                 acc = acc + w_ref[blk * block_c + c, k] * y
-            conv = acc[:lat_rows, :lon_cols].astype(jnp.bfloat16).astype(jnp.float32)
-            out_ref[c] = (conv + jax.nn.gelu(syn_ref[c], approximate=True)).astype(jnp.bfloat16)
+            out_ref[c] = acc[:lat_rows, :lon_cols].astype(jnp.bfloat16)
 
     return pl.pallas_call(
         body,
         grid_spec=pltpu.PrefetchScalarGridSpec(
             num_scalar_prefetch=2,
             grid=(channels // block_c,),
-            in_specs=[
-                pl.BlockSpec((block_c, rim_rows, rim_cols), lambda b, o, w: (b, 0, 0)),
-                pl.BlockSpec((block_c, lat_rows, lon_cols), lambda b, o, w: (b, 0, 0)),
-            ],
+            in_specs=[pl.BlockSpec((block_c, rim_rows, rim_cols), lambda b, o, w: (b, 0, 0))],
             out_specs=pl.BlockSpec((block_c, lat_rows, lon_cols), lambda b, o, w: (b, 0, 0)),
         ),
         out_shape=jax.ShapeDtypeStruct((channels, lat_rows, lon_cols), jnp.bfloat16),
-    )(offsets, conv_weight, rim, synthesis)
+        cost_estimate=pl.CostEstimate(
+            flops=40 * KTAPS * channels * rim_rows * rim_cols,
+            transcendentals=0,
+            bytes_accessed=channels * (rim_rows * rim_cols + lat_rows * lon_cols) * 2,
+        ),
+    )(offsets, conv_weight, rim)
 
 
 def solution(mesh):

time: 119 us -> 119 us (level)
  local copies, waits for them, and re-layouts: 23.6 us -> 27.2 us
  waiting for transfers between devices: 3.01 us -> 0.02 us
  Pallas kernels: 23.4 us -> 21.6 us
    all_to_all x1, waiting for transfers between devices: 2.99 us -> 0.01 us  [per_device(): full_rows = lax.all_to_all(outgoing, BOTH, 0, 0, tiled=True)]
    convert_element_type x0 -> x1, other arithmetic: none -> 2.63 us  [per_device(): (conv_out.astype(jnp.float32) + jax.nn.gelu(synthesis, approximate=True))...]
    unnamed x29 -> x23, local copies, waits for them, and re-layouts: 11.2 us -> 13.9 us
    all_to_all x1, starting transfers between devices: 5.6 us -> 7.58 us  [per_device(): gathered = lax.all_to_all(partial, BOTH, 0, 0, tiled=True)]
    dot_general x1, matrix products: 2.66 us -> 0.69 us  [per_device(): lax.dot_general(spectral_rows, inverse_rows, (((0,), (0,)), ((), ())), pr...]
    pallas_call x1, Pallas kernels: 23.4 us -> 21.6 us  [depthwise_conv(): pl.pallas_call(body, grid_spec=pltpu.PrefetchScalarGridSpec(num_scalar_pr...]
    another operation x5, other arithmetic: 4.83 us -> 3.29 us
    convert_element_type x2, local copies, waits for them, and re-layouts: 1.54 us -> 0.19 us  [per_device(): coeffs = (coeffs * triangle[:, :, None, None]).astype(jnp.bfloat16)]
  transfers between devices with their start and end apart: 6 -> 6, of which waited for: 1 -> 0; matrix products, arithmetic and copies ran while one was open for 45% -> 45% of each run, Pallas kernels for 0% -> 18%
where the time goes in v3:
time: 119 us; the launch traced here: 118 us
  local copies, waits for them, and re-layouts  27.2 us (23%)
  other arithmetic  23.1 us (19%)
  Pallas kernels  21.6 us (18%)
  starting transfers between devices  21.4 us (18%)
  matrix products  12.5 us (11%)
  between operations  11.7 us (10%)
    pallas_call x1, Pallas kernels, depthwise_conv(): pl.pallas_call(body, grid_spec=pltpu.PrefetchScalarGridSpec(num_scalar_pr...  21.6 us
    unnamed x23, local copies, waits for them, and re-layouts  13.9 us
    all_to_all x1, starting transfers between devices, per_device(): gathered = lax.all_to_all(partial, BOTH, 0, 0, tiled=True)  7.58 us
    all_to_all x1, starting transfers between devices, per_device(): full_rows = lax.all_to_all(outgoing, BOTH, 0, 0, tiled=True)  6.16 us
    concatenate x1, other arithmetic, per_device(): jnp.concatenate([rows_ext, east, jnp.zeros((channels, rim_rows, rim_cols...  5.18 us
    ppermute x1, starting transfers between devices, per_device(): lax.ppermute(field[:, lat_rows - 2:], 'lat', [(i, i + 1) for i in range(l...  4.87 us
    dot_general x1, matrix products, per_device(): lax.dot_general(forward_rows, flat_field, (((1,), (1,)), ((), ())), prefe...  3.32 us
    another operation x5, other arithmetic  3.29 us
  transfers between devices with their start and end apart: 6, of which 0 were waited for; matrix products, arithmetic and copies ran while one was open for 45% of the time, Pallas kernels for 18%

profile of v3, /device:TPU:0, one launch (start us, length us, event | category | flops | bytes accessed | tf_op | source)
XLA Modules:
  0.0 117.5 jit_solution(15808209103250321145)
XLA Ops:
  0.0 2.1 %fusion.73 = (bf16[32,2,900]{2,1,0:T(2,128)(2,1)}, bf16[32,2,900]{2,1,0:T(2,128)(2,1)S(1)}) fusion(bf16[32,32,900]{2,1,0:T(8,128)(2,1)} %param.7), kind=kLoop, calls=%fused_computation.202 | loop fusion | bytes 460800 | tf_op jit(solution)/shard_map/slice | solution.py:131
  2.1 4.9 %collective-permute-start = (bf16[32,2,900]{2,1,0:T(2,128)(2,1)}, bf16[32,2,900]{2,1,0:T(2,128)(2,1)S(1)}, u32[]{:S(2)}, u32[]{:S(2)}) collective-permute-start(bf16[32,2,900]{2,1,0:T(2,128)(2,1)} %get-tuple-element.7), channel_id=1, source_target_pairs={{0,4},{4,8},{8,12},{12,16},{16,20},{20,24},{24,28},{1,5},{5,9},{9,... | collective-permute-start | bytes 345608 | tf_op jit(solution)/shard_map/ppermute | solution.py:130
  6.9 1.3 %collective-permute-start.1 = (bf16[32,2,900]{2,1,0:T(2,128)(2,1)S(1)}, bf16[32,2,900]{2,1,0:T(2,128)(2,1)}, u32[]{:S(2)}, u32[]{:S(2)}) collective-permute-start(bf16[32,2,900]{2,1,0:T(2,128)(2,1)S(1)} %get-tuple-element.8), channel_id=1, source_target_pairs={{4,0},{8,4},{12,8},{16,12},{20,16},{24,20},{28,24},{5,1},{9,5},{13... | collective-permute-start | bytes 345608 | tf_op jit(solution)/shard_map/ppermute | solution.py:127
  8.3 1.3 %multiply_convert_fusion.3 = (bf16[32,2,1,900]{3,0,2,1:T(8,128)(2,1)S(1)}, bf16[32,2,1,900]{3,0,2,1:T(8,128)(2,1)S(1)}) fusion(s32[900]{0:T(1024)S(1)} %iota_add_fusion, s32[32,2]{0,1:T(2,128)S(1)} %multiply_add_fusion.9), kind=kLoop, calls=%fused_computation.69 | loop fusion | flops 748800 | bytes 234256 | tf_op jit(solution)/shard_map/convert.10
  9.6 3.3 %fusion.9 = f32[32,2,2,32,32]{4,0,3,2,1:T(8,128)S(1)} fusion(bf16[32,32,900]{2,1,0:T(8,128)(2,1)} %param.7, bf16[32,2,1,900]{3,0,2,1:T(8,128)(2,1)S(1)} %get-tuple-element.73, bf16[32,2,1,900]{3,0,2,1:T(8,128)(2,1)S(1)} %get-tuple-element.72), kind=kOutput, calls=%fused_computation.11 | convolution fusion | flops 236390400 | bytes 2597888 | tf_op jit(solution)/shard_map/dot_general | solution.py:45
  12.9 2.5 %copy.76 = f32[32,2,2,32,32]{4,3,2,1,0:T(8,128)} copy(f32[32,2,2,32,32]{4,0,3,2,1:T(8,128)S(1)} %fusion.9) | data formatting | bytes 1048576 | tf_op jit(solution)/shard_map/dot_general | solution.py:45
  15.5 3.3 %reshape.474 = f32[32,1,4096]{2,1,0:T(1,128)} reshape(f32[32,2,2,32,32]{4,3,2,1,0:T(8,128)} %copy.76) | data formatting | bytes 1048576
  18.8 7.6 %all-to-all-start = ((f32[32,1,4096]{2,1,0:T(1,128)}), f32[32,1,4096]{2,1,0:T(1,128)S(1)}, u32[]{:S(2)}, u32[]{:S(2)}) async-start(f32[32,1,4096]{2,1,0:T(1,128)} %reshape.474), calls=%async_computation | async-start | bytes 1048576 | tf_op jit(solution)/shard_map/all_to_all | solution.py:48
  26.4 0.7 fusion.75
  32.2 0.7 fusion.65
  32.9 0.6 slice_bitcast_fusion.35
  33.5 0.7 compare_convert_fusion.2
  34.1 1.1 multiply_convert_fusion.1
  35.3 0.1 fusion.59
  35.4 0.7 slice_bitcast_fusion.8
  36.1 0.7 fusion.74
  43.0 0.7 copy.74.offs_ref
  43.7 0.7 copy.75.w_ref
  44.4 0.3 copy.93
  44.7 0.9 convert_element_type.122
  45.5 3.4 %copy.79 = bf16[2,64,32,32]{3,2,1,0:T(8,128)(2,1)} copy(bf16[2,64,32,32]{1,3,2,0:T(8,128)(2,1)} %param.13) | data formatting | bytes 524288 | tf_op args[6]
  48.9 0.1 pad.38.clone
  49.0 0.6 fusion.66
  49.6 1.9 %pad_maximum_fusion.4 = (bf16[32,40,2]{2,1,0:T(8,128)(2,1)}, bf16[32,40,2]{2,1,0:T(8,128)(2,1)}) fusion(bf16[32,4,900]{2,1,0:T(4,128)(2,1)S(1)} %broadcast_in_dim.84, bf16[32,2,900]{2,1,0:T(2,128)(2,1)} %collective-permute-done.1, bf16[32,32,900]{2,1,0:T(8,128)(2,1)S(1)} %copy-done, bf16[32,2,900]{2,1,0:T(2,128)(2,1)S(1)} %collective-permute-done), kind=kLoop, calls=%fused_computation.47 | loop fusion | flops 40960 | bytes 2314240 | tf_op jit(solution)/shard_map/slice | solution.py:138
  51.6 1.5 %collective-permute-start.2 = (bf16[32,40,2]{2,1,0:T(8,128)(2,1)}, bf16[32,40,2]{2,1,0:T(8,128)(2,1)}, u32[]{:S(2)}, u32[]{:S(2)}) collective-permute-start(bf16[32,40,2]{2,1,0:T(8,128)(2,1)} %get-tuple-element.5), channel_id=1, source_target_pairs={{1,0},{2,1},{3,2},{0,3},{5,4},{6,5},{7,6},{4,7},{9,8},{10,9},{11,1... | collective-permute-start | bytes 15368 | tf_op jit(solution)/shard_map/ppermute | solution.py:137
  53.1 0.5 broadcast.510
  53.6 1.9 %reduce = f32[32,4096]{1,0:T(8,128)S(1)} reduce(f32[32,1,4096]{2,1,0:T(1,128)S(1)} %all-to-all-done, f32[]{:T(128)} %broadcast.510), dimensions={1}, to_apply=%all_to_all.6.reduce_sub_computation | reduce | bytes 1048580 | tf_op jit(solution)/shard_map/all_to_all | solution.py:48
  55.5 2.0 %reshape.475 = f32[32,2,2,32,32]{4,3,2,1,0:T(8,128)} reshape(f32[32,4096]{1,0:T(8,128)S(1)} %reduce) | data formatting | bytes 1048576
  57.5 1.9 %bitcast_reduce_fusion = f32[8,2,2,32,32]{4,3,2,1,0:T(8,128)S(1)} fusion(f32[32,2,2,32,32]{4,3,2,1,0:T(8,128)} %reshape.475), kind=kLoop, calls=%fused_computation.13 | loop fusion | flops 98304 | bytes 655360 | tf_op jit(solution)/shard_map/reduce_sum | solution.py:49
  59.4 0.3 copy.77
  59.7 0.2 reshape.460
  59.9 0.9 multiply_subtract_fusion.1
  60.9 1.0 multiply_subtract_fusion
  61.9 1.0 multiply_subtract_fusion.2
  62.9 0.8 fusion.37
  63.7 0.1 rev.8
  63.8 1.0 fusion.14
  64.8 0.1 copy.81
  64.9 1.2 convolution_bitcast_fusion.2
  66.1 1.2 convolution_bitcast_fusion.3
  67.2 1.0 fusion.13
  68.2 0.1 copy.87
  68.3 1.2 convolution_bitcast_fusion
  69.4 1.2 convolution_bitcast_fusion.1
  70.6 0.1 fusion.45
  70.7 0.1 pad_maximum_fusion.6
  70.8 1.0 fusion.48
  71.8 0.1 pad_maximum_fusion.7
  71.9 1.0 subtract_multiply_fusion
  72.9 0.7 multiply_convert_fusion.4
  73.6 0.1 rev.9
  73.7 0.1 concatenate.20
  73.8 0.1 concatenate.19
  74.0 0.2 maximum_bitcast_fusion.2
  74.2 0.2 broadcast_in_dim.89
  74.4 1.7 %reshape.476 = bf16[32,2,2048]{2,1,0:T(2,128)(2,1)} reshape(bf16[32,2,2,32,32]{4,3,2,1,0:T(8,128)(2,1)S(1)} %bitcast.174) | data formatting | bytes 524288
  76.1 6.2 %all-to-all-start.1 = ((bf16[32,2,2048]{2,1,0:T(2,128)(2,1)}), bf16[32,2,2048]{2,1,0:T(2,128)(2,1)}, u32[]{:S(2)}, u32[]{:S(2)}) async-start(bf16[32,2,2048]{2,1,0:T(2,128)(2,1)} %reshape.476), calls=%async_computation.1 | async-start | bytes 524288 | tf_op jit(solution)/shard_map/all_to_all | solution.py:116
  82.3 5.2 %pad_maximum_fusion.rim_ref = bf16[32,40,1024]{2,1,0:T(8,128)(2,1)} fusion(bf16[32,40,2]{2,1,0:T(8,128)(2,1)} %collective-permute-done.3, bf16[32,40,2]{2,1,0:T(8,128)(2,1)} %collective-permute-done.2, bf16[32,4,900]{2,1,0:T(4,128)(2,1)S(1)} %broadcast_in_dim.84, bf16[32,2,900]{2,1,0:T(2,128)(2,1)} %collective-permute-done.1, ...), kind=kLoop, calls=%fused_computation.10 | loop fusion | flops 18350080 | bytes 4937728 | tf_op jit(solution)/shard_map/concatenate | solution.py:143
  87.5 21.6 %shard_map.73 = bf16[32,32,900]{2,1,0:T(8,128)(2,1)} custom-call(s32[9,2]{1,0:T(8,128)} %copy.74.offs_ref, f32[32,9]{1,0:T(8,128)} %copy.75.w_ref, bf16[32,40,1024]{2,1,0:T(8,128)(2,1)} %pad_maximum_fusion.rim_ref), custom_call_target="tpu_custom_call" | custom-call | flops 471859200 | bytes 4464640 | tf_op jit(solution)/shard_map/pallas_call | solution.py:175
  109.1 2.1 %reshape.477 = bf16[32,2,2,32,32]{4,3,2,1,0:T(8,128)(2,1)S(1)} reshape(bf16[32,2,2048]{2,1,0:T(2,128)(2,1)} %all-to-all-done.1) | data formatting | bytes 524288
  111.2 1.8 %reshape.464 = bf16[128,1024]{1,0:T(8,128)(2,1)} reshape(bf16[32,2,2,32,32]{4,3,2,1,0:T(8,128)(2,1)S(1)} %reshape.477) | data formatting | bytes 524288 | tf_op jit(solution)/shard_map/reshape | solution.py:117
  113.0 1.1 copy.92
  114.2 0.7 fusion.21
  114.9 2.6 %fusion.8 = bf16[32,32,900]{2,1,0:T(8,128)(2,1)} fusion(f32[32,32,900]{2,1,0:T(8,128)S(1)} %fusion.21, bf16[32,32,900]{2,1,0:T(8,128)(2,1)S(1)} %copy-done.1), kind=kLoop, calls=%fused_computation.9 | loop fusion | flops 10137600 | bytes 7372800 | tf_op jit(solution)/shard_map/convert_element_type | solution.py:153
  (36 shorter events, 0.4 us)
Async XLA Ops:
  2.1 47.5 %collective-permute-start = (bf16[32,2,900]{2,1,0:T(2,128)(2,1)}, bf16[32,2,900]{2,1,0:T(2,128)(2,1)S(1)}, u32[]{:S(2)}, u32[]{:S(2)}) collective-permute-start(bf16[32,2,900]{2,1,0:T(2,128)(2,1)} %get-tuple-element.7), channel_id=1, source_target_pairs={{0,4},{4,8},{8,12},{12,16},{16,20},{20,24},{24,28},{1,5},{5,9},{9,... | collective-permute-start | bytes 345608 | tf_op jit(solution)/shard_map/ppermute | solution.py:130
  6.9 42.6 %collective-permute-start.1 = (bf16[32,2,900]{2,1,0:T(2,128)(2,1)S(1)}, bf16[32,2,900]{2,1,0:T(2,128)(2,1)}, u32[]{:S(2)}, u32[]{:S(2)}) collective-permute-start(bf16[32,2,900]{2,1,0:T(2,128)(2,1)S(1)} %get-tuple-element.8), channel_id=1, source_target_pairs={{4,0},{8,4},{12,8},{16,12},{20,16},{24,20},{28,24},{5,1},{9,5},{13... | collective-permute-start | bytes 345608 | tf_op jit(solution)/shard_map/ppermute | solution.py:127
  12.9 13.5 %copy-start.4 = (s32[9,2]{0,1:T(2,128)S(1)}, s32[9,2]{0,1:T(2,128)}, u32[]{:S(2)}) copy-start(s32[9,2]{0,1:T(2,128)} %param.8) | copy-start | bytes 220
  12.9 19.2 %copy-start.6 = (s32[128]{0:T(128)S(1)}, s32[128]{0:T(128)}, u32[]{:S(2)}) copy-start(s32[128]{0:T(128)} %param.12) | copy-start | bytes 1540
  12.9 19.3 %copy-start.7 = (f32[128]{0:T(128)S(1)}, f32[128]{0:T(128)}, u32[]{:S(2)}) copy-start(f32[128]{0:T(128)} %param.11) | copy-start | bytes 1540
  12.9 20.0 %copy-start.5 = (f32[32,9]{0,1:T(8,128)S(1)}, f32[32,9]{0,1:T(8,128)}, u32[]{:S(2)}) copy-start(f32[32,9]{0,1:T(8,128)} %param.9) | copy-start | bytes 3460
  12.9 23.2 %copy-start.3 = (bf16[2,64,128]{2,1,0:T(8,128)(2,1)S(1)}, bf16[2,64,128]{2,1,0:T(8,128)(2,1)}, u32[]{:S(2)}) copy-start(bf16[2,64,128]{2,1,0:T(8,128)(2,1)} %param.10) | copy-start | bytes 98308
  15.5 34.1 %copy-start = (bf16[32,32,900]{2,1,0:T(8,128)(2,1)S(1)}, bf16[32,32,900]{2,1,0:T(8,128)(2,1)}, u32[]{:S(2)}) copy-start(bf16[32,32,900]{2,1,0:T(8,128)(2,1)} %param.7) | copy-start | bytes 5529604
  18.8 34.3 %all-to-all-start = ((f32[32,1,4096]{2,1,0:T(1,128)}), f32[32,1,4096]{2,1,0:T(1,128)S(1)}, u32[]{:S(2)}, u32[]{:S(2)}) async-start(f32[32,1,4096]{2,1,0:T(1,128)} %reshape.474), calls=%async_computation | async-start | bytes 1048576 | tf_op jit(solution)/shard_map/all_to_all | solution.py:48
  51.6 30.8 %collective-permute-start.2 = (bf16[32,40,2]{2,1,0:T(8,128)(2,1)}, bf16[32,40,2]{2,1,0:T(8,128)(2,1)}, u32[]{:S(2)}, u32[]{:S(2)}) collective-permute-start(bf16[32,40,2]{2,1,0:T(8,128)(2,1)} %get-tuple-element.5), channel_id=1, source_target_pairs={{1,0},{2,1},{3,2},{0,3},{5,4},{6,5},{7,6},{4,7},{9,8},{10,9},{11,1... | collective-permute-start | bytes 15368 | tf_op jit(solution)/shard_map/ppermute | solution.py:137
  53.1 29.2 %collective-permute-start.3 = (bf16[32,40,2]{2,1,0:T(8,128)(2,1)}, bf16[32,40,2]{2,1,0:T(8,128)(2,1)}, u32[]{:S(2)}, u32[]{:S(2)}) collective-permute-start(bf16[32,40,2]{2,1,0:T(8,128)(2,1)} %get-tuple-element.6), channel_id=1, source_target_pairs={{0,1},{1,2},{2,3},{3,0},{4,5},{5,6},{6,7},{7,4},{8,9},{9,10},{10,1... | collective-permute-start | bytes 15368 | tf_op jit(solution)/shard_map/ppermute | solution.py:140
  76.1 33.0 %all-to-all-start.1 = ((bf16[32,2,2048]{2,1,0:T(2,128)(2,1)}), bf16[32,2,2048]{2,1,0:T(2,128)(2,1)}, u32[]{:S(2)}, u32[]{:S(2)}) async-start(bf16[32,2,2048]{2,1,0:T(2,128)(2,1)} %reshape.476), calls=%async_computation.1 | async-start | bytes 524288 | tf_op jit(solution)/shard_map/all_to_all | solution.py:116
  87.5 26.7 %copy-start.2 = (bf16[128,900]{1,0:T(8,128)(2,1)S(1)}, bf16[128,900]{1,0:T(8,128)(2,1)}, u32[]{:S(2)}) copy-start(bf16[128,900]{1,0:T(8,128)(2,1)} %convert_element_type.122) | copy-start | bytes 691204
  109.1 5.8 %copy-start.1 = (bf16[32,32,900]{2,1,0:T(8,128)(2,1)S(1)}, bf16[32,32,900]{2,1,0:T(8,128)(2,1)}, u32[]{:S(2)}) copy-start(bf16[32,32,900]{2,1,0:T(8,128)(2,1)} %shard_map.73) | copy-start | bytes 5529604

commit v4 on v3

--- a/solution.py
+++ b/solution.py
@@ -45,7 +45,36 @@
     partial = lax.dot_general(
         forward_rows, flat_field, (((1,), (1,)), ((), ())), preferred_element_type=jnp.float32
     ).reshape(n_dev, m_dev, 2, channels, lat_rows)
-    gathered = lax.all_to_all(partial, BOTH, 0, 0, tiled=True)
+    gathered_raw = lax.all_to_all(partial, BOTH, 0, 0, tiled=True)
+    rim_cols = ((lon_cols + 4 + 127) // 128) * 128
+    lat_n = lax.axis_size("lat")
+    south = lax.ppermute(
+        field[:, :2], "lat", [((i + 1), i) for i in range(lat_n - 1)]
+    )
+    north = lax.ppermute(
+        field[:, lat_rows - 2 :], "lat", [(i, (i + 1)) for i in range(lat_n - 1)]
+    )
+    rows_ext = jnp.concatenate(
+        [north, field, south, jnp.zeros((channels, 4, lon_cols), field.dtype)], axis=1
+    )
+    rim_rows = rows_ext.shape[1]
+    east = lax.ppermute(
+        rows_ext[:, :, :2], "lon", [((i + 1) % lon_count, i) for i in range(lon_count)]
+    )
+    west = lax.ppermute(
+        rows_ext[:, :, lon_cols - 2 :], "lon", [(i, (i + 1) % lon_count) for i in range(lon_count)]
+    )
+    rim = jnp.concatenate(
+        [
+            rows_ext,
+            east,
+            jnp.zeros((channels, rim_rows, rim_cols - lon_cols - 4), field.dtype),
+            west,
+        ],
+        axis=2,
+    )
+    conv_out = depthwise_conv(offsets, conv_weight, rim, lat_rows, lon_cols)
+    gathered, conv_out = lax.optimization_barrier((gathered_raw, conv_out))
     summed = gathered.reshape(lat_count, lon_count, m_dev, 2, channels, lat_rows).sum(axis=1)
     raw_spec = jnp.transpose(summed, (1, 2, 3, 0, 4)).reshape(m_dev, 2, channels, total_lat)
 
@@ -122,34 +151,6 @@
         spectral_rows, inverse_rows, (((0,), (0,)), ((), ())), preferred_element_type=jnp.float32
     ).reshape(channels, lat_rows, lon_cols)
 
-    rim_cols = ((lon_cols + 4 + 127) // 128) * 128
-    lat_n = lax.axis_size("lat")
-    south = lax.ppermute(
-        field[:, :2], "lat", [((i + 1), i) for i in range(lat_n - 1)]
-    )
-    north = lax.ppermute(
-        field[:, lat_rows - 2 :], "lat", [(i, (i + 1)) for i in range(lat_n - 1)]
-    )
-    rows_ext = jnp.concatenate(
-        [north, field, south, jnp.zeros((channels, 4, lon_cols), field.dtype)], axis=1
-    )
-    rim_rows = rows_ext.shape[1]
-    east = lax.ppermute(
-        rows_ext[:, :, :2], "lon", [((i + 1) % lon_count, i) for i in range(lon_count)]
-    )
-    west = lax.ppermute(
-        rows_ext[:, :, lon_cols - 2 :], "lon", [(i, (i + 1) % lon_count) for i in range(lon_count)]
-    )
-    rim = jnp.concatenate(
-        [
-            rows_ext,
-            east,
-            jnp.zeros((channels, rim_rows, rim_cols - lon_cols - 4), field.dtype),
-            west,
-        ],
-        axis=2,
-    )
-    conv_out = depthwise_conv(offsets, conv_weight, rim, lat_rows, lon_cols)
     return (conv_out.astype(jnp.float32) + jax.nn.gelu(synthesis, approximate=True)).astype(
         jnp.bfloat16
     )

time: 119 us -> 112 us (0.941)
  waiting for transfers between devices: 0.02 us -> 8.23 us
  matrix products: 12.5 us -> 6.55 us
  other arithmetic: 23.1 us -> 18.7 us
  local copies, waits for them, and re-layouts: 27.2 us -> 23.4 us
    all_to_all x1, waiting for transfers between devices: 0.01 us -> 8.21 us  [per_device(): full_rows = lax.all_to_all(outgoing, BOTH, 0, 0, tiled=True)]
    unnamed x23 -> x94, local copies, waits for them, and re-layouts: 13.9 us -> 9.29 us
    sub x3, other arithmetic: 2.94 us -> 0.91 us  [per_device(): real_part = cos_t * window[:, 0] - sin_t * window[:, 1]]
    dot_general x2, matrix products: 2.31 us -> 0.39 us  [per_device(): jnp.einsum('mupc,ucd->mupd', coeffs, mix_pairs[1, :, parity], preferred_e...]
    dot_general x2, matrix products: 2.31 us -> 0.39 us  [per_device(): jnp.einsum('mupc,ucd->mupd', coeffs, mix_pairs[0, :, parity], preferred_e...]
    reduce_sum x1, other arithmetic: 1.91 us -> 0.27 us  [per_device(): gathered.reshape(lat_count, lon_count, m_dev, 2, channels, lat_rows)]
    dot_general x2, matrix products: 1.93 us -> 0.39 us  [per_device(): jnp.einsum('mui,mpci->mupc', degree_plane, operand, preferred_element_typ...]
    dot_general x2, matrix products: 1.92 us -> 0.4 us  [per_device(): jnp.einsum('mui,mupc->mpci', degree_plane, mixed, preferred_element_type=...]
  transfers between devices with their start and end apart: 6 -> 6, of which waited for: 0 -> 1; matrix products, arithmetic and copies ran while one was open for 45% -> 26% of each run, Pallas kernels for 18% -> 19%
where the time goes in v4:
time: 112 us
  local copies, waits for them, and re-layouts  23.4 us (21%)
  Pallas kernels  21.5 us (19%)
  starting transfers between devices  21.1 us (19%)
  other arithmetic  18.7 us (17%)
  between operations  12.3 us (11%)
  waiting for transfers between devices  8.23 us (7%)
  matrix products  6.55 us (6%)
    pallas_call x1, Pallas kernels, depthwise_conv(): pl.pallas_call(body, grid_spec=pltpu.PrefetchScalarGridSpec(num_scalar_pr...  21.5 us
    unnamed x94, local copies, waits for them, and re-layouts  9.29 us
    all_to_all x1, waiting for transfers between devices, per_device(): full_rows = lax.all_to_all(outgoing, BOTH, 0, 0, tiled=True)  8.21 us
    all_to_all x1, starting transfers between devices, per_device(): gathered_raw = lax.all_to_all(partial, BOTH, 0, 0, tiled=True)  7.58 us
    all_to_all x1, starting transfers between devices, per_device(): full_rows = lax.all_to_all(outgoing, BOTH, 0, 0, tiled=True)  5.81 us
    concatenate x1, other arithmetic, per_device(): jnp.concatenate([rows_ext, east, jnp.zeros((channels, rim_rows, rim_cols...  5.17 us
    ppermute x1, starting transfers between devices, per_device(): lax.ppermute(field[:, lat_rows - 2:], 'lat', [(i, i + 1) for i in range(l...  4.87 us
    dot_general x1, matrix products, per_device(): lax.dot_general(forward_rows, flat_field, (((1,), (1,)), ((), ())), prefe...  3.32 us
  transfers between devices with their start and end apart: 6, of which 1 were waited for; matrix products, arithmetic and copies ran while one was open for 26% of the time, Pallas kernels for 19%

profile of v4, /device:TPU:0, one launch (start us, length us, event | category | flops | bytes accessed | tf_op | source)
XLA Modules:
  0.0 111.7 jit_solution(2560726036224434473)
XLA Ops:
  0.0 2.0 %fusion.73 = (bf16[32,2,900]{2,1,0:T(2,128)(2,1)}, bf16[32,2,900]{2,1,0:T(2,128)(2,1)S(1)}) fusion(bf16[32,32,900]{2,1,0:T(8,128)(2,1)} %param.7), kind=kLoop, calls=%fused_computation.202 | loop fusion | bytes 460800 | tf_op jit(solution)/shard_map/slice | solution.py:55
  2.1 4.9 %collective-permute-start = (bf16[32,2,900]{2,1,0:T(2,128)(2,1)}, bf16[32,2,900]{2,1,0:T(2,128)(2,1)S(1)}, u32[]{:S(2)}, u32[]{:S(2)}) collective-permute-start(bf16[32,2,900]{2,1,0:T(2,128)(2,1)} %get-tuple-element.11), channel_id=1, source_target_pairs={{0,4},{4,8},{8,12},{12,16},{16,20},{20,24},{24,28},{1,5},{5,9},{9,... | collective-permute-start | bytes 345608 | tf_op jit(solution)/shard_map/ppermute | solution.py:54
  6.9 1.3 %collective-permute-start.1 = (bf16[32,2,900]{2,1,0:T(2,128)(2,1)S(1)}, bf16[32,2,900]{2,1,0:T(2,128)(2,1)}, u32[]{:S(2)}, u32[]{:S(2)}) collective-permute-start(bf16[32,2,900]{2,1,0:T(2,128)(2,1)S(1)} %get-tuple-element.12), channel_id=1, source_target_pairs={{4,0},{8,4},{12,8},{16,12},{20,16},{24,20},{28,24},{5,1},{9,5},{13... | collective-permute-start | bytes 345608 | tf_op jit(solution)/shard_map/ppermute | solution.py:51
  8.3 1.3 %multiply_convert_fusion.3 = (bf16[32,2,1,900]{3,0,2,1:T(8,128)(2,1)S(1)}, bf16[32,2,1,900]{3,0,2,1:T(8,128)(2,1)S(1)}) fusion(s32[900]{0:T(1024)S(1)} %iota_add_fusion, s32[32,2]{0,1:T(2,128)S(1)} %multiply_add_fusion.9), kind=kLoop, calls=%fused_computation.69 | loop fusion | flops 748800 | bytes 234256 | tf_op jit(solution)/shard_map/convert.10
  9.5 3.3 %fusion.9 = f32[32,2,2,32,32]{4,0,3,2,1:T(8,128)S(1)} fusion(bf16[32,32,900]{2,1,0:T(8,128)(2,1)} %param.7, bf16[32,2,1,900]{3,0,2,1:T(8,128)(2,1)S(1)} %get-tuple-element.77, bf16[32,2,1,900]{3,0,2,1:T(8,128)(2,1)S(1)} %get-tuple-element.76), kind=kOutput, calls=%fused_computation.11 | convolution fusion | flops 236390400 | bytes 2597888 | tf_op jit(solution)/shard_map/dot_general | solution.py:45
  12.9 2.5 %copy.74 = f32[32,2,2,32,32]{4,3,2,1,0:T(8,128)} copy(f32[32,2,2,32,32]{4,0,3,2,1:T(8,128)S(1)} %fusion.9) | data formatting | bytes 1048576 | tf_op jit(solution)/shard_map/dot_general | solution.py:45
  15.5 3.2 %reshape.474 = f32[32,1,4096]{2,1,0:T(1,128)} reshape(f32[32,2,2,32,32]{4,3,2,1,0:T(8,128)} %copy.74) | data formatting | bytes 1048576
  18.6 7.6 %all-to-all-start = ((f32[32,1,4096]{2,1,0:T(1,128)}), f32[32,1,4096]{2,1,0:T(1,128)S(1)}, u32[]{:S(2)}, u32[]{:S(2)}) async-start(f32[32,1,4096]{2,1,0:T(1,128)} %reshape.474), calls=%async_computation | async-start | bytes 1048576 | tf_op jit(solution)/shard_map/all_to_all | solution.py:48
  26.3 0.6 slice_bitcast_fusion.35
  26.9 0.7 fusion.74
  27.6 0.1 fusion.59
  27.7 0.7 fusion.65
  28.4 0.6 compare_convert_fusion.2
  29.0 0.7 slice_bitcast_fusion.8
  29.6 0.6 compare_convert_fusion
  30.3 0.7 fusion.75
  31.1 1.9 %pad_maximum_fusion.4 = (bf16[32,40,2]{2,1,0:T(8,128)(2,1)}, bf16[32,40,2]{2,1,0:T(8,128)(2,1)}) fusion(bf16[32,4,900]{2,1,0:T(4,128)(2,1)S(1)} %broadcast_in_dim.84, bf16[32,2,900]{2,1,0:T(2,128)(2,1)} %collective-permute-done.1, bf16[32,32,900]{2,1,0:T(8,128)(2,1)S(1)} %copy-done, bf16[32,2,900]{2,1,0:T(2,128)(2,1)S(1)} %collective-permute-done), kind=kLoop, calls=%fused_computation.47 | loop fusion | flops 40960 | bytes 2314240 | tf_op jit(solution)/shard_map/slice | solution.py:62
  33.0 1.5 %collective-permute-start.2 = (bf16[32,40,2]{2,1,0:T(8,128)(2,1)}, bf16[32,40,2]{2,1,0:T(8,128)(2,1)}, u32[]{:S(2)}, u32[]{:S(2)}) collective-permute-start(bf16[32,40,2]{2,1,0:T(8,128)(2,1)} %get-tuple-element.9), channel_id=1, source_target_pairs={{1,0},{2,1},{3,2},{0,3},{5,4},{6,5},{7,6},{4,7},{9,8},{10,9},{11,1... | collective-permute-start | bytes 15368 | tf_op jit(solution)/shard_map/ppermute | solution.py:61
  34.5 0.6 fusion.66
  46.4 0.7 copy.75.offs_ref
  47.1 0.7 copy.76.w_ref
  47.8 2.3 %copy.79 = bf16[2,64,32,32]{3,2,1,0:T(8,128)(2,1)} copy(bf16[2,64,32,32]{1,3,2,0:T(8,128)(2,1)S(1)} %copy-done.3) | data formatting | bytes 524288 | tf_op args[6]
  50.2 5.2 %pad_maximum_fusion.rim_ref = bf16[32,40,1024]{2,1,0:T(8,128)(2,1)} fusion(bf16[32,40,2]{2,1,0:T(8,128)(2,1)} %collective-permute-done.3, bf16[32,40,2]{2,1,0:T(8,128)(2,1)} %collective-permute-done.2, bf16[32,4,900]{2,1,0:T(4,128)(2,1)S(1)} %broadcast_in_dim.84, bf16[32,2,900]{2,1,0:T(2,128)(2,1)} %collective-permute-done.1, ...), kind=kLoop, calls=%fused_computation.10 | loop fusion | flops 18350080 | bytes 4937728 | tf_op jit(solution)/shard_map/concatenate | solution.py:67
  55.4 21.5 %shard_map.73 = bf16[32,32,900]{2,1,0:T(8,128)(2,1)} custom-call(s32[9,2]{1,0:T(8,128)} %copy.75.offs_ref, f32[32,9]{1,0:T(8,128)} %copy.76.w_ref, bf16[32,40,1024]{2,1,0:T(8,128)(2,1)} %pad_maximum_fusion.rim_ref), custom_call_target="tpu_custom_call" | custom-call | flops 471859200 | bytes 4464640 | tf_op jit(solution)/shard_map/pallas_call | solution.py:176
  76.9 0.6 broadcast.510
  77.5 1.9 %reduce = f32[32,4096]{1,0:T(8,128)S(1)} reduce(f32[32,1,4096]{2,1,0:T(1,128)S(1)} %all-to-all-done, f32[]{:T(128)} %broadcast.510), dimensions={1}, to_apply=%all_to_all.6.reduce_sub_computation | reduce | bytes 1048580 | tf_op jit(solution)/shard_map/all_to_all | solution.py:48
  79.6 0.7 reshape.475
  80.4 0.3 bitcast_reduce_fusion
  80.7 0.3 copy.77
  81.0 0.2 reshape.460
  81.2 0.3 multiply_subtract_fusion.1
  81.6 0.3 multiply_subtract_fusion
  82.0 0.3 multiply_subtract_fusion.2
  82.4 0.2 fusion.37
  82.5 0.1 rev.8
  82.7 0.2 fusion.14
  82.9 0.1 copy.81
  83.0 0.2 convolution_bitcast_fusion.2
  83.2 0.2 convolution_bitcast_fusion.3
  83.4 0.2 fusion.13
  83.6 0.1 copy.87
  83.7 0.2 convolution_bitcast_fusion
  83.9 0.2 convolution_bitcast_fusion.1
  84.2 0.1 pad_maximum_fusion.6
  84.3 0.2 fusion.48
  84.6 0.1 pad_maximum_fusion.7
  84.7 0.2 subtract_multiply_fusion
  84.9 0.1 multiply_convert_fusion.4
  85.0 0.1 rev.9
  85.1 0.1 concatenate.20
  85.2 0.1 concatenate.19
  85.3 0.2 maximum_bitcast_fusion.2
  85.5 0.2 broadcast_in_dim.89
  85.8 1.7 %reshape.476 = bf16[32,2,2048]{2,1,0:T(2,128)(2,1)} reshape(bf16[32,2,2,32,32]{4,3,2,1,0:T(8,128)(2,1)S(1)} %bitcast.174) | data formatting | bytes 524288
  87.5 5.8 %all-to-all-start.1 = ((bf16[32,2,2048]{2,1,0:T(2,128)(2,1)}), bf16[32,2,2048]{2,1,0:T(2,128)(2,1)S(1)}, u32[]{:S(2)}, u32[]{:S(2)}) async-start(bf16[32,2,2048]{2,1,0:T(2,128)(2,1)} %reshape.476), calls=%async_computation.1 | async-start | bytes 524288 | tf_op jit(solution)/shard_map/all_to_all | solution.py:145
  93.4 1.1 %multiply_convert_fusion.1 = (bf16[64,1,900]{2,0,1:T(8,128)(2,1)S(1)}, bf16[64,1,900]{2,0,1:T(8,128)(2,1)S(1)}) fusion(s32[900]{0:T(1024)S(1)} %iota_add_fusion, f32[64]{0:T(128)S(1)} %get-tuple-element.97, f32[64]{0:T(128)S(1)} %get-tuple-element.98), kind=kLoop, calls=%fused_computation.64 | loop fusion | flops 748800 | bytes 234512 | tf_op jit(solution)/shard_map/convert
  94.6 0.3 copy.93
  94.8 0.9 convert_element_type.122
  95.7 8.2 %all-to-all-done.1 = bf16[32,2,2048]{2,1,0:T(2,128)(2,1)S(1)} async-done(((bf16[32,2,2048]{2,1,0:T(2,128)(2,1)}), bf16[32,2,2048]{2,1,0:T(2,128)(2,1)S(1)}, u32[]{:S(2)}, u32[]{:S(2)}) %all-to-all-start.1) | async-done | bytes 262176 | tf_op jit(solution)/shard_map/all_to_all | solution.py:145
  103.9 0.5 reshape.477
  104.5 1.8 %reshape.464 = bf16[128,1024]{1,0:T(8,128)(2,1)} reshape(bf16[32,2,2,32,32]{4,3,2,1,0:T(8,128)(2,1)S(1)} %reshape.477) | data formatting | bytes 524288 | tf_op jit(solution)/shard_map/reshape | solution.py:146
  106.3 1.1 copy.92
  107.4 1.6 %fusion.21 = f32[32,32,900]{2,1,0:T(8,128)S(1)} fusion(bf16[32,32,128]{2,1,0:T(8,128)(2,1)S(1)} %bitcast.176, bf16[128,900]{1,0:T(8,128)(2,1)} %convert_element_type.122), kind=kOutput, calls=%fused_computation.61 | convolution fusion | flops 235929600 | bytes 4178944 | tf_op jit(solution)/shard_map/dot_general | solution.py:150
  109.1 2.6 %fusion.8 = bf16[32,32,900]{2,1,0:T(8,128)(2,1)} fusion(f32[32,32,900]{2,1,0:T(8,128)S(1)} %fusion.21, bf16[32,32,900]{2,1,0:T(8,128)(2,1)S(1)} %copy-done.1), kind=kLoop, calls=%fused_computation.9 | loop fusion | flops 10137600 | bytes 7372800 | tf_op jit(solution)/shard_map/convert_element_type | solution.py:154
  (108 shorter events, 0.6 us)
Async XLA Ops:
  2.1 28.9 %collective-permute-start = (bf16[32,2,900]{2,1,0:T(2,128)(2,1)}, bf16[32,2,900]{2,1,0:T(2,128)(2,1)S(1)}, u32[]{:S(2)}, u32[]{:S(2)}) collective-permute-start(bf16[32,2,900]{2,1,0:T(2,128)(2,1)} %get-tuple-element.11), channel_id=1, source_target_pairs={{0,4},{4,8},{8,12},{12,16},{16,20},{20,24},{24,28},{1,5},{5,9},{9,... | collective-permute-start | bytes 345608 | tf_op jit(solution)/shard_map/ppermute | solution.py:54
  6.9 24.0 %collective-permute-start.1 = (bf16[32,2,900]{2,1,0:T(2,128)(2,1)S(1)}, bf16[32,2,900]{2,1,0:T(2,128)(2,1)}, u32[]{:S(2)}, u32[]{:S(2)}) collective-permute-start(bf16[32,2,900]{2,1,0:T(2,128)(2,1)S(1)} %get-tuple-element.12), channel_id=1, source_target_pairs={{4,0},{8,4},{12,8},{16,12},{20,16},{24,20},{28,24},{5,1},{9,5},{13... | collective-permute-start | bytes 345608 | tf_op jit(solution)/shard_map/ppermute | solution.py:51
  12.9 13.4 %copy-start.7 = (s32[9,2]{0,1:T(2,128)S(1)}, s32[9,2]{0,1:T(2,128)}, u32[]{:S(2)}) copy-start(s32[9,2]{0,1:T(2,128)} %param.8) | copy-start | bytes 220
  12.9 13.4 %copy-start.8 = (f32[32,9]{0,1:T(8,128)S(1)}, f32[32,9]{0,1:T(8,128)}, u32[]{:S(2)}) copy-start(f32[32,9]{0,1:T(8,128)} %param.9) | copy-start | bytes 3460
  12.9 14.0 %copy-start.4 = (bf16[2,64,128]{2,1,0:T(8,128)(2,1)S(1)}, bf16[2,64,128]{2,1,0:T(8,128)(2,1)}, u32[]{:S(2)}) copy-start(bf16[2,64,128]{2,1,0:T(8,128)(2,1)} %param.10) | copy-start | bytes 98308
  12.9 14.8 %copy-start.19 = (s32[128]{0:T(128)S(1)}, s32[128]{0:T(128)}, u32[]{:S(2)}) copy-start(s32[128]{0:T(128)} %param.12) | copy-start | bytes 1540
  12.9 14.8 %copy-start.41 = (f32[128]{0:T(128)S(1)}, f32[128]{0:T(128)}, u32[]{:S(2)}) copy-start(f32[128]{0:T(128)} %param.11) | copy-start | bytes 1540
  12.9 18.1 %copy-start = (bf16[32,32,900]{2,1,0:T(8,128)(2,1)S(1)}, bf16[32,32,900]{2,1,0:T(8,128)(2,1)}, u32[]{:S(2)}) copy-start(bf16[32,32,900]{2,1,0:T(8,128)(2,1)} %param.7) | copy-start | bytes 5529604
  15.5 32.3 %copy-start.3 = (bf16[2,64,32,32]{1,3,2,0:T(8,128)(2,1)S(1)}, bf16[2,64,32,32]{1,3,2,0:T(8,128)(2,1)}, u32[]{:S(2)}) copy-start(bf16[2,64,32,32]{1,3,2,0:T(8,128)(2,1)} %param.13) | copy-start | bytes 786436
  18.6 58.2 %all-to-all-start = ((f32[32,1,4096]{2,1,0:T(1,128)}), f32[32,1,4096]{2,1,0:T(1,128)S(1)}, u32[]{:S(2)}, u32[]{:S(2)}) async-start(f32[32,1,4096]{2,1,0:T(1,128)} %reshape.474), calls=%async_computation | async-start | bytes 1048576 | tf_op jit(solution)/shard_map/all_to_all | solution.py:48
  33.0 17.2 %collective-permute-start.2 = (bf16[32,40,2]{2,1,0:T(8,128)(2,1)}, bf16[32,40,2]{2,1,0:T(8,128)(2,1)}, u32[]{:S(2)}, u32[]{:S(2)}) collective-permute-start(bf16[32,40,2]{2,1,0:T(8,128)(2,1)} %get-tuple-element.9), channel_id=1, source_target_pairs={{1,0},{2,1},{3,2},{0,3},{5,4},{6,5},{7,6},{4,7},{9,8},{10,9},{11,1... | collective-permute-start | bytes 15368 | tf_op jit(solution)/shard_map/ppermute | solution.py:61
  34.5 15.7 %collective-permute-start.3 = (bf16[32,40,2]{2,1,0:T(8,128)(2,1)}, bf16[32,40,2]{2,1,0:T(8,128)(2,1)}, u32[]{:S(2)}, u32[]{:S(2)}) collective-permute-start(bf16[32,40,2]{2,1,0:T(8,128)(2,1)} %get-tuple-element.10), channel_id=1, source_target_pairs={{0,1},{1,2},{2,3},{3,0},{4,5},{5,6},{6,7},{7,4},{8,9},{9,10},{10,1... | collective-permute-start | bytes 15368 | tf_op jit(solution)/shard_map/ppermute | solution.py:64
  76.8 4.3 %copy-start.32 = (f32[2]{0:T(128)S(1)}, f32[2]{0:T(128)}, u32[]{:S(2)}) copy-start(f32[2]{0:T(128)} %get-tuple-element.68) | copy-start | bytes 28
  76.8 4.3 %copy-start.33 = (f32[2]{0:T(128)S(1)}, f32[2]{0:T(128)}, u32[]{:S(2)}) copy-start(f32[2]{0:T(128)} %get-tuple-element.72) | copy-start | bytes 28
  76.8 4.3 %copy-start.34 = (f32[2]{0:T(128)S(1)}, f32[2]{0:T(128)}, u32[]{:S(2)}) copy-start(f32[2]{0:T(128)} %get-tuple-element.73) | copy-start | bytes 28
  76.8 4.3 %copy-start.35 = (f32[2]{0:T(128)S(1)}, f32[2]{0:T(128)}, u32[]{:S(2)}) copy-start(f32[2]{0:T(128)} %get-tuple-element.103) | copy-start | bytes 28
  76.9 4.3 %copy-start.36 = (f32[2]{0:T(128)S(1)}, f32[2]{0:T(128)}, u32[]{:S(2)}) copy-start(f32[2]{0:T(128)} %get-tuple-element.104) | copy-start | bytes 28
  76.9 4.3 %copy-start.37 = (f32[2]{0:T(128)S(1)}, f32[2]{0:T(128)}, u32[]{:S(2)}) copy-start(f32[2]{0:T(128)} %get-tuple-element.108) | copy-start | bytes 28
  77.5 4.0 %copy-start.26 = (f32[2]{0:T(128)S(1)}, f32[2]{0:T(128)}, u32[]{:S(2)}) copy-start(f32[2]{0:T(128)} %get-tuple-element.67) | copy-start | bytes 28
  77.5 4.1 %copy-start.27 = (f32[2]{0:T(128)S(1)}, f32[2]{0:T(128)}, u32[]{:S(2)}) copy-start(f32[2]{0:T(128)} %get-tuple-element.74) | copy-start | bytes 28
  77.5 4.1 %copy-start.28 = (f32[2]{0:T(128)S(1)}, f32[2]{0:T(128)}, u32[]{:S(2)}) copy-start(f32[2]{0:T(128)} %get-tuple-element.75) | copy-start | bytes 28
  77.5 4.1 %copy-start.29 = (f32[2]{0:T(128)S(1)}, f32[2]{0:T(128)}, u32[]{:S(2)}) copy-start(f32[2]{0:T(128)} %get-tuple-element.101) | copy-start | bytes 28
  77.5 4.1 %copy-start.30 = (f32[2]{0:T(128)S(1)}, f32[2]{0:T(128)}, u32[]{:S(2)}) copy-start(f32[2]{0:T(128)} %get-tuple-element.102) | copy-start | bytes 28
  77.5 4.1 %copy-start.31 = (f32[2]{0:T(128)S(1)}, f32[2]{0:T(128)}, u32[]{:S(2)}) copy-start(f32[2]{0:T(128)} %get-tuple-element.109) | copy-start | bytes 28
  79.5 2.4 %copy-start.20 = (f32[2]{0:T(128)S(1)}, f32[2]{0:T(128)}, u32[]{:S(2)}) copy-start(f32[2]{0:T(128)} %get-tuple-element.69) | copy-start | bytes 28
  79.5 2.4 %copy-start.21 = (f32[2]{0:T(128)S(1)}, f32[2]{0:T(128)}, u32[]{:S(2)}) copy-start(f32[2]{0:T(128)} %get-tuple-element.70) | copy-start | bytes 28
  79.5 2.4 %copy-start.22 = (f32[2]{0:T(128)S(1)}, f32[2]{0:T(128)}, u32[]{:S(2)}) copy-start(f32[2]{0:T(128)} %get-tuple-element.71) | copy-start | bytes 28
  79.5 2.4 %copy-start.23 = (f32[2]{0:T(128)S(1)}, f32[2]{0:T(128)}, u32[]{:S(2)}) copy-start(f32[2]{0:T(128)} %get-tuple-element.105) | copy-start | bytes 28
  79.5 2.4 %copy-start.24 = (f32[2]{0:T(128)S(1)}, f32[2]{0:T(128)}, u32[]{:S(2)}) copy-start(f32[2]{0:T(128)} %get-tuple-element.106) | copy-start | bytes 28
  79.5 2.4 %copy-start.25 = (f32[2]{0:T(128)S(1)}, f32[2]{0:T(128)}, u32[]{:S(2)}) copy-start(f32[2]{0:T(128)} %get-tuple-element.107) | copy-start | bytes 28
  79.5 2.8 %copy-start.10 = (f32[32]{0:T(128)S(1)}, f32[32]{0:T(128)}, u32[]{:S(2)}) copy-start(f32[32]{0:T(128)} %get-tuple-element.49) | copy-start | bytes 388
  79.5 2.8 %copy-start.11 = (f32[32]{0:T(128)S(1)}, f32[32]{0:T(128)}, u32[]{:S(2)}) copy-start(f32[32]{0:T(128)} %get-tuple-element.50) | copy-start | bytes 388
  79.5 2.8 %copy-start.12 = (f32[32]{0:T(128)S(1)}, f32[32]{0:T(128)}, u32[]{:S(2)}) copy-start(f32[32]{0:T(128)} %get-tuple-element.51) | copy-start | bytes 388
  79.5 2.8 %copy-start.13 = (f32[32]{0:T(128)S(1)}, f32[32]{0:T(128)}, u32[]{:S(2)}) copy-start(f32[32]{0:T(128)} %get-tuple-element.52) | copy-start | bytes 388
  79.6 2.8 %copy-start.14 = (f32[32]{0:T(128)S(1)}, f32[32]{0:T(128)}, u32[]{:S(2)}) copy-start(f32[32]{0:T(128)} %get-tuple-element.53) | copy-start | bytes 388
  79.6 2.8 %copy-start.15 = (f32[32]{0:T(128)S(1)}, f32[32]{0:T(128)}, u32[]{:S(2)}) copy-start(f32[32]{0:T(128)} %get-tuple-element.54) | copy-start | bytes 388
  79.6 2.8 %copy-start.16 = (f32[32]{0:T(128)S(1)}, f32[32]{0:T(128)}, u32[]{:S(2)}) copy-start(f32[32]{0:T(128)} %get-tuple-element.55) | copy-start | bytes 388
  79.6 2.8 %copy-start.17 = (f32[32]{0:T(128)S(1)}, f32[32]{0:T(128)}, u32[]{:S(2)}) copy-start(f32[32]{0:T(128)} %get-tuple-element.56) | copy-start | bytes 388
  79.6 2.8 %copy-start.18 = (f32[32]{0:T(128)S(1)}, f32[32]{0:T(128)}, u32[]{:S(2)}) copy-start(f32[32]{0:T(128)} %get-tuple-element.57) | copy-start | bytes 388
  80.3 2.3 %copy-start.5 = (bf16[2,32,1,128]{3,2,1,0:T(2,128)(2,1)S(1)}, bf16[2,32,1,128]{3,2,1,0:T(2,128)(2,1)}, u32[]{:S(2)}) copy-start(bf16[2,32,1,128]{3,2,1,0:T(2,128)(2,1)} %get-tuple-element.47) | copy-start | bytes 49156
  80.3 2.3 %copy-start.39 = (f32[2,32]{1,0:T(2,128)S(1)}, f32[2,32]{1,0:T(2,128)}, u32[]{:S(2)}) copy-start(f32[2,32]{1,0:T(2,128)} %get-tuple-element.91) | copy-start | bytes 772
  80.3 2.3 %copy-start.40 = (f32[2,128]{1,0:T(2,128)S(1)}, f32[2,128]{1,0:T(2,128)}, u32[]{:S(2)}) copy-start(f32[2,128]{1,0:T(2,128)} %fusion.65) | copy-start | bytes 3076
  80.3 2.3 %copy-start.42 = (pred[2]{0:T(512)(128)(4,1)S(1)}, pred[2]{0:T(512)(128)(4,1)}, u32[]{:S(2)}) copy-start(pred[2]{0:T(512)(128)(4,1)} %get-tuple-element.95) | copy-start | bytes 10
  80.3 2.6 %copy-start.2 = (bf16[2,64,32,32]{3,2,1,0:T(8,128)(2,1)S(1)}, bf16[2,64,32,32]{3,2,1,0:T(8,128)(2,1)}, u32[]{:S(2)}) copy-start(bf16[2,64,32,32]{3,2,1,0:T(8,128)(2,1)} %copy.79) | copy-start | bytes 786436
  80.3 3.0 %copy-start.6 = (bf16[2,32,1,128]{3,2,1,0:T(2,128)(2,1)S(1)}, bf16[2,32,1,128]{3,2,1,0:T(2,128)(2,1)}, u32[]{:S(2)}) copy-start(bf16[2,32,1,128]{3,2,1,0:T(2,128)(2,1)} %get-tuple-element.48) | copy-start | bytes 49156
  80.4 3.0 %copy-start.38 = (f32[2,32]{1,0:T(2,128)S(1)}, f32[2,32]{1,0:T(2,128)}, u32[]{:S(2)}) copy-start(f32[2,32]{1,0:T(2,128)} %get-tuple-element.92) | copy-start | bytes 772
  80.4 3.0 %copy-start.43 = (pred[2]{0:T(512)(128)(4,1)S(1)}, pred[2]{0:T(512)(128)(4,1)}, u32[]{:S(2)}) copy-start(pred[2]{0:T(512)(128)(4,1)} %get-tuple-element.96) | copy-start | bytes 10
  80.6 4.0 %copy-start.9 = (f32[2,128]{1,0:T(2,128)S(1)}, f32[2,128]{1,0:T(2,128)}, u32[]{:S(2)}) copy-start(f32[2,128]{1,0:T(2,128)} %compare_convert_fusion) | copy-start | bytes 3076
  87.5 16.4 %all-to-all-start.1 = ((bf16[32,2,2048]{2,1,0:T(2,128)(2,1)}), bf16[32,2,2048]{2,1,0:T(2,128)(2,1)S(1)}, u32[]{:S(2)}, u32[]{:S(2)}) async-start(bf16[32,2,2048]{2,1,0:T(2,128)(2,1)} %reshape.476), calls=%async_computation.1 | async-start | bytes 524288 | tf_op jit(solution)/shard_map/all_to_all | solution.py:145
  94.8 14.2 %copy-start.1 = (bf16[32,32,900]{2,1,0:T(8,128)(2,1)S(1)}, bf16[32,32,900]{2,1,0:T(8,128)(2,1)}, u32[]{:S(2)}) copy-start(bf16[32,32,900]{2,1,0:T(8,128)(2,1)} %shard_map.73) | copy-start | bytes 5529604

commit v5 on v4

--- a/solution.py
+++ b/solution.py
@@ -48,30 +48,49 @@
     gathered_raw = lax.all_to_all(partial, BOTH, 0, 0, tiled=True)
     rim_cols = ((lon_cols + 4 + 127) // 128) * 128
     lat_n = lax.axis_size("lat")
-    south = lax.ppermute(
-        field[:, :2], "lat", [((i + 1), i) for i in range(lat_n - 1)]
-    )
-    north = lax.ppermute(
-        field[:, lat_rows - 2 :], "lat", [(i, (i + 1)) for i in range(lat_n - 1)]
-    )
-    rows_ext = jnp.concatenate(
-        [north, field, south, jnp.zeros((channels, 4, lon_cols), field.dtype)], axis=1
-    )
-    rim_rows = rows_ext.shape[1]
-    east = lax.ppermute(
-        rows_ext[:, :, :2], "lon", [((i + 1) % lon_count, i) for i in range(lon_count)]
-    )
+    lon_n = lon_count
+
+    def lin(a, b):
+        return a * lon_n + b % lon_n
+
+    down = [(i, i + 1) for i in range(lat_n - 1)]
+    up = [(i + 1, i) for i in range(lat_n - 1)]
+    north = lax.ppermute(field[:, lat_rows - 2 :], "lat", down)
+    south = lax.ppermute(field[:, :2], "lat", up)
+    east = lax.ppermute(field[:, :, :2], "lon", [((i + 1) % lon_n, i) for i in range(lon_n)])
     west = lax.ppermute(
-        rows_ext[:, :, lon_cols - 2 :], "lon", [(i, (i + 1) % lon_count) for i in range(lon_count)]
-    )
+        field[:, :, lon_cols - 2 :], "lon", [(i, (i + 1) % lon_n) for i in range(lon_n)]
+    )
+    grid_pairs = [(a, b) for a in range(lat_n) for b in range(lon_n)]
+    north_east = lax.ppermute(
+        field[:, lat_rows - 2 :, :2], BOTH,
+        [(lin(a, b), lin(a + 1, b - 1)) for a, b in grid_pairs if a < lat_n - 1],
+    )
+    north_west = lax.ppermute(
+        field[:, lat_rows - 2 :, lon_cols - 2 :], BOTH,
+        [(lin(a, b), lin(a + 1, b + 1)) for a, b in grid_pairs if a < lat_n - 1],
+    )
+    south_east = lax.ppermute(
+        field[:, :2, :2], BOTH,
+        [(lin(a, b), lin(a - 1, b - 1)) for a, b in grid_pairs if a > 0],
+    )
+    south_west = lax.ppermute(
+        field[:, :2, lon_cols - 2 :], BOTH,
+        [(lin(a, b), lin(a - 1, b + 1)) for a, b in grid_pairs if a > 0],
+    )
+
+    def band(centre, right, left):
+        gap = jnp.zeros((channels, centre.shape[1], rim_cols - lon_cols - 4), field.dtype)
+        return jnp.concatenate([centre, right, gap, left], axis=2)
+
     rim = jnp.concatenate(
         [
-            rows_ext,
-            east,
-            jnp.zeros((channels, rim_rows, rim_cols - lon_cols - 4), field.dtype),
-            west,
+            band(north, north_east, north_west),
+            band(field, east, west),
+            band(south, south_east, south_west),
+            jnp.zeros((channels, 4, rim_cols), field.dtype),
         ],
-        axis=2,
+        axis=1,
     )
     conv_out = depthwise_conv(offsets, conv_weight, rim, lat_rows, lon_cols)
     gathered, conv_out = lax.optimization_barrier((gathered_raw, conv_out))

time: 112 us -> 133 us (1.19)
  waiting for transfers between devices: 8.23 us -> 19.1 us
  starting transfers between devices: 21.1 us -> 30.7 us
    ppermute x4 -> x8, waiting for transfers between devices: 0.01 us -> 10.8 us  [the longest x1 4.84 us: per_device(): lax.ppermute(field[:, :2, lon_cols - 2:], BOTH, [(lin(a, b), lin(a - 1, b...]
    ppermute x4 -> x8, starting transfers between devices: 7.68 us -> 17.3 us  [the longest x1 5.23 us: per_device(): lax.ppermute(field[:, lat_rows - 2:, :2], BOTH, [(lin(a, b), lin(a + 1, b...]
    slice x1 -> x3, local copies, waits for them, and re-layouts: 2.05 us -> 5.69 us  [the longest x1 2.13 us: per_device(): north = lax.ppermute(field[:, lat_rows - 2:], 'lat', down)]
    slice x1 -> x0, other arithmetic: 1.9 us -> none  [per_device(): rows_ext[:, :, :2]]
    concatenate x1, other arithmetic: 5.17 us -> 6.98 us  [per_device(): jnp.concatenate([band(north, north_east, north_west), band(field, east, w...]
    unnamed x94 -> x90, local copies, waits for them, and re-layouts: 9.29 us -> 7.86 us
    all_to_all x1, starting transfers between devices: 5.81 us -> 7.18 us  [per_device(): full_rows = lax.all_to_all(outgoing, BOTH, 0, 0, tiled=True)]
    all_to_all x1, starting transfers between devices: 7.58 us -> 6.25 us  [per_device(): gathered_raw = lax.all_to_all(partial, BOTH, 0, 0, tiled=True)]
  transfers between devices with their start and end apart: 6 -> 10, of which waited for: 1 -> 4; matrix products, arithmetic and copies ran while one was open for 26% -> 23% of each run, Pallas kernels for 19% -> 16%
where the time goes in v5:
time: 133 us; the launch traced here: 132 us
  starting transfers between devices  30.7 us (23%)
  local copies, waits for them, and re-layouts  24.7 us (19%)
  Pallas kernels  21.5 us (16%)
  waiting for transfers between devices  19.1 us (14%)
  other arithmetic  17.8 us (13%)
  between operations  12.1 us (9%)
  matrix products  6.55 us (5%)
    pallas_call x1, Pallas kernels, depthwise_conv(): pl.pallas_call(body, grid_spec=pltpu.PrefetchScalarGridSpec(num_scalar_pr...  21.5 us
    all_to_all x1, waiting for transfers between devices, per_device(): full_rows = lax.all_to_all(outgoing, BOTH, 0, 0, tiled=True)  8.23 us
    unnamed x90, local copies, waits for them, and re-layouts  7.86 us
    all_to_all x1, starting transfers between devices, per_device(): full_rows = lax.all_to_all(outgoing, BOTH, 0, 0, tiled=True)  7.18 us
    concatenate x1, other arithmetic, per_device(): jnp.concatenate([band(north, north_east, north_west), band(field, east, w...  6.98 us
    all_to_all x1, starting transfers between devices, per_device(): gathered_raw = lax.all_to_all(partial, BOTH, 0, 0, tiled=True)  6.25 us
    ppermute x1, starting transfers between devices, per_device(): lax.ppermute(field[:, lat_rows - 2:, :2], BOTH, [(lin(a, b), lin(a + 1, b...  5.23 us
    ppermute x1, waiting for transfers between devices, per_device(): lax.ppermute(field[:, :2, lon_cols - 2:], BOTH, [(lin(a, b), lin(a - 1, b...  4.84 us
  transfers between devices with their start and end apart: 10, of which 4 were waited for; matrix products, arithmetic and copies ran while one was open for 23% of the time, Pallas kernels for 16%

profile of v5, /device:TPU:0, one launch (start us, length us, event | category | flops | bytes accessed | tf_op | source)
XLA Modules:
  0.0 132.5 jit_solution(11661594573511698722)
XLA Ops:
  0.0 1.7 %fusion.74 = (bf16[32,2,2]{2,1,0:T(2,128)(2,1)}, bf16[32,2,2]{2,1,0:T(2,128)(2,1)}, bf16[32,2,2]{2,1,0:T(2,128)(2,1)}, bf16[32,2,2]{2,1,0:T(2,128)(2,1)}) fusion(bf16[32,32,900]{2,1,0:T(8,128)(2,1)} %param.7), kind=kLoop, calls=%fused_computation.199 | loop fusion | bytes 2048 | tf_op jit(solution)/shard_map/slice | solution.py:66
  1.7 5.2 %collective-permute-start.1 = (bf16[32,2,2]{2,1,0:T(2,128)(2,1)}, bf16[32,2,2]{2,1,0:T(2,128)(2,1)S(1)}, u32[]{:S(2)}, u32[]{:S(2)}) collective-permute-start(bf16[32,2,2]{2,1,0:T(2,128)(2,1)} %get-tuple-element.11), channel_id=1, source_target_pairs={{0,7},{1,4},{2,5},{3,6},{4,11},{5,8},{6,9},{7,10},{8,15},{9,12},{1... | collective-permute-start | bytes 776 | tf_op jit(solution)/shard_map/ppermute | solution.py:65
  6.9 2.1 %fusion.73 = (bf16[32,2,900]{2,1,0:T(2,128)(2,1)}, bf16[32,2,900]{2,1,0:T(2,128)(2,1)}) fusion(bf16[32,32,900]{2,1,0:T(8,128)(2,1)} %param.7), kind=kLoop, calls=%fused_computation.198 | loop fusion | bytes 460800 | tf_op jit(solution)/shard_map/slice | solution.py:58
  9.0 4.1 %collective-permute-start = (bf16[32,2,900]{2,1,0:T(2,128)(2,1)}, bf16[32,2,900]{2,1,0:T(2,128)(2,1)}, u32[]{:S(2)}, u32[]{:S(2)}) collective-permute-start(bf16[32,2,900]{2,1,0:T(2,128)(2,1)} %get-tuple-element.9), channel_id=1, source_target_pairs={{0,4},{4,8},{8,12},{12,16},{16,20},{20,24},{24,28},{1,5},{5,9},{9,... | collective-permute-start | bytes 345608 | tf_op jit(solution)/shard_map/ppermute | solution.py:58
  13.1 1.3 collective-permute-start.5
  14.4 1.9 %fusion.75 = (bf16[32,32,2]{2,1,0:T(8,128)(2,1)}, bf16[32,32,2]{2,1,0:T(8,128)(2,1)}) fusion(bf16[32,32,900]{2,1,0:T(8,128)(2,1)} %param.7), kind=kLoop, calls=%fused_computation.200 | loop fusion | bytes 16384 | tf_op jit(solution)/shard_map/slice | solution.py:60
  16.3 0.6 collective-permute-start.3
  16.9 1.3 multiply_convert_fusion.3
  18.1 3.3 %fusion.9 = f32[32,2,2,32,32]{4,0,3,2,1:T(8,128)S(1)} fusion(bf16[32,32,900]{2,1,0:T(8,128)(2,1)} %param.7, bf16[32,2,1,900]{3,0,2,1:T(8,128)(2,1)S(1)} %get-tuple-element.81, bf16[32,2,1,900]{3,0,2,1:T(8,128)(2,1)S(1)} %get-tuple-element.80), kind=kOutput, calls=%fused_computation.11 | convolution fusion | flops 236390400 | bytes 2597888 | tf_op jit(solution)/shard_map/dot_general | solution.py:45
  21.5 1.2 copy.74
  22.8 1.7 %reshape.474 = f32[32,1,4096]{2,1,0:T(1,128)} reshape(f32[32,2,2,32,32]{4,3,2,1,0:T(8,128)S(1)} %copy.74) | data formatting | bytes 1048576
  24.5 6.2 %all-to-all-start = ((f32[32,1,4096]{2,1,0:T(1,128)}), f32[32,1,4096]{2,1,0:T(1,128)S(1)}, u32[]{:S(2)}, u32[]{:S(2)}) async-start(f32[32,1,4096]{2,1,0:T(1,128)} %reshape.474), calls=%async_computation | async-start | bytes 1048576 | tf_op jit(solution)/shard_map/all_to_all | solution.py:48
  30.8 0.7 fusion.77
  31.6 0.6 fusion.65
  32.1 0.6 slice_bitcast_fusion.35
  34.0 0.1 fusion.59
  34.2 0.7 fusion.76
  34.8 0.6 compare_convert_fusion.2
  35.5 0.7 slice_bitcast_fusion.8
  36.1 0.6 fusion.66
  46.5 0.7 copy.75.offs_ref
  47.2 0.7 copy.76.w_ref
  47.9 0.6 pad.43.clone
  48.6 2.3 %copy.79 = bf16[2,64,32,32]{3,2,1,0:T(8,128)(2,1)} copy(bf16[2,64,32,32]{1,3,2,0:T(8,128)(2,1)S(1)} %copy-done.3) | data formatting | bytes 524288 | tf_op args[6]
  50.9 3.4 %collective-permute-start.2 = (bf16[32,2,2]{2,1,0:T(2,128)(2,1)}, bf16[32,2,2]{2,1,0:T(2,128)(2,1)S(1)}, u32[]{:S(2)}, u32[]{:S(2)}) collective-permute-start(bf16[32,2,2]{2,1,0:T(2,128)(2,1)} %get-tuple-element.12), channel_id=1, source_target_pairs={{0,5},{1,6},{2,7},{3,4},{4,9},{5,10},{6,11},{7,8},{8,13},{9,14},{1... | collective-permute-start | bytes 776 | tf_op jit(solution)/shard_map/ppermute | solution.py:69
  54.4 1.6 %collective-permute-done.2 = bf16[32,2,2]{2,1,0:T(2,128)(2,1)S(1)} collective-permute-done((bf16[32,2,2]{2,1,0:T(2,128)(2,1)}, bf16[32,2,2]{2,1,0:T(2,128)(2,1)S(1)}, u32[]{:S(2)}, u32[]{:S(2)}) %collective-permute-start.2) | collective-permute-done | bytes 288 | tf_op jit(solution)/shard_map/ppermute | solution.py:69
  56.0 1.3 collective-permute-start.7
  57.3 4.8 %collective-permute-done.7 = bf16[32,2,2]{2,1,0:T(2,128)(2,1)S(1)} collective-permute-done((bf16[32,2,2]{2,1,0:T(2,128)(2,1)}, bf16[32,2,2]{2,1,0:T(2,128)(2,1)S(1)}, u32[]{:S(2)}, u32[]{:S(2)}) %collective-permute-start.7) | collective-permute-done | bytes 288 | tf_op jit(solution)/shard_map/ppermute | solution.py:77
  62.1 1.5 %collective-permute-start.6 = (bf16[32,2,2]{2,1,0:T(2,128)(2,1)}, bf16[32,2,2]{2,1,0:T(2,128)(2,1)S(1)}, u32[]{:S(2)}, u32[]{:S(2)}) collective-permute-start(bf16[32,2,2]{2,1,0:T(2,128)(2,1)} %get-tuple-element.14), channel_id=1, source_target_pairs={{4,3},{5,0},{6,1},{7,2},{8,7},{9,4},{10,5},{11,6},{12,11},{13,8},{... | collective-permute-start | bytes 776 | tf_op jit(solution)/shard_map/ppermute | solution.py:73
  63.6 4.3 %collective-permute-done.6 = bf16[32,2,2]{2,1,0:T(2,128)(2,1)S(1)} collective-permute-done((bf16[32,2,2]{2,1,0:T(2,128)(2,1)}, bf16[32,2,2]{2,1,0:T(2,128)(2,1)S(1)}, u32[]{:S(2)}, u32[]{:S(2)}) %collective-permute-start.6) | collective-permute-done | bytes 288 | tf_op jit(solution)/shard_map/ppermute | solution.py:73
  68.0 7.0 %maximum_maximum_fusion.rim_ref = bf16[32,40,1024]{2,1,0:T(8,128)(2,1)} fusion(bf16[32,2,2]{2,1,0:T(2,128)(2,1)S(1)} %collective-permute-done.7, bf16[32,2,120]{2,1,0:T(2,128)(2,1)S(1)} %broadcast.494, bf16[32,2,2]{2,1,0:T(2,128)(2,1)S(1)} %collective-permute-done.6, bf16[32,2,900]{2,1,0:T(2,128)(2,1)} %collective-permute-done.5, ...), kind=kLoop, calls=%fused_computation.10 | loop fusion | flops 34078720 | bytes 4801616 | tf_op jit(solution)/shard_map/concatenate | solution.py:86
  75.0 21.5 %shard_map.73 = bf16[32,32,900]{2,1,0:T(8,128)(2,1)} custom-call(s32[9,2]{1,0:T(8,128)} %copy.75.offs_ref, f32[32,9]{1,0:T(8,128)} %copy.76.w_ref, bf16[32,40,1024]{2,1,0:T(8,128)(2,1)} %maximum_maximum_fusion.rim_ref), custom_call_target="tpu_custom_call" | custom-call | flops 471859200 | bytes 4464640 | tf_op jit(solution)/shard_map/pallas_call | solution.py:195
  96.5 0.5 broadcast.516
  97.1 1.8 %reduce = f32[32,4096]{1,0:T(8,128)S(1)} reduce(f32[32,1,4096]{2,1,0:T(1,128)S(1)} %all-to-all-done, f32[]{:T(128)} %broadcast.516), dimensions={1}, to_apply=%all_to_all.6.reduce_sub_computation | reduce | bytes 1048580 | tf_op jit(solution)/shard_map/all_to_all | solution.py:48
  99.0 0.7 reshape.475
  99.8 0.3 bitcast_reduce_fusion
  100.1 0.3 copy.77
  100.4 0.2 reshape.460
  100.6 0.3 multiply_subtract_fusion.1
  101.0 0.3 multiply_subtract_fusion
  101.4 0.3 multiply_subtract_fusion.2
  101.7 0.2 fusion.37
  102.0 0.2 fusion.14
  102.3 0.2 convolution_bitcast_fusion.2
  102.5 0.2 convolution_bitcast_fusion.3
  102.8 0.2 fusion.13
  103.1 0.2 convolution_bitcast_fusion
  103.3 0.2 convolution_bitcast_fusion.1
  103.6 0.2 fusion.48
  104.0 0.2 subtract_multiply_fusion
  104.5 0.1 concatenate.28
  104.7 0.2 maximum_bitcast_fusion.2
  104.9 0.2 broadcast_in_dim.89
  105.2 1.7 %reshape.476 = bf16[32,2,2048]{2,1,0:T(2,128)(2,1)} reshape(bf16[32,2,2,32,32]{4,3,2,1,0:T(8,128)(2,1)S(1)} %bitcast.174) | data formatting | bytes 524288
  106.9 7.2 %all-to-all-start.1 = ((bf16[32,2,2048]{2,1,0:T(2,128)(2,1)}), bf16[32,2,2048]{2,1,0:T(2,128)(2,1)S(1)}, u32[]{:S(2)}, u32[]{:S(2)}) async-start(bf16[32,2,2048]{2,1,0:T(2,128)(2,1)} %reshape.476), calls=%async_computation.1 | async-start | bytes 524288 | tf_op jit(solution)/shard_map/all_to_all | solution.py:164
  114.1 1.1 multiply_convert_fusion.1
  115.3 0.3 copy.93
  115.6 0.9 convert_element_type.122
  116.5 8.2 %all-to-all-done.1 = bf16[32,2,2048]{2,1,0:T(2,128)(2,1)S(1)} async-done(((bf16[32,2,2048]{2,1,0:T(2,128)(2,1)}), bf16[32,2,2048]{2,1,0:T(2,128)(2,1)S(1)}, u32[]{:S(2)}, u32[]{:S(2)}) %all-to-all-start.1) | async-done | bytes 262176 | tf_op jit(solution)/shard_map/all_to_all | solution.py:164
  124.7 0.5 reshape.477
  125.2 1.8 %reshape.464 = bf16[128,1024]{1,0:T(8,128)(2,1)} reshape(bf16[32,2,2,32,32]{4,3,2,1,0:T(8,128)(2,1)S(1)} %reshape.477) | data formatting | bytes 524288 | tf_op jit(solution)/shard_map/reshape | solution.py:165
  127.0 1.1 copy.92
  128.2 1.6 %fusion.21 = f32[32,32,900]{2,1,0:T(8,128)S(1)} fusion(bf16[32,32,128]{2,1,0:T(8,128)(2,1)S(1)} %bitcast.176, bf16[128,900]{1,0:T(8,128)(2,1)} %convert_element_type.122), kind=kOutput, calls=%fused_computation.57 | convolution fusion | flops 235929600 | bytes 4178944 | tf_op jit(solution)/shard_map/dot_general | solution.py:169
  129.8 2.6 %fusion.8 = bf16[32,32,900]{2,1,0:T(8,128)(2,1)} fusion(f32[32,32,900]{2,1,0:T(8,128)S(1)} %fusion.21, bf16[32,32,900]{2,1,0:T(8,128)(2,1)S(1)} %copy-done), kind=kLoop, calls=%fused_computation.9 | loop fusion | flops 10137600 | bytes 7372800 | tf_op jit(solution)/shard_map/convert_element_type | solution.py:173
  (115 shorter events, 1.4 us)
Async XLA Ops:
  1.7 49.3 %collective-permute-start.1 = (bf16[32,2,2]{2,1,0:T(2,128)(2,1)}, bf16[32,2,2]{2,1,0:T(2,128)(2,1)S(1)}, u32[]{:S(2)}, u32[]{:S(2)}) collective-permute-start(bf16[32,2,2]{2,1,0:T(2,128)(2,1)} %get-tuple-element.11), channel_id=1, source_target_pairs={{0,7},{1,4},{2,5},{3,6},{4,11},{5,8},{6,9},{7,10},{8,15},{9,12},{1... | collective-permute-start | bytes 776 | tf_op jit(solution)/shard_map/ppermute | solution.py:65
  9.0 59.0 %collective-permute-start = (bf16[32,2,900]{2,1,0:T(2,128)(2,1)}, bf16[32,2,900]{2,1,0:T(2,128)(2,1)}, u32[]{:S(2)}, u32[]{:S(2)}) collective-permute-start(bf16[32,2,900]{2,1,0:T(2,128)(2,1)} %get-tuple-element.9), channel_id=1, source_target_pairs={{0,4},{4,8},{8,12},{12,16},{16,20},{20,24},{24,28},{1,5},{5,9},{9,... | collective-permute-start | bytes 345608 | tf_op jit(solution)/shard_map/ppermute | solution.py:58
  13.1 54.9 %collective-permute-start.5 = (bf16[32,2,900]{2,1,0:T(2,128)(2,1)}, bf16[32,2,900]{2,1,0:T(2,128)(2,1)}, u32[]{:S(2)}, u32[]{:S(2)}) collective-permute-start(bf16[32,2,900]{2,1,0:T(2,128)(2,1)} %get-tuple-element.10), channel_id=1, source_target_pairs={{4,0},{8,4},{12,8},{16,12},{20,16},{24,20},{28,24},{5,1},{9,5},{13... | collective-permute-start | bytes 345608 | tf_op jit(solution)/shard_map/ppermute | solution.py:59
  16.3 51.7 %collective-permute-start.3 = (bf16[32,32,2]{2,1,0:T(8,128)(2,1)}, bf16[32,32,2]{2,1,0:T(8,128)(2,1)S(1)}, u32[]{:S(2)}, u32[]{:S(2)}) collective-permute-start(bf16[32,32,2]{2,1,0:T(8,128)(2,1)} %get-tuple-element.15), channel_id=1, source_target_pairs={{1,0},{2,1},{3,2},{0,3},{5,4},{6,5},{7,6},{4,7},{9,8},{10,9},{11,1... | collective-permute-start | bytes 12296 | tf_op jit(solution)/shard_map/ppermute | solution.py:60
  16.9 51.1 %collective-permute-start.4 = (bf16[32,32,2]{2,1,0:T(8,128)(2,1)}, bf16[32,32,2]{2,1,0:T(8,128)(2,1)}, u32[]{:S(2)}, u32[]{:S(2)}) collective-permute-start(bf16[32,32,2]{2,1,0:T(8,128)(2,1)} %get-tuple-element.16), channel_id=1, source_target_pairs={{0,1},{1,2},{2,3},{3,0},{4,5},{5,6},{6,7},{7,4},{8,9},{9,10},{10,1... | collective-permute-start | bytes 12296 | tf_op jit(solution)/shard_map/ppermute | solution.py:61
  21.5 9.3 %copy-start.6 = (s32[9,2]{0,1:T(2,128)S(1)}, s32[9,2]{0,1:T(2,128)}, u32[]{:S(2)}) copy-start(s32[9,2]{0,1:T(2,128)} %param.8) | copy-start | bytes 220
  21.5 10.0 %copy-start.15 = (s32[128]{0:T(128)S(1)}, s32[128]{0:T(128)}, u32[]{:S(2)}) copy-start(s32[128]{0:T(128)} %param.12) | copy-start | bytes 1540
  21.5 10.1 %copy-start.37 = (f32[128]{0:T(128)S(1)}, f32[128]{0:T(128)}, u32[]{:S(2)}) copy-start(f32[128]{0:T(128)} %param.11) | copy-start | bytes 1540
  21.5 10.6 %copy-start.7 = (f32[32,9]{0,1:T(8,128)S(1)}, f32[32,9]{0,1:T(8,128)}, u32[]{:S(2)}) copy-start(f32[32,9]{0,1:T(8,128)} %param.9) | copy-start | bytes 3460
  21.5 12.6 %copy-start.4 = (bf16[2,64,128]{2,1,0:T(8,128)(2,1)S(1)}, bf16[2,64,128]{2,1,0:T(8,128)(2,1)}, u32[]{:S(2)}) copy-start(bf16[2,64,128]{2,1,0:T(8,128)(2,1)} %param.10) | copy-start | bytes 98308
  21.5 27.0 %copy-start.3 = (bf16[2,64,32,32]{1,3,2,0:T(8,128)(2,1)S(1)}, bf16[2,64,32,32]{1,3,2,0:T(8,128)(2,1)}, u32[]{:S(2)}) copy-start(bf16[2,64,32,32]{1,3,2,0:T(8,128)(2,1)} %param.13) | copy-start | bytes 786436
  24.5 43.5 %copy-start.1 = (bf16[32,32,900]{2,1,0:T(8,128)(2,1)S(1)}, bf16[32,32,900]{2,1,0:T(8,128)(2,1)}, u32[]{:S(2)}) copy-start(bf16[32,32,900]{2,1,0:T(8,128)(2,1)} %param.7) | copy-start | bytes 5529604
  24.5 72.0 %all-to-all-start = ((f32[32,1,4096]{2,1,0:T(1,128)}), f32[32,1,4096]{2,1,0:T(1,128)S(1)}, u32[]{:S(2)}, u32[]{:S(2)}) async-start(f32[32,1,4096]{2,1,0:T(1,128)} %reshape.474), calls=%async_computation | async-start | bytes 1048576 | tf_op jit(solution)/shard_map/all_to_all | solution.py:48
  50.9 5.1 %collective-permute-start.2 = (bf16[32,2,2]{2,1,0:T(2,128)(2,1)}, bf16[32,2,2]{2,1,0:T(2,128)(2,1)S(1)}, u32[]{:S(2)}, u32[]{:S(2)}) collective-permute-start(bf16[32,2,2]{2,1,0:T(2,128)(2,1)} %get-tuple-element.12), channel_id=1, source_target_pairs={{0,5},{1,6},{2,7},{3,4},{4,9},{5,10},{6,11},{7,8},{8,13},{9,14},{1... | collective-permute-start | bytes 776 | tf_op jit(solution)/shard_map/ppermute | solution.py:69
  56.0 6.2 %collective-permute-start.7 = (bf16[32,2,2]{2,1,0:T(2,128)(2,1)}, bf16[32,2,2]{2,1,0:T(2,128)(2,1)S(1)}, u32[]{:S(2)}, u32[]{:S(2)}) collective-permute-start(bf16[32,2,2]{2,1,0:T(2,128)(2,1)} %get-tuple-element.13), channel_id=1, source_target_pairs={{4,1},{5,2},{6,3},{7,0},{8,5},{9,6},{10,7},{11,4},{12,9},{13,10},{... | collective-permute-start | bytes 776 | tf_op jit(solution)/shard_map/ppermute | solution.py:77
  62.1 5.8 %collective-permute-start.6 = (bf16[32,2,2]{2,1,0:T(2,128)(2,1)}, bf16[32,2,2]{2,1,0:T(2,128)(2,1)S(1)}, u32[]{:S(2)}, u32[]{:S(2)}) collective-permute-start(bf16[32,2,2]{2,1,0:T(2,128)(2,1)} %get-tuple-element.14), channel_id=1, source_target_pairs={{4,3},{5,0},{6,1},{7,2},{8,7},{9,4},{10,5},{11,6},{12,11},{13,8},{... | collective-permute-start | bytes 776 | tf_op jit(solution)/shard_map/ppermute | solution.py:73
  96.5 4.1 %copy-start.28 = (f32[2]{0:T(128)S(1)}, f32[2]{0:T(128)}, u32[]{:S(2)}) copy-start(f32[2]{0:T(128)} %get-tuple-element.72) | copy-start | bytes 28
  96.5 4.1 %copy-start.29 = (f32[2]{0:T(128)S(1)}, f32[2]{0:T(128)}, u32[]{:S(2)}) copy-start(f32[2]{0:T(128)} %get-tuple-element.76) | copy-start | bytes 28
  96.5 4.1 %copy-start.30 = (f32[2]{0:T(128)S(1)}, f32[2]{0:T(128)}, u32[]{:S(2)}) copy-start(f32[2]{0:T(128)} %get-tuple-element.77) | copy-start | bytes 28
  96.5 4.1 %copy-start.31 = (f32[2]{0:T(128)S(1)}, f32[2]{0:T(128)}, u32[]{:S(2)}) copy-start(f32[2]{0:T(128)} %get-tuple-element.107) | copy-start | bytes 28
  96.5 4.1 %copy-start.32 = (f32[2]{0:T(128)S(1)}, f32[2]{0:T(128)}, u32[]{:S(2)}) copy-start(f32[2]{0:T(128)} %get-tuple-element.108) | copy-start | bytes 28
  96.5 4.1 %copy-start.33 = (f32[2]{0:T(128)S(1)}, f32[2]{0:T(128)}, u32[]{:S(2)}) copy-start(f32[2]{0:T(128)} %get-tuple-element.112) | copy-start | bytes 28
  97.0 3.9 %copy-start.22 = (f32[2]{0:T(128)S(1)}, f32[2]{0:T(128)}, u32[]{:S(2)}) copy-start(f32[2]{0:T(128)} %get-tuple-element.71) | copy-start | bytes 28
  97.0 3.9 %copy-start.23 = (f32[2]{0:T(128)S(1)}, f32[2]{0:T(128)}, u32[]{:S(2)}) copy-start(f32[2]{0:T(128)} %get-tuple-element.78) | copy-start | bytes 28
  97.0 3.9 %copy-start.24 = (f32[2]{0:T(128)S(1)}, f32[2]{0:T(128)}, u32[]{:S(2)}) copy-start(f32[2]{0:T(128)} %get-tuple-element.79) | copy-start | bytes 28
  97.0 3.9 %copy-start.25 = (f32[2]{0:T(128)S(1)}, f32[2]{0:T(128)}, u32[]{:S(2)}) copy-start(f32[2]{0:T(128)} %get-tuple-element.105) | copy-start | bytes 28
  97.0 3.9 %copy-start.26 = (f32[2]{0:T(128)S(1)}, f32[2]{0:T(128)}, u32[]{:S(2)}) copy-start(f32[2]{0:T(128)} %get-tuple-element.106) | copy-start | bytes 28
  97.0 3.9 %copy-start.27 = (f32[2]{0:T(128)S(1)}, f32[2]{0:T(128)}, u32[]{:S(2)}) copy-start(f32[2]{0:T(128)} %get-tuple-element.113) | copy-start | bytes 28
  98.9 2.4 %copy-start.16 = (f32[2]{0:T(128)S(1)}, f32[2]{0:T(128)}, u32[]{:S(2)}) copy-start(f32[2]{0:T(128)} %get-tuple-element.73) | copy-start | bytes 28
  98.9 2.4 %copy-start.17 = (f32[2]{0:T(128)S(1)}, f32[2]{0:T(128)}, u32[]{:S(2)}) copy-start(f32[2]{0:T(128)} %get-tuple-element.74) | copy-start | bytes 28
  98.9 2.4 %copy-start.18 = (f32[2]{0:T(128)S(1)}, f32[2]{0:T(128)}, u32[]{:S(2)}) copy-start(f32[2]{0:T(128)} %get-tuple-element.75) | copy-start | bytes 28
  98.9 2.4 %copy-start.19 = (f32[2]{0:T(128)S(1)}, f32[2]{0:T(128)}, u32[]{:S(2)}) copy-start(f32[2]{0:T(128)} %get-tuple-element.109) | copy-start | bytes 28
  98.9 2.4 %copy-start.20 = (f32[2]{0:T(128)S(1)}, f32[2]{0:T(128)}, u32[]{:S(2)}) copy-start(f32[2]{0:T(128)} %get-tuple-element.110) | copy-start | bytes 28
  98.9 2.4 %copy-start.21 = (f32[2]{0:T(128)S(1)}, f32[2]{0:T(128)}, u32[]{:S(2)}) copy-start(f32[2]{0:T(128)} %get-tuple-element.111) | copy-start | bytes 28
  98.9 2.7 %copy-start.8 = (f32[32]{0:T(128)S(1)}, f32[32]{0:T(128)}, u32[]{:S(2)}) copy-start(f32[32]{0:T(128)} %get-tuple-element.55) | copy-start | bytes 388
  98.9 2.7 %copy-start.9 = (f32[32]{0:T(128)S(1)}, f32[32]{0:T(128)}, u32[]{:S(2)}) copy-start(f32[32]{0:T(128)} %get-tuple-element.56) | copy-start | bytes 388
  99.0 2.7 %copy-start.10 = (f32[32]{0:T(128)S(1)}, f32[32]{0:T(128)}, u32[]{:S(2)}) copy-start(f32[32]{0:T(128)} %get-tuple-element.57) | copy-start | bytes 388
  99.0 2.7 %copy-start.11 = (f32[32]{0:T(128)S(1)}, f32[32]{0:T(128)}, u32[]{:S(2)}) copy-start(f32[32]{0:T(128)} %get-tuple-element.58) | copy-start | bytes 388
  99.0 2.7 %copy-start.12 = (f32[32]{0:T(128)S(1)}, f32[32]{0:T(128)}, u32[]{:S(2)}) copy-start(f32[32]{0:T(128)} %get-tuple-element.59) | copy-start | bytes 388
  99.0 2.7 %copy-start.13 = (f32[32]{0:T(128)S(1)}, f32[32]{0:T(128)}, u32[]{:S(2)}) copy-start(f32[32]{0:T(128)} %get-tuple-element.60) | copy-start | bytes 388
  99.0 2.7 %copy-start.14 = (f32[32]{0:T(128)S(1)}, f32[32]{0:T(128)}, u32[]{:S(2)}) copy-start(f32[32]{0:T(128)} %get-tuple-element.61) | copy-start | bytes 388
  99.7 2.3 %copy-start.35 = (f32[2,32]{1,0:T(2,128)S(1)}, f32[2,32]{1,0:T(2,128)}, u32[]{:S(2)}) copy-start(f32[2,32]{1,0:T(2,128)} %get-tuple-element.95) | copy-start | bytes 772
  99.7 2.3 %copy-start.36 = (f32[2,128]{1,0:T(2,128)S(1)}, f32[2,128]{1,0:T(2,128)}, u32[]{:S(2)}) copy-start(f32[2,128]{1,0:T(2,128)} %fusion.65) | copy-start | bytes 3076
  99.7 2.3 %copy-start.38 = (pred[2]{0:T(512)(128)(4,1)S(1)}, pred[2]{0:T(512)(128)(4,1)}, u32[]{:S(2)}) copy-start(pred[2]{0:T(512)(128)(4,1)} %get-tuple-element.99) | copy-start | bytes 10
  99.7 2.6 %copy-start.2 = (bf16[2,64,32,32]{3,2,1,0:T(8,128)(2,1)S(1)}, bf16[2,64,32,32]{3,2,1,0:T(8,128)(2,1)}, u32[]{:S(2)}) copy-start(bf16[2,64,32,32]{3,2,1,0:T(8,128)(2,1)} %copy.79) | copy-start | bytes 786436
  99.7 3.0 %copy-start.5 = (bf16[2,32,1,128]{3,2,1,0:T(2,128)(2,1)S(1)}, bf16[2,32,1,128]{3,2,1,0:T(2,128)(2,1)}, u32[]{:S(2)}) copy-start(bf16[2,32,1,128]{3,2,1,0:T(2,128)(2,1)} %get-tuple-element.52) | copy-start | bytes 49156
  99.7 3.0 %copy-start.34 = (f32[2,32]{1,0:T(2,128)S(1)}, f32[2,32]{1,0:T(2,128)}, u32[]{:S(2)}) copy-start(f32[2,32]{1,0:T(2,128)} %get-tuple-element.96) | copy-start | bytes 772
  99.8 3.0 %copy-start.40 = (pred[2]{0:T(512)(128)(4,1)S(1)}, pred[2]{0:T(512)(128)(4,1)}, u32[]{:S(2)}) copy-start(pred[2]{0:T(512)(128)(4,1)} %get-tuple-element.100) | copy-start | bytes 10
  100.0 4.0 %copy-start.39 = (pred[2]{0:T(512)(128)(4,1)S(1)}, pred[2]{0:T(512)(128)(4,1)}, u32[]{:S(2)}) copy-start(pred[2]{0:T(512)(128)(4,1)} %get-tuple-element.99) | copy-start | bytes 10
  100.0 4.0 %copy-start.41 = (pred[2]{0:T(512)(128)(4,1)S(1)}, pred[2]{0:T(512)(128)(4,1)}, u32[]{:S(2)}) copy-start(pred[2]{0:T(512)(128)(4,1)} %get-tuple-element.100) | copy-start | bytes 10
  106.9 17.8 %all-to-all-start.1 = ((bf16[32,2,2048]{2,1,0:T(2,128)(2,1)}), bf16[32,2,2048]{2,1,0:T(2,128)(2,1)S(1)}, u32[]{:S(2)}, u32[]{:S(2)}) async-start(bf16[32,2,2048]{2,1,0:T(2,128)(2,1)} %reshape.476), calls=%async_computation.1 | async-start | bytes 524288 | tf_op jit(solution)/shard_map/all_to_all | solution.py:164
  115.6 14.2 %copy-start = (bf16[32,32,900]{2,1,0:T(8,128)(2,1)S(1)}, bf16[32,32,900]{2,1,0:T(8,128)(2,1)}, u32[]{:S(2)}) copy-start(bf16[32,32,900]{2,1,0:T(8,128)(2,1)} %shard_map.73) | copy-start | bytes 5529604

commit v6 on v4

--- a/solution.py
+++ b/solution.py
@@ -159,35 +159,67 @@
 def depthwise_conv(offsets, conv_weight, rim, lat_rows, lon_cols):
     channels, rim_rows, rim_cols = rim.shape
     block_c = 8
-
-    def body(offs_ref, w_ref, rim_ref, out_ref):
-        blk = pl.program_id(0)
+    chunk = 4
+    flat = rim_rows * rim_cols
+
+    def body(offs_ref, rim_ref, w_ref, out_ref, planes, shifted, result):
+        tiles = rim_cols // 128
         for c in range(block_c):
             x = rim_ref[c].astype(jnp.float32)
-            acc = jnp.zeros((rim_rows, rim_cols), jnp.float32)
+            for t in range(tiles):
+                planes[t, pl.ds(c * rim_rows, rim_rows), :] = x[:, t * 128 : (t + 1) * 128]
+        for row in range(rim_rows):
+            v = jnp.concatenate(
+                [planes[t, pl.ds(row, block_c, stride=rim_rows), :] for t in range(tiles)], axis=1
+            )
+            for s in range(5):
+                turn = (2 - s) % rim_cols
+                shifted[s, :, pl.ds(row * rim_cols, rim_cols)] = (
+                    v if turn == 0 else pltpu.roll(v, turn, 1)
+                )
+        weights = w_ref[...]
+        for r0 in range(0, lat_rows, chunk):
+            acc = jnp.zeros((block_c, chunk * rim_cols), jnp.float32)
             for k in range(KTAPS):
                 dr = offs_ref[k, 0]
                 dc = offs_ref[k, 1]
-                y = pltpu.roll(x, lax.rem(rim_rows - dr - 2, rim_rows), 0)
-                y = pltpu.roll(y, lax.rem(rim_cols - dc, rim_cols), 1)
-                acc = acc + w_ref[blk * block_c + c, k] * y
-            out_ref[c] = acc[:lat_rows, :lon_cols].astype(jnp.bfloat16)
+                start = pl.multiple_of((r0 + 2 + dr) * rim_cols, rim_cols)
+                acc = acc + weights[:, k : k + 1] * shifted[dc + 2, :, pl.ds(start, chunk * rim_cols)]
+            for i in range(chunk):
+                for t in range(tiles):
+                    result[t, pl.ds(r0 + i, block_c, stride=lat_rows), :] = acc[
+                        :, i * rim_cols + t * 128 : i * rim_cols + (t + 1) * 128
+                    ]
+        for c in range(block_c):
+            full = jnp.concatenate(
+                [result[t, pl.ds(c * lat_rows, lat_rows), :] for t in range(tiles)], axis=1
+            )
+            out_ref[c] = full[:, :lon_cols].astype(jnp.bfloat16)
 
     return pl.pallas_call(
         body,
         grid_spec=pltpu.PrefetchScalarGridSpec(
-            num_scalar_prefetch=2,
+            num_scalar_prefetch=1,
             grid=(channels // block_c,),
-            in_specs=[pl.BlockSpec((block_c, rim_rows, rim_cols), lambda b, o, w: (b, 0, 0))],
-            out_specs=pl.BlockSpec((block_c, lat_rows, lon_cols), lambda b, o, w: (b, 0, 0)),
+            in_specs=[
+                pl.BlockSpec((block_c, rim_rows, rim_cols), lambda b, o: (b, 0, 0)),
+                pl.BlockSpec((block_c, KTAPS), lambda b, o: (b, 0)),
+            ],
+            out_specs=pl.BlockSpec((block_c, lat_rows, lon_cols), lambda b, o: (b, 0, 0)),
+            scratch_shapes=[
+                pltpu.VMEM((rim_cols // 128, block_c * rim_rows, 128), jnp.float32),
+                pltpu.VMEM((5, block_c, flat), jnp.float32),
+                pltpu.VMEM((rim_cols // 128, block_c * lat_rows, 128), jnp.float32),
+            ],
         ),
         out_shape=jax.ShapeDtypeStruct((channels, lat_rows, lon_cols), jnp.bfloat16),
+        compiler_params=pltpu.CompilerParams(vmem_limit_bytes=48 * 1024 * 1024),
         cost_estimate=pl.CostEstimate(
-            flops=40 * KTAPS * channels * rim_rows * rim_cols,
+            flops=8 * KTAPS * channels * rim_rows * rim_cols,
             transcendentals=0,
             bytes_accessed=channels * (rim_rows * rim_cols + lat_rows * lon_cols) * 2,
         ),
-    )(offsets, conv_weight, rim)
+    )(offsets, rim, conv_weight)
 
 
 def solution(mesh):

time: 112 us -> 107 us (0.955)
  Pallas kernels: 21.5 us -> 13.7 us
  matrix products: 6.55 us -> 8.47 us
    pallas_call x1, Pallas kernels: 21.5 us -> 13.7 us  [depthwise_conv(): pl.pallas_call(body, grid_spec=pltpu.PrefetchScalarGridSpec(num_scalar_pr...]
    reduce_sum x1, other arithmetic: 0.27 us -> 1.91 us  [per_device(): gathered.reshape(lat_count, lon_count, m_dev, 2, channels, lat_rows)]
    optimization_barrier x1, local copies, waits for them, and re-layouts: 0.68 us -> 2.01 us  [per_device(): gathered, conv_out = lax.optimization_barrier((gathered_raw, conv_out))]
    unnamed x94 -> x72, local copies, waits for them, and re-layouts: 9.29 us -> 8.71 us
  transfers between devices with their start and end apart: 6 -> 6, of which waited for: 1 -> 1; matrix products, arithmetic and copies ran while one was open for 26% -> 24% of each run, Pallas kernels for 19% -> 13%
where the time goes in v6:
time: 107 us; the launch traced here: 106 us
  local copies, waits for them, and re-layouts  23.4 us (22%)
  starting transfers between devices  21.3 us (20%)
  other arithmetic  19 us (18%)
  Pallas kernels  13.7 us (13%)
  between operations  12.1 us (11%)
  matrix products  8.47 us (8%)
  waiting for transfers between devices  8.04 us (8%)
    pallas_call x1, Pallas kernels, depthwise_conv(): pl.pallas_call(body, grid_spec=pltpu.PrefetchScalarGridSpec(num_scalar_pr...  13.7 us
    unnamed x72, local copies, waits for them, and re-layouts  8.71 us
    all_to_all x1, waiting for transfers between devices, per_device(): full_rows = lax.all_to_all(outgoing, BOTH, 0, 0, tiled=True)  8.03 us
    all_to_all x1, starting transfers between devices, per_device(): gathered_raw = lax.all_to_all(partial, BOTH, 0, 0, tiled=True)  7.59 us
    all_to_all x1, starting transfers between devices, per_device(): full_rows = lax.all_to_all(outgoing, BOTH, 0, 0, tiled=True)  6.03 us
    ppermute x1, starting transfers between devices, per_device(): lax.ppermute(field[:, lat_rows - 2:], 'lat', [(i, i + 1) for i in range(l...  4.87 us
    concatenate x1, other arithmetic, per_device(): jnp.concatenate([rows_ext, east, jnp.zeros((channels, rim_rows, rim_cols...  4.34 us
    dot_general x1, matrix products, per_device(): lax.dot_general(forward_rows, flat_field, (((1,), (1,)), ((), ())), prefe...  3.32 us
  transfers between devices with their start and end apart: 6, of which 1 were waited for; matrix products, arithmetic and copies ran while one was open for 24% of the time, Pallas kernels for 13%

profile of v6, /device:TPU:0, one launch (start us, length us, event | category | flops | bytes accessed | tf_op | source)
XLA Modules:
  0.0 106.0 jit_solution(4659875397888090553)
XLA Ops:
  0.0 2.1 %fusion.73 = (bf16[32,2,900]{2,1,0:T(2,128)(2,1)}, bf16[32,2,900]{2,1,0:T(2,128)(2,1)}) fusion(bf16[32,32,900]{2,1,0:T(8,128)(2,1)} %param.7), kind=kLoop, calls=%fused_computation.202 | loop fusion | bytes 460800 | tf_op jit(solution)/shard_map/slice | solution.py:55
  2.1 4.9 %collective-permute-start = (bf16[32,2,900]{2,1,0:T(2,128)(2,1)}, bf16[32,2,900]{2,1,0:T(2,128)(2,1)S(1)}, u32[]{:S(2)}, u32[]{:S(2)}) collective-permute-start(bf16[32,2,900]{2,1,0:T(2,128)(2,1)} %get-tuple-element.11), channel_id=1, source_target_pairs={{0,4},{4,8},{8,12},{12,16},{16,20},{20,24},{24,28},{1,5},{5,9},{9,... | collective-permute-start | bytes 345608 | tf_op jit(solution)/shard_map/ppermute | solution.py:54
  7.0 1.3 %collective-permute-start.1 = (bf16[32,2,900]{2,1,0:T(2,128)(2,1)}, bf16[32,2,900]{2,1,0:T(2,128)(2,1)}, u32[]{:S(2)}, u32[]{:S(2)}) collective-permute-start(bf16[32,2,900]{2,1,0:T(2,128)(2,1)} %get-tuple-element.12), channel_id=1, source_target_pairs={{4,0},{8,4},{12,8},{16,12},{20,16},{24,20},{28,24},{5,1},{9,5},{13... | collective-permute-start | bytes 345608 | tf_op jit(solution)/shard_map/ppermute | solution.py:51
  8.3 1.3 %multiply_convert_fusion.3 = (bf16[32,2,1,900]{3,0,2,1:T(8,128)(2,1)S(1)}, bf16[32,2,1,900]{3,0,2,1:T(8,128)(2,1)S(1)}) fusion(s32[900]{0:T(1024)S(1)} %iota_add_fusion, s32[32,2]{0,1:T(2,128)S(1)} %multiply_add_fusion.9), kind=kLoop, calls=%fused_computation.69 | loop fusion | flops 748800 | bytes 234256 | tf_op jit(solution)/shard_map/convert.10
  9.6 3.3 %fusion.9 = f32[32,2,2,32,32]{4,0,3,2,1:T(8,128)S(1)} fusion(bf16[32,32,900]{2,1,0:T(8,128)(2,1)} %param.7, bf16[32,2,1,900]{3,0,2,1:T(8,128)(2,1)S(1)} %get-tuple-element.77, bf16[32,2,1,900]{3,0,2,1:T(8,128)(2,1)S(1)} %get-tuple-element.76), kind=kOutput, calls=%fused_computation.11 | convolution fusion | flops 236390400 | bytes 2597888 | tf_op jit(solution)/shard_map/dot_general | solution.py:45
  13.0 2.5 %copy.74 = f32[32,2,2,32,32]{4,3,2,1,0:T(8,128)} copy(f32[32,2,2,32,32]{4,0,3,2,1:T(8,128)S(1)} %fusion.9) | data formatting | bytes 1048576 | tf_op jit(solution)/shard_map/dot_general | solution.py:45
  15.5 3.2 %reshape.474 = f32[32,1,4096]{2,1,0:T(1,128)} reshape(f32[32,2,2,32,32]{4,3,2,1,0:T(8,128)} %copy.74) | data formatting | bytes 1048576
  18.7 7.6 %all-to-all-start = ((f32[32,1,4096]{2,1,0:T(1,128)}), f32[32,1,4096]{2,1,0:T(1,128)S(1)}, u32[]{:S(2)}, u32[]{:S(2)}) async-start(f32[32,1,4096]{2,1,0:T(1,128)} %reshape.474), calls=%async_computation | async-start | bytes 1048576 | tf_op jit(solution)/shard_map/all_to_all | solution.py:48
  26.4 0.5 slice_bitcast_fusion.35
  26.9 0.1 fusion.59
  27.1 0.7 fusion.65
  27.7 0.7 compare_convert_fusion.2
  28.4 0.6 slice_bitcast_fusion.8
  29.1 0.7 fusion.75
  29.8 0.6 copy-done.3
  30.5 1.9 %pad_maximum_fusion.4 = (bf16[32,40,2]{2,1,0:T(8,128)(2,1)}, bf16[32,40,2]{2,1,0:T(8,128)(2,1)}) fusion(bf16[32,4,900]{2,1,0:T(4,128)(2,1)S(1)} %broadcast_in_dim.84, bf16[32,2,900]{2,1,0:T(2,128)(2,1)} %collective-permute-done.1, bf16[32,32,900]{2,1,0:T(8,128)(2,1)S(1)} %copy-done, bf16[32,2,900]{2,1,0:T(2,128)(2,1)} %copy-done.3), kind=kLoop, calls=%fused_computation.47 | loop fusion | flops 40960 | bytes 2314240 | tf_op jit(solution)/shard_map/slice | solution.py:62
  32.5 1.5 %collective-permute-start.2 = (bf16[32,40,2]{2,1,0:T(8,128)(2,1)}, bf16[32,40,2]{2,1,0:T(8,128)(2,1)}, u32[]{:S(2)}, u32[]{:S(2)}) collective-permute-start(bf16[32,40,2]{2,1,0:T(8,128)(2,1)} %get-tuple-element.9), channel_id=1, source_target_pairs={{1,0},{2,1},{3,2},{0,3},{5,4},{6,5},{7,6},{4,7},{9,8},{10,9},{11,1... | collective-permute-start | bytes 15368 | tf_op jit(solution)/shard_map/ppermute | solution.py:61
  34.0 0.6 fusion.66
  45.9 0.1 copy.75.offs_ref
  46.0 0.1 copy.76.w_ref
  46.1 2.4 %copy.79 = bf16[2,64,32,32]{3,2,1,0:T(8,128)(2,1)} copy(bf16[2,64,32,32]{1,3,2,0:T(8,128)(2,1)S(1)} %copy-done.2) | data formatting | bytes 524288 | tf_op args[6]
  48.5 0.1 pad.36.clone
  48.5 4.3 %pad_maximum_fusion.rim_ref = bf16[32,40,1024]{2,1,0:T(8,128)(2,1)S(1)} fusion(bf16[32,40,2]{2,1,0:T(8,128)(2,1)} %collective-permute-done.3, bf16[32,40,2]{2,1,0:T(8,128)(2,1)} %collective-permute-done.2, bf16[32,4,900]{2,1,0:T(4,128)(2,1)S(1)} %broadcast_in_dim.84, bf16[32,2,900]{2,1,0:T(2,128)(2,1)} %collective-permute-done.1, ...), kind=kLoop, calls=%fused_computation.10 | loop fusion | flops 18350080 | bytes 4937728 | tf_op jit(solution)/shard_map/concatenate | solution.py:67
  52.9 13.7 %shard_map.73 = bf16[32,32,900]{2,1,0:T(8,128)(2,1)S(1)} custom-call(s32[9,2]{1,0:T(8,128)S(1)} %copy.75.offs_ref, bf16[32,40,1024]{2,1,0:T(8,128)(2,1)S(1)} %pad_maximum_fusion.rim_ref, f32[32,9]{1,0:T(8,128)S(1)} %copy.76.w_ref), custom_call_target="tpu_custom_call" | custom-call | flops 94371840 | bytes 4464640 | tf_op jit(solution)/shard_map/pallas_call | solution.py:199
  66.7 0.5 broadcast.510
  67.2 1.9 %reduce = f32[32,4096]{1,0:T(8,128)S(1)} reduce(f32[32,1,4096]{2,1,0:T(1,128)S(1)} %all-to-all-done, f32[]{:T(128)} %broadcast.510), dimensions={1}, to_apply=%all_to_all.6.reduce_sub_computation | reduce | bytes 1048580 | tf_op jit(solution)/shard_map/all_to_all | solution.py:48
  69.2 2.0 %reshape.475 = f32[32,2,2,32,32]{4,3,2,1,0:T(8,128)} reshape(f32[32,4096]{1,0:T(8,128)S(1)} %reduce) | data formatting | bytes 1048576 | tf_op jit(solution)/shard_map/optimization_barrier | solution.py:77
  71.3 1.9 %bitcast_reduce_fusion = f32[8,2,2,32,32]{4,3,2,1,0:T(8,128)S(1)} fusion(f32[32,2,2,32,32]{4,3,2,1,0:T(8,128)} %reshape.475), kind=kLoop, calls=%fused_computation.13 | loop fusion | flops 98304 | bytes 655360 | tf_op jit(solution)/shard_map/reduce_sum | solution.py:78
  73.2 0.3 copy.77
  73.5 0.2 reshape.460
  73.7 0.3 multiply_subtract_fusion.1
  74.1 0.3 multiply_subtract_fusion
  74.5 0.3 multiply_subtract_fusion.2
  74.8 0.2 fusion.37
  75.0 0.1 rev.8
  75.1 0.2 fusion.14
  75.3 0.1 copy.81
  75.4 1.2 %convolution_bitcast_fusion.2 = f32[2,32,2,32]{3,2,0,1:T(2,128)S(1)} fusion(bf16[2,32,2,32]{3,2,0,1:T(2,128)(2,1)S(1)} %copy.81, bf16[2,32,2,32,32]{4,3,2,1,0:T(8,128)(2,1)} %bitcast.178), kind=kOutput, calls=%fused_computation.17 | convolution fusion | flops 262144 | bytes 286720 | tf_op jit(solution)/shard_map/mupc,ucd->mupd/dot_general | solution.py:121
  76.6 1.2 %convolution_bitcast_fusion.3 = f32[2,32,2,32]{3,2,0,1:T(2,128)S(1)} fusion(bf16[2,32,2,32]{3,2,0,1:T(2,128)(2,1)S(1)} %copy.81, bf16[2,32,2,32,32]{4,3,2,1,0:T(8,128)(2,1)} %bitcast.179), kind=kOutput, calls=%fused_computation.18 | convolution fusion | flops 262144 | bytes 286720 | tf_op jit(solution)/shard_map/mupc,ucd->mupd/dot_general | solution.py:118
  77.7 0.2 fusion.13
  77.9 0.1 copy.87
  78.0 0.2 convolution_bitcast_fusion
  78.2 0.2 convolution_bitcast_fusion.1
  78.5 0.1 pad_maximum_fusion.6
  78.6 0.2 fusion.48
  78.9 0.1 pad_maximum_fusion.7
  79.0 0.2 subtract_multiply_fusion
  79.2 0.1 multiply_convert_fusion.4
  79.3 0.1 rev.9
  79.4 0.1 concatenate.20
  79.5 0.1 concatenate.19
  79.6 0.2 maximum_bitcast_fusion.2
  79.9 0.2 broadcast_in_dim.89
  80.1 1.7 %reshape.476 = bf16[32,2,2048]{2,1,0:T(2,128)(2,1)} reshape(bf16[32,2,2,32,32]{4,3,2,1,0:T(8,128)(2,1)S(1)} %bitcast.174) | data formatting | bytes 524288
  81.9 6.0 %all-to-all-start.1 = ((bf16[32,2,2048]{2,1,0:T(2,128)(2,1)}), bf16[32,2,2048]{2,1,0:T(2,128)(2,1)S(1)}, u32[]{:S(2)}, u32[]{:S(2)}) async-start(bf16[32,2,2048]{2,1,0:T(2,128)(2,1)} %reshape.476), calls=%async_computation.1 | async-start | bytes 524288 | tf_op jit(solution)/shard_map/all_to_all | solution.py:145
  87.9 1.1 %multiply_convert_fusion.1 = (bf16[64,1,900]{2,0,1:T(8,128)(2,1)S(1)}, bf16[64,1,900]{2,0,1:T(8,128)(2,1)S(1)}) fusion(s32[900]{0:T(1024)S(1)} %iota_add_fusion, f32[64]{0:T(128)S(1)} %get-tuple-element.97, f32[64]{0:T(128)S(1)} %get-tuple-element.98), kind=kLoop, calls=%fused_computation.64 | loop fusion | flops 748800 | bytes 234512 | tf_op jit(solution)/shard_map/convert
  89.1 0.3 copy.93
  89.4 0.9 convert_element_type.122
  90.2 8.0 %all-to-all-done.1 = bf16[32,2,2048]{2,1,0:T(2,128)(2,1)S(1)} async-done(((bf16[32,2,2048]{2,1,0:T(2,128)(2,1)}), bf16[32,2,2048]{2,1,0:T(2,128)(2,1)S(1)}, u32[]{:S(2)}, u32[]{:S(2)}) %all-to-all-start.1) | async-done | bytes 262176 | tf_op jit(solution)/shard_map/all_to_all | solution.py:145
  98.3 0.5 reshape.477
  98.8 1.8 %reshape.464 = bf16[128,1024]{1,0:T(8,128)(2,1)} reshape(bf16[32,2,2,32,32]{4,3,2,1,0:T(8,128)(2,1)S(1)} %reshape.477) | data formatting | bytes 524288 | tf_op jit(solution)/shard_map/reshape | solution.py:146
  100.6 1.1 %copy.92 = bf16[1024,128]{1,0:T(8,128)(2,1)S(1)} copy(bf16[1024,128]{0,1:T(8,128)(2,1)} %bitcast.177) | data formatting | bytes 524288 | tf_op jit(solution)/shard_map/dot_general | solution.py:150
  101.7 1.6 %fusion.21 = f32[32,32,900]{2,1,0:T(8,128)S(1)} fusion(bf16[32,32,128]{2,1,0:T(8,128)(2,1)S(1)} %bitcast.176, bf16[128,900]{1,0:T(8,128)(2,1)} %convert_element_type.122), kind=kOutput, calls=%fused_computation.61 | convolution fusion | flops 235929600 | bytes 4178944 | tf_op jit(solution)/shard_map/dot_general | solution.py:150
  103.4 2.6 %fusion.8 = bf16[32,32,900]{2,1,0:T(8,128)(2,1)} fusion(f32[32,32,900]{2,1,0:T(8,128)S(1)} %fusion.21, bf16[32,32,900]{2,1,0:T(8,128)(2,1)S(1)} %shard_map.73), kind=kLoop, calls=%fused_computation.9 | loop fusion | flops 10137600 | bytes 7372800 | tf_op jit(solution)/shard_map/convert_element_type | solution.py:154
  (86 shorter events, 0.6 us)
Async XLA Ops:
  2.1 27.7 %collective-permute-start = (bf16[32,2,900]{2,1,0:T(2,128)(2,1)}, bf16[32,2,900]{2,1,0:T(2,128)(2,1)S(1)}, u32[]{:S(2)}, u32[]{:S(2)}) collective-permute-start(bf16[32,2,900]{2,1,0:T(2,128)(2,1)} %get-tuple-element.11), channel_id=1, source_target_pairs={{0,4},{4,8},{8,12},{12,16},{16,20},{20,24},{24,28},{1,5},{5,9},{9,... | collective-permute-start | bytes 345608 | tf_op jit(solution)/shard_map/ppermute | solution.py:54
  7.0 23.5 %collective-permute-start.1 = (bf16[32,2,900]{2,1,0:T(2,128)(2,1)}, bf16[32,2,900]{2,1,0:T(2,128)(2,1)}, u32[]{:S(2)}, u32[]{:S(2)}) collective-permute-start(bf16[32,2,900]{2,1,0:T(2,128)(2,1)} %get-tuple-element.12), channel_id=1, source_target_pairs={{4,0},{8,4},{12,8},{16,12},{20,16},{24,20},{28,24},{5,1},{9,5},{13... | collective-permute-start | bytes 345608 | tf_op jit(solution)/shard_map/ppermute | solution.py:51
  12.9 13.4 %copy-start.5 = (s32[9,2]{0,1:T(2,128)S(1)}, s32[9,2]{0,1:T(2,128)}, u32[]{:S(2)}) copy-start(s32[9,2]{0,1:T(2,128)} %param.8) | copy-start | bytes 220
  12.9 13.4 %copy-start.6 = (f32[32,9]{0,1:T(8,128)S(1)}, f32[32,9]{0,1:T(8,128)}, u32[]{:S(2)}) copy-start(f32[32,9]{0,1:T(8,128)} %param.9) | copy-start | bytes 3460
  13.0 13.9 %copy-start.4 = (bf16[2,64,128]{2,1,0:T(8,128)(2,1)S(1)}, bf16[2,64,128]{2,1,0:T(8,128)(2,1)}, u32[]{:S(2)}) copy-start(bf16[2,64,128]{2,1,0:T(8,128)(2,1)} %param.10) | copy-start | bytes 98308
  13.0 14.1 %copy-start.8 = (s32[128]{0:T(128)S(1)}, s32[128]{0:T(128)}, u32[]{:S(2)}) copy-start(s32[128]{0:T(128)} %param.12) | copy-start | bytes 1540
  13.0 14.1 %copy-start.30 = (f32[128]{0:T(128)S(1)}, f32[128]{0:T(128)}, u32[]{:S(2)}) copy-start(f32[128]{0:T(128)} %param.11) | copy-start | bytes 1540
  13.0 17.5 %copy-start = (bf16[32,32,900]{2,1,0:T(8,128)(2,1)S(1)}, bf16[32,32,900]{2,1,0:T(8,128)(2,1)}, u32[]{:S(2)}) copy-start(bf16[32,32,900]{2,1,0:T(8,128)(2,1)} %param.7) | copy-start | bytes 5529604
  15.5 30.5 %copy-start.2 = (bf16[2,64,32,32]{1,3,2,0:T(8,128)(2,1)S(1)}, bf16[2,64,32,32]{1,3,2,0:T(8,128)(2,1)}, u32[]{:S(2)}) copy-start(bf16[2,64,32,32]{1,3,2,0:T(8,128)(2,1)} %param.13) | copy-start | bytes 786436
  18.7 48.0 %all-to-all-start = ((f32[32,1,4096]{2,1,0:T(1,128)}), f32[32,1,4096]{2,1,0:T(1,128)S(1)}, u32[]{:S(2)}, u32[]{:S(2)}) async-start(f32[32,1,4096]{2,1,0:T(1,128)} %reshape.474), calls=%async_computation | async-start | bytes 1048576 | tf_op jit(solution)/shard_map/all_to_all | solution.py:48
  29.8 0.7 copy-start.3
  32.5 16.0 %collective-permute-start.2 = (bf16[32,40,2]{2,1,0:T(8,128)(2,1)}, bf16[32,40,2]{2,1,0:T(8,128)(2,1)}, u32[]{:S(2)}, u32[]{:S(2)}) collective-permute-start(bf16[32,40,2]{2,1,0:T(8,128)(2,1)} %get-tuple-element.9), channel_id=1, source_target_pairs={{1,0},{2,1},{3,2},{0,3},{5,4},{6,5},{7,6},{4,7},{9,8},{10,9},{11,1... | collective-permute-start | bytes 15368 | tf_op jit(solution)/shard_map/ppermute | solution.py:61
  34.0 14.5 %collective-permute-start.3 = (bf16[32,40,2]{2,1,0:T(8,128)(2,1)}, bf16[32,40,2]{2,1,0:T(8,128)(2,1)}, u32[]{:S(2)}, u32[]{:S(2)}) collective-permute-start(bf16[32,40,2]{2,1,0:T(8,128)(2,1)} %get-tuple-element.10), channel_id=1, source_target_pairs={{0,1},{1,2},{2,3},{3,0},{4,5},{5,6},{6,7},{7,4},{8,9},{9,10},{10,1... | collective-permute-start | bytes 15368 | tf_op jit(solution)/shard_map/ppermute | solution.py:64
  66.6 7.0 %copy-start.21 = (f32[2]{0:T(128)S(1)}, f32[2]{0:T(128)}, u32[]{:S(2)}) copy-start(f32[2]{0:T(128)} %get-tuple-element.68) | copy-start | bytes 28
  66.6 7.0 %copy-start.22 = (f32[2]{0:T(128)S(1)}, f32[2]{0:T(128)}, u32[]{:S(2)}) copy-start(f32[2]{0:T(128)} %get-tuple-element.72) | copy-start | bytes 28
  66.7 7.0 %copy-start.23 = (f32[2]{0:T(128)S(1)}, f32[2]{0:T(128)}, u32[]{:S(2)}) copy-start(f32[2]{0:T(128)} %get-tuple-element.73) | copy-start | bytes 28
  66.7 7.0 %copy-start.24 = (f32[2]{0:T(128)S(1)}, f32[2]{0:T(128)}, u32[]{:S(2)}) copy-start(f32[2]{0:T(128)} %get-tuple-element.103) | copy-start | bytes 28
  66.7 7.0 %copy-start.25 = (f32[2]{0:T(128)S(1)}, f32[2]{0:T(128)}, u32[]{:S(2)}) copy-start(f32[2]{0:T(128)} %get-tuple-element.104) | copy-start | bytes 28
  66.7 7.0 %copy-start.26 = (f32[2]{0:T(128)S(1)}, f32[2]{0:T(128)}, u32[]{:S(2)}) copy-start(f32[2]{0:T(128)} %get-tuple-element.108) | copy-start | bytes 28
  67.2 6.8 %copy-start.15 = (f32[2]{0:T(128)S(1)}, f32[2]{0:T(128)}, u32[]{:S(2)}) copy-start(f32[2]{0:T(128)} %get-tuple-element.67) | copy-start | bytes 28
  67.2 6.8 %copy-start.16 = (f32[2]{0:T(128)S(1)}, f32[2]{0:T(128)}, u32[]{:S(2)}) copy-start(f32[2]{0:T(128)} %get-tuple-element.74) | copy-start | bytes 28
  67.2 6.9 %copy-start.17 = (f32[2]{0:T(128)S(1)}, f32[2]{0:T(128)}, u32[]{:S(2)}) copy-start(f32[2]{0:T(128)} %get-tuple-element.75) | copy-start | bytes 28
  67.2 6.9 %copy-start.18 = (f32[2]{0:T(128)S(1)}, f32[2]{0:T(128)}, u32[]{:S(2)}) copy-start(f32[2]{0:T(128)} %get-tuple-element.101) | copy-start | bytes 28
  67.2 6.9 %copy-start.19 = (f32[2]{0:T(128)S(1)}, f32[2]{0:T(128)}, u32[]{:S(2)}) copy-start(f32[2]{0:T(128)} %get-tuple-element.102) | copy-start | bytes 28
  67.2 6.9 %copy-start.20 = (f32[2]{0:T(128)S(1)}, f32[2]{0:T(128)}, u32[]{:S(2)}) copy-start(f32[2]{0:T(128)} %get-tuple-element.109) | copy-start | bytes 28
  69.2 5.3 %copy-start.9 = (f32[2]{0:T(128)S(1)}, f32[2]{0:T(128)}, u32[]{:S(2)}) copy-start(f32[2]{0:T(128)} %get-tuple-element.69) | copy-start | bytes 28
  69.2 5.3 %copy-start.10 = (f32[2]{0:T(128)S(1)}, f32[2]{0:T(128)}, u32[]{:S(2)}) copy-start(f32[2]{0:T(128)} %get-tuple-element.70) | copy-start | bytes 28
  69.2 5.3 %copy-start.11 = (f32[2]{0:T(128)S(1)}, f32[2]{0:T(128)}, u32[]{:S(2)}) copy-start(f32[2]{0:T(128)} %get-tuple-element.71) | copy-start | bytes 28
  69.2 5.3 %copy-start.12 = (f32[2]{0:T(128)S(1)}, f32[2]{0:T(128)}, u32[]{:S(2)}) copy-start(f32[2]{0:T(128)} %get-tuple-element.105) | copy-start | bytes 28
  69.2 5.3 %copy-start.13 = (f32[2]{0:T(128)S(1)}, f32[2]{0:T(128)}, u32[]{:S(2)}) copy-start(f32[2]{0:T(128)} %get-tuple-element.106) | copy-start | bytes 28
  69.2 5.3 %copy-start.14 = (f32[2]{0:T(128)S(1)}, f32[2]{0:T(128)}, u32[]{:S(2)}) copy-start(f32[2]{0:T(128)} %get-tuple-element.107) | copy-start | bytes 28
  69.2 5.6 %copy-start.7 = (f32[32]{0:T(128)S(1)}, f32[32]{0:T(128)}, u32[]{:S(2)}) copy-start(f32[32]{0:T(128)} %get-tuple-element.57) | copy-start | bytes 388
  71.2 3.8 %copy-start.28 = (f32[2,32]{1,0:T(2,128)S(1)}, f32[2,32]{1,0:T(2,128)}, u32[]{:S(2)}) copy-start(f32[2,32]{1,0:T(2,128)} %get-tuple-element.91) | copy-start | bytes 772
  71.2 3.8 %copy-start.29 = (f32[2,128]{1,0:T(2,128)S(1)}, f32[2,128]{1,0:T(2,128)}, u32[]{:S(2)}) copy-start(f32[2,128]{1,0:T(2,128)} %fusion.65) | copy-start | bytes 3076
  71.2 3.9 %copy-start.31 = (pred[2]{0:T(512)(128)(4,1)S(1)}, pred[2]{0:T(512)(128)(4,1)}, u32[]{:S(2)}) copy-start(pred[2]{0:T(512)(128)(4,1)} %get-tuple-element.95) | copy-start | bytes 10
  71.2 6.5 %copy-start.27 = (f32[2,32]{1,0:T(2,128)S(1)}, f32[2,32]{1,0:T(2,128)}, u32[]{:S(2)}) copy-start(f32[2,32]{1,0:T(2,128)} %get-tuple-element.92) | copy-start | bytes 772
  71.2 6.5 %copy-start.32 = (pred[2]{0:T(512)(128)(4,1)S(1)}, pred[2]{0:T(512)(128)(4,1)}, u32[]{:S(2)}) copy-start(pred[2]{0:T(512)(128)(4,1)} %get-tuple-element.96) | copy-start | bytes 10
  73.7 4.4 %copy-start.1 = (bf16[2,64,32,32]{3,2,1,0:T(8,128)(2,1)S(1)}, bf16[2,64,32,32]{3,2,1,0:T(8,128)(2,1)}, u32[]{:S(2)}) copy-start(bf16[2,64,32,32]{3,2,1,0:T(8,128)(2,1)} %copy.79) | copy-start | bytes 786436
  81.9 16.4 %all-to-all-start.1 = ((bf16[32,2,2048]{2,1,0:T(2,128)(2,1)}), bf16[32,2,2048]{2,1,0:T(2,128)(2,1)S(1)}, u32[]{:S(2)}, u32[]{:S(2)}) async-start(bf16[32,2,2048]{2,1,0:T(2,128)(2,1)} %reshape.476), calls=%async_computation.1 | async-start | bytes 524288 | tf_op jit(solution)/shard_map/all_to_all | solution.py:145

commit v7 on v6

--- a/solution.py
+++ b/solution.py
@@ -44,7 +44,7 @@
     flat_field = field.reshape(channels * lat_rows, lon_cols)
     partial = lax.dot_general(
         forward_rows, flat_field, (((1,), (1,)), ((), ())), preferred_element_type=jnp.float32
-    ).reshape(n_dev, m_dev, 2, channels, lat_rows)
+    ).reshape(n_dev, m_dev * 2 * channels * lat_rows)
     gathered_raw = lax.all_to_all(partial, BOTH, 0, 0, tiled=True)
     rim_cols = ((lon_cols + 4 + 127) // 128) * 128
     lat_n = lax.axis_size("lat")
@@ -75,7 +75,8 @@
     )
     conv_out = depthwise_conv(offsets, conv_weight, rim, lat_rows, lon_cols)
     gathered, conv_out = lax.optimization_barrier((gathered_raw, conv_out))
-    summed = gathered.reshape(lat_count, lon_count, m_dev, 2, channels, lat_rows).sum(axis=1)
+    summed = gathered.reshape(lat_count, lon_count, m_dev * 2 * channels * lat_rows).sum(axis=1)
+    summed = summed.reshape(lat_count, m_dev, 2, channels, lat_rows)
     raw_spec = jnp.transpose(summed, (1, 2, 3, 0, 4)).reshape(m_dev, 2, channels, total_lat)
 
     rim = jnp.pad(raw_spec, ((0, 0), (0, 0), (0, 0), (2, 2)))
@@ -141,7 +142,7 @@
     )
     outgoing = jnp.broadcast_to(
         by_group[:, None], (lat_count, lon_count, m_dev, 2, channels, lat_rows)
-    ).reshape(n_dev, m_dev, 2, channels, lat_rows)
+    ).reshape(n_dev, m_dev * 2 * channels * lat_rows)
     full_rows = lax.all_to_all(outgoing, BOTH, 0, 0, tiled=True)
     spectral_rows = full_rows.reshape(orders_all * 2, channels * lat_rows)
     inverse_rows = wave_table(

time: 107 us -> 104 us (0.972)
  local copies, waits for them, and re-layouts: 23.4 us -> 15.6 us
  other arithmetic: 19 us -> 21.1 us
  waiting for transfers between devices: 8.04 us -> 9.88 us
  matrix products: 8.47 us -> 10.2 us
    unnamed x72 -> x56, local copies, waits for them, and re-layouts: 8.71 us -> 4.35 us
    all_to_all x1 -> x2, other arithmetic: 1.9 us -> 4.66 us  [per_device(): full_rows = lax.all_to_all(outgoing, BOTH, 0, 0, tiled=True)]
    dot_general x1 -> x0, local copies, waits for them, and re-layouts: 2.54 us -> none  [per_device(): lax.dot_general(forward_rows, flat_field, (((1,), (1,)), ((), ())), prefe...]
    optimization_barrier x1 -> x0, local copies, waits for them, and re-layouts: 2.01 us -> none  [per_device(): gathered, conv_out = lax.optimization_barrier((gathered_raw, conv_out))]
    all_to_all x0 -> x2, local copies, waits for them, and re-layouts: none -> 1.84 us  [per_device(): full_rows = lax.all_to_all(outgoing, BOTH, 0, 0, tiled=True)]
    all_to_all x1, waiting for transfers between devices: 8.03 us -> 9.87 us  [per_device(): full_rows = lax.all_to_all(outgoing, BOTH, 0, 0, tiled=True)]
    reshape x1, local copies, waits for them, and re-layouts: 1.81 us -> 0.17 us  [per_device(): spectral_rows = full_rows.reshape(orders_all * 2, channels * lat_rows)]
    reduce_sum x1, other arithmetic: 1.91 us -> 0.31 us  [per_device(): gathered.reshape(lat_count, lon_count, m_dev * 2 * channels * lat_rows)]
  transfers between devices with their start and end apart: 6 -> 6, of which waited for: 1 -> 1; matrix products, arithmetic and copies ran while one was open for 24% -> 18% of each run, Pallas kernels for 13% -> 13%
where the time goes in v7:
time: 104 us; the launch traced here: 103 us
  starting transfers between devices  21.3 us (20%)
  other arithmetic  21.1 us (20%)
  local copies, waits for them, and re-layouts  15.6 us (15%)
  Pallas kernels  13.7 us (13%)
  between operations  11.4 us (11%)
  matrix products  10.2 us (10%)
  waiting for transfers between devices  9.88 us (10%)
    pallas_call x1, Pallas kernels, depthwise_conv(): pl.pallas_call(body, grid_spec=pltpu.PrefetchScalarGridSpec(num_scalar_pr...  13.7 us
    all_to_all x1, waiting for transfers between devices, per_device(): full_rows = lax.all_to_all(outgoing, BOTH, 0, 0, tiled=True)  9.87 us
    all_to_all x1, starting transfers between devices, per_device(): gathered_raw = lax.all_to_all(partial, BOTH, 0, 0, tiled=True)  6.96 us
    all_to_all x1, starting transfers between devices, per_device(): full_rows = lax.all_to_all(outgoing, BOTH, 0, 0, tiled=True)  6.03 us
    ppermute x1, starting transfers between devices, per_device(): lax.ppermute(field[:, lat_rows - 2:], 'lat', [(i, i + 1) for i in range(l...  5.53 us
    all_to_all x2, other arithmetic, per_device(): full_rows = lax.all_to_all(outgoing, BOTH, 0, 0, tiled=True)  4.66 us
    unnamed x56, local copies, waits for them, and re-layouts  4.35 us
    concatenate x1, other arithmetic, per_device(): jnp.concatenate([rows_ext, east, jnp.zeros((channels, rim_rows, rim_cols...  4.34 us
  transfers between devices with their start and end apart: 6, of which 1 were waited for; matrix products, arithmetic and copies ran while one was open for 18% of the time, Pallas kernels for 13%

profile of v7, /device:TPU:0, one launch (start us, length us, event | category | flops | bytes accessed | tf_op | source)
XLA Modules:
  0.0 103.3 jit_solution(9484444516736938846)
XLA Ops:
  0.0 2.3 %fusion.65 = (bf16[32,2,900]{2,1,0:T(2,128)(2,1)}, bf16[32,2,900]{2,1,0:T(2,128)(2,1)}) fusion(bf16[32,32,900]{2,1,0:T(8,128)(2,1)} %param.7), kind=kLoop, calls=%fused_computation.191 | loop fusion | bytes 460800 | tf_op jit(solution)/shard_map/slice | solution.py:55
  2.3 5.5 %collective-permute-start = (bf16[32,2,900]{2,1,0:T(2,128)(2,1)}, bf16[32,2,900]{2,1,0:T(2,128)(2,1)}, u32[]{:S(2)}, u32[]{:S(2)}) collective-permute-start(bf16[32,2,900]{2,1,0:T(2,128)(2,1)} %get-tuple-element.11), channel_id=1, source_target_pairs={{0,4},{4,8},{8,12},{12,16},{16,20},{20,24},{24,28},{1,5},{5,9},{9,... | collective-permute-start | bytes 345608 | tf_op jit(solution)/shard_map/ppermute | solution.py:54
  7.8 1.3 %collective-permute-start.1 = (bf16[32,2,900]{2,1,0:T(2,128)(2,1)}, bf16[32,2,900]{2,1,0:T(2,128)(2,1)}, u32[]{:S(2)}, u32[]{:S(2)}) collective-permute-start(bf16[32,2,900]{2,1,0:T(2,128)(2,1)} %get-tuple-element.12), channel_id=1, source_target_pairs={{4,0},{8,4},{12,8},{16,12},{20,16},{24,20},{28,24},{5,1},{9,5},{13... | collective-permute-start | bytes 345608 | tf_op jit(solution)/shard_map/ppermute | solution.py:51
  9.1 1.8 %multiply_convert_fusion.1 = (bf16[64,1,900]{2,0,1:T(8,128)(2,1)}, bf16[64,1,900]{2,0,1:T(8,128)(2,1)}, bf16[64,1,900]{2,0,1:T(8,128)(2,1)S(1)}, bf16[64,1,900]{2,0,1:T(8,128)(2,1)S(1)}) fusion(f32[64]{0:T(128)S(1)} %get-tuple-element.97, s32[900]{0:T(1024)S(1)} %iota_add_fusion, f32[64]{0:T(128)S(1)} %get-tuple-element.98), kind=kLoop, calls=%fused_computation.57 | loop fusion | flops 979200 | bytes 464912 | tf_op jit(solution)/shard_map/convert
  11.0 0.3 copy.77
  11.3 0.2 convert_element_type.109
  11.4 2.5 %fusion.68 = f32[128,1024]{1,0:T(8,128)S(1)} fusion(bf16[128,900]{1,0:T(8,128)(2,1)S(1)} %convert_element_type.109, bf16[1024,900]{1,0:T(8,128)(2,1)} %bitcast.167), kind=kOutput, calls=%fused_computation.194 | convolution fusion | flops 235929600 | bytes 2597888 | tf_op jit(solution)/shard_map/dot_general | solution.py:45
  13.9 1.4 %all_to_all.19 = f32[32,1,4096]{2,1,0:T(1,128)} reshape(f32[128,1024]{1,0:T(8,128)S(1)} %fusion.68) | data formatting | bytes 1048576 | tf_op jit(solution)/shard_map/all_to_all | solution.py:48
  15.3 7.0 %all-to-all-start = ((f32[32,1,4096]{2,1,0:T(1,128)}), f32[32,1,4096]{2,1,0:T(1,128)S(1)}, u32[]{:S(2)}, u32[]{:S(2)}) async-start(f32[32,1,4096]{2,1,0:T(1,128)} %all_to_all.19), calls=%async_computation | async-start | bytes 1048576 | tf_op jit(solution)/shard_map/all_to_all | solution.py:48
  22.4 0.7 fusion.66
  23.0 0.1 fusion.52
  23.2 0.7 fusion.58
  23.9 0.7 compare_convert_fusion.2
  24.5 0.6 slice_bitcast_fusion.8
  25.2 0.7 fusion.67
  26.0 1.9 %pad_maximum_fusion.4 = (bf16[32,40,2]{2,1,0:T(8,128)(2,1)}, bf16[32,40,2]{2,1,0:T(8,128)(2,1)}) fusion(bf16[32,4,900]{2,1,0:T(4,128)(2,1)S(1)} %broadcast_in_dim.84, bf16[32,2,900]{2,1,0:T(2,128)(2,1)} %collective-permute-done.1, bf16[32,32,900]{2,1,0:T(8,128)(2,1)S(1)} %copy-done, bf16[32,2,900]{2,1,0:T(2,128)(2,1)} %collective-permute-done), kind=kLoop, calls=%fused_computation.44 | loop fusion | flops 40960 | bytes 2314240 | tf_op jit(solution)/shard_map/slice | solution.py:62
  27.9 1.5 %collective-permute-start.2 = (bf16[32,40,2]{2,1,0:T(8,128)(2,1)}, bf16[32,40,2]{2,1,0:T(8,128)(2,1)}, u32[]{:S(2)}, u32[]{:S(2)}) collective-permute-start(bf16[32,40,2]{2,1,0:T(8,128)(2,1)} %get-tuple-element.9), channel_id=1, source_target_pairs={{1,0},{2,1},{3,2},{0,3},{5,4},{6,5},{7,6},{4,7},{9,8},{10,9},{11,1... | collective-permute-start | bytes 15368 | tf_op jit(solution)/shard_map/ppermute | solution.py:61
  29.4 0.6 fusion.59
  40.7 0.1 copy.79.offs_ref
  40.9 2.3 %copy.83 = bf16[2,64,32,32]{3,2,1,0:T(8,128)(2,1)} copy(bf16[2,64,32,32]{1,3,2,0:T(8,128)(2,1)S(1)} %copy-done.2) | data formatting | bytes 524288 | tf_op args[6]
  43.3 4.3 %pad_maximum_fusion.rim_ref = bf16[32,40,1024]{2,1,0:T(8,128)(2,1)S(1)} fusion(bf16[32,40,2]{2,1,0:T(8,128)(2,1)} %collective-permute-done.3, bf16[32,40,2]{2,1,0:T(8,128)(2,1)} %collective-permute-done.2, bf16[32,4,900]{2,1,0:T(4,128)(2,1)S(1)} %broadcast_in_dim.84, bf16[32,2,900]{2,1,0:T(2,128)(2,1)} %collective-permute-done.1, ...), kind=kLoop, calls=%fused_computation.10 | loop fusion | flops 18350080 | bytes 4937728 | tf_op jit(solution)/shard_map/concatenate | solution.py:67
  47.8 13.7 %shard_map.73 = bf16[32,32,900]{2,1,0:T(8,128)(2,1)S(1)} custom-call(s32[9,2]{1,0:T(8,128)S(1)} %copy.79.offs_ref, bf16[32,40,1024]{2,1,0:T(8,128)(2,1)S(1)} %pad_maximum_fusion.rim_ref, f32[32,9]{1,0:T(8,128)S(1)} %copy.80.w_ref), custom_call_target="tpu_custom_call" | custom-call | flops 94371840 | bytes 4464640 | tf_op jit(solution)/shard_map/pallas_call | solution.py:200
  61.5 0.3 copy.130
  61.9 0.1 reshape.461
  62.0 0.3 reduce_sum.9
  62.3 0.2 reshape.462
  62.5 0.3 copy.81
  62.8 0.2 reshape.463
  63.1 0.3 multiply_subtract_fusion.1
  63.4 0.3 multiply_subtract_fusion
  63.7 0.3 multiply_subtract_fusion.2
  64.0 0.2 fusion.30
  64.4 0.2 fusion.12
  64.7 0.3 copy-done.7
  64.9 1.1 %convolution_bitcast_fusion.2 = f32[2,32,2,32]{3,2,0,1:T(2,128)S(1)} fusion(bf16[2,32,2,32]{3,2,0,1:T(2,128)(2,1)S(1)} %copy.85, bf16[2,32,2,32,32]{4,3,2,1,0:T(8,128)(2,1)} %bitcast.171), kind=kOutput, calls=%fused_computation.14 | convolution fusion | flops 262144 | bytes 286720 | tf_op jit(solution)/shard_map/mupc,ucd->mupd/dot_general | solution.py:122
  66.1 1.8 %convolution_bitcast_fusion.3 = f32[2,32,2,32]{3,2,0,1:T(2,128)} fusion(bf16[2,32,2,32]{3,2,0,1:T(2,128)(2,1)S(1)} %copy.85, bf16[2,32,2,32,32]{4,3,2,1,0:T(8,128)(2,1)} %bitcast.172), kind=kOutput, calls=%fused_computation.15 | convolution fusion | flops 262144 | bytes 286720 | tf_op jit(solution)/shard_map/mupc,ucd->mupd/dot_general | solution.py:119
  67.9 1.6 %fusion.11 = bf16[2,32,2,32]{1,3,2,0:T(8,128)(2,1)} fusion(f32[2,32]{1,0:T(2,128)} %get-tuple-element.92, pred[2]{0:T(512)(128)(4,1)} %get-tuple-element.96, bf16[2,32,1,128]{3,2,1,0:T(2,128)(2,1)} %get-tuple-element.48, bf16[2,2,32,128]{3,2,1,0:T(8,128)(2,1)} %copy-done.7, f32[2,128]{1,0:T(2,128)} %fusion.58, bf16[2,2,32,256]{3,2,1,0:T(8,128)(2,1)S(1)} %fusion.30), kind=kOutput, calls=%fused_computation.19 | convolution fusion | flops 1204224 | bytes 91394 | tf_op jit(solution)/shard_map/mui,mpci->mupc/dot_general | solution.py:113
  69.5 0.8 copy.91
  70.4 0.2 convolution_bitcast_fusion
  70.6 0.2 convolution_bitcast_fusion.1
  70.8 1.0 fusion.38
  71.8 0.1 pad_maximum_fusion.7
  71.9 1.0 fusion.41
  72.9 0.1 pad_maximum_fusion.8
  73.0 1.0 subtract_multiply_fusion
  74.0 0.8 multiply_convert_fusion.4
  74.8 0.1 concatenate.18
  75.0 0.1 concatenate.17
  75.1 0.2 maximum_bitcast_fusion
  75.3 0.2 broadcast_in_dim.89
  75.6 1.3 %all_to_all.20 = bf16[32,1,4096]{2,1,0:T(2,128)(2,1)} reshape(bf16[8,4,2,2,32,32]{5,4,3,2,1,0:T(8,128)(2,1)S(1)} %broadcast_in_dim.89) | data formatting | bytes 524288 | tf_op jit(solution)/shard_map/all_to_all | solution.py:146
  76.9 0.5 broadcast.480
  77.4 3.1 %reduce.1 = bf16[32,4096]{1,0:T(8,128)(2,1)S(1)} reduce(bf16[32,1,4096]{2,1,0:T(2,128)(2,1)} %all_to_all.20, bf16[]{:T(256)} %broadcast.480), dimensions={1}, to_apply=%all_to_all.20.reduce_sub_computation | reduce | bytes 524290 | tf_op jit(solution)/shard_map/all_to_all | solution.py:146
  80.5 0.9 reshape.475
  81.4 6.0 %all-to-all-start.1 = ((bf16[32,2,2048]{2,1,0:T(2,128)(2,1)}), bf16[32,2,2048]{2,1,0:T(2,128)(2,1)S(1)}, u32[]{:S(2)}, u32[]{:S(2)}) async-start(bf16[32,2,2048]{2,1,0:T(2,128)(2,1)} %reshape.475), calls=%async_computation.1 | async-start | bytes 524288 | tf_op jit(solution)/shard_map/all_to_all | solution.py:146
  87.5 0.3 copy.98
  87.8 0.2 convert_element_type.124
  88.0 9.9 %all-to-all-done.1 = bf16[32,2,2048]{2,1,0:T(2,128)(2,1)S(1)} async-done(((bf16[32,2,2048]{2,1,0:T(2,128)(2,1)}), bf16[32,2,2048]{2,1,0:T(2,128)(2,1)S(1)}, u32[]{:S(2)}, u32[]{:S(2)}) %all-to-all-start.1) | async-done | bytes 262176 | tf_op jit(solution)/shard_map/all_to_all | solution.py:146
  97.8 0.3 reshape.476
  98.1 1.5 %reduce = bf16[32,4096]{1,0:T(8,128)(2,1)S(1)} reduce(bf16[32,1,4096]{2,1,0:T(2,128)(2,1)S(1)} %reshape.476, bf16[]{:T(256)} %constant.120), dimensions={1}, to_apply=%all_to_all.18.reduce_sub_computation | reduce | bytes 524290 | tf_op jit(solution)/shard_map/all_to_all | solution.py:146
  99.6 0.2 reshape.466
  99.8 0.2 copy.97
  100.0 0.7 fusion.15
  100.7 2.6 %fusion.8 = bf16[32,32,900]{2,1,0:T(8,128)(2,1)} fusion(f32[32,32,900]{2,1,0:T(8,128)S(1)} %fusion.15, bf16[32,32,900]{2,1,0:T(8,128)(2,1)S(1)} %shard_map.73), kind=kLoop, calls=%fused_computation.9 | loop fusion | flops 10137600 | bytes 7372800 | tf_op jit(solution)/shard_map/convert_element_type | solution.py:155
  (74 shorter events, 0.9 us)
Async XLA Ops:
  0.0 26.0 %copy-start = (bf16[32,32,900]{2,1,0:T(8,128)(2,1)S(1)}, bf16[32,32,900]{2,1,0:T(8,128)(2,1)}, u32[]{:S(2)}) copy-start(bf16[32,32,900]{2,1,0:T(8,128)(2,1)} %param.7) | copy-start | bytes 5529604
  0.0 22.3 %copy-start.8 = (s32[9,2]{0,1:T(2,128)S(1)}, s32[9,2]{0,1:T(2,128)}, u32[]{:S(2)}) copy-start(s32[9,2]{0,1:T(2,128)} %param.8) | copy-start | bytes 220
  0.0 22.3 %copy-start.9 = (f32[32,9]{0,1:T(8,128)S(1)}, f32[32,9]{0,1:T(8,128)}, u32[]{:S(2)}) copy-start(f32[32,9]{0,1:T(8,128)} %param.9) | copy-start | bytes 3460
  0.0 22.4 %copy-start.5 = (bf16[2,64,128]{2,1,0:T(8,128)(2,1)S(1)}, bf16[2,64,128]{2,1,0:T(8,128)(2,1)}, u32[]{:S(2)}) copy-start(bf16[2,64,128]{2,1,0:T(8,128)(2,1)} %param.10) | copy-start | bytes 98308
  0.0 23.2 %copy-start.10 = (s32[128]{0:T(128)S(1)}, s32[128]{0:T(128)}, u32[]{:S(2)}) copy-start(s32[128]{0:T(128)} %param.12) | copy-start | bytes 1540
  0.0 23.2 %copy-start.23 = (f32[128]{0:T(128)S(1)}, f32[128]{0:T(128)}, u32[]{:S(2)}) copy-start(f32[128]{0:T(128)} %param.11) | copy-start | bytes 1540
  2.3 23.6 %collective-permute-start = (bf16[32,2,900]{2,1,0:T(2,128)(2,1)}, bf16[32,2,900]{2,1,0:T(2,128)(2,1)}, u32[]{:S(2)}, u32[]{:S(2)}) collective-permute-start(bf16[32,2,900]{2,1,0:T(2,128)(2,1)} %get-tuple-element.11), channel_id=1, source_target_pairs={{0,4},{4,8},{8,12},{12,16},{16,20},{20,24},{24,28},{1,5},{5,9},{9,... | collective-permute-start | bytes 345608 | tf_op jit(solution)/shard_map/ppermute | solution.py:54
  7.8 18.1 %collective-permute-start.1 = (bf16[32,2,900]{2,1,0:T(2,128)(2,1)}, bf16[32,2,900]{2,1,0:T(2,128)(2,1)}, u32[]{:S(2)}, u32[]{:S(2)}) collective-permute-start(bf16[32,2,900]{2,1,0:T(2,128)(2,1)} %get-tuple-element.12), channel_id=1, source_target_pairs={{4,0},{8,4},{12,8},{16,12},{20,16},{24,20},{28,24},{5,1},{9,5},{13... | collective-permute-start | bytes 345608 | tf_op jit(solution)/shard_map/ppermute | solution.py:51
  11.4 29.5 %copy-start.2 = (bf16[2,64,32,32]{1,3,2,0:T(8,128)(2,1)S(1)}, bf16[2,64,32,32]{1,3,2,0:T(8,128)(2,1)}, u32[]{:S(2)}) copy-start(bf16[2,64,32,32]{1,3,2,0:T(8,128)(2,1)} %param.13) | copy-start | bytes 786436
  15.3 46.2 %all-to-all-start = ((f32[32,1,4096]{2,1,0:T(1,128)}), f32[32,1,4096]{2,1,0:T(1,128)S(1)}, u32[]{:S(2)}, u32[]{:S(2)}) async-start(f32[32,1,4096]{2,1,0:T(1,128)} %all_to_all.19), calls=%async_computation | async-start | bytes 1048576 | tf_op jit(solution)/shard_map/all_to_all | solution.py:48
  23.0 43.0 %copy-start.6 = (bf16[2,32,1,128]{3,2,1,0:T(2,128)(2,1)}, bf16[2,32,1,128]{3,2,1,0:T(2,128)(2,1)S(1)}, u32[]{:S(2)}) copy-start(bf16[2,32,1,128]{3,2,1,0:T(2,128)(2,1)S(1)} %get-tuple-element.47) | copy-start | bytes 49156
  27.9 15.4 %collective-permute-start.2 = (bf16[32,40,2]{2,1,0:T(8,128)(2,1)}, bf16[32,40,2]{2,1,0:T(8,128)(2,1)}, u32[]{:S(2)}, u32[]{:S(2)}) collective-permute-start(bf16[32,40,2]{2,1,0:T(8,128)(2,1)} %get-tuple-element.9), channel_id=1, source_target_pairs={{1,0},{2,1},{3,2},{0,3},{5,4},{6,5},{7,6},{4,7},{9,8},{10,9},{11,1... | collective-permute-start | bytes 15368 | tf_op jit(solution)/shard_map/ppermute | solution.py:61
  29.4 13.9 %collective-permute-start.3 = (bf16[32,40,2]{2,1,0:T(8,128)(2,1)}, bf16[32,40,2]{2,1,0:T(8,128)(2,1)}, u32[]{:S(2)}, u32[]{:S(2)}) collective-permute-start(bf16[32,40,2]{2,1,0:T(8,128)(2,1)} %get-tuple-element.10), channel_id=1, source_target_pairs={{0,1},{1,2},{2,3},{3,0},{4,5},{5,6},{6,7},{7,4},{8,9},{9,10},{10,1... | collective-permute-start | bytes 15368 | tf_op jit(solution)/shard_map/ppermute | solution.py:64
  30.0 34.3 %copy-start.24 = (pred[2]{0:T(512)(128)(4,1)}, pred[2]{0:T(512)(128)(4,1)S(1)}, u32[]{:S(2)}) copy-start(pred[2]{0:T(512)(128)(4,1)S(1)} %get-tuple-element.95) | copy-start | bytes 10
  47.7 15.3 %copy-start.15 = (f32[2]{0:T(128)S(1)}, f32[2]{0:T(128)}, u32[]{:S(2)}) copy-start(f32[2]{0:T(128)} %get-tuple-element.68) | copy-start | bytes 28
  47.7 15.3 %copy-start.16 = (f32[2]{0:T(128)S(1)}, f32[2]{0:T(128)}, u32[]{:S(2)}) copy-start(f32[2]{0:T(128)} %get-tuple-element.72) | copy-start | bytes 28
  47.7 15.3 %copy-start.17 = (f32[2]{0:T(128)S(1)}, f32[2]{0:T(128)}, u32[]{:S(2)}) copy-start(f32[2]{0:T(128)} %get-tuple-element.73) | copy-start | bytes 28
  47.7 15.3 %copy-start.18 = (f32[2]{0:T(128)S(1)}, f32[2]{0:T(128)}, u32[]{:S(2)}) copy-start(f32[2]{0:T(128)} %get-tuple-element.103) | copy-start | bytes 28
  47.7 15.3 %copy-start.19 = (f32[2]{0:T(128)S(1)}, f32[2]{0:T(128)}, u32[]{:S(2)}) copy-start(f32[2]{0:T(128)} %get-tuple-element.104) | copy-start | bytes 28
  47.7 15.3 %copy-start.20 = (f32[2]{0:T(128)S(1)}, f32[2]{0:T(128)}, u32[]{:S(2)}) copy-start(f32[2]{0:T(128)} %get-tuple-element.108) | copy-start | bytes 28
  47.7 15.7 %copy-start.11 = (f32[2]{0:T(128)S(1)}, f32[2]{0:T(128)}, u32[]{:S(2)}) copy-start(f32[2]{0:T(128)} %get-tuple-element.75) | copy-start | bytes 28
  47.7 15.7 %copy-start.12 = (f32[2]{0:T(128)S(1)}, f32[2]{0:T(128)}, u32[]{:S(2)}) copy-start(f32[2]{0:T(128)} %get-tuple-element.101) | copy-start | bytes 28
  47.8 15.7 %copy-start.13 = (f32[2]{0:T(128)S(1)}, f32[2]{0:T(128)}, u32[]{:S(2)}) copy-start(f32[2]{0:T(128)} %get-tuple-element.102) | copy-start | bytes 28
  47.8 15.7 %copy-start.14 = (f32[2]{0:T(128)S(1)}, f32[2]{0:T(128)}, u32[]{:S(2)}) copy-start(f32[2]{0:T(128)} %get-tuple-element.109) | copy-start | bytes 28
  61.5 2.8 %copy-start.21 = (f32[2,32]{1,0:T(2,128)S(1)}, f32[2,32]{1,0:T(2,128)}, u32[]{:S(2)}) copy-start(f32[2,32]{1,0:T(2,128)} %get-tuple-element.91) | copy-start | bytes 772
  61.5 2.8 %copy-start.22 = (f32[2,128]{1,0:T(2,128)S(1)}, f32[2,128]{1,0:T(2,128)}, u32[]{:S(2)}) copy-start(f32[2,128]{1,0:T(2,128)} %fusion.58) | copy-start | bytes 3076
  63.0 7.4 %copy-start.1 = (bf16[2,64,32,32]{3,2,1,0:T(8,128)(2,1)S(1)}, bf16[2,64,32,32]{3,2,1,0:T(8,128)(2,1)}, u32[]{:S(2)}) copy-start(bf16[2,64,32,32]{3,2,1,0:T(8,128)(2,1)} %copy.83) | copy-start | bytes 786436
  64.3 0.6 copy-start.7
  67.9 19.6 %copy-start.3 = (bf16[64,1,900]{2,0,1:T(8,128)(2,1)S(1)}, bf16[64,1,900]{2,0,1:T(8,128)(2,1)}, u32[]{:S(2)}) copy-start(bf16[64,1,900]{2,0,1:T(8,128)(2,1)} %get-tuple-element.76) | copy-start | bytes 345604
  67.9 19.6 %copy-start.4 = (bf16[64,1,900]{2,0,1:T(8,128)(2,1)S(1)}, bf16[64,1,900]{2,0,1:T(8,128)(2,1)}, u32[]{:S(2)}) copy-start(bf16[64,1,900]{2,0,1:T(8,128)(2,1)} %get-tuple-element.77) | copy-start | bytes 345604
  81.4 16.4 %all-to-all-start.1 = ((bf16[32,2,2048]{2,1,0:T(2,128)(2,1)}), bf16[32,2,2048]{2,1,0:T(2,128)(2,1)S(1)}, u32[]{:S(2)}, u32[]{:S(2)}) async-start(bf16[32,2,2048]{2,1,0:T(2,128)(2,1)} %reshape.475), calls=%async_computation.1 | async-start | bytes 524288 | tf_op jit(solution)/shard_map/all_to_all | solution.py:146

commit v8 on v7

--- a/solution.py
+++ b/solution.py
@@ -58,11 +58,25 @@
         [north, field, south, jnp.zeros((channels, 4, lon_cols), field.dtype)], axis=1
     )
     rim_rows = rows_ext.shape[1]
-    east = lax.ppermute(
-        rows_ext[:, :, :2], "lon", [((i + 1) % lon_count, i) for i in range(lon_count)]
-    )
-    west = lax.ppermute(
-        rows_ext[:, :, lon_cols - 2 :], "lon", [(i, (i + 1) % lon_count) for i in range(lon_count)]
+    def lane_dense(edge):
+        return jnp.transpose(edge, (2, 0, 1)).reshape(2, channels * rim_rows)
+
+    def from_lanes(packed):
+        return jnp.transpose(packed.reshape(2, channels, rim_rows), (1, 2, 0))
+
+    east = from_lanes(
+        lax.ppermute(
+            lane_dense(rows_ext[:, :, :2]),
+            "lon",
+            [((i + 1) % lon_count, i) for i in range(lon_count)],
+        )
+    )
+    west = from_lanes(
+        lax.ppermute(
+            lane_dense(rows_ext[:, :, lon_cols - 2 :]),
+            "lon",
+            [(i, (i + 1) % lon_count) for i in range(lon_count)],
+        )
     )
     rim = jnp.concatenate(
         [

time: 104 us -> 105 us (level)
  no operation moved by 1% of the time
where the time goes in v8:
time: 105 us; the launch traced here: 104 us
  starting transfers between devices  21.6 us (21%)
  other arithmetic  21.1 us (20%)
  local copies, waits for them, and re-layouts  15.6 us (15%)
  Pallas kernels  13.7 us (13%)
  between operations  11.4 us (11%)
  matrix products  10.2 us (10%)
  waiting for transfers between devices  9.88 us (9%)
    pallas_call x1, Pallas kernels, depthwise_conv(): pl.pallas_call(body, grid_spec=pltpu.PrefetchScalarGridSpec(num_scalar_pr...  13.7 us
    all_to_all x1, waiting for transfers between devices, per_device(): full_rows = lax.all_to_all(outgoing, BOTH, 0, 0, tiled=True)  9.87 us
    all_to_all x1, starting transfers between devices, per_device(): gathered_raw = lax.all_to_all(partial, BOTH, 0, 0, tiled=True)  6.96 us
    all_to_all x1, starting transfers between devices, per_device(): full_rows = lax.all_to_all(outgoing, BOTH, 0, 0, tiled=True)  6.05 us
    ppermute x1, starting transfers between devices, per_device(): lax.ppermute(field[:, lat_rows - 2:], 'lat', [(i, i + 1) for i in range(l...  5.53 us
    all_to_all x2, other arithmetic, per_device(): full_rows = lax.all_to_all(outgoing, BOTH, 0, 0, tiled=True)  4.66 us
    unnamed x56, local copies, waits for them, and re-layouts  4.35 us
    concatenate x1, other arithmetic, per_device(): jnp.concatenate([rows_ext, east, jnp.zeros((channels, rim_rows, rim_cols...  4.34 us
  transfers between devices with their start and end apart: 6, of which 1 were waited for; matrix products, arithmetic and copies ran while one was open for 18% of the time, Pallas kernels for 13%

profile of v8, /device:TPU:0, one launch (start us, length us, event | category | flops | bytes accessed | tf_op | source)
XLA Modules:
  0.0 103.6 jit_solution(16496083346194975520)
XLA Ops:
  0.0 2.3 %fusion.65 = (bf16[32,2,900]{2,1,0:T(2,128)(2,1)}, bf16[32,2,900]{2,1,0:T(2,128)(2,1)}) fusion(bf16[32,32,900]{2,1,0:T(8,128)(2,1)} %param.7), kind=kLoop, calls=%fused_computation.191 | loop fusion | bytes 460800 | tf_op jit(solution)/shard_map/slice | solution.py:55
  2.3 5.5 %collective-permute-start = (bf16[32,2,900]{2,1,0:T(2,128)(2,1)}, bf16[32,2,900]{2,1,0:T(2,128)(2,1)}, u32[]{:S(2)}, u32[]{:S(2)}) collective-permute-start(bf16[32,2,900]{2,1,0:T(2,128)(2,1)} %get-tuple-element.11), channel_id=1, source_target_pairs={{0,4},{4,8},{8,12},{12,16},{16,20},{20,24},{24,28},{1,5},{5,9},{9,... | collective-permute-start | bytes 345608 | tf_op jit(solution)/shard_map/ppermute | solution.py:54
  7.8 1.3 %collective-permute-start.1 = (bf16[32,2,900]{2,1,0:T(2,128)(2,1)}, bf16[32,2,900]{2,1,0:T(2,128)(2,1)}, u32[]{:S(2)}, u32[]{:S(2)}) collective-permute-start(bf16[32,2,900]{2,1,0:T(2,128)(2,1)} %get-tuple-element.12), channel_id=1, source_target_pairs={{4,0},{8,4},{12,8},{16,12},{20,16},{24,20},{28,24},{5,1},{9,5},{13... | collective-permute-start | bytes 345608 | tf_op jit(solution)/shard_map/ppermute | solution.py:51
  9.1 1.8 %multiply_convert_fusion.1 = (bf16[64,1,900]{2,0,1:T(8,128)(2,1)}, bf16[64,1,900]{2,0,1:T(8,128)(2,1)}, bf16[64,1,900]{2,0,1:T(8,128)(2,1)S(1)}, bf16[64,1,900]{2,0,1:T(8,128)(2,1)S(1)}) fusion(f32[64]{0:T(128)S(1)} %get-tuple-element.97, s32[900]{0:T(1024)S(1)} %iota_add_fusion, f32[64]{0:T(128)S(1)} %get-tuple-element.98), kind=kLoop, calls=%fused_computation.57 | loop fusion | flops 979200 | bytes 464912 | tf_op jit(solution)/shard_map/convert
  11.0 0.3 copy.77
  11.3 0.2 convert_element_type.109
  11.4 2.5 %fusion.68 = f32[128,1024]{1,0:T(8,128)S(1)} fusion(bf16[128,900]{1,0:T(8,128)(2,1)S(1)} %convert_element_type.109, bf16[1024,900]{1,0:T(8,128)(2,1)} %bitcast.179), kind=kOutput, calls=%fused_computation.194 | convolution fusion | flops 235929600 | bytes 2597888 | tf_op jit(solution)/shard_map/dot_general | solution.py:45
  13.9 1.4 %all_to_all.19 = f32[32,1,4096]{2,1,0:T(1,128)} reshape(f32[128,1024]{1,0:T(8,128)S(1)} %fusion.68) | data formatting | bytes 1048576 | tf_op jit(solution)/shard_map/all_to_all | solution.py:48
  15.3 7.0 %all-to-all-start = ((f32[32,1,4096]{2,1,0:T(1,128)}), f32[32,1,4096]{2,1,0:T(1,128)S(1)}, u32[]{:S(2)}, u32[]{:S(2)}) async-start(f32[32,1,4096]{2,1,0:T(1,128)} %all_to_all.19), calls=%async_computation | async-start | bytes 1048576 | tf_op jit(solution)/shard_map/all_to_all | solution.py:48
  22.4 0.7 fusion.66
  23.0 0.1 fusion.52
  23.2 0.7 fusion.58
  23.9 0.7 compare_convert_fusion.2
  24.5 0.6 slice_bitcast_fusion.8
  25.2 0.7 fusion.67
  26.0 1.9 %pad_maximum_fusion.4 = (bf16[32,40,2]{2,1,0:T(8,128)(2,1)}, bf16[32,40,2]{2,1,0:T(8,128)(2,1)}) fusion(bf16[32,4,900]{2,1,0:T(4,128)(2,1)S(1)} %broadcast_in_dim.84, bf16[32,2,900]{2,1,0:T(2,128)(2,1)} %collective-permute-done.1, bf16[32,32,900]{2,1,0:T(8,128)(2,1)S(1)} %copy-done, bf16[32,2,900]{2,1,0:T(2,128)(2,1)} %collective-permute-done), kind=kLoop, calls=%fused_computation.44 | loop fusion | flops 40960 | bytes 2314240 | tf_op jit(solution)/shard_map/slice | solution.py:69
  27.9 0.3 collective-permute-start.3
  28.2 1.5 %collective-permute-start.2 = (bf16[2,1280]{0,1:T(8,128)(2,1)}, bf16[2,1280]{0,1:T(8,128)(2,1)}, u32[]{:S(2)}, u32[]{:S(2)}) collective-permute-start(bf16[2,1280]{0,1:T(8,128)(2,1)} %bitcast.2), channel_id=1, source_target_pairs={{1,0},{2,1},{3,2},{0,3},{5,4},{6,5},{7,6},{4,7},{9,8},{10,9},{11,1... | collective-permute-start | bytes 15368 | tf_op jit(solution)/shard_map/ppermute | solution.py:68
  29.7 0.6 fusion.59
  40.9 0.1 copy.79.offs_ref
  41.1 2.3 %copy.83 = bf16[2,64,32,32]{3,2,1,0:T(8,128)(2,1)} copy(bf16[2,64,32,32]{1,3,2,0:T(8,128)(2,1)S(1)} %copy-done.2) | data formatting | bytes 524288 | tf_op args[6]
  43.6 4.3 %pad_maximum_fusion.rim_ref = bf16[32,40,1024]{2,1,0:T(8,128)(2,1)S(1)} fusion(bf16[32,40,2]{2,1,0:T(8,128)(2,1)} %bitcast.8, bf16[32,40,2]{2,1,0:T(8,128)(2,1)} %bitcast.4, bf16[32,4,900]{2,1,0:T(4,128)(2,1)S(1)} %broadcast_in_dim.84, bf16[32,2,900]{2,1,0:T(2,128)(2,1)} %collective-permute-done.1, bf16[32,32,900]{2,1,0:T(8,128)(2,1)S(1)} %copy-done, ...), kind=kLoop, calls=%fused_computation.10 | loop fusion | flops 18350080 | bytes 4937728 | tf_op jit(solution)/shard_map/concatenate | solution.py:81
  48.0 13.7 %shard_map.73 = bf16[32,32,900]{2,1,0:T(8,128)(2,1)S(1)} custom-call(s32[9,2]{1,0:T(8,128)S(1)} %copy.79.offs_ref, bf16[32,40,1024]{2,1,0:T(8,128)(2,1)S(1)} %pad_maximum_fusion.rim_ref, f32[32,9]{1,0:T(8,128)S(1)} %copy.80.w_ref), custom_call_target="tpu_custom_call" | custom-call | flops 94371840 | bytes 4464640 | tf_op jit(solution)/shard_map/pallas_call | solution.py:214
  61.8 0.3 copy.130
  62.1 0.1 reshape.477
  62.2 0.3 reduce_sum.9
  62.6 0.2 reshape.478
  62.7 0.3 copy.81
  63.0 0.2 reshape.479
  63.3 0.3 multiply_subtract_fusion.1
  63.6 0.3 multiply_subtract_fusion
  64.0 0.3 multiply_subtract_fusion.2
  64.3 0.2 fusion.30
  64.6 0.2 fusion.12
  64.9 0.3 copy-done.7
  65.1 1.1 %convolution_bitcast_fusion.2 = f32[2,32,2,32]{3,2,0,1:T(2,128)S(1)} fusion(bf16[2,32,2,32]{3,2,0,1:T(2,128)(2,1)S(1)} %copy.85, bf16[2,32,2,32,32]{4,3,2,1,0:T(8,128)(2,1)} %bitcast.183), kind=kOutput, calls=%fused_computation.14 | convolution fusion | flops 262144 | bytes 286720 | tf_op jit(solution)/shard_map/mupc,ucd->mupd/dot_general | solution.py:136
  66.3 1.8 %convolution_bitcast_fusion.3 = f32[2,32,2,32]{3,2,0,1:T(2,128)} fusion(bf16[2,32,2,32]{3,2,0,1:T(2,128)(2,1)S(1)} %copy.85, bf16[2,32,2,32,32]{4,3,2,1,0:T(8,128)(2,1)} %bitcast.184), kind=kOutput, calls=%fused_computation.15 | convolution fusion | flops 262144 | bytes 286720 | tf_op jit(solution)/shard_map/mupc,ucd->mupd/dot_general | solution.py:133
  68.1 1.6 %fusion.11 = bf16[2,32,2,32]{1,3,2,0:T(8,128)(2,1)} fusion(f32[2,32]{1,0:T(2,128)} %get-tuple-element.92, pred[2]{0:T(512)(128)(4,1)} %get-tuple-element.96, bf16[2,32,1,128]{3,2,1,0:T(2,128)(2,1)} %get-tuple-element.48, bf16[2,2,32,128]{3,2,1,0:T(8,128)(2,1)} %copy-done.7, f32[2,128]{1,0:T(2,128)} %fusion.58, bf16[2,2,32,256]{3,2,1,0:T(8,128)(2,1)S(1)} %fusion.30), kind=kOutput, calls=%fused_computation.19 | convolution fusion | flops 1204224 | bytes 91394 | tf_op jit(solution)/shard_map/mui,mpci->mupc/dot_general | solution.py:127
  69.7 0.8 copy.91
  70.6 0.2 convolution_bitcast_fusion
  70.8 0.2 convolution_bitcast_fusion.1
  71.0 1.0 fusion.38
  72.0 0.1 pad_maximum_fusion.7
  72.1 1.0 fusion.41
  73.2 1.0 subtract_multiply_fusion
  74.2 0.8 multiply_convert_fusion.4
  75.0 0.1 concatenate.18
  75.2 0.1 concatenate.17
  75.3 0.2 maximum_bitcast_fusion
  75.5 0.2 broadcast_in_dim.89
  75.8 1.3 %all_to_all.20 = bf16[32,1,4096]{2,1,0:T(2,128)(2,1)} reshape(bf16[8,4,2,2,32,32]{5,4,3,2,1,0:T(8,128)(2,1)S(1)} %broadcast_in_dim.89) | data formatting | bytes 524288 | tf_op jit(solution)/shard_map/all_to_all | solution.py:160
  77.1 0.5 broadcast.480
  77.6 3.1 %reduce.1 = bf16[32,4096]{1,0:T(8,128)(2,1)S(1)} reduce(bf16[32,1,4096]{2,1,0:T(2,128)(2,1)} %all_to_all.20, bf16[]{:T(256)} %broadcast.480), dimensions={1}, to_apply=%all_to_all.20.reduce_sub_computation | reduce | bytes 524290 | tf_op jit(solution)/shard_map/all_to_all | solution.py:160
  80.8 0.9 reshape.491
  81.6 6.1 %all-to-all-start.1 = ((bf16[32,2,2048]{2,1,0:T(2,128)(2,1)}), bf16[32,2,2048]{2,1,0:T(2,128)(2,1)S(1)}, u32[]{:S(2)}, u32[]{:S(2)}) async-start(bf16[32,2,2048]{2,1,0:T(2,128)(2,1)} %reshape.491), calls=%async_computation.1 | async-start | bytes 524288 | tf_op jit(solution)/shard_map/all_to_all | solution.py:160
  87.8 0.3 copy.98
  88.0 0.2 convert_element_type.124
  88.2 9.9 %all-to-all-done.1 = bf16[32,2,2048]{2,1,0:T(2,128)(2,1)S(1)} async-done(((bf16[32,2,2048]{2,1,0:T(2,128)(2,1)}), bf16[32,2,2048]{2,1,0:T(2,128)(2,1)S(1)}, u32[]{:S(2)}, u32[]{:S(2)}) %all-to-all-start.1) | async-done | bytes 262176 | tf_op jit(solution)/shard_map/all_to_all | solution.py:160
  98.1 0.3 reshape.492
  98.4 1.5 %reduce = bf16[32,4096]{1,0:T(8,128)(2,1)S(1)} reduce(bf16[32,1,4096]{2,1,0:T(2,128)(2,1)S(1)} %reshape.492, bf16[]{:T(256)} %constant.120), dimensions={1}, to_apply=%all_to_all.18.reduce_sub_computation | reduce | bytes 524290 | tf_op jit(solution)/shard_map/all_to_all | solution.py:160
  99.9 0.2 reshape.482
  100.1 0.2 copy.97
  100.2 0.7 fusion.15
  100.9 2.6 %fusion.8 = bf16[32,32,900]{2,1,0:T(8,128)(2,1)} fusion(f32[32,32,900]{2,1,0:T(8,128)S(1)} %fusion.15, bf16[32,32,900]{2,1,0:T(8,128)(2,1)S(1)} %shard_map.73), kind=kLoop, calls=%fused_computation.9 | loop fusion | flops 10137600 | bytes 7372800 | tf_op jit(solution)/shard_map/convert_element_type | solution.py:169
  (74 shorter events, 1.0 us)
Async XLA Ops:
  0.0 26.0 %copy-start = (bf16[32,32,900]{2,1,0:T(8,128)(2,1)S(1)}, bf16[32,32,900]{2,1,0:T(8,128)(2,1)}, u32[]{:S(2)}) copy-start(bf16[32,32,900]{2,1,0:T(8,128)(2,1)} %param.7) | copy-start | bytes 5529604
  0.0 22.3 %copy-start.8 = (s32[9,2]{0,1:T(2,128)S(1)}, s32[9,2]{0,1:T(2,128)}, u32[]{:S(2)}) copy-start(s32[9,2]{0,1:T(2,128)} %param.8) | copy-start | bytes 220
  0.0 22.3 %copy-start.9 = (f32[32,9]{0,1:T(8,128)S(1)}, f32[32,9]{0,1:T(8,128)}, u32[]{:S(2)}) copy-start(f32[32,9]{0,1:T(8,128)} %param.9) | copy-start | bytes 3460
  0.0 22.4 %copy-start.5 = (bf16[2,64,128]{2,1,0:T(8,128)(2,1)S(1)}, bf16[2,64,128]{2,1,0:T(8,128)(2,1)}, u32[]{:S(2)}) copy-start(bf16[2,64,128]{2,1,0:T(8,128)(2,1)} %param.10) | copy-start | bytes 98308
  0.0 23.2 %copy-start.10 = (s32[128]{0:T(128)S(1)}, s32[128]{0:T(128)}, u32[]{:S(2)}) copy-start(s32[128]{0:T(128)} %param.12) | copy-start | bytes 1540
  0.0 23.2 %copy-start.23 = (f32[128]{0:T(128)S(1)}, f32[128]{0:T(128)}, u32[]{:S(2)}) copy-start(f32[128]{0:T(128)} %param.11) | copy-start | bytes 1540
  2.3 23.6 %collective-permute-start = (bf16[32,2,900]{2,1,0:T(2,128)(2,1)}, bf16[32,2,900]{2,1,0:T(2,128)(2,1)}, u32[]{:S(2)}, u32[]{:S(2)}) collective-permute-start(bf16[32,2,900]{2,1,0:T(2,128)(2,1)} %get-tuple-element.11), channel_id=1, source_target_pairs={{0,4},{4,8},{8,12},{12,16},{16,20},{20,24},{24,28},{1,5},{5,9},{9,... | collective-permute-start | bytes 345608 | tf_op jit(solution)/shard_map/ppermute | solution.py:54
  7.8 18.1 %collective-permute-start.1 = (bf16[32,2,900]{2,1,0:T(2,128)(2,1)}, bf16[32,2,900]{2,1,0:T(2,128)(2,1)}, u32[]{:S(2)}, u32[]{:S(2)}) collective-permute-start(bf16[32,2,900]{2,1,0:T(2,128)(2,1)} %get-tuple-element.12), channel_id=1, source_target_pairs={{4,0},{8,4},{12,8},{16,12},{20,16},{24,20},{28,24},{5,1},{9,5},{13... | collective-permute-start | bytes 345608 | tf_op jit(solution)/shard_map/ppermute | solution.py:51
  11.4 29.7 %copy-start.2 = (bf16[2,64,32,32]{1,3,2,0:T(8,128)(2,1)S(1)}, bf16[2,64,32,32]{1,3,2,0:T(8,128)(2,1)}, u32[]{:S(2)}) copy-start(bf16[2,64,32,32]{1,3,2,0:T(8,128)(2,1)} %param.13) | copy-start | bytes 786436
  15.3 46.4 %all-to-all-start = ((f32[32,1,4096]{2,1,0:T(1,128)}), f32[32,1,4096]{2,1,0:T(1,128)S(1)}, u32[]{:S(2)}, u32[]{:S(2)}) async-start(f32[32,1,4096]{2,1,0:T(1,128)} %all_to_all.19), calls=%async_computation | async-start | bytes 1048576 | tf_op jit(solution)/shard_map/all_to_all | solution.py:48
  23.0 43.3 %copy-start.6 = (bf16[2,32,1,128]{3,2,1,0:T(2,128)(2,1)}, bf16[2,32,1,128]{3,2,1,0:T(2,128)(2,1)S(1)}, u32[]{:S(2)}) copy-start(bf16[2,32,1,128]{3,2,1,0:T(2,128)(2,1)S(1)} %get-tuple-element.47) | copy-start | bytes 49156
  27.9 15.6 %collective-permute-start.3 = (bf16[2,1280]{0,1:T(8,128)(2,1)}, bf16[2,1280]{0,1:T(8,128)(2,1)}, u32[]{:S(2)}, u32[]{:S(2)}) collective-permute-start(bf16[2,1280]{0,1:T(8,128)(2,1)} %bitcast.6), channel_id=1, source_target_pairs={{0,1},{1,2},{2,3},{3,0},{4,5},{5,6},{6,7},{7,4},{8,9},{9,10},{10,1... | collective-permute-start | bytes 15368 | tf_op jit(solution)/shard_map/ppermute | solution.py:75
  28.2 15.4 %collective-permute-start.2 = (bf16[2,1280]{0,1:T(8,128)(2,1)}, bf16[2,1280]{0,1:T(8,128)(2,1)}, u32[]{:S(2)}, u32[]{:S(2)}) collective-permute-start(bf16[2,1280]{0,1:T(8,128)(2,1)} %bitcast.2), channel_id=1, source_target_pairs={{1,0},{2,1},{3,2},{0,3},{5,4},{6,5},{7,6},{4,7},{9,8},{10,9},{11,1... | collective-permute-start | bytes 15368 | tf_op jit(solution)/shard_map/ppermute | solution.py:68
  30.3 34.3 %copy-start.24 = (pred[2]{0:T(512)(128)(4,1)}, pred[2]{0:T(512)(128)(4,1)S(1)}, u32[]{:S(2)}) copy-start(pred[2]{0:T(512)(128)(4,1)S(1)} %get-tuple-element.95) | copy-start | bytes 10
  47.9 15.3 %copy-start.15 = (f32[2]{0:T(128)S(1)}, f32[2]{0:T(128)}, u32[]{:S(2)}) copy-start(f32[2]{0:T(128)} %get-tuple-element.68) | copy-start | bytes 28
  47.9 15.3 %copy-start.16 = (f32[2]{0:T(128)S(1)}, f32[2]{0:T(128)}, u32[]{:S(2)}) copy-start(f32[2]{0:T(128)} %get-tuple-element.72) | copy-start | bytes 28
  47.9 15.3 %copy-start.17 = (f32[2]{0:T(128)S(1)}, f32[2]{0:T(128)}, u32[]{:S(2)}) copy-start(f32[2]{0:T(128)} %get-tuple-element.73) | copy-start | bytes 28
  47.9 15.3 %copy-start.18 = (f32[2]{0:T(128)S(1)}, f32[2]{0:T(128)}, u32[]{:S(2)}) copy-start(f32[2]{0:T(128)} %get-tuple-element.103) | copy-start | bytes 28
  47.9 15.3 %copy-start.19 = (f32[2]{0:T(128)S(1)}, f32[2]{0:T(128)}, u32[]{:S(2)}) copy-start(f32[2]{0:T(128)} %get-tuple-element.104) | copy-start | bytes 28
  47.9 15.3 %copy-start.20 = (f32[2]{0:T(128)S(1)}, f32[2]{0:T(128)}, u32[]{:S(2)}) copy-start(f32[2]{0:T(128)} %get-tuple-element.108) | copy-start | bytes 28
  48.0 15.7 %copy-start.11 = (f32[2]{0:T(128)S(1)}, f32[2]{0:T(128)}, u32[]{:S(2)}) copy-start(f32[2]{0:T(128)} %get-tuple-element.75) | copy-start | bytes 28
  48.0 15.7 %copy-start.12 = (f32[2]{0:T(128)S(1)}, f32[2]{0:T(128)}, u32[]{:S(2)}) copy-start(f32[2]{0:T(128)} %get-tuple-element.101) | copy-start | bytes 28
  48.0 15.7 %copy-start.13 = (f32[2]{0:T(128)S(1)}, f32[2]{0:T(128)}, u32[]{:S(2)}) copy-start(f32[2]{0:T(128)} %get-tuple-element.102) | copy-start | bytes 28
  48.0 15.7 %copy-start.14 = (f32[2]{0:T(128)S(1)}, f32[2]{0:T(128)}, u32[]{:S(2)}) copy-start(f32[2]{0:T(128)} %get-tuple-element.109) | copy-start | bytes 28
  61.7 2.8 %copy-start.21 = (f32[2,32]{1,0:T(2,128)S(1)}, f32[2,32]{1,0:T(2,128)}, u32[]{:S(2)}) copy-start(f32[2,32]{1,0:T(2,128)} %get-tuple-element.91) | copy-start | bytes 772
  61.7 2.8 %copy-start.22 = (f32[2,128]{1,0:T(2,128)S(1)}, f32[2,128]{1,0:T(2,128)}, u32[]{:S(2)}) copy-start(f32[2,128]{1,0:T(2,128)} %fusion.58) | copy-start | bytes 3076
  63.2 7.4 %copy-start.1 = (bf16[2,64,32,32]{3,2,1,0:T(8,128)(2,1)S(1)}, bf16[2,64,32,32]{3,2,1,0:T(8,128)(2,1)}, u32[]{:S(2)}) copy-start(bf16[2,64,32,32]{3,2,1,0:T(8,128)(2,1)} %copy.83) | copy-start | bytes 786436
  64.5 0.6 copy-start.7
  68.1 19.6 %copy-start.3 = (bf16[64,1,900]{2,0,1:T(8,128)(2,1)S(1)}, bf16[64,1,900]{2,0,1:T(8,128)(2,1)}, u32[]{:S(2)}) copy-start(bf16[64,1,900]{2,0,1:T(8,128)(2,1)} %get-tuple-element.76) | copy-start | bytes 345604
  68.1 19.6 %copy-start.4 = (bf16[64,1,900]{2,0,1:T(8,128)(2,1)S(1)}, bf16[64,1,900]{2,0,1:T(8,128)(2,1)}, u32[]{:S(2)}) copy-start(bf16[64,1,900]{2,0,1:T(8,128)(2,1)} %get-tuple-element.77) | copy-start | bytes 345604
  81.6 16.4 %all-to-all-start.1 = ((bf16[32,2,2048]{2,1,0:T(2,128)(2,1)}), bf16[32,2,2048]{2,1,0:T(2,128)(2,1)S(1)}, u32[]{:S(2)}, u32[]{:S(2)}) async-start(bf16[32,2,2048]{2,1,0:T(2,128)(2,1)} %reshape.491), calls=%async_computation.1 | async-start | bytes 524288 | tf_op jit(solution)/shard_map/all_to_all | solution.py:160

commit v9 on v8

--- a/solution.py
+++ b/solution.py
@@ -44,7 +44,7 @@
     flat_field = field.reshape(channels * lat_rows, lon_cols)
     partial = lax.dot_general(
         forward_rows, flat_field, (((1,), (1,)), ((), ())), preferred_element_type=jnp.float32
-    ).reshape(n_dev, m_dev * 2 * channels * lat_rows)
+    ).reshape(n_dev, 8, m_dev * 2 * channels * lat_rows // 8)
     gathered_raw = lax.all_to_all(partial, BOTH, 0, 0, tiled=True)
     rim_cols = ((lon_cols + 4 + 127) // 128) * 128
     lat_n = lax.axis_size("lat")
@@ -156,7 +156,7 @@
     )
     outgoing = jnp.broadcast_to(
         by_group[:, None], (lat_count, lon_count, m_dev, 2, channels, lat_rows)
-    ).reshape(n_dev, m_dev * 2 * channels * lat_rows)
+    ).reshape(n_dev, 16, m_dev * 2 * channels * lat_rows // 16)
     full_rows = lax.all_to_all(outgoing, BOTH, 0, 0, tiled=True)
     spectral_rows = full_rows.reshape(orders_all * 2, channels * lat_rows)
     inverse_rows = wave_table(

time: 105 us -> 98.8 us (0.941)
  other arithmetic: 21.1 us -> 16.3 us
  local copies, waits for them, and re-layouts: 15.6 us -> 13.7 us
    all_to_all x2 -> x0, other arithmetic: 4.66 us -> none  [per_device(): full_rows = lax.all_to_all(outgoing, BOTH, 0, 0, tiled=True)]
    all_to_all x3 -> x0, local copies, waits for them, and re-layouts: 3.24 us -> none  [the longest x2 1.84 us: per_device(): full_rows = lax.all_to_all(outgoing, BOTH, 0, 0, tiled=True)]
    reshape x0 -> x2, local copies, waits for them, and re-layouts: none -> 2.31 us  [the longest x1 1.44 us: per_device(): outgoing = jnp.broadcast_to(by_group[:, None], (lat_count, lon_count, m_d...]
    unnamed x56 -> x29, local copies, waits for them, and re-layouts: 4.35 us -> 2.57 us
  transfers between devices with their start and end apart: 6 -> 6, of which waited for: 1 -> 1; matrix products, arithmetic and copies ran while one was open for 18% -> 19% of each run, Pallas kernels for 13% -> 14%
where the time goes in v9:
time: 98.8 us; the launch traced here: 97.8 us
  starting transfers between devices  21.4 us (22%)
  other arithmetic  16.3 us (16%)
  local copies, waits for them, and re-layouts  13.7 us (14%)
  Pallas kernels  13.7 us (14%)
  between operations  11.6 us (12%)
  matrix products  11 us (11%)
  waiting for transfers between devices  10.1 us (10%)
    pallas_call x1, Pallas kernels, depthwise_conv(): pl.pallas_call(body, grid_spec=pltpu.PrefetchScalarGridSpec(num_scalar_pr...  13.7 us
    all_to_all x1, waiting for transfers between devices, per_device(): full_rows = lax.all_to_all(outgoing, BOTH, 0, 0, tiled=True)  10.1 us
    all_to_all x1, starting transfers between devices, per_device(): gathered_raw = lax.all_to_all(partial, BOTH, 0, 0, tiled=True)  6.97 us
    all_to_all x1, starting transfers between devices, per_device(): full_rows = lax.all_to_all(outgoing, BOTH, 0, 0, tiled=True)  5.83 us
    ppermute x1, starting transfers between devices, per_device(): lax.ppermute(field[:, lat_rows - 2:], 'lat', [(i, i + 1) for i in range(l...  5.53 us
    concatenate x1, other arithmetic, per_device(): jnp.concatenate([rows_ext, east, jnp.zeros((channels, rim_rows, rim_cols...  4.16 us
    another operation x4, other arithmetic  3.68 us
    convert_element_type x1, other arithmetic, per_device(): (conv_out.astype(jnp.float32) + jax.nn.gelu(synthesis, approximate=True))...  2.63 us
  transfers between devices with their start and end apart: 6, of which 1 were waited for; matrix products, arithmetic and copies ran while one was open for 19% of the time, Pallas kernels for 14%

profile of v9, /device:TPU:0, one launch (start us, length us, event | category | flops | bytes accessed | tf_op | source)
XLA Modules:
  0.0 97.8 jit_solution(4254926427939173139)
XLA Ops:
  0.0 2.3 %fusion.65 = (bf16[32,2,900]{2,1,0:T(2,128)(2,1)}, bf16[32,2,900]{2,1,0:T(2,128)(2,1)}) fusion(bf16[32,32,900]{2,1,0:T(8,128)(2,1)} %param.7), kind=kLoop, calls=%fused_computation.190 | loop fusion | bytes 460800 | tf_op jit(solution)/shard_map/slice | solution.py:55
  2.3 5.5 %collective-permute-start = (bf16[32,2,900]{2,1,0:T(2,128)(2,1)}, bf16[32,2,900]{2,1,0:T(2,128)(2,1)}, u32[]{:S(2)}, u32[]{:S(2)}) collective-permute-start(bf16[32,2,900]{2,1,0:T(2,128)(2,1)} %get-tuple-element.11), channel_id=1, source_target_pairs={{0,4},{4,8},{8,12},{12,16},{16,20},{20,24},{24,28},{1,5},{5,9},{9,... | collective-permute-start | bytes 345608 | tf_op jit(solution)/shard_map/ppermute | solution.py:54
  7.8 1.3 %collective-permute-start.1 = (bf16[32,2,900]{2,1,0:T(2,128)(2,1)}, bf16[32,2,900]{2,1,0:T(2,128)(2,1)}, u32[]{:S(2)}, u32[]{:S(2)}) collective-permute-start(bf16[32,2,900]{2,1,0:T(2,128)(2,1)} %get-tuple-element.12), channel_id=1, source_target_pairs={{4,0},{8,4},{12,8},{16,12},{20,16},{24,20},{28,24},{5,1},{9,5},{13... | collective-permute-start | bytes 345608 | tf_op jit(solution)/shard_map/ppermute | solution.py:51
  9.1 1.8 %multiply_convert_fusion.1 = (bf16[64,1,900]{2,0,1:T(8,128)(2,1)}, bf16[64,1,900]{2,0,1:T(8,128)(2,1)}, bf16[64,1,900]{2,0,1:T(8,128)(2,1)S(1)}, bf16[64,1,900]{2,0,1:T(8,128)(2,1)S(1)}) fusion(f32[64]{0:T(128)S(1)} %get-tuple-element.97, s32[900]{0:T(1024)S(1)} %iota_add_fusion, f32[64]{0:T(128)S(1)} %get-tuple-element.98), kind=kLoop, calls=%fused_computation.56 | loop fusion | flops 979200 | bytes 464912 | tf_op jit(solution)/shard_map/convert
  11.0 0.3 copy.36
  11.3 0.2 convert_element_type.109
  11.5 2.5 %fusion.68 = f32[128,1024]{1,0:T(8,128)S(1)} fusion(bf16[128,900]{1,0:T(8,128)(2,1)S(1)} %convert_element_type.109, bf16[1024,900]{1,0:T(8,128)(2,1)} %bitcast.176), kind=kOutput, calls=%fused_computation.193 | convolution fusion | flops 235929600 | bytes 2597888 | tf_op jit(solution)/shard_map/dot_general | solution.py:45
  13.9 0.9 reshape.470
  14.8 7.0 %all-to-all-start = ((f32[32,8,512]{2,1,0:T(8,128)}), f32[32,8,512]{2,1,0:T(8,128)S(1)}, u32[]{:S(2)}, u32[]{:S(2)}) async-start(f32[32,8,512]{2,1,0:T(8,128)} %reshape.470), calls=%async_computation | async-start | bytes 1048576 | tf_op jit(solution)/shard_map/all_to_all | solution.py:48
  21.9 0.7 fusion.66
  22.5 0.1 fusion.52
  22.7 0.6 fusion.58
  23.3 0.7 compare_convert_fusion.2
  24.0 0.6 slice_bitcast_fusion.8
  24.6 0.7 fusion.67
  25.4 1.9 %pad_maximum_fusion.4 = (bf16[32,40,2]{2,1,0:T(8,128)(2,1)}, bf16[32,40,2]{2,1,0:T(8,128)(2,1)}) fusion(bf16[32,4,900]{2,1,0:T(4,128)(2,1)S(1)} %broadcast_in_dim.84, bf16[32,2,900]{2,1,0:T(2,128)(2,1)} %collective-permute-done.1, bf16[32,32,900]{2,1,0:T(8,128)(2,1)S(1)} %copy-done, bf16[32,2,900]{2,1,0:T(2,128)(2,1)} %collective-permute-done), kind=kLoop, calls=%fused_computation.43 | loop fusion | flops 40960 | bytes 2314240 | tf_op jit(solution)/shard_map/slice | solution.py:69
  27.4 0.3 collective-permute-start.3
  27.6 1.5 %collective-permute-start.2 = (bf16[2,1280]{0,1:T(8,128)(2,1)}, bf16[2,1280]{0,1:T(8,128)(2,1)}, u32[]{:S(2)}, u32[]{:S(2)}) collective-permute-start(bf16[2,1280]{0,1:T(8,128)(2,1)} %bitcast.2), channel_id=1, source_target_pairs={{1,0},{2,1},{3,2},{0,3},{5,4},{6,5},{7,6},{4,7},{9,8},{10,9},{11,1... | collective-permute-start | bytes 15368 | tf_op jit(solution)/shard_map/ppermute | solution.py:68
  29.1 0.6 fusion.59
  40.8 0.1 copy.37.offs_ref
  40.9 0.1 copy.38.w_ref
  41.0 2.3 %copy.41 = bf16[2,64,32,32]{3,2,1,0:T(8,128)(2,1)} copy(bf16[2,64,32,32]{1,3,2,0:T(8,128)(2,1)S(1)} %copy-done.2) | data formatting | bytes 524288 | tf_op args[6]
  43.3 0.1 pad.36.clone
  43.4 4.2 %pad_maximum_fusion.rim_ref = bf16[32,40,1024]{2,1,0:T(8,128)(2,1)S(1)} fusion(bf16[32,40,2]{2,1,0:T(8,128)(2,1)} %bitcast.8, bf16[32,40,2]{2,1,0:T(8,128)(2,1)} %bitcast.4, bf16[32,4,900]{2,1,0:T(4,128)(2,1)S(1)} %broadcast_in_dim.84, bf16[32,2,900]{2,1,0:T(2,128)(2,1)} %collective-permute-done.1, bf16[32,32,900]{2,1,0:T(8,128)(2,1)S(1)} %copy-done, ...), kind=kLoop, calls=%fused_computation.10 | loop fusion | flops 18350080 | bytes 4937728 | tf_op jit(solution)/shard_map/concatenate | solution.py:81
  47.6 13.7 %shard_map.73 = bf16[32,32,900]{2,1,0:T(8,128)(2,1)S(1)} custom-call(s32[9,2]{1,0:T(8,128)S(1)} %copy.37.offs_ref, bf16[32,40,1024]{2,1,0:T(8,128)(2,1)S(1)} %pad_maximum_fusion.rim_ref, f32[32,9]{1,0:T(8,128)S(1)} %copy.38.w_ref), custom_call_target="tpu_custom_call" | custom-call | flops 94371840 | bytes 4464640 | tf_op jit(solution)/shard_map/pallas_call | solution.py:214
  61.4 0.4 reshape.475
  61.7 0.3 reduce_sum.9
  62.0 0.2 reshape.476
  62.2 0.3 copy.39
  62.5 0.2 reshape.477
  62.7 0.3 multiply_subtract_fusion.1
  63.0 0.3 multiply_subtract_fusion
  63.4 0.3 multiply_subtract_fusion.2
  63.7 0.2 fusion.30
  63.9 0.1 rev.8
  64.0 1.0 fusion.12
  64.9 0.7 copy.43
  65.7 1.2 %convolution_bitcast_fusion.2 = f32[2,32,2,32]{3,2,0,1:T(2,128)S(1)} fusion(bf16[2,32,2,32]{3,2,0,1:T(2,128)(2,1)} %copy.43, bf16[2,32,2,32,32]{4,3,2,1,0:T(8,128)(2,1)} %bitcast.179), kind=kOutput, calls=%fused_computation.14 | convolution fusion | flops 262144 | bytes 311296 | tf_op jit(solution)/shard_map/mupc,ucd->mupd/dot_general | solution.py:136
  66.8 1.8 %convolution_bitcast_fusion.3 = f32[2,32,2,32]{3,2,0,1:T(2,128)} fusion(bf16[2,32,2,32]{3,2,0,1:T(2,128)(2,1)} %copy.43, bf16[2,32,2,32,32]{4,3,2,1,0:T(8,128)(2,1)} %bitcast.180), kind=kOutput, calls=%fused_computation.15 | convolution fusion | flops 262144 | bytes 311296 | tf_op jit(solution)/shard_map/mupc,ucd->mupd/dot_general | solution.py:133
  68.6 1.6 %fusion.11 = bf16[2,32,2,32]{1,3,2,0:T(8,128)(2,1)} fusion(f32[2,32]{1,0:T(2,128)} %get-tuple-element.92, pred[2]{0:T(512)(128)(4,1)} %get-tuple-element.96, bf16[2,32,1,128]{3,2,1,0:T(2,128)(2,1)} %get-tuple-element.48, bf16[2,2,32,128]{3,2,1,0:T(8,128)(2,1)} %copy-done.6, f32[2,128]{1,0:T(2,128)} %fusion.58, bf16[2,2,32,256]{3,2,1,0:T(8,128)(2,1)S(1)} %fusion.30), kind=kOutput, calls=%fused_computation.19 | convolution fusion | flops 1204224 | bytes 91394 | tf_op jit(solution)/shard_map/mui,mpci->mupc/dot_general | solution.py:127
  70.2 0.8 copy.49
  71.1 0.2 convolution_bitcast_fusion
  71.3 0.2 convolution_bitcast_fusion.1
  71.5 1.0 %fusion.38 = (bf16[2,32,1,32]{3,2,0,1:T(2,128)(2,1)S(1)}, bf16[2,32,1,32]{3,2,0,1:T(2,128)(2,1)S(1)}) fusion(f32[2,32,2,32]{3,2,0,1:T(2,128)S(1)} %convolution_bitcast_fusion.2, f32[2,32,2,32]{3,2,0,1:T(2,128)} %convolution_bitcast_fusion.3), kind=kLoop, calls=%fused_computation.118 | loop fusion | flops 8192 | bytes 40960 | tf_op jit(solution)/shard_map/convert.8
  72.5 0.1 pad_maximum_fusion.7
  72.6 1.0 fusion.41
  73.5 0.1 fusion.36
  73.6 0.1 pad_maximum_fusion.8
  73.7 1.0 subtract_multiply_fusion
  74.7 0.8 multiply_convert_fusion.4
  75.5 0.1 rev.9
  75.6 0.1 concatenate.18
  75.7 0.1 concatenate.17
  75.8 0.2 maximum_bitcast_fusion
  76.0 0.2 broadcast_in_dim.89
  76.3 1.4 %reshape.480 = bf16[32,16,256]{2,1,0:T(8,128)(2,1)} reshape(bf16[8,4,2,2,32,32]{5,4,3,2,1,0:T(8,128)(2,1)S(1)} %broadcast_in_dim.89) | data formatting | bytes 524288 | tf_op jit(solution)/shard_map/reshape | solution.py:159
  77.7 5.8 %all-to-all-start.1 = ((bf16[32,16,256]{2,1,0:T(8,128)(2,1)}), bf16[32,16,256]{2,1,0:T(8,128)(2,1)S(1)}, u32[]{:S(2)}, u32[]{:S(2)}) async-start(bf16[32,16,256]{2,1,0:T(8,128)(2,1)} %reshape.480), calls=%async_computation.1 | async-start | bytes 524288 | tf_op jit(solution)/shard_map/all_to_all | solution.py:160
  83.6 0.3 copy.55
  83.9 0.2 convert_element_type.124
  84.1 10.1 %all-to-all-done.1 = bf16[32,16,256]{2,1,0:T(8,128)(2,1)S(1)} async-done(((bf16[32,16,256]{2,1,0:T(8,128)(2,1)}), bf16[32,16,256]{2,1,0:T(8,128)(2,1)S(1)}, u32[]{:S(2)}, u32[]{:S(2)}) %all-to-all-start.1) | async-done | bytes 262176 | tf_op jit(solution)/shard_map/all_to_all | solution.py:160
  94.2 0.2 reshape.481
  94.3 0.2 copy.54
  94.5 0.7 fusion.15
  95.2 2.6 %fusion.8 = bf16[32,32,900]{2,1,0:T(8,128)(2,1)} fusion(f32[32,32,900]{2,1,0:T(8,128)S(1)} %fusion.15, bf16[32,32,900]{2,1,0:T(8,128)(2,1)S(1)} %shard_map.73), kind=kLoop, calls=%fused_computation.9 | loop fusion | flops 10137600 | bytes 7372800 | tf_op jit(solution)/shard_map/convert_element_type | solution.py:169
  (44 shorter events, 0.3 us)
Async XLA Ops:
  0.0 25.4 %copy-start = (bf16[32,32,900]{2,1,0:T(8,128)(2,1)S(1)}, bf16[32,32,900]{2,1,0:T(8,128)(2,1)}, u32[]{:S(2)}) copy-start(bf16[32,32,900]{2,1,0:T(8,128)(2,1)} %param.7) | copy-start | bytes 5529604
  0.0 21.8 %copy-start.7 = (s32[9,2]{0,1:T(2,128)S(1)}, s32[9,2]{0,1:T(2,128)}, u32[]{:S(2)}) copy-start(s32[9,2]{0,1:T(2,128)} %param.8) | copy-start | bytes 220
  0.0 21.8 %copy-start.8 = (f32[32,9]{0,1:T(8,128)S(1)}, f32[32,9]{0,1:T(8,128)}, u32[]{:S(2)}) copy-start(f32[32,9]{0,1:T(8,128)} %param.9) | copy-start | bytes 3460
  0.0 21.9 %copy-start.5 = (bf16[2,64,128]{2,1,0:T(8,128)(2,1)S(1)}, bf16[2,64,128]{2,1,0:T(8,128)(2,1)}, u32[]{:S(2)}) copy-start(bf16[2,64,128]{2,1,0:T(8,128)(2,1)} %param.10) | copy-start | bytes 98308
  0.0 22.7 %copy-start.9 = (s32[128]{0:T(128)S(1)}, s32[128]{0:T(128)}, u32[]{:S(2)}) copy-start(s32[128]{0:T(128)} %param.12) | copy-start | bytes 1540
  0.0 22.7 %copy-start.12 = (f32[128]{0:T(128)S(1)}, f32[128]{0:T(128)}, u32[]{:S(2)}) copy-start(f32[128]{0:T(128)} %param.11) | copy-start | bytes 1540
  2.3 23.0 %collective-permute-start = (bf16[32,2,900]{2,1,0:T(2,128)(2,1)}, bf16[32,2,900]{2,1,0:T(2,128)(2,1)}, u32[]{:S(2)}, u32[]{:S(2)}) collective-permute-start(bf16[32,2,900]{2,1,0:T(2,128)(2,1)} %get-tuple-element.11), channel_id=1, source_target_pairs={{0,4},{4,8},{8,12},{12,16},{16,20},{20,24},{24,28},{1,5},{5,9},{9,... | collective-permute-start | bytes 345608 | tf_op jit(solution)/shard_map/ppermute | solution.py:54
  7.8 17.5 %collective-permute-start.1 = (bf16[32,2,900]{2,1,0:T(2,128)(2,1)}, bf16[32,2,900]{2,1,0:T(2,128)(2,1)}, u32[]{:S(2)}, u32[]{:S(2)}) collective-permute-start(bf16[32,2,900]{2,1,0:T(2,128)(2,1)} %get-tuple-element.12), channel_id=1, source_target_pairs={{4,0},{8,4},{12,8},{16,12},{20,16},{24,20},{28,24},{5,1},{9,5},{13... | collective-permute-start | bytes 345608 | tf_op jit(solution)/shard_map/ppermute | solution.py:51
  11.4 29.5 %copy-start.2 = (bf16[2,64,32,32]{1,3,2,0:T(8,128)(2,1)S(1)}, bf16[2,64,32,32]{1,3,2,0:T(8,128)(2,1)}, u32[]{:S(2)}) copy-start(bf16[2,64,32,32]{1,3,2,0:T(8,128)(2,1)} %param.13) | copy-start | bytes 786436
  14.8 46.5 %all-to-all-start = ((f32[32,8,512]{2,1,0:T(8,128)}), f32[32,8,512]{2,1,0:T(8,128)S(1)}, u32[]{:S(2)}, u32[]{:S(2)}) async-start(f32[32,8,512]{2,1,0:T(8,128)} %reshape.470), calls=%async_computation | async-start | bytes 1048576 | tf_op jit(solution)/shard_map/all_to_all | solution.py:48
  27.4 16.1 %collective-permute-start.3 = (bf16[2,1280]{0,1:T(8,128)(2,1)}, bf16[2,1280]{0,1:T(8,128)(2,1)}, u32[]{:S(2)}, u32[]{:S(2)}) collective-permute-start(bf16[2,1280]{0,1:T(8,128)(2,1)} %bitcast.6), channel_id=1, source_target_pairs={{0,1},{1,2},{2,3},{3,0},{4,5},{5,6},{6,7},{7,4},{8,9},{9,10},{10,1... | collective-permute-start | bytes 15368 | tf_op jit(solution)/shard_map/ppermute | solution.py:75
  27.6 15.8 %collective-permute-start.2 = (bf16[2,1280]{0,1:T(8,128)(2,1)}, bf16[2,1280]{0,1:T(8,128)(2,1)}, u32[]{:S(2)}, u32[]{:S(2)}) collective-permute-start(bf16[2,1280]{0,1:T(8,128)(2,1)} %bitcast.2), channel_id=1, source_target_pairs={{1,0},{2,1},{3,2},{0,3},{5,4},{6,5},{7,6},{4,7},{9,8},{10,9},{11,1... | collective-permute-start | bytes 15368 | tf_op jit(solution)/shard_map/ppermute | solution.py:68
  47.6 15.1 %copy-start.10 = (f32[2]{0:T(128)S(1)}, f32[2]{0:T(128)}, u32[]{:S(2)}) copy-start(f32[2]{0:T(128)} %get-tuple-element.104) | copy-start | bytes 28
  47.6 15.1 %copy-start.11 = (f32[2]{0:T(128)S(1)}, f32[2]{0:T(128)}, u32[]{:S(2)}) copy-start(f32[2]{0:T(128)} %get-tuple-element.108) | copy-start | bytes 28
  62.7 8.4 %copy-start.1 = (bf16[2,64,32,32]{3,2,1,0:T(8,128)(2,1)S(1)}, bf16[2,64,32,32]{3,2,1,0:T(8,128)(2,1)}, u32[]{:S(2)}) copy-start(bf16[2,64,32,32]{3,2,1,0:T(8,128)(2,1)} %copy.41) | copy-start | bytes 786436
  63.8 19.7 %copy-start.3 = (bf16[64,1,900]{2,0,1:T(8,128)(2,1)S(1)}, bf16[64,1,900]{2,0,1:T(8,128)(2,1)}, u32[]{:S(2)}) copy-start(bf16[64,1,900]{2,0,1:T(8,128)(2,1)} %get-tuple-element.76) | copy-start | bytes 345604
  63.8 19.7 %copy-start.4 = (bf16[64,1,900]{2,0,1:T(8,128)(2,1)S(1)}, bf16[64,1,900]{2,0,1:T(8,128)(2,1)}, u32[]{:S(2)}) copy-start(bf16[64,1,900]{2,0,1:T(8,128)(2,1)} %get-tuple-element.77) | copy-start | bytes 345604
  64.0 1.7 %copy-start.6 = (bf16[2,2,32,128]{3,2,1,0:T(8,128)(2,1)}, bf16[2,2,32,128]{3,2,1,0:T(8,128)(2,1)S(1)}, u32[]{:S(2)}) copy-start(bf16[2,2,32,128]{3,2,1,0:T(8,128)(2,1)S(1)} %rev.8) | copy-start | bytes 98308
  77.7 16.4 %all-to-all-start.1 = ((bf16[32,16,256]{2,1,0:T(8,128)(2,1)}), bf16[32,16,256]{2,1,0:T(8,128)(2,1)S(1)}, u32[]{:S(2)}, u32[]{:S(2)}) async-start(bf16[32,16,256]{2,1,0:T(8,128)(2,1)} %reshape.480), calls=%async_computation.1 | async-start | bytes 524288 | tf_op jit(solution)/shard_map/all_to_all | solution.py:160

commit v10 on v9

--- a/solution.py
+++ b/solution.py
@@ -44,8 +44,8 @@
     flat_field = field.reshape(channels * lat_rows, lon_cols)
     partial = lax.dot_general(
         forward_rows, flat_field, (((1,), (1,)), ((), ())), preferred_element_type=jnp.float32
-    ).reshape(n_dev, 8, m_dev * 2 * channels * lat_rows // 8)
-    gathered_raw = lax.all_to_all(partial, BOTH, 0, 0, tiled=True)
+    ).reshape(n_dev, 16, m_dev * 2 * channels * lat_rows // 16)
+    gathered_raw = lax.all_to_all(partial.astype(jnp.bfloat16), BOTH, 0, 0, tiled=True)
     rim_cols = ((lon_cols + 4 + 127) // 128) * 128
     lat_n = lax.axis_size("lat")
     south = lax.ppermute(
@@ -89,7 +89,11 @@
     )
     conv_out = depthwise_conv(offsets, conv_weight, rim, lat_rows, lon_cols)
     gathered, conv_out = lax.optimization_barrier((gathered_raw, conv_out))
-    summed = gathered.reshape(lat_count, lon_count, m_dev * 2 * channels * lat_rows).sum(axis=1)
+    summed = (
+        gathered.astype(jnp.float32)
+        .reshape(lat_count, lon_count, m_dev * 2 * channels * lat_rows)
+        .sum(axis=1)
+    )
     summed = summed.reshape(lat_count, m_dev, 2, channels, lat_rows)
     raw_spec = jnp.transpose(summed, (1, 2, 3, 0, 4)).reshape(m_dev, 2, channels, total_lat)
 

time: 98.8 us -> 96.8 us (0.980)
    unnamed x29 -> x43, local copies, waits for them, and re-layouts: 2.57 us -> 2.6 us
where the time goes in v10:
time: 96.8 us; the launch traced here: 95.9 us
  starting transfers between devices  20.7 us (21%)
  other arithmetic  15.5 us (16%)
  Pallas kernels  13.7 us (14%)
  local copies, waits for them, and re-layouts  13.6 us (14%)
  between operations  11.5 us (12%)
  matrix products  10.7 us (11%)
  waiting for transfers between devices  10.1 us (10%)
    pallas_call x1, Pallas kernels, depthwise_conv(): pl.pallas_call(body, grid_spec=pltpu.PrefetchScalarGridSpec(num_scalar_pr...  13.7 us
    all_to_all x1, waiting for transfers between devices, per_device(): full_rows = lax.all_to_all(outgoing, BOTH, 0, 0, tiled=True)  10.1 us
    all_to_all x1, starting transfers between devices, per_device(): lax.all_to_all(partial.astype(jnp.bfloat16), BOTH, 0, 0, tiled=True)  6.98 us
    all_to_all x1, starting transfers between devices, per_device(): full_rows = lax.all_to_all(outgoing, BOTH, 0, 0, tiled=True)  5.83 us
    ppermute x1, starting transfers between devices, per_device(): lax.ppermute(field[:, lat_rows - 2:], 'lat', [(i, i + 1) for i in range(l...  4.88 us
    concatenate x1, other arithmetic, per_device(): jnp.concatenate([rows_ext, east, jnp.zeros((channels, rim_rows, rim_cols...  4.12 us
    another operation x4, other arithmetic  3.66 us
    convert_element_type x1, other arithmetic, per_device(): (conv_out.astype(jnp.float32) + jax.nn.gelu(synthesis, approximate=True))...  2.63 us
  transfers between devices with their start and end apart: 6, of which 1 were waited for; matrix products, arithmetic and copies ran while one was open for 19% of the time, Pallas kernels for 14%

profile of v10, /device:TPU:0, one launch (start us, length us, event | category | flops | bytes accessed | tf_op | source)
XLA Modules:
  0.0 95.9 jit_solution(10757519857583779377)
XLA Ops:
  0.0 2.3 %fusion.65 = (bf16[32,2,900]{2,1,0:T(2,128)(2,1)}, bf16[32,2,900]{2,1,0:T(2,128)(2,1)}) fusion(bf16[32,32,900]{2,1,0:T(8,128)(2,1)} %param.7), kind=kLoop, calls=%fused_computation.191 | loop fusion | bytes 460800 | tf_op jit(solution)/shard_map/slice | solution.py:55
  2.3 4.9 %collective-permute-start = (bf16[32,2,900]{2,1,0:T(2,128)(2,1)}, bf16[32,2,900]{2,1,0:T(2,128)(2,1)S(1)}, u32[]{:S(2)}, u32[]{:S(2)}) collective-permute-start(bf16[32,2,900]{2,1,0:T(2,128)(2,1)} %get-tuple-element.11), channel_id=1, source_target_pairs={{0,4},{4,8},{8,12},{12,16},{16,20},{20,24},{24,28},{1,5},{5,9},{9,... | collective-permute-start | bytes 345608 | tf_op jit(solution)/shard_map/ppermute | solution.py:54
  7.2 1.3 %collective-permute-start.1 = (bf16[32,2,900]{2,1,0:T(2,128)(2,1)}, bf16[32,2,900]{2,1,0:T(2,128)(2,1)S(1)}, u32[]{:S(2)}, u32[]{:S(2)}) collective-permute-start(bf16[32,2,900]{2,1,0:T(2,128)(2,1)} %get-tuple-element.12), channel_id=1, source_target_pairs={{4,0},{8,4},{12,8},{16,12},{20,16},{24,20},{28,24},{5,1},{9,5},{13... | collective-permute-start | bytes 345608 | tf_op jit(solution)/shard_map/ppermute | solution.py:51
  8.5 1.8 %multiply_convert_fusion.1 = (bf16[64,1,900]{2,0,1:T(8,128)(2,1)}, bf16[64,1,900]{2,0,1:T(8,128)(2,1)}, bf16[64,1,900]{2,0,1:T(8,128)(2,1)S(1)}, bf16[64,1,900]{2,0,1:T(8,128)(2,1)S(1)}) fusion(f32[64]{0:T(128)S(1)} %get-tuple-element.97, s32[900]{0:T(1024)S(1)} %iota_add_fusion, f32[64]{0:T(128)S(1)} %get-tuple-element.98), kind=kLoop, calls=%fused_computation.57 | loop fusion | flops 979200 | bytes 464912 | tf_op jit(solution)/shard_map/convert.1
  10.4 0.3 copy.36
  10.6 0.2 convert_element_type.116
  10.8 2.4 %convolution_convert_fusion = bf16[128,1024]{1,0:T(8,128)(2,1)S(1)} fusion(bf16[128,900]{1,0:T(8,128)(2,1)S(1)} %convert_element_type.116, bf16[1024,900]{1,0:T(8,128)(2,1)} %bitcast.176), kind=kOutput, calls=%fused_computation.11 | convolution fusion | flops 236060672 | bytes 2335744 | tf_op jit(solution)/shard_map/dot_general | solution.py:45
  13.2 0.9 convert_element_type.118
  14.1 7.0 %all-to-all-start = ((bf16[32,16,256]{2,1,0:T(8,128)(2,1)}), bf16[32,16,256]{2,1,0:T(8,128)(2,1)S(1)}, u32[]{:S(2)}, u32[]{:S(2)}) async-start(bf16[32,16,256]{2,1,0:T(8,128)(2,1)} %convert_element_type.118), calls=%async_computation | async-start | bytes 524288 | tf_op jit(solution)/shard_map/all_to_all | solution.py:48
  21.2 0.6 fusion.66
  21.8 0.1 fusion.52
  22.0 0.6 fusion.58
  22.6 0.7 compare_convert_fusion.2
  23.3 0.6 slice_bitcast_fusion.8
  24.0 0.7 fusion.67
  24.7 1.2 %pad_maximum_fusion.4 = (bf16[32,40,2]{2,1,0:T(8,128)(2,1)}, bf16[32,40,2]{2,1,0:T(8,128)(2,1)}) fusion(bf16[32,4,900]{2,1,0:T(4,128)(2,1)S(1)} %broadcast_in_dim.84, bf16[32,2,900]{2,1,0:T(2,128)(2,1)S(1)} %collective-permute-done.1, bf16[32,32,900]{2,1,0:T(8,128)(2,1)S(1)} %copy-done, bf16[32,2,900]{2,1,0:T(2,128)(2,1)S(1)} %collective-permute-done), kind=kLoop, calls=%fused_computation.44 | loop fusion | flops 40960 | bytes 2314240 | tf_op jit(solution)/shard_map/slice | solution.py:69
  25.9 0.3 collective-permute-start.3
  26.2 1.5 %collective-permute-start.2 = (bf16[2,1280]{0,1:T(8,128)(2,1)}, bf16[2,1280]{0,1:T(8,128)(2,1)}, u32[]{:S(2)}, u32[]{:S(2)}) collective-permute-start(bf16[2,1280]{0,1:T(8,128)(2,1)} %bitcast.2), channel_id=1, source_target_pairs={{1,0},{2,1},{3,2},{0,3},{5,4},{6,5},{7,6},{4,7},{9,8},{10,9},{11,1... | collective-permute-start | bytes 15368 | tf_op jit(solution)/shard_map/ppermute | solution.py:68
  27.7 0.6 fusion.59
  39.1 0.1 copy.37.offs_ref
  39.2 0.1 copy.38.w_ref
  39.3 2.3 %copy.41 = bf16[2,64,32,32]{3,2,1,0:T(8,128)(2,1)} copy(bf16[2,64,32,32]{1,3,2,0:T(8,128)(2,1)S(1)} %copy-done.2) | data formatting | bytes 524288 | tf_op args[6]
  41.6 0.1 pad.36.clone
  41.7 4.1 %pad_maximum_fusion.rim_ref = bf16[32,40,1024]{2,1,0:T(8,128)(2,1)S(1)} fusion(bf16[32,40,2]{2,1,0:T(8,128)(2,1)} %bitcast.8, bf16[32,40,2]{2,1,0:T(8,128)(2,1)} %bitcast.4, bf16[32,4,900]{2,1,0:T(4,128)(2,1)S(1)} %broadcast_in_dim.84, bf16[32,2,900]{2,1,0:T(2,128)(2,1)S(1)} %collective-permute-done.1, bf16[32,32,900]{2,1,0:T(8,128)(2,1)S(1)} %copy-done, ...), kind=kLoop, calls=%fused_computation.10 | loop fusion | flops 18350080 | bytes 4937728 | tf_op jit(solution)/shard_map/concatenate | solution.py:81
  46.0 13.7 %shard_map.73 = bf16[32,32,900]{2,1,0:T(8,128)(2,1)S(1)} custom-call(s32[9,2]{1,0:T(8,128)S(1)} %copy.37.offs_ref, bf16[32,40,1024]{2,1,0:T(8,128)(2,1)S(1)} %pad_maximum_fusion.rim_ref, f32[32,9]{1,0:T(8,128)S(1)} %copy.38.w_ref), custom_call_target="tpu_custom_call" | custom-call | flops 94371840 | bytes 4464640 | tf_op jit(solution)/shard_map/pallas_call | solution.py:218
  59.7 0.2 reshape.485
  60.0 0.3 reduce_sum.9
  60.3 0.2 reshape.478
  60.5 0.3 copy.39
  60.8 0.2 reshape.479
  61.0 0.3 multiply_subtract_fusion.1
  61.4 0.3 multiply_subtract_fusion
  61.7 0.3 multiply_subtract_fusion.2
  62.0 0.2 fusion.30
  62.2 0.7 rev.8
  62.9 1.6 %fusion.12 = bf16[2,32,2,32]{1,3,2,0:T(8,128)(2,1)} fusion(f32[2,32]{1,0:T(2,128)} %get-tuple-element.91, pred[2]{0:T(512)(128)(4,1)} %get-tuple-element.95, bf16[2,32,1,128]{3,2,1,0:T(2,128)(2,1)S(1)} %get-tuple-element.47, bf16[2,2,32,128]{3,2,1,0:T(8,128)(2,1)} %rev.8, f32[2,128]{1,0:T(2,128)} %fusion.58, bf16[2,2,32,256]{3,2,1,0:T(8,128)(2,1)S(1)} %fusion.30), kind=kOutput, calls=%fused_computation.21 | convolution fusion | flops 1204224 | bytes 107778 | tf_op jit(solution)/shard_map/mui,mpci->mupc/dot_general | solution.py:131
  64.4 0.8 copy.43
  65.3 1.8 %convolution_bitcast_fusion.2 = f32[2,32,2,32]{3,2,0,1:T(2,128)} fusion(bf16[2,32,2,32]{3,2,0,1:T(2,128)(2,1)S(1)} %copy.43, bf16[2,32,2,32,32]{4,3,2,1,0:T(8,128)(2,1)} %bitcast.179), kind=kOutput, calls=%fused_computation.15 | convolution fusion | flops 262144 | bytes 286720 | tf_op jit(solution)/shard_map/mupc,ucd->mupd/dot_general | solution.py:140
  67.1 1.8 %convolution_bitcast_fusion.3 = f32[2,32,2,32]{3,2,0,1:T(2,128)} fusion(bf16[2,32,2,32]{3,2,0,1:T(2,128)(2,1)S(1)} %copy.43, bf16[2,32,2,32,32]{4,3,2,1,0:T(8,128)(2,1)} %bitcast.180), kind=kOutput, calls=%fused_computation.16 | convolution fusion | flops 262144 | bytes 286720 | tf_op jit(solution)/shard_map/mupc,ucd->mupd/dot_general | solution.py:137
  68.8 1.0 %fusion.11 = bf16[2,32,2,32]{1,3,2,0:T(8,128)(2,1)S(1)} fusion(f32[2,32]{1,0:T(2,128)} %get-tuple-element.92, pred[2]{0:T(512)(128)(4,1)} %get-tuple-element.96, bf16[2,32,1,128]{3,2,1,0:T(2,128)(2,1)} %get-tuple-element.48, bf16[2,2,32,128]{3,2,1,0:T(8,128)(2,1)} %rev.8, f32[2,128]{1,0:T(2,128)} %fusion.58, bf16[2,2,32,256]{3,2,1,0:T(8,128)(2,1)S(1)} %fusion.30), kind=kOutput, calls=%fused_computation.20 | convolution fusion | flops 1204224 | bytes 91394 | tf_op jit(solution)/shard_map/mui,mpci->mupc/dot_general | solution.py:131
  69.8 0.1 copy.49
  69.9 0.2 convolution_bitcast_fusion
  70.1 0.2 convolution_bitcast_fusion.1
  70.3 1.0 %fusion.38 = (bf16[2,32,1,32]{3,2,0,1:T(2,128)(2,1)S(1)}, bf16[2,32,1,32]{3,2,0,1:T(2,128)(2,1)S(1)}) fusion(f32[2,32,2,32]{3,2,0,1:T(2,128)} %convolution_bitcast_fusion.2, f32[2,32,2,32]{3,2,0,1:T(2,128)} %convolution_bitcast_fusion.3), kind=kLoop, calls=%fused_computation.119 | loop fusion | flops 8192 | bytes 40960 | tf_op jit(solution)/shard_map/convert.9
  71.3 0.1 pad_maximum_fusion.7
  71.4 0.2 fusion.41
  71.6 0.1 fusion.36
  71.7 0.1 pad_maximum_fusion.8
  71.8 1.0 %subtract_multiply_fusion = (bf16[2,2,32,128]{3,2,1,0:T(8,128)(2,1)S(1)}, f32[2,2,32,128]{3,2,1,0:T(8,128)S(1)}) fusion(f32[2,128]{1,0:T(2,128)S(1)} %compare_convert_fusion, pred[2]{0:T(512)(128)(4,1)} %get-tuple-element.96, f32[2,2,32,128]{3,2,1,0:T(8,128)S(1)} %fusion.41, pred[2]{0:T(512)(128)(4,1)} %get-tuple-element.95, ...), kind=kOutput, calls=%fused_computation.90 | convolution fusion | flops 1196032 | bytes 189444 | tf_op jit(solution)/shard_map/mui,mupc->mpci/dot_general | solution.py:147
  72.8 0.7 multiply_convert_fusion.4
  73.5 0.1 rev.9
  73.6 0.1 concatenate.18
  73.7 0.1 concatenate.17
  73.9 0.2 maximum_bitcast_fusion
  74.1 0.2 broadcast_in_dim.89
  74.3 1.4 %reshape.482 = bf16[32,16,256]{2,1,0:T(8,128)(2,1)} reshape(bf16[8,4,2,2,32,32]{5,4,3,2,1,0:T(8,128)(2,1)S(1)} %broadcast_in_dim.89) | data formatting | bytes 524288 | tf_op jit(solution)/shard_map/reshape | solution.py:163
  75.8 5.8 %all-to-all-start.1 = ((bf16[32,16,256]{2,1,0:T(8,128)(2,1)}), bf16[32,16,256]{2,1,0:T(8,128)(2,1)S(1)}, u32[]{:S(2)}, u32[]{:S(2)}) async-start(bf16[32,16,256]{2,1,0:T(8,128)(2,1)} %reshape.482), calls=%async_computation.1 | async-start | bytes 524288 | tf_op jit(solution)/shard_map/all_to_all | solution.py:164
  81.7 0.3 copy.55
  82.0 0.2 convert_element_type.133
  82.1 10.1 %all-to-all-done.1 = bf16[32,16,256]{2,1,0:T(8,128)(2,1)S(1)} async-done(((bf16[32,16,256]{2,1,0:T(8,128)(2,1)}), bf16[32,16,256]{2,1,0:T(8,128)(2,1)S(1)}, u32[]{:S(2)}, u32[]{:S(2)}) %all-to-all-start.1) | async-done | bytes 262176 | tf_op jit(solution)/shard_map/all_to_all | solution.py:164
  92.2 0.2 reshape.483
  92.4 0.2 copy.54
  92.6 0.7 fusion.15
  93.3 2.6 %fusion.8 = bf16[32,32,900]{2,1,0:T(8,128)(2,1)} fusion(f32[32,32,900]{2,1,0:T(8,128)S(1)} %fusion.15, bf16[32,32,900]{2,1,0:T(8,128)(2,1)S(1)} %shard_map.73), kind=kLoop, calls=%fused_computation.9 | loop fusion | flops 10137600 | bytes 7372800 | tf_op jit(solution)/shard_map/convert_element_type | solution.py:173
  (58 shorter events, 0.4 us)
Async XLA Ops:
  0.0 24.7 %copy-start = (bf16[32,32,900]{2,1,0:T(8,128)(2,1)S(1)}, bf16[32,32,900]{2,1,0:T(8,128)(2,1)}, u32[]{:S(2)}) copy-start(bf16[32,32,900]{2,1,0:T(8,128)(2,1)} %param.7) | copy-start | bytes 5529604
  0.0 21.1 %copy-start.6 = (s32[9,2]{0,1:T(2,128)S(1)}, s32[9,2]{0,1:T(2,128)}, u32[]{:S(2)}) copy-start(s32[9,2]{0,1:T(2,128)} %param.8) | copy-start | bytes 220
  0.0 21.1 %copy-start.7 = (f32[32,9]{0,1:T(8,128)S(1)}, f32[32,9]{0,1:T(8,128)}, u32[]{:S(2)}) copy-start(f32[32,9]{0,1:T(8,128)} %param.9) | copy-start | bytes 3460
  0.0 21.2 %copy-start.5 = (bf16[2,64,128]{2,1,0:T(8,128)(2,1)S(1)}, bf16[2,64,128]{2,1,0:T(8,128)(2,1)}, u32[]{:S(2)}) copy-start(bf16[2,64,128]{2,1,0:T(8,128)(2,1)} %param.10) | copy-start | bytes 98308
  0.0 22.0 %copy-start.8 = (s32[128]{0:T(128)S(1)}, s32[128]{0:T(128)}, u32[]{:S(2)}) copy-start(s32[128]{0:T(128)} %param.12) | copy-start | bytes 1540
  0.0 22.0 %copy-start.19 = (f32[128]{0:T(128)S(1)}, f32[128]{0:T(128)}, u32[]{:S(2)}) copy-start(f32[128]{0:T(128)} %param.11) | copy-start | bytes 1540
  2.3 22.4 %collective-permute-start = (bf16[32,2,900]{2,1,0:T(2,128)(2,1)}, bf16[32,2,900]{2,1,0:T(2,128)(2,1)S(1)}, u32[]{:S(2)}, u32[]{:S(2)}) collective-permute-start(bf16[32,2,900]{2,1,0:T(2,128)(2,1)} %get-tuple-element.11), channel_id=1, source_target_pairs={{0,4},{4,8},{8,12},{12,16},{16,20},{20,24},{24,28},{1,5},{5,9},{9,... | collective-permute-start | bytes 345608 | tf_op jit(solution)/shard_map/ppermute | solution.py:54
  7.2 17.5 %collective-permute-start.1 = (bf16[32,2,900]{2,1,0:T(2,128)(2,1)}, bf16[32,2,900]{2,1,0:T(2,128)(2,1)S(1)}, u32[]{:S(2)}, u32[]{:S(2)}) collective-permute-start(bf16[32,2,900]{2,1,0:T(2,128)(2,1)} %get-tuple-element.12), channel_id=1, source_target_pairs={{4,0},{8,4},{12,8},{16,12},{20,16},{24,20},{28,24},{5,1},{9,5},{13... | collective-permute-start | bytes 345608 | tf_op jit(solution)/shard_map/ppermute | solution.py:51
  10.3 29.0 %copy-start.2 = (bf16[2,64,32,32]{1,3,2,0:T(8,128)(2,1)S(1)}, bf16[2,64,32,32]{1,3,2,0:T(8,128)(2,1)}, u32[]{:S(2)}) copy-start(bf16[2,64,32,32]{1,3,2,0:T(8,128)(2,1)} %param.13) | copy-start | bytes 786436
  14.1 45.6 %all-to-all-start = ((bf16[32,16,256]{2,1,0:T(8,128)(2,1)}), bf16[32,16,256]{2,1,0:T(8,128)(2,1)S(1)}, u32[]{:S(2)}, u32[]{:S(2)}) async-start(bf16[32,16,256]{2,1,0:T(8,128)(2,1)} %convert_element_type.118), calls=%async_computation | async-start | bytes 524288 | tf_op jit(solution)/shard_map/all_to_all | solution.py:48
  25.9 15.8 %collective-permute-start.3 = (bf16[2,1280]{0,1:T(8,128)(2,1)}, bf16[2,1280]{0,1:T(8,128)(2,1)}, u32[]{:S(2)}, u32[]{:S(2)}) collective-permute-start(bf16[2,1280]{0,1:T(8,128)(2,1)} %bitcast.6), channel_id=1, source_target_pairs={{0,1},{1,2},{2,3},{3,0},{4,5},{5,6},{6,7},{7,4},{8,9},{9,10},{10,1... | collective-permute-start | bytes 15368 | tf_op jit(solution)/shard_map/ppermute | solution.py:75
  26.2 15.5 %collective-permute-start.2 = (bf16[2,1280]{0,1:T(8,128)(2,1)}, bf16[2,1280]{0,1:T(8,128)(2,1)}, u32[]{:S(2)}, u32[]{:S(2)}) collective-permute-start(bf16[2,1280]{0,1:T(8,128)(2,1)} %bitcast.2), channel_id=1, source_target_pairs={{1,0},{2,1},{3,2},{0,3},{5,4},{6,5},{7,6},{4,7},{9,8},{10,9},{11,1... | collective-permute-start | bytes 15368 | tf_op jit(solution)/shard_map/ppermute | solution.py:68
  45.9 15.1 %copy-start.13 = (f32[2]{0:T(128)S(1)}, f32[2]{0:T(128)}, u32[]{:S(2)}) copy-start(f32[2]{0:T(128)} %get-tuple-element.68) | copy-start | bytes 28
  45.9 15.1 %copy-start.14 = (f32[2]{0:T(128)S(1)}, f32[2]{0:T(128)}, u32[]{:S(2)}) copy-start(f32[2]{0:T(128)} %get-tuple-element.72) | copy-start | bytes 28
  45.9 15.1 %copy-start.15 = (f32[2]{0:T(128)S(1)}, f32[2]{0:T(128)}, u32[]{:S(2)}) copy-start(f32[2]{0:T(128)} %get-tuple-element.73) | copy-start | bytes 28
  45.9 15.1 %copy-start.16 = (f32[2]{0:T(128)S(1)}, f32[2]{0:T(128)}, u32[]{:S(2)}) copy-start(f32[2]{0:T(128)} %get-tuple-element.103) | copy-start | bytes 28
  45.9 15.1 %copy-start.17 = (f32[2]{0:T(128)S(1)}, f32[2]{0:T(128)}, u32[]{:S(2)}) copy-start(f32[2]{0:T(128)} %get-tuple-element.104) | copy-start | bytes 28
  45.9 15.1 %copy-start.18 = (f32[2]{0:T(128)S(1)}, f32[2]{0:T(128)}, u32[]{:S(2)}) copy-start(f32[2]{0:T(128)} %get-tuple-element.108) | copy-start | bytes 28
  45.9 15.4 %copy-start.9 = (f32[2]{0:T(128)S(1)}, f32[2]{0:T(128)}, u32[]{:S(2)}) copy-start(f32[2]{0:T(128)} %get-tuple-element.75) | copy-start | bytes 28
  45.9 15.4 %copy-start.10 = (f32[2]{0:T(128)S(1)}, f32[2]{0:T(128)}, u32[]{:S(2)}) copy-start(f32[2]{0:T(128)} %get-tuple-element.101) | copy-start | bytes 28
  45.9 15.4 %copy-start.11 = (f32[2]{0:T(128)S(1)}, f32[2]{0:T(128)}, u32[]{:S(2)}) copy-start(f32[2]{0:T(128)} %get-tuple-element.102) | copy-start | bytes 28
  46.0 15.4 %copy-start.12 = (f32[2]{0:T(128)S(1)}, f32[2]{0:T(128)}, u32[]{:S(2)}) copy-start(f32[2]{0:T(128)} %get-tuple-element.109) | copy-start | bytes 28
  61.0 8.9 %copy-start.1 = (bf16[2,64,32,32]{3,2,1,0:T(8,128)(2,1)S(1)}, bf16[2,64,32,32]{3,2,1,0:T(8,128)(2,1)}, u32[]{:S(2)}) copy-start(bf16[2,64,32,32]{3,2,1,0:T(8,128)(2,1)} %copy.41) | copy-start | bytes 786436
  62.2 19.5 %copy-start.3 = (bf16[64,1,900]{2,0,1:T(8,128)(2,1)S(1)}, bf16[64,1,900]{2,0,1:T(8,128)(2,1)}, u32[]{:S(2)}) copy-start(bf16[64,1,900]{2,0,1:T(8,128)(2,1)} %get-tuple-element.76) | copy-start | bytes 345604
  62.2 19.5 %copy-start.4 = (bf16[64,1,900]{2,0,1:T(8,128)(2,1)S(1)}, bf16[64,1,900]{2,0,1:T(8,128)(2,1)}, u32[]{:S(2)}) copy-start(bf16[64,1,900]{2,0,1:T(8,128)(2,1)} %get-tuple-element.77) | copy-start | bytes 345604
  75.8 16.4 %all-to-all-start.1 = ((bf16[32,16,256]{2,1,0:T(8,128)(2,1)}), bf16[32,16,256]{2,1,0:T(8,128)(2,1)S(1)}, u32[]{:S(2)}, u32[]{:S(2)}) async-start(bf16[32,16,256]{2,1,0:T(8,128)(2,1)} %reshape.482), calls=%async_computation.1 | async-start | bytes 524288 | tf_op jit(solution)/shard_map/all_to_all | solution.py:164

commit v11 on v10

--- a/solution.py
+++ b/solution.py
@@ -103,15 +103,16 @@
     )
     cos_all = jnp.cos(turns)
     sin_all = jnp.sin(turns)
-    spec_acc = jnp.zeros(raw_spec.shape, jnp.float32)
-    for tap_index in range(KTAPS):
-        window = lax.dynamic_slice_in_dim(rim, 2 + offsets[tap_index, 0], total_lat, axis=3)
-        cos_t = cos_all[tap_index][:, None, None]
-        sin_t = sin_all[tap_index][:, None, None]
-        real_part = cos_t * window[:, 0] - sin_t * window[:, 1]
-        imag_part = sin_t * window[:, 0] + cos_t * window[:, 1]
-        tap_w = conv_weight[:, tap_index][None, None, :, None]
-        spec_acc = spec_acc + tap_w * jnp.stack([real_part, imag_part], axis=1)
+    real_acc = jnp.zeros((m_dev, channels, total_lat), jnp.float32)
+    imag_acc = jnp.zeros((m_dev, channels, total_lat), jnp.float32)
+    for shift in range(-2, 3):
+        chosen = (offsets[:, 0] == shift).astype(jnp.float32)[:, None] * conv_weight.T
+        coef_re = jnp.einsum("kc,ko->oc", chosen, cos_all)[:, :, None]
+        coef_im = jnp.einsum("kc,ko->oc", chosen, sin_all)[:, :, None]
+        window = rim[..., 2 + shift : 2 + shift + total_lat]
+        real_acc = real_acc + coef_re * window[:, 0] - coef_im * window[:, 1]
+        imag_acc = imag_acc + coef_im * window[:, 0] + coef_re * window[:, 1]
+    spec_acc = jnp.stack([real_acc, imag_acc], axis=1)
     spectrum = spec_acc.astype(jnp.bfloat16)
 
     north_part = spectrum[..., :half_rows].astype(jnp.float32)

time: 96.8 us -> 88.7 us (0.916)
  between operations: 11.5 us -> 0.5 us
  waiting for transfers between devices: 10.1 us -> 15.4 us
  matrix products: 10.7 us -> 15.1 us
  other arithmetic: 15.5 us -> 11.6 us
  local copies, waits for them, and re-layouts: 13.6 us -> 10.3 us
    dot_general x0 -> x10, matrix products: none -> 6.53 us  [the longest x5 3.28 us: per_device(): coef_re = jnp.einsum('kc,ko->oc', chosen, cos_all)[:, :, None]]
    ppermute x1, waiting for transfers between devices: 0.01 us -> 3.82 us  [per_device(): lax.ppermute(lane_dense(rows_ext[:, :, lon_cols - 2:]), 'lon', [(i, (i +...]
    dot_general x2, matrix products: 2.52 us -> 0.39 us  [per_device(): jnp.einsum('mui,mpci->mupc', degree_plane, operand, preferred_element_typ...]
    another operation x4 -> x6, other arithmetic: 3.66 us -> 1.86 us
    ppermute x1, waiting for transfers between devices: 0.01 us -> 1.45 us  [per_device(): lax.ppermute(lane_dense(rows_ext[:, :, :2]), 'lon', [((i + 1) % lon_count...]
    unnamed x43 -> x29, local copies, waits for them, and re-layouts: 2.6 us -> 2.57 us
  transfers between devices with their start and end apart: 6 -> 6, of which waited for: 1 -> 3; matrix products, arithmetic and copies ran while one was open for 19% -> 24% of each run, Pallas kernels for 14% -> 16%
where the time goes in v11:
time: 88.7 us; the launch traced here: 88.2 us
  starting transfers between devices  21.5 us (24%)
  waiting for transfers between devices  15.4 us (17%)
  matrix products  15.1 us (17%)
  Pallas kernels  13.7 us (15%)
  other arithmetic  11.6 us (13%)
  local copies, waits for them, and re-layouts  10.3 us (12%)
    pallas_call x1, Pallas kernels, depthwise_conv(): pl.pallas_call(body, grid_spec=pltpu.PrefetchScalarGridSpec(num_scalar_pr...  13.7 us
    all_to_all x1, waiting for transfers between devices, per_device(): full_rows = lax.all_to_all(outgoing, BOTH, 0, 0, tiled=True)  10.1 us
    all_to_all x1, starting transfers between devices, per_device(): lax.all_to_all(partial.astype(jnp.bfloat16), BOTH, 0, 0, tiled=True)  6.97 us
    all_to_all x1, starting transfers between devices, per_device(): full_rows = lax.all_to_all(outgoing, BOTH, 0, 0, tiled=True)  5.96 us
    ppermute x1, starting transfers between devices, per_device(): lax.ppermute(field[:, lat_rows - 2:], 'lat', [(i, i + 1) for i in range(l...  5.53 us
    concatenate x1, other arithmetic, per_device(): jnp.concatenate([rows_ext, east, jnp.zeros((channels, rim_rows, rim_cols...  4.15 us
    ppermute x1, waiting for transfers between devices, per_device(): lax.ppermute(lane_dense(rows_ext[:, :, lon_cols - 2:]), 'lon', [(i, (i +...  3.82 us
    dot_general x5, matrix products, per_device(): coef_re = jnp.einsum('kc,ko->oc', chosen, cos_all)[:, :, None]  3.28 us
  transfers between devices with their start and end apart: 6, of which 3 were waited for; matrix products, arithmetic and copies ran while one was open for 24% of the time, Pallas kernels for 16%

profile of v11, /device:TPU:0, one launch (start us, length us, event | category | flops | bytes accessed | tf_op | source)
XLA Modules:
  0.0 88.2 jit_solution(4385676201089875380)
XLA Ops:
  0.0 2.3 %fusion.174 = (bf16[32,2,900]{2,1,0:T(2,128)(2,1)}, bf16[32,2,900]{2,1,0:T(2,128)(2,1)}) fusion(bf16[32,32,900]{2,1,0:T(8,128)(2,1)} %param.7), kind=kLoop, calls=%fused_computation.224 | loop fusion | bytes 460800 | tf_op jit(solution)/shard_map/slice | solution.py:55
  2.3 5.5 %collective-permute-start = (bf16[32,2,900]{2,1,0:T(2,128)(2,1)}, bf16[32,2,900]{2,1,0:T(2,128)(2,1)}, u32[]{:S(2)}, u32[]{:S(2)}) collective-permute-start(bf16[32,2,900]{2,1,0:T(2,128)(2,1)} %get-tuple-element.11), channel_id=1, source_target_pairs={{0,4},{4,8},{8,12},{12,16},{16,20},{20,24},{24,28},{1,5},{5,9},{9,... | collective-permute-start | bytes 345608 | tf_op jit(solution)/shard_map/ppermute | solution.py:54
  7.8 1.3 %collective-permute-start.1 = (bf16[32,2,900]{2,1,0:T(2,128)(2,1)}, bf16[32,2,900]{2,1,0:T(2,128)(2,1)}, u32[]{:S(2)}, u32[]{:S(2)}) collective-permute-start(bf16[32,2,900]{2,1,0:T(2,128)(2,1)} %get-tuple-element.12), channel_id=1, source_target_pairs={{4,0},{8,4},{12,8},{16,12},{20,16},{24,20},{28,24},{5,1},{9,5},{13... | collective-permute-start | bytes 345608 | tf_op jit(solution)/shard_map/ppermute | solution.py:51
  9.1 1.2 %multiply_convert_fusion.1 = (bf16[64,1,900]{2,0,1:T(8,128)(2,1)S(1)}, bf16[64,1,900]{2,0,1:T(8,128)(2,1)S(1)}, bf16[64,1,900]{2,0,1:T(8,128)(2,1)S(1)}, bf16[64,1,900]{2,0,1:T(8,128)(2,1)S(1)}) fusion(f32[64]{0:T(128)S(1)} %fusion.138, s32[900]{0:T(1024)S(1)} %iota_add_fusion, f32[64]{0:T(128)S(1)} %fusion.141), kind=kLoop, calls=%fused_computation.47 | loop fusion | flops 979200 | bytes 464912 | tf_op jit(solution)/shard_map/convert.6
  10.4 0.3 copy.36
  10.7 0.2 convert_element_type.124
  10.8 2.5 %convolution_convert_fusion = bf16[128,1024]{1,0:T(8,128)(2,1)S(1)} fusion(bf16[128,900]{1,0:T(8,128)(2,1)S(1)} %convert_element_type.124, bf16[1024,900]{1,0:T(8,128)(2,1)} %bitcast.114), kind=kOutput, calls=%fused_computation.11 | convolution fusion | flops 236060672 | bytes 2335744 | tf_op jit(solution)/shard_map/dot_general | solution.py:45
  13.3 0.9 convert_element_type.126
  14.2 7.0 %all-to-all-start = ((bf16[32,16,256]{2,1,0:T(8,128)(2,1)}), bf16[32,16,256]{2,1,0:T(8,128)(2,1)S(1)}, u32[]{:S(2)}, u32[]{:S(2)}) async-start(bf16[32,16,256]{2,1,0:T(8,128)(2,1)} %convert_element_type.126), calls=%async_computation | async-start | bytes 524288 | tf_op jit(solution)/shard_map/all_to_all | solution.py:48
  21.2 0.3 fusion.63
  21.6 0.3 fusion.53
  21.9 0.3 fusion.61
  22.2 0.3 fusion.51
  22.5 0.9 %fusion.59 = f32[2,32]{1,0:T(2,128)} fusion(f32[32,9]{0,1:T(8,128)S(1)} %copy-done.3, f32[9]{0:T(128)S(1)} %get-tuple-element.27, s32[9]{0:T(128)S(1)} %slice_bitcast_fusion.8, s32[2]{0:T(128)S(1)} %iota_add_fusion.1), kind=kOutput, calls=%fused_computation.107 | convolution fusion | flops 1602 | bytes 1488 | tf_op jit(solution)/shard_map/kc,ko->oc/dot_general | solution.py:111
  23.4 0.9 %fusion.49 = f32[2,32]{1,0:T(2,128)} fusion(f32[32,9]{0,1:T(8,128)S(1)} %copy-done.3, f32[9]{0:T(128)S(1)} %get-tuple-element.27, s32[9]{0:T(128)S(1)} %slice_bitcast_fusion.8, s32[2]{0:T(128)S(1)} %iota_add_fusion.1), kind=kOutput, calls=%fused_computation.102 | convolution fusion | flops 1602 | bytes 1488 | tf_op jit(solution)/shard_map/kc,ko->oc/dot_general | solution.py:110
  24.3 0.9 %fusion.57 = f32[2,32]{1,0:T(2,128)} fusion(f32[32,9]{0,1:T(8,128)S(1)} %copy-done.3, f32[9]{0:T(128)S(1)} %get-tuple-element.28, s32[9]{0:T(128)S(1)} %slice_bitcast_fusion.8, s32[2]{0:T(128)S(1)} %iota_add_fusion.1), kind=kOutput, calls=%fused_computation.106 | convolution fusion | flops 1602 | bytes 1488 | tf_op jit(solution)/shard_map/kc,ko->oc/dot_general | solution.py:111
  25.2 0.9 fusion.47
  26.1 0.8 fusion.55
  26.9 0.9 %fusion.45 = f32[2,32]{1,0:T(2,128)} fusion(f32[32,9]{0,1:T(8,128)S(1)} %copy-done.3, f32[9]{0:T(128)S(1)} %get-tuple-element.29, s32[9]{0:T(128)S(1)} %slice_bitcast_fusion.8, s32[2]{0:T(128)S(1)} %iota_add_fusion.1), kind=kOutput, calls=%fused_computation.100 | convolution fusion | flops 1602 | bytes 1488 | tf_op jit(solution)/shard_map/kc,ko->oc/dot_general | solution.py:110
  28.2 2.0 %pad_maximum_fusion.4 = (bf16[32,40,2]{2,1,0:T(8,128)(2,1)}, bf16[32,40,2]{2,1,0:T(8,128)(2,1)}) fusion(bf16[32,4,900]{2,1,0:T(4,128)(2,1)S(1)} %broadcast_in_dim.53, bf16[32,2,900]{2,1,0:T(2,128)(2,1)} %collective-permute-done.1, bf16[32,32,900]{2,1,0:T(8,128)(2,1)S(1)} %copy-done, bf16[32,2,900]{2,1,0:T(2,128)(2,1)} %collective-permute-done), kind=kLoop, calls=%fused_computation.34 | loop fusion | flops 40960 | bytes 2314240 | tf_op jit(solution)/shard_map/slice | solution.py:69
  30.1 0.3 collective-permute-start.3
  30.4 1.5 %collective-permute-start.2 = (bf16[2,1280]{0,1:T(8,128)(2,1)}, bf16[2,1280]{0,1:T(8,128)(2,1)}, u32[]{:S(2)}, u32[]{:S(2)}) collective-permute-start(bf16[2,1280]{0,1:T(8,128)(2,1)} %bitcast.2), channel_id=1, source_target_pairs={{1,0},{2,1},{3,2},{0,3},{5,4},{6,5},{7,6},{4,7},{9,8},{10,9},{11,1... | collective-permute-start | bytes 15368 | tf_op jit(solution)/shard_map/ppermute | solution.py:68
  31.9 0.1 copy.37.offs_ref
  32.0 0.1 copy.38.w_ref
  32.1 2.3 %copy.41 = bf16[2,64,32,32]{3,2,1,0:T(8,128)(2,1)} copy(bf16[2,64,32,32]{1,3,2,0:T(8,128)(2,1)S(1)} %copy-done.1) | data formatting | bytes 524288 | tf_op args[6]
  34.4 0.1 pad.20.clone
  34.5 3.8 %collective-permute-done.3 = bf16[2,1280]{0,1:T(8,128)(2,1)} collective-permute-done((bf16[2,1280]{0,1:T(8,128)(2,1)}, bf16[2,1280]{0,1:T(8,128)(2,1)}, u32[]{:S(2)}, u32[]{:S(2)}) %collective-permute-start.3) | collective-permute-done | bytes 5152 | tf_op jit(solution)/shard_map/ppermute | solution.py:75
  38.3 1.4 %collective-permute-done.2 = bf16[2,1280]{0,1:T(8,128)(2,1)} collective-permute-done((bf16[2,1280]{0,1:T(8,128)(2,1)}, bf16[2,1280]{0,1:T(8,128)(2,1)}, u32[]{:S(2)}, u32[]{:S(2)}) %collective-permute-start.2) | collective-permute-done | bytes 5152 | tf_op jit(solution)/shard_map/ppermute | solution.py:68
  39.8 4.2 %pad_maximum_fusion.rim_ref = bf16[32,40,1024]{2,1,0:T(8,128)(2,1)S(1)} fusion(bf16[32,40,2]{2,1,0:T(8,128)(2,1)} %bitcast.8, bf16[32,40,2]{2,1,0:T(8,128)(2,1)} %bitcast.4, bf16[32,4,900]{2,1,0:T(4,128)(2,1)S(1)} %broadcast_in_dim.53, bf16[32,2,900]{2,1,0:T(2,128)(2,1)} %collective-permute-done.1, bf16[32,32,900]{2,1,0:T(8,128)(2,1)S(1)} %copy-done, ...), kind=kLoop, calls=%fused_computation.10 | loop fusion | flops 18350080 | bytes 4937728 | tf_op jit(solution)/shard_map/concatenate | solution.py:81
  44.0 13.7 %shard_map.73 = bf16[32,32,900]{2,1,0:T(8,128)(2,1)S(1)} custom-call(s32[9,2]{1,0:T(8,128)S(1)} %copy.37.offs_ref, bf16[32,40,1024]{2,1,0:T(8,128)(2,1)S(1)} %pad_maximum_fusion.rim_ref, f32[32,9]{1,0:T(8,128)S(1)} %copy.38.w_ref), custom_call_target="tpu_custom_call" | custom-call | flops 94371840 | bytes 4464640 | tf_op jit(solution)/shard_map/pallas_call | solution.py:219
  57.7 0.2 reshape.433
  58.0 0.3 reduce_sum.9
  58.3 0.2 reshape.425
  58.5 0.3 copy.39
  58.8 0.2 reshape.426
  59.0 0.4 subtract_convert_fusion
  59.5 0.1 rev.8
  59.6 0.2 fusion.12
  59.8 0.1 copy.43
  59.9 1.2 %convolution_bitcast_fusion.2 = f32[2,32,2,32]{3,2,0,1:T(2,128)S(1)} fusion(bf16[2,32,2,32]{3,2,0,1:T(2,128)(2,1)S(1)} %copy.43, bf16[2,32,2,32,32]{4,3,2,1,0:T(8,128)(2,1)} %bitcast.117), kind=kOutput, calls=%fused_computation.15 | convolution fusion | flops 262144 | bytes 286720 | tf_op jit(solution)/shard_map/mupc,ucd->mupd/dot_general | solution.py:141
  61.1 1.2 %convolution_bitcast_fusion.3 = f32[2,32,2,32]{3,2,0,1:T(2,128)S(1)} fusion(bf16[2,32,2,32]{3,2,0,1:T(2,128)(2,1)S(1)} %copy.43, bf16[2,32,2,32,32]{4,3,2,1,0:T(8,128)(2,1)} %bitcast.118), kind=kOutput, calls=%fused_computation.16 | convolution fusion | flops 262144 | bytes 286720 | tf_op jit(solution)/shard_map/mupc,ucd->mupd/dot_general | solution.py:138
  62.2 0.2 fusion.11
  62.4 0.1 copy.49
  62.5 1.2 %convolution_bitcast_fusion = f32[2,32,2,32]{3,2,0,1:T(2,128)S(1)} fusion(bf16[2,32,2,32]{3,2,0,1:T(2,128)(2,1)S(1)} %copy.49, bf16[2,32,2,32,32]{4,3,2,1,0:T(8,128)(2,1)} %bitcast.119), kind=kOutput, calls=%fused_computation.12 | convolution fusion | flops 262144 | bytes 286720 | tf_op jit(solution)/shard_map/mupc,ucd->mupd/dot_general | solution.py:141
  63.7 1.2 %convolution_bitcast_fusion.1 = f32[2,32,2,32]{3,2,0,1:T(2,128)S(1)} fusion(bf16[2,32,2,32]{3,2,0,1:T(2,128)(2,1)S(1)} %copy.49, bf16[2,32,2,32,32]{4,3,2,1,0:T(8,128)(2,1)} %bitcast.120), kind=kOutput, calls=%fused_computation.13 | convolution fusion | flops 262144 | bytes 286720 | tf_op jit(solution)/shard_map/mupc,ucd->mupd/dot_general | solution.py:138
  64.9 0.1 pad_maximum_fusion.8
  65.0 0.2 fusion.33
  65.3 0.1 pad_maximum_fusion.9
  65.4 0.2 subtract_multiply_fusion
  65.6 0.1 multiply_convert_fusion.4
  65.7 0.1 rev.9
  65.8 0.1 concatenate.18
  65.9 0.1 concatenate.17
  66.0 0.2 maximum_bitcast_fusion
  66.3 0.2 broadcast_in_dim.58
  66.5 1.4 %reshape.429 = bf16[32,16,256]{2,1,0:T(8,128)(2,1)} reshape(bf16[8,4,2,2,32,32]{5,4,3,2,1,0:T(8,128)(2,1)S(1)} %broadcast_in_dim.58) | data formatting | bytes 524288 | tf_op jit(solution)/shard_map/reshape | solution.py:164
  68.0 6.0 %all-to-all-start.1 = ((bf16[32,16,256]{2,1,0:T(8,128)(2,1)}), bf16[32,16,256]{2,1,0:T(8,128)(2,1)S(1)}, u32[]{:S(2)}, u32[]{:S(2)}) async-start(bf16[32,16,256]{2,1,0:T(8,128)(2,1)} %reshape.429), calls=%async_computation.1 | async-start | bytes 524288 | tf_op jit(solution)/shard_map/all_to_all | solution.py:165
  73.9 0.3 copy.55
  74.2 0.2 convert_element_type.140
  74.4 10.1 %all-to-all-done.1 = bf16[32,16,256]{2,1,0:T(8,128)(2,1)S(1)} async-done(((bf16[32,16,256]{2,1,0:T(8,128)(2,1)}), bf16[32,16,256]{2,1,0:T(8,128)(2,1)S(1)}, u32[]{:S(2)}, u32[]{:S(2)}) %all-to-all-start.1) | async-done | bytes 262176 | tf_op jit(solution)/shard_map/all_to_all | solution.py:165
  84.5 0.2 reshape.430
  84.7 0.2 copy.54
  84.9 0.7 fusion.15
  85.6 2.6 %fusion.8 = bf16[32,32,900]{2,1,0:T(8,128)(2,1)} fusion(f32[32,32,900]{2,1,0:T(8,128)S(1)} %fusion.15, bf16[32,32,900]{2,1,0:T(8,128)(2,1)S(1)} %shard_map.73), kind=kLoop, calls=%fused_computation.9 | loop fusion | flops 10137600 | bytes 7372800 | tf_op jit(solution)/shard_map/convert_element_type | solution.py:174
  (48 shorter events, 0.7 us)
Async XLA Ops:
  0.0 28.2 %copy-start = (bf16[32,32,900]{2,1,0:T(8,128)(2,1)S(1)}, bf16[32,32,900]{2,1,0:T(8,128)(2,1)}, u32[]{:S(2)}) copy-start(bf16[32,32,900]{2,1,0:T(8,128)(2,1)} %param.7) | copy-start | bytes 5529604
  0.0 21.2 %copy-start.4 = (s32[9,2]{0,1:T(2,128)S(1)}, s32[9,2]{0,1:T(2,128)}, u32[]{:S(2)}) copy-start(s32[9,2]{0,1:T(2,128)} %param.8) | copy-start | bytes 220
  0.0 21.2 %copy-start.3 = (f32[32,9]{0,1:T(8,128)S(1)}, f32[32,9]{0,1:T(8,128)}, u32[]{:S(2)}) copy-start(f32[32,9]{0,1:T(8,128)} %param.9) | copy-start | bytes 3460
  0.0 27.8 %copy-start.2 = (bf16[2,64,128]{2,1,0:T(8,128)(2,1)S(1)}, bf16[2,64,128]{2,1,0:T(8,128)(2,1)}, u32[]{:S(2)}) copy-start(bf16[2,64,128]{2,1,0:T(8,128)(2,1)} %param.10) | copy-start | bytes 98308
  0.0 27.8 %copy-start.5 = (s32[128]{0:T(128)S(1)}, s32[128]{0:T(128)}, u32[]{:S(2)}) copy-start(s32[128]{0:T(128)} %param.12) | copy-start | bytes 1540
  0.0 27.8 %copy-start.12 = (f32[128]{0:T(128)S(1)}, f32[128]{0:T(128)}, u32[]{:S(2)}) copy-start(f32[128]{0:T(128)} %param.11) | copy-start | bytes 1540
  2.3 25.8 %collective-permute-start = (bf16[32,2,900]{2,1,0:T(2,128)(2,1)}, bf16[32,2,900]{2,1,0:T(2,128)(2,1)}, u32[]{:S(2)}, u32[]{:S(2)}) collective-permute-start(bf16[32,2,900]{2,1,0:T(2,128)(2,1)} %get-tuple-element.11), channel_id=1, source_target_pairs={{0,4},{4,8},{8,12},{12,16},{16,20},{20,24},{24,28},{1,5},{5,9},{9,... | collective-permute-start | bytes 345608 | tf_op jit(solution)/shard_map/ppermute | solution.py:54
  7.8 20.3 %collective-permute-start.1 = (bf16[32,2,900]{2,1,0:T(2,128)(2,1)}, bf16[32,2,900]{2,1,0:T(2,128)(2,1)}, u32[]{:S(2)}, u32[]{:S(2)}) collective-permute-start(bf16[32,2,900]{2,1,0:T(2,128)(2,1)} %get-tuple-element.12), channel_id=1, source_target_pairs={{4,0},{8,4},{12,8},{16,12},{20,16},{24,20},{28,24},{5,1},{9,5},{13... | collective-permute-start | bytes 345608 | tf_op jit(solution)/shard_map/ppermute | solution.py:51
  10.8 21.3 %copy-start.1 = (bf16[2,64,32,32]{1,3,2,0:T(8,128)(2,1)S(1)}, bf16[2,64,32,32]{1,3,2,0:T(8,128)(2,1)}, u32[]{:S(2)}) copy-start(bf16[2,64,32,32]{1,3,2,0:T(8,128)(2,1)} %param.13) | copy-start | bytes 786436
  14.2 43.5 %all-to-all-start = ((bf16[32,16,256]{2,1,0:T(8,128)(2,1)}), bf16[32,16,256]{2,1,0:T(8,128)(2,1)S(1)}, u32[]{:S(2)}, u32[]{:S(2)}) async-start(bf16[32,16,256]{2,1,0:T(8,128)(2,1)} %convert_element_type.126), calls=%async_computation | async-start | bytes 524288 | tf_op jit(solution)/shard_map/all_to_all | solution.py:48
  30.1 8.2 %collective-permute-start.3 = (bf16[2,1280]{0,1:T(8,128)(2,1)}, bf16[2,1280]{0,1:T(8,128)(2,1)}, u32[]{:S(2)}, u32[]{:S(2)}) collective-permute-start(bf16[2,1280]{0,1:T(8,128)(2,1)} %bitcast.6), channel_id=1, source_target_pairs={{0,1},{1,2},{2,3},{3,0},{4,5},{5,6},{6,7},{7,4},{8,9},{9,10},{10,1... | collective-permute-start | bytes 15368 | tf_op jit(solution)/shard_map/ppermute | solution.py:75
  30.4 9.4 %collective-permute-start.2 = (bf16[2,1280]{0,1:T(8,128)(2,1)}, bf16[2,1280]{0,1:T(8,128)(2,1)}, u32[]{:S(2)}, u32[]{:S(2)}) collective-permute-start(bf16[2,1280]{0,1:T(8,128)(2,1)} %bitcast.2), channel_id=1, source_target_pairs={{1,0},{2,1},{3,2},{0,3},{5,4},{6,5},{7,6},{4,7},{9,8},{10,9},{11,1... | collective-permute-start | bytes 15368 | tf_op jit(solution)/shard_map/ppermute | solution.py:68
  43.9 15.1 %copy-start.6 = (f32[2,32]{1,0:T(2,128)S(1)}, f32[2,32]{1,0:T(2,128)}, u32[]{:S(2)}) copy-start(f32[2,32]{1,0:T(2,128)} %fusion.59) | copy-start | bytes 772
  43.9 15.1 %copy-start.7 = (f32[2,32]{1,0:T(2,128)S(1)}, f32[2,32]{1,0:T(2,128)}, u32[]{:S(2)}) copy-start(f32[2,32]{1,0:T(2,128)} %fusion.49) | copy-start | bytes 772
  44.0 15.1 %copy-start.8 = (f32[2,32]{1,0:T(2,128)S(1)}, f32[2,32]{1,0:T(2,128)}, u32[]{:S(2)}) copy-start(f32[2,32]{1,0:T(2,128)} %fusion.57) | copy-start | bytes 772
  44.0 15.1 %copy-start.9 = (f32[2,32]{1,0:T(2,128)S(1)}, f32[2,32]{1,0:T(2,128)}, u32[]{:S(2)}) copy-start(f32[2,32]{1,0:T(2,128)} %fusion.47) | copy-start | bytes 772
  44.0 15.1 %copy-start.10 = (f32[2,32]{1,0:T(2,128)S(1)}, f32[2,32]{1,0:T(2,128)}, u32[]{:S(2)}) copy-start(f32[2,32]{1,0:T(2,128)} %fusion.55) | copy-start | bytes 772
  44.0 15.1 %copy-start.11 = (f32[2,32]{1,0:T(2,128)S(1)}, f32[2,32]{1,0:T(2,128)}, u32[]{:S(2)}) copy-start(f32[2,32]{1,0:T(2,128)} %fusion.45) | copy-start | bytes 772
  68.0 16.6 %all-to-all-start.1 = ((bf16[32,16,256]{2,1,0:T(8,128)(2,1)}), bf16[32,16,256]{2,1,0:T(8,128)(2,1)S(1)}, u32[]{:S(2)}, u32[]{:S(2)}) async-start(bf16[32,16,256]{2,1,0:T(8,128)(2,1)} %reshape.429), calls=%async_computation.1 | async-start | bytes 524288 | tf_op jit(solution)/shard_map/all_to_all | solution.py:165

commit v12 on v11

--- a/solution.py
+++ b/solution.py
@@ -88,7 +88,7 @@
         axis=2,
     )
     conv_out = depthwise_conv(offsets, conv_weight, rim, lat_rows, lon_cols)
-    gathered, conv_out = lax.optimization_barrier((gathered_raw, conv_out))
+    gathered = gathered_raw
     summed = (
         gathered.astype(jnp.float32)
         .reshape(lat_count, lon_count, m_dev * 2 * channels * lat_rows)
@@ -163,6 +163,7 @@
         by_group[:, None], (lat_count, lon_count, m_dev, 2, channels, lat_rows)
     ).reshape(n_dev, 16, m_dev * 2 * channels * lat_rows // 16)
     full_rows = lax.all_to_all(outgoing, BOTH, 0, 0, tiled=True)
+    full_rows, conv_out = lax.optimization_barrier((full_rows, conv_out))
     spectral_rows = full_rows.reshape(orders_all * 2, channels * lat_rows)
     inverse_rows = wave_table(
         lax.iota(jnp.int32, orders_all), lon_points, total_lon, True

time: 88.7 us -> 79.8 us (0.90)
  waiting for transfers between devices: 15.4 us -> 0.02 us
  matrix products: 15.1 us -> 18.5 us
  other arithmetic: 11.6 us -> 14 us
    all_to_all x1, waiting for transfers between devices: 10.1 us -> 0.01 us  [per_device(): full_rows = lax.all_to_all(outgoing, BOTH, 0, 0, tiled=True)]
    ppermute x1, waiting for transfers between devices: 3.82 us -> 0.01 us  [per_device(): lax.ppermute(lane_dense(rows_ext[:, :, lon_cols - 2:]), 'lon', [(i, (i +...]
    ppermute x1, waiting for transfers between devices: 1.45 us -> 0.01 us  [per_device(): lax.ppermute(lane_dense(rows_ext[:, :, :2]), 'lon', [((i + 1) % lon_count...]
    dot_general x2, matrix products: 0.39 us -> 1.77 us  [per_device(): jnp.einsum('mui,mpci->mupc', degree_plane, operand, preferred_element_typ...]
    mul x1, other arithmetic: 0.07 us -> 1.32 us  [per_device(): weight_q = quad_weight[None, :] * kept_mask * (1.0 / math.sqrt(half_rows))]
    unnamed x29 -> x33, local copies, waits for them, and re-layouts: 2.57 us -> 2.58 us
  transfers between devices with their start and end apart: 6 -> 6, of which waited for: 3 -> 0; matrix products, arithmetic and copies ran while one was open for 24% -> 47% of each run, Pallas kernels for 16% -> 17%
where the time goes in v12:
time: 79.8 us; the launch traced here: 79.3 us
  starting transfers between devices  21.5 us (27%)
  matrix products  18.5 us (23%)
  other arithmetic  14 us (18%)
  Pallas kernels  13.7 us (17%)
  local copies, waits for them, and re-layouts  11 us (14%)
    pallas_call x1, Pallas kernels, depthwise_conv(): pl.pallas_call(body, grid_spec=pltpu.PrefetchScalarGridSpec(num_scalar_pr...  13.7 us
    all_to_all x1, starting transfers between devices, per_device(): lax.all_to_all(partial.astype(jnp.bfloat16), BOTH, 0, 0, tiled=True)  6.94 us
    all_to_all x1, starting transfers between devices, per_device(): full_rows = lax.all_to_all(outgoing, BOTH, 0, 0, tiled=True)  6.01 us
    ppermute x1, starting transfers between devices, per_device(): lax.ppermute(field[:, lat_rows - 2:], 'lat', [(i, i + 1) for i in range(l...  5.55 us
    concatenate x1, other arithmetic, per_device(): jnp.concatenate([rows_ext, east, jnp.zeros((channels, rim_rows, rim_cols...  4.16 us
    dot_general x5, matrix products, per_device(): coef_im = jnp.einsum('kc,ko->oc', chosen, sin_all)[:, :, None]  3.91 us
    dot_general x5, matrix products, per_device(): coef_re = jnp.einsum('kc,ko->oc', chosen, cos_all)[:, :, None]  3.89 us
    convert_element_type x1, other arithmetic, per_device(): (conv_out.astype(jnp.float32) + jax.nn.gelu(synthesis, approximate=True))...  2.63 us
  transfers between devices with their start and end apart: 6, of which 0 were waited for; matrix products, arithmetic and copies ran while one was open for 47% of the time, Pallas kernels for 17%

profile of v12, /device:TPU:0, one launch (start us, length us, event | category | flops | bytes accessed | tf_op | source)
XLA Modules:
  0.0 79.3 jit_solution(49992759740887396)
XLA Ops:
  0.0 2.1 %fusion.174 = (bf16[32,2,900]{2,1,0:T(2,128)(2,1)}, bf16[32,2,900]{2,1,0:T(2,128)(2,1)}) fusion(bf16[32,32,900]{2,1,0:T(8,128)(2,1)} %param.7), kind=kLoop, calls=%fused_computation.224 | loop fusion | bytes 460800 | tf_op jit(solution)/shard_map/slice | solution.py:55
  2.2 5.5 %collective-permute-start = (bf16[32,2,900]{2,1,0:T(2,128)(2,1)}, bf16[32,2,900]{2,1,0:T(2,128)(2,1)}, u32[]{:S(2)}, u32[]{:S(2)}) collective-permute-start(bf16[32,2,900]{2,1,0:T(2,128)(2,1)} %get-tuple-element.11), channel_id=1, source_target_pairs={{0,4},{4,8},{8,12},{12,16},{16,20},{20,24},{24,28},{1,5},{5,9},{9,... | collective-permute-start | bytes 345608 | tf_op jit(solution)/shard_map/ppermute | solution.py:54
  7.7 1.3 %collective-permute-start.1 = (bf16[32,2,900]{2,1,0:T(2,128)(2,1)}, bf16[32,2,900]{2,1,0:T(2,128)(2,1)}, u32[]{:S(2)}, u32[]{:S(2)}) collective-permute-start(bf16[32,2,900]{2,1,0:T(2,128)(2,1)} %get-tuple-element.12), channel_id=1, source_target_pairs={{4,0},{8,4},{12,8},{16,12},{20,16},{24,20},{28,24},{5,1},{9,5},{13... | collective-permute-start | bytes 345608 | tf_op jit(solution)/shard_map/ppermute | solution.py:51
  9.0 1.2 %multiply_convert_fusion.1 = (bf16[64,1,900]{2,0,1:T(8,128)(2,1)S(1)}, bf16[64,1,900]{2,0,1:T(8,128)(2,1)S(1)}, bf16[64,1,900]{2,0,1:T(8,128)(2,1)S(1)}, bf16[64,1,900]{2,0,1:T(8,128)(2,1)S(1)}) fusion(f32[64]{0:T(128)S(1)} %fusion.138, s32[900]{0:T(1024)S(1)} %iota_add_fusion, f32[64]{0:T(128)S(1)} %fusion.141), kind=kLoop, calls=%fused_computation.47 | loop fusion | flops 979200 | bytes 464912 | tf_op jit(solution)/shard_map/convert.6
  10.3 0.3 copy.55
  10.6 0.2 convert_element_type.125
  10.8 2.5 %convolution_convert_fusion = bf16[128,1024]{1,0:T(8,128)(2,1)S(1)} fusion(bf16[128,900]{1,0:T(8,128)(2,1)S(1)} %convert_element_type.125, bf16[1024,900]{1,0:T(8,128)(2,1)} %bitcast.114), kind=kOutput, calls=%fused_computation.11 | convolution fusion | flops 236060672 | bytes 2335744 | tf_op jit(solution)/shard_map/dot_general | solution.py:45
  13.3 0.9 %convert_element_type.127 = bf16[32,16,256]{2,1,0:T(8,128)(2,1)} reshape(bf16[128,1024]{1,0:T(8,128)(2,1)S(1)} %convolution_convert_fusion) | data formatting | bytes 524288 | tf_op jit(solution)/shard_map/convert_element_type | solution.py:48
  14.2 6.9 %all-to-all-start = ((bf16[32,16,256]{2,1,0:T(8,128)(2,1)}), bf16[32,16,256]{2,1,0:T(8,128)(2,1)S(1)}, u32[]{:S(2)}, u32[]{:S(2)}) async-start(bf16[32,16,256]{2,1,0:T(8,128)(2,1)} %convert_element_type.127), calls=%async_computation | async-start | bytes 524288 | tf_op jit(solution)/shard_map/all_to_all | solution.py:48
  21.2 0.3 fusion.63
  21.5 0.3 fusion.53
  21.8 0.9 %fusion.61 = f32[2,32]{1,0:T(2,128)} fusion(f32[32,9]{0,1:T(8,128)S(1)} %copy-done.4, f32[9]{0:T(128)S(1)} %get-tuple-element.26, s32[9]{0:T(128)S(1)} %slice_bitcast_fusion.8, s32[2]{0:T(128)S(1)} %iota_add_fusion.1), kind=kOutput, calls=%fused_computation.108 | convolution fusion | flops 1602 | bytes 1488 | tf_op jit(solution)/shard_map/kc,ko->oc/dot_general | solution.py:111
  22.7 0.9 %fusion.51 = f32[2,32]{1,0:T(2,128)} fusion(f32[32,9]{0,1:T(8,128)S(1)} %copy-done.4, f32[9]{0:T(128)S(1)} %get-tuple-element.26, s32[9]{0:T(128)S(1)} %slice_bitcast_fusion.8, s32[2]{0:T(128)S(1)} %iota_add_fusion.1), kind=kOutput, calls=%fused_computation.103 | convolution fusion | flops 1602 | bytes 1488 | tf_op jit(solution)/shard_map/kc,ko->oc/dot_general | solution.py:110
  23.6 0.9 %fusion.59 = f32[2,32]{1,0:T(2,128)} fusion(f32[32,9]{0,1:T(8,128)S(1)} %copy-done.4, f32[9]{0:T(128)S(1)} %get-tuple-element.27, s32[9]{0:T(128)S(1)} %slice_bitcast_fusion.8, s32[2]{0:T(128)S(1)} %iota_add_fusion.1), kind=kOutput, calls=%fused_computation.107 | convolution fusion | flops 1602 | bytes 1488 | tf_op jit(solution)/shard_map/kc,ko->oc/dot_general | solution.py:111
  24.5 0.9 %fusion.49 = f32[2,32]{1,0:T(2,128)} fusion(f32[32,9]{0,1:T(8,128)S(1)} %copy-done.4, f32[9]{0:T(128)S(1)} %get-tuple-element.27, s32[9]{0:T(128)S(1)} %slice_bitcast_fusion.8, s32[2]{0:T(128)S(1)} %iota_add_fusion.1), kind=kOutput, calls=%fused_computation.102 | convolution fusion | flops 1602 | bytes 1488 | tf_op jit(solution)/shard_map/kc,ko->oc/dot_general | solution.py:110
  25.4 0.9 %fusion.57 = f32[2,32]{1,0:T(2,128)} fusion(f32[32,9]{0,1:T(8,128)S(1)} %copy-done.4, f32[9]{0:T(128)S(1)} %get-tuple-element.28, s32[9]{0:T(128)S(1)} %slice_bitcast_fusion.8, s32[2]{0:T(128)S(1)} %iota_add_fusion.1), kind=kOutput, calls=%fused_computation.106 | convolution fusion | flops 1602 | bytes 1488 | tf_op jit(solution)/shard_map/kc,ko->oc/dot_general | solution.py:111
  26.3 0.9 %fusion.47 = f32[2,32]{1,0:T(2,128)} fusion(f32[32,9]{0,1:T(8,128)S(1)} %copy-done.4, f32[9]{0:T(128)S(1)} %get-tuple-element.28, s32[9]{0:T(128)S(1)} %slice_bitcast_fusion.8, s32[2]{0:T(128)S(1)} %iota_add_fusion.1), kind=kOutput, calls=%fused_computation.101 | convolution fusion | flops 1602 | bytes 1488 | tf_op jit(solution)/shard_map/kc,ko->oc/dot_general | solution.py:110
  27.2 0.9 %fusion.55 = f32[2,32]{1,0:T(2,128)} fusion(f32[32,9]{0,1:T(8,128)S(1)} %copy-done.4, f32[9]{0:T(128)S(1)} %get-tuple-element.29, s32[9]{0:T(128)S(1)} %slice_bitcast_fusion.8, s32[2]{0:T(128)S(1)} %iota_add_fusion.1), kind=kOutput, calls=%fused_computation.105 | convolution fusion | flops 1602 | bytes 1488 | tf_op jit(solution)/shard_map/kc,ko->oc/dot_general | solution.py:111
  28.1 0.9 %fusion.45 = f32[2,32]{1,0:T(2,128)} fusion(f32[32,9]{0,1:T(8,128)S(1)} %copy-done.4, f32[9]{0:T(128)S(1)} %get-tuple-element.29, s32[9]{0:T(128)S(1)} %slice_bitcast_fusion.8, s32[2]{0:T(128)S(1)} %iota_add_fusion.1), kind=kOutput, calls=%fused_computation.100 | convolution fusion | flops 1602 | bytes 1488 | tf_op jit(solution)/shard_map/kc,ko->oc/dot_general | solution.py:110
  29.2 1.3 %fusion.130 = f32[2,128]{1,0:T(2,128)} fusion(f32[128]{0:T(128)} %param.11, s32[128]{0:T(128)S(1)} %copy-done.6, s32[2]{0:T(128)S(1)} %iota_add_fusion.1), kind=kLoop, calls=%fused_computation.188 | loop fusion | flops 768 | bytes 2056 | tf_op jit(solution)/shard_map/mul | solution.py:121
  30.5 0.1 copy.71.offs_ref
  30.6 0.1 copy.72.w_ref
  30.7 0.3 copy.74
  31.0 0.9 %convert_element_type.140 = bf16[128,900]{1,0:T(8,128)(2,1)} reshape(bf16[64,2,900]{2,1,0:T(2,128)(2,1)S(1)} %copy.74) | data formatting | bytes 460800 | tf_op jit(solution)/shard_map/convert_element_type | solution.py:24
  31.9 2.3 %copy.58 = bf16[2,64,32,32]{3,2,1,0:T(8,128)(2,1)} copy(bf16[2,64,32,32]{1,3,2,0:T(8,128)(2,1)S(1)} %copy-done.2) | data formatting | bytes 524288 | tf_op args[6]
  34.3 0.1 pad.12.clone
  34.3 0.6 fusion.131
  35.0 2.0 %pad_maximum_fusion.4 = (bf16[32,40,2]{2,1,0:T(8,128)(2,1)}, bf16[32,40,2]{2,1,0:T(8,128)(2,1)}) fusion(bf16[32,4,900]{2,1,0:T(4,128)(2,1)S(1)} %broadcast_in_dim.57, bf16[32,2,900]{2,1,0:T(2,128)(2,1)} %collective-permute-done.1, bf16[32,32,900]{2,1,0:T(8,128)(2,1)S(1)} %copy-done, bf16[32,2,900]{2,1,0:T(2,128)(2,1)} %collective-permute-done), kind=kLoop, calls=%fused_computation.34 | loop fusion | flops 40960 | bytes 2314240 | tf_op jit(solution)/shard_map/slice | solution.py:69
  37.0 0.3 collective-permute-start.3
  37.2 1.5 %collective-permute-start.2 = (bf16[2,1280]{0,1:T(8,128)(2,1)}, bf16[2,1280]{0,1:T(8,128)(2,1)}, u32[]{:S(2)}, u32[]{:S(2)}) collective-permute-start(bf16[2,1280]{0,1:T(8,128)(2,1)} %bitcast.36), channel_id=1, source_target_pairs={{1,0},{2,1},{3,2},{0,3},{5,4},{6,5},{7,6},{4,7},{9,8},{10,9},{11,1... | collective-permute-start | bytes 15368 | tf_op jit(solution)/shard_map/ppermute | solution.py:68
  38.7 0.2 reshape.433
  39.0 0.3 reduce_sum.9
  39.3 0.2 reshape.421
  39.5 0.3 copy.56
  39.8 0.2 reshape.422
  40.0 0.4 subtract_convert_fusion
  40.5 0.1 rev.8
  40.6 0.9 %fusion.11 = bf16[2,32,2,32]{1,3,2,0:T(8,128)(2,1)S(1)} fusion(f32[2,32]{1,0:T(2,128)S(1)} %get-tuple-element.31, pred[2]{0:T(512)(128)(4,1)} %get-tuple-element.35, bf16[2,2,32,128]{3,2,1,0:T(8,128)(2,1)S(1)} %rev.8, f32[2,128]{1,0:T(2,128)} %fusion.130, bf16[2,32,1,128]{3,2,1,0:T(2,128)(2,1)S(1)} %get-tuple-element.20, ...), kind=kOutput, calls=%fused_computation.20 | convolution fusion | flops 1220608 | bytes 124162 | tf_op jit(solution)/shard_map/mui,mpci->mupc/dot_general | solution.py:132
  41.5 0.1 copy.66
  41.6 1.2 %convolution_bitcast_fusion.1 = f32[2,32,2,32]{3,2,0,1:T(2,128)S(1)} fusion(bf16[2,32,2,32]{3,2,0,1:T(2,128)(2,1)S(1)} %copy.66, bf16[2,32,2,32,32]{4,3,2,1,0:T(8,128)(2,1)} %bitcast.117), kind=kOutput, calls=%fused_computation.13 | convolution fusion | flops 262144 | bytes 286720 | tf_op jit(solution)/shard_map/mupc,ucd->mupd/dot_general | solution.py:138
  42.7 1.2 %convolution_bitcast_fusion = f32[2,32,2,32]{3,2,0,1:T(2,128)S(1)} fusion(bf16[2,32,2,32]{3,2,0,1:T(2,128)(2,1)S(1)} %copy.66, bf16[2,32,2,32,32]{4,3,2,1,0:T(8,128)(2,1)} %bitcast.118), kind=kOutput, calls=%fused_computation.12 | convolution fusion | flops 262144 | bytes 286720 | tf_op jit(solution)/shard_map/mupc,ucd->mupd/dot_general | solution.py:141
  43.9 0.9 %fusion.12 = bf16[2,32,2,32]{1,3,2,0:T(8,128)(2,1)S(1)} fusion(f32[2,32]{1,0:T(2,128)S(1)} %get-tuple-element.30, pred[2]{0:T(512)(128)(4,1)} %get-tuple-element.34, bf16[2,2,32,128]{3,2,1,0:T(8,128)(2,1)S(1)} %rev.8, f32[2,128]{1,0:T(2,128)} %fusion.130, bf16[2,32,1,128]{3,2,1,0:T(2,128)(2,1)S(1)} %get-tuple-element.19, ...), kind=kOutput, calls=%fused_computation.21 | convolution fusion | flops 1220608 | bytes 124162 | tf_op jit(solution)/shard_map/mui,mpci->mupc/dot_general | solution.py:132
  44.8 0.1 copy.60
  44.9 1.2 %convolution_bitcast_fusion.2 = f32[2,32,2,32]{3,2,0,1:T(2,128)S(1)} fusion(bf16[2,32,2,32]{3,2,0,1:T(2,128)(2,1)S(1)} %copy.60, bf16[2,32,2,32,32]{4,3,2,1,0:T(8,128)(2,1)} %bitcast.119), kind=kOutput, calls=%fused_computation.15 | convolution fusion | flops 262144 | bytes 286720 | tf_op jit(solution)/shard_map/mupc,ucd->mupd/dot_general | solution.py:141
  46.0 1.2 %convolution_bitcast_fusion.3 = f32[2,32,2,32]{3,2,0,1:T(2,128)S(1)} fusion(bf16[2,32,2,32]{3,2,0,1:T(2,128)(2,1)S(1)} %copy.60, bf16[2,32,2,32,32]{4,3,2,1,0:T(8,128)(2,1)} %bitcast.120), kind=kOutput, calls=%fused_computation.16 | convolution fusion | flops 262144 | bytes 286720 | tf_op jit(solution)/shard_map/mupc,ucd->mupd/dot_general | solution.py:138
  47.2 0.1 fusion.30
  47.3 0.1 pad_maximum_fusion.8
  47.4 0.2 fusion.33
  47.7 0.1 pad_maximum_fusion.9
  47.8 0.8 %subtract_multiply_fusion = (bf16[2,2,32,128]{3,2,1,0:T(8,128)(2,1)S(1)}, f32[2,2,32,128]{3,2,1,0:T(8,128)S(1)}) fusion(f32[2,128]{1,0:T(2,128)S(1)} %compare_convert_fusion, pred[2]{0:T(512)(128)(4,1)} %get-tuple-element.35, f32[2,2,32,128]{3,2,1,0:T(8,128)S(1)} %fusion.33, pred[2]{0:T(512)(128)(4,1)} %get-tuple-element.34, ...), kind=kOutput, calls=%fused_computation.64 | convolution fusion | flops 1196032 | bytes 189444 | tf_op jit(solution)/shard_map/mui,mupc->mpci/dot_general | solution.py:148
  48.6 0.7 multiply_convert_fusion.4
  49.4 0.1 rev.9
  49.4 0.1 concatenate.16
  49.6 0.1 concatenate.15
  49.7 0.2 maximum_bitcast_fusion
  49.9 0.2 broadcast_in_dim.56
  50.2 1.4 %reshape.425 = bf16[32,16,256]{2,1,0:T(8,128)(2,1)} reshape(bf16[8,4,2,2,32,32]{5,4,3,2,1,0:T(8,128)(2,1)S(1)} %broadcast_in_dim.56) | data formatting | bytes 524288 | tf_op jit(solution)/shard_map/reshape | solution.py:164
  51.6 6.0 %all-to-all-start.1 = ((bf16[32,16,256]{2,1,0:T(8,128)(2,1)}), bf16[32,16,256]{2,1,0:T(8,128)(2,1)S(1)}, u32[]{:S(2)}, u32[]{:S(2)}) async-start(bf16[32,16,256]{2,1,0:T(8,128)(2,1)} %reshape.425), calls=%async_computation.1 | async-start | bytes 524288 | tf_op jit(solution)/shard_map/all_to_all | solution.py:165
  57.7 4.2 %pad_maximum_fusion.rim_ref = bf16[32,40,1024]{2,1,0:T(8,128)(2,1)S(1)} fusion(bf16[32,40,2]{2,1,0:T(8,128)(2,1)} %bitcast.42, bf16[32,40,2]{2,1,0:T(8,128)(2,1)} %bitcast.38, bf16[32,4,900]{2,1,0:T(4,128)(2,1)S(1)} %broadcast_in_dim.57, bf16[32,2,900]{2,1,0:T(2,128)(2,1)} %collective-permute-done.1, bf16[32,32,900]{2,1,0:T(8,128)(2,1)S(1)} %copy-done, ...), kind=kLoop, calls=%fused_computation.10 | loop fusion | flops 18350080 | bytes 4937728 | tf_op jit(solution)/shard_map/concatenate | solution.py:81
  61.8 13.7 %shard_map.73 = bf16[32,32,900]{2,1,0:T(8,128)(2,1)S(1)} custom-call(s32[9,2]{1,0:T(8,128)S(1)} %copy.71.offs_ref, bf16[32,40,1024]{2,1,0:T(8,128)(2,1)S(1)} %pad_maximum_fusion.rim_ref, f32[32,9]{1,0:T(8,128)S(1)} %copy.72.w_ref), custom_call_target="tpu_custom_call" | custom-call | flops 94371840 | bytes 4464640 | tf_op jit(solution)/shard_map/pallas_call | solution.py:220
  75.6 0.2 reshape.430
  75.8 0.2 copy.73
  75.9 0.7 fusion.15
  76.6 2.6 %fusion.8 = bf16[32,32,900]{2,1,0:T(8,128)(2,1)} fusion(f32[32,32,900]{2,1,0:T(8,128)S(1)} %fusion.15, bf16[32,32,900]{2,1,0:T(8,128)(2,1)S(1)} %shard_map.73), kind=kLoop, calls=%fused_computation.9 | loop fusion | flops 10137600 | bytes 7372800 | tf_op jit(solution)/shard_map/convert_element_type | solution.py:175
  (52 shorter events, 0.6 us)
Async XLA Ops:
  0.0 21.2 %copy-start.5 = (s32[9,2]{0,1:T(2,128)S(1)}, s32[9,2]{0,1:T(2,128)}, u32[]{:S(2)}) copy-start(s32[9,2]{0,1:T(2,128)} %param.8) | copy-start | bytes 220
  0.0 21.2 %copy-start.4 = (f32[32,9]{0,1:T(8,128)S(1)}, f32[32,9]{0,1:T(8,128)}, u32[]{:S(2)}) copy-start(f32[32,9]{0,1:T(8,128)} %param.9) | copy-start | bytes 3460
  0.0 29.0 %copy-start.3 = (bf16[2,64,128]{2,1,0:T(8,128)(2,1)S(1)}, bf16[2,64,128]{2,1,0:T(8,128)(2,1)}, u32[]{:S(2)}) copy-start(bf16[2,64,128]{2,1,0:T(8,128)(2,1)} %param.10) | copy-start | bytes 98308
  0.0 29.1 %copy-start.6 = (s32[128]{0:T(128)S(1)}, s32[128]{0:T(128)}, u32[]{:S(2)}) copy-start(s32[128]{0:T(128)} %param.12) | copy-start | bytes 1540
  2.2 32.8 %collective-permute-start = (bf16[32,2,900]{2,1,0:T(2,128)(2,1)}, bf16[32,2,900]{2,1,0:T(2,128)(2,1)}, u32[]{:S(2)}, u32[]{:S(2)}) collective-permute-start(bf16[32,2,900]{2,1,0:T(2,128)(2,1)} %get-tuple-element.11), channel_id=1, source_target_pairs={{0,4},{4,8},{8,12},{12,16},{16,20},{20,24},{24,28},{1,5},{5,9},{9,... | collective-permute-start | bytes 345608 | tf_op jit(solution)/shard_map/ppermute | solution.py:54
  7.7 27.2 %collective-permute-start.1 = (bf16[32,2,900]{2,1,0:T(2,128)(2,1)}, bf16[32,2,900]{2,1,0:T(2,128)(2,1)}, u32[]{:S(2)}, u32[]{:S(2)}) collective-permute-start(bf16[32,2,900]{2,1,0:T(2,128)(2,1)} %get-tuple-element.12), channel_id=1, source_target_pairs={{4,0},{8,4},{12,8},{16,12},{20,16},{24,20},{28,24},{5,1},{9,5},{13... | collective-permute-start | bytes 345608 | tf_op jit(solution)/shard_map/ppermute | solution.py:51
  10.2 21.7 %copy-start.2 = (bf16[2,64,32,32]{1,3,2,0:T(8,128)(2,1)S(1)}, bf16[2,64,32,32]{1,3,2,0:T(8,128)(2,1)}, u32[]{:S(2)}) copy-start(bf16[2,64,32,32]{1,3,2,0:T(8,128)(2,1)} %param.13) | copy-start | bytes 786436
  10.6 24.4 %copy-start = (bf16[32,32,900]{2,1,0:T(8,128)(2,1)S(1)}, bf16[32,32,900]{2,1,0:T(8,128)(2,1)}, u32[]{:S(2)}) copy-start(bf16[32,32,900]{2,1,0:T(8,128)(2,1)} %param.7) | copy-start | bytes 5529604
  14.2 24.5 %all-to-all-start = ((bf16[32,16,256]{2,1,0:T(8,128)(2,1)}), bf16[32,16,256]{2,1,0:T(8,128)(2,1)S(1)}, u32[]{:S(2)}, u32[]{:S(2)}) async-start(bf16[32,16,256]{2,1,0:T(8,128)(2,1)} %convert_element_type.127), calls=%async_computation | async-start | bytes 524288 | tf_op jit(solution)/shard_map/all_to_all | solution.py:48
  31.9 8.1 %copy-start.7 = (f32[2,32]{1,0:T(2,128)S(1)}, f32[2,32]{1,0:T(2,128)}, u32[]{:S(2)}) copy-start(f32[2,32]{1,0:T(2,128)} %fusion.61) | copy-start | bytes 772
  31.9 8.1 %copy-start.8 = (f32[2,32]{1,0:T(2,128)S(1)}, f32[2,32]{1,0:T(2,128)}, u32[]{:S(2)}) copy-start(f32[2,32]{1,0:T(2,128)} %fusion.51) | copy-start | bytes 772
  31.9 8.1 %copy-start.9 = (f32[2,32]{1,0:T(2,128)S(1)}, f32[2,32]{1,0:T(2,128)}, u32[]{:S(2)}) copy-start(f32[2,32]{1,0:T(2,128)} %fusion.59) | copy-start | bytes 772
  31.9 8.1 %copy-start.10 = (f32[2,32]{1,0:T(2,128)S(1)}, f32[2,32]{1,0:T(2,128)}, u32[]{:S(2)}) copy-start(f32[2,32]{1,0:T(2,128)} %fusion.49) | copy-start | bytes 772
  31.9 8.1 %copy-start.11 = (f32[2,32]{1,0:T(2,128)S(1)}, f32[2,32]{1,0:T(2,128)}, u32[]{:S(2)}) copy-start(f32[2,32]{1,0:T(2,128)} %fusion.57) | copy-start | bytes 772
  31.9 8.1 %copy-start.12 = (f32[2,32]{1,0:T(2,128)S(1)}, f32[2,32]{1,0:T(2,128)}, u32[]{:S(2)}) copy-start(f32[2,32]{1,0:T(2,128)} %fusion.47) | copy-start | bytes 772
  31.9 8.1 %copy-start.13 = (f32[2,32]{1,0:T(2,128)S(1)}, f32[2,32]{1,0:T(2,128)}, u32[]{:S(2)}) copy-start(f32[2,32]{1,0:T(2,128)} %fusion.55) | copy-start | bytes 772
  31.9 8.1 %copy-start.14 = (f32[2,32]{1,0:T(2,128)S(1)}, f32[2,32]{1,0:T(2,128)}, u32[]{:S(2)}) copy-start(f32[2,32]{1,0:T(2,128)} %fusion.45) | copy-start | bytes 772
  37.0 20.7 %collective-permute-start.3 = (bf16[2,1280]{0,1:T(8,128)(2,1)}, bf16[2,1280]{0,1:T(8,128)(2,1)}, u32[]{:S(2)}, u32[]{:S(2)}) collective-permute-start(bf16[2,1280]{0,1:T(8,128)(2,1)} %bitcast.40), channel_id=1, source_target_pairs={{0,1},{1,2},{2,3},{3,0},{4,5},{5,6},{6,7},{7,4},{8,9},{9,10},{10,1... | collective-permute-start | bytes 15368 | tf_op jit(solution)/shard_map/ppermute | solution.py:75
  37.2 20.4 %collective-permute-start.2 = (bf16[2,1280]{0,1:T(8,128)(2,1)}, bf16[2,1280]{0,1:T(8,128)(2,1)}, u32[]{:S(2)}, u32[]{:S(2)}) collective-permute-start(bf16[2,1280]{0,1:T(8,128)(2,1)} %bitcast.36), channel_id=1, source_target_pairs={{1,0},{2,1},{3,2},{0,3},{5,4},{6,5},{7,6},{4,7},{9,8},{10,9},{11,1... | collective-permute-start | bytes 15368 | tf_op jit(solution)/shard_map/ppermute | solution.py:68
  51.6 24.0 %all-to-all-start.1 = ((bf16[32,16,256]{2,1,0:T(8,128)(2,1)}), bf16[32,16,256]{2,1,0:T(8,128)(2,1)S(1)}, u32[]{:S(2)}, u32[]{:S(2)}) async-start(bf16[32,16,256]{2,1,0:T(8,128)(2,1)} %reshape.425), calls=%async_computation.1 | async-start | bytes 524288 | tf_op jit(solution)/shard_map/all_to_all | solution.py:165
  61.8 14.1 %copy-start.1 = (bf16[128,900]{1,0:T(8,128)(2,1)S(1)}, bf16[128,900]{1,0:T(8,128)(2,1)}, u32[]{:S(2)}) copy-start(bf16[128,900]{1,0:T(8,128)(2,1)} %convert_element_type.140) | copy-start | bytes 691204

commit v13 on v12

--- a/solution.py
+++ b/solution.py
@@ -103,15 +103,18 @@
     )
     cos_all = jnp.cos(turns)
     sin_all = jnp.sin(turns)
+    shifts = lax.iota(jnp.int32, 5) - 2
+    chosen = (offsets[None, :, 0] == shifts[:, None]).astype(jnp.float32)
+    coef_re = jnp.einsum("dk,ck,ko->doc", chosen, conv_weight, cos_all)[..., None]
+    coef_im = jnp.einsum("dk,ck,ko->doc", chosen, conv_weight, sin_all)[..., None]
     real_acc = jnp.zeros((m_dev, channels, total_lat), jnp.float32)
     imag_acc = jnp.zeros((m_dev, channels, total_lat), jnp.float32)
     for shift in range(-2, 3):
-        chosen = (offsets[:, 0] == shift).astype(jnp.float32)[:, None] * conv_weight.T
-        coef_re = jnp.einsum("kc,ko->oc", chosen, cos_all)[:, :, None]
-        coef_im = jnp.einsum("kc,ko->oc", chosen, sin_all)[:, :, None]
         window = rim[..., 2 + shift : 2 + shift + total_lat]
-        real_acc = real_acc + coef_re * window[:, 0] - coef_im * window[:, 1]
-        imag_acc = imag_acc + coef_im * window[:, 0] + coef_re * window[:, 1]
+        c_re = coef_re[shift + 2]
+        c_im = coef_im[shift + 2]
+        real_acc = real_acc + c_re * window[:, 0] - c_im * window[:, 1]
+        imag_acc = imag_acc + c_im * window[:, 0] + c_re * window[:, 1]
     spec_acc = jnp.stack([real_acc, imag_acc], axis=1)
     spectrum = spec_acc.astype(jnp.bfloat16)
 
@@ -179,20 +182,13 @@
 
 def depthwise_conv(offsets, conv_weight, rim, lat_rows, lon_cols):
     channels, rim_rows, rim_cols = rim.shape
-    block_c = 8
-    chunk = 4
-    flat = rim_rows * rim_cols
-
-    def body(offs_ref, rim_ref, w_ref, out_ref, planes, shifted, result):
-        tiles = rim_cols // 128
-        for c in range(block_c):
-            x = rim_ref[c].astype(jnp.float32)
-            for t in range(tiles):
-                planes[t, pl.ds(c * rim_rows, rim_rows), :] = x[:, t * 128 : (t + 1) * 128]
+    by_rows = jnp.transpose(rim, (1, 0, 2))
+    block_c = 16
+    chunk = 2
+
+    def body(offs_ref, rim_ref, w_ref, out_ref, shifted):
         for row in range(rim_rows):
-            v = jnp.concatenate(
-                [planes[t, pl.ds(row, block_c, stride=rim_rows), :] for t in range(tiles)], axis=1
-            )
+            v = rim_ref[row].astype(jnp.float32)
             for s in range(5):
                 turn = (2 - s) % rim_cols
                 shifted[s, :, pl.ds(row * rim_cols, rim_cols)] = (
@@ -207,40 +203,29 @@
                 start = pl.multiple_of((r0 + 2 + dr) * rim_cols, rim_cols)
                 acc = acc + weights[:, k : k + 1] * shifted[dc + 2, :, pl.ds(start, chunk * rim_cols)]
             for i in range(chunk):
-                for t in range(tiles):
-                    result[t, pl.ds(r0 + i, block_c, stride=lat_rows), :] = acc[
-                        :, i * rim_cols + t * 128 : i * rim_cols + (t + 1) * 128
-                    ]
-        for c in range(block_c):
-            full = jnp.concatenate(
-                [result[t, pl.ds(c * lat_rows, lat_rows), :] for t in range(tiles)], axis=1
-            )
-            out_ref[c] = full[:, :lon_cols].astype(jnp.bfloat16)
-
-    return pl.pallas_call(
+                out_ref[r0 + i] = acc[:, i * rim_cols : i * rim_cols + lon_cols].astype(jnp.bfloat16)
+
+    by_rows_out = pl.pallas_call(
         body,
         grid_spec=pltpu.PrefetchScalarGridSpec(
             num_scalar_prefetch=1,
             grid=(channels // block_c,),
             in_specs=[
-                pl.BlockSpec((block_c, rim_rows, rim_cols), lambda b, o: (b, 0, 0)),
+                pl.BlockSpec((rim_rows, block_c, rim_cols), lambda b, o: (0, b, 0)),
                 pl.BlockSpec((block_c, KTAPS), lambda b, o: (b, 0)),
             ],
-            out_specs=pl.BlockSpec((block_c, lat_rows, lon_cols), lambda b, o: (b, 0, 0)),
-            scratch_shapes=[
-                pltpu.VMEM((rim_cols // 128, block_c * rim_rows, 128), jnp.float32),
-                pltpu.VMEM((5, block_c, flat), jnp.float32),
-                pltpu.VMEM((rim_cols // 128, block_c * lat_rows, 128), jnp.float32),
-            ],
+            out_specs=pl.BlockSpec((lat_rows, block_c, lon_cols), lambda b, o: (0, b, 0)),
+            scratch_shapes=[pltpu.VMEM((5, block_c, rim_rows * rim_cols), jnp.float32)],
         ),
-        out_shape=jax.ShapeDtypeStruct((channels, lat_rows, lon_cols), jnp.bfloat16),
+        out_shape=jax.ShapeDtypeStruct((lat_rows, channels, lon_cols), jnp.bfloat16),
         compiler_params=pltpu.CompilerParams(vmem_limit_bytes=48 * 1024 * 1024),
         cost_estimate=pl.CostEstimate(
             flops=8 * KTAPS * channels * rim_rows * rim_cols,
             transcendentals=0,
             bytes_accessed=channels * (rim_rows * rim_cols + lat_rows * lon_cols) * 2,
         ),
-    )(offsets, rim, conv_weight)
+    )(offsets, by_rows, conv_weight)
+    return jnp.transpose(by_rows_out, (1, 0, 2))
 
 
 def solution(mesh):

time: 79.8 us -> 71.7 us (0.90)
  local copies, waits for them, and re-layouts: 11 us -> 19.9 us
  matrix products: 18.5 us -> 10.3 us
  Pallas kernels: 13.7 us -> 6.93 us
  waiting for transfers between devices: 0.02 us -> 4.58 us
  other arithmetic: 14 us -> 10.3 us
  starting transfers between devices: 21.5 us -> 18.5 us
    dot_general x10 -> x2, matrix products: 7.8 us -> 0.25 us  [the longest x1 0.12 us: per_device(): jnp.einsum('dk,ck,ko->doc', chosen, conv_weight, cos_all)[..., None]]
    pallas_call x1, Pallas kernels: 13.7 us -> 6.93 us  [depthwise_conv(): pl.pallas_call(body, grid_spec=pltpu.PrefetchScalarGridSpec(num_scalar_pr...]
    transpose x0 -> x2, other arithmetic: none -> 5.43 us  [the longest x1 4.5 us: depthwise_conv(): by_rows = jnp.transpose(rim, (1, 0, 2))]
    concatenate x1 -> x0, other arithmetic: 4.16 us -> none  [per_device(): jnp.concatenate([rows_ext, east, jnp.zeros((channels, rim_rows, rim_cols...]
    ppermute x1, waiting for transfers between devices: 0.01 us -> 3.78 us  [per_device(): lax.ppermute(field[:, :2], 'lat', [(i + 1, i) for i in range(lat_n - 1)])]
    unnamed x33 -> x24, local copies, waits for them, and re-layouts: 2.58 us -> 6.3 us
    reshape x0 -> x6, local copies, waits for them, and re-layouts: none -> 3.05 us  [the longest x4 2.85 us: from_lanes(): return jnp.transpose(packed.reshape(2, channels, rim_rows), (1, 2, 0))]
    convert_element_type x1 -> x0, other arithmetic: 2.63 us -> none  [per_device(): (conv_out.astype(jnp.float32) + jax.nn.gelu(synthesis, approximate=True))...]
  transfers between devices with their start and end apart: 6 -> 6, of which waited for: 0 -> 2; matrix products, arithmetic and copies ran while one was open for 47% -> 28% of each run, Pallas kernels for 17% -> 10%
where the time goes in v13:
time: 71.7 us; the launch traced here: 71 us
  local copies, waits for them, and re-layouts  19.9 us (28%)
  starting transfers between devices  18.5 us (26%)
  other arithmetic  10.3 us (14%)
  matrix products  10.3 us (14%)
  Pallas kernels  6.93 us (10%)
  waiting for transfers between devices  4.58 us (6%)
    all_to_all x1, starting transfers between devices, per_device(): lax.all_to_all(partial.astype(jnp.bfloat16), BOTH, 0, 0, tiled=True)  7.31 us
    pallas_call x1, Pallas kernels, depthwise_conv(): pl.pallas_call(body, grid_spec=pltpu.PrefetchScalarGridSpec(num_scalar_pr...  6.93 us
    unnamed x24, local copies, waits for them, and re-layouts  6.3 us
    all_to_all x1, starting transfers between devices, per_device(): full_rows = lax.all_to_all(outgoing, BOTH, 0, 0, tiled=True)  5.62 us
    transpose x1, other arithmetic, depthwise_conv(): by_rows = jnp.transpose(rim, (1, 0, 2))  4.5 us
    ppermute x1, waiting for transfers between devices, per_device(): lax.ppermute(field[:, :2], 'lat', [(i + 1, i) for i in range(lat_n - 1)])  3.78 us
    ppermute x1, starting transfers between devices, per_device(): lax.ppermute(field[:, lat_rows - 2:], 'lat', [(i, i + 1) for i in range(l...  3.68 us
    reshape x4, local copies, waits for them, and re-layouts, from_lanes(): return jnp.transpose(packed.reshape(2, channels, rim_rows), (1, 2, 0))  2.85 us
  transfers between devices with their start and end apart: 6, of which 2 were waited for; matrix products, arithmetic and copies ran while one was open for 28% of the time, Pallas kernels for 10%

profile of v13, /device:TPU:0, one launch (start us, length us, event | category | flops | bytes accessed | tf_op | source)
XLA Modules:
  0.0 71.0 jit_solution(18044149266677807602)
XLA Ops:
  0.0 1.2 %multiply_convert_fusion.1 = (bf16[64,1,900]{2,0,1:T(8,128)(2,1)S(1)}, bf16[64,1,900]{2,0,1:T(8,128)(2,1)S(1)}, bf16[64,1,900]{2,0,1:T(8,128)(2,1)S(1)}, bf16[64,1,900]{2,0,1:T(8,128)(2,1)S(1)}) fusion(f32[64]{0:T(128)S(1)} %fusion.57, s32[900]{0:T(1024)S(1)} %iota_add_fusion, f32[64]{0:T(128)S(1)} %fusion.62), kind=kLoop, calls=%fused_computation.50 | loop fusion | flops 979200 | bytes 464912 | tf_op jit(solution)/shard_map/convert.5
  1.2 0.8 %pad_maximum_fusion.3 = (bf16[64,2,900]{2,0,1:T(8,128)(2,1)S(1)}, bf16[64,2,900]{2,0,1:T(8,128)(2,1)}) fusion(bf16[64,1,900]{2,0,1:T(8,128)(2,1)S(1)} %get-tuple-element.33, bf16[64,1,900]{2,0,1:T(8,128)(2,1)S(1)} %get-tuple-element.34, bf16[64,1,900]{2,0,1:T(8,128)(2,1)S(1)} %get-tuple-element.32, bf16[64,1,900]{2,0,1:T(8,128)(2,1)S(1)} %get-tuple-element.31), kind=kLoop, calls=%fused_computation.44 | loop fusion | flops 230400 | bytes 921600 | tf_op jit(solution)/shard_map/stack | solution.py:21
  2.0 0.3 copy.90
  2.2 0.2 convert_element_type.116
  2.4 0.8 %convolution_convert_fusion = bf16[128,1024]{1,0:T(8,128)(2,1)S(1)} fusion(bf16[128,900]{1,0:T(8,128)(2,1)S(1)} %convert_element_type.116, bf16[1024,900]{1,0:T(8,128)(2,1)S(1)} %bitcast.142), kind=kOutput, calls=%fused_computation.11 | convolution fusion | flops 236060672 | bytes 2335744 | tf_op jit(solution)/shard_map/dot_general | solution.py:45
  3.3 0.9 %convert_element_type.118 = bf16[32,16,256]{2,1,0:T(8,128)(2,1)} reshape(bf16[128,1024]{1,0:T(8,128)(2,1)S(1)} %convolution_convert_fusion) | data formatting | bytes 524288 | tf_op jit(solution)/shard_map/convert_element_type | solution.py:48
  4.1 7.3 %all-to-all-start = ((bf16[32,16,256]{2,1,0:T(8,128)(2,1)}), bf16[32,16,256]{2,1,0:T(8,128)(2,1)S(1)}, u32[]{:S(2)}, u32[]{:S(2)}) async-start(bf16[32,16,256]{2,1,0:T(8,128)(2,1)} %convert_element_type.118), calls=%async_computation | async-start | bytes 524288 | tf_op jit(solution)/shard_map/all_to_all | solution.py:48
  11.5 2.7 %copy.106 = bf16[32,32,900]{2,0,1:T(8,128)(2,1)S(1)} copy(bf16[32,32,900]{2,1,0:T(8,128)(2,1)} %param.7) | data formatting | bytes 3686400 | tf_op args[0]
  14.2 3.7 %collective-permute-start = (bf16[32,2,900]{2,0,1:T(8,128)(2,1)S(1)}, bf16[32,2,900]{2,0,1:T(8,128)(2,1)S(1)}, u32[]{:S(2)}, u32[]{:S(2)}) collective-permute-start(bf16[32,2,900]{2,0,1:T(8,128)(2,1)S(1)} %get-tuple-element.11), channel_id=1, source_target_pairs={{0,4},{4,8},{8,12},{12,16},{16,20},{20,24},{24,28},{1,5},{5,9},{9,... | collective-permute-start | bytes 345608 | tf_op jit(solution)/shard_map/ppermute | solution.py:54
  17.9 1.3 %collective-permute-start.1 = (bf16[32,2,900]{2,0,1:T(8,128)(2,1)S(1)}, bf16[32,2,900]{2,0,1:T(8,128)(2,1)}, u32[]{:S(2)}, u32[]{:S(2)}) collective-permute-start(bf16[32,2,900]{2,0,1:T(8,128)(2,1)S(1)} %get-tuple-element.12), channel_id=1, source_target_pairs={{4,0},{8,4},{12,8},{16,12},{20,16},{24,20},{28,24},{5,1},{9,5},{13... | collective-permute-start | bytes 345608 | tf_op jit(solution)/shard_map/ppermute | solution.py:51
  19.3 0.1 fusion.61
  19.5 0.1 convolution_bitcast_fusion.5
  19.6 0.1 convolution_bitcast_fusion.4
  19.9 0.7 fusion.54
  20.6 0.8 %collective-permute-done = bf16[32,2,900]{2,0,1:T(8,128)(2,1)S(1)} collective-permute-done((bf16[32,2,900]{2,0,1:T(8,128)(2,1)S(1)}, bf16[32,2,900]{2,0,1:T(8,128)(2,1)S(1)}, u32[]{:S(2)}, u32[]{:S(2)}) %collective-permute-start) | collective-permute-done | bytes 115232 | tf_op jit(solution)/shard_map/ppermute | solution.py:54
  21.4 3.8 %collective-permute-done.1 = bf16[32,2,900]{2,0,1:T(8,128)(2,1)} collective-permute-done((bf16[32,2,900]{2,0,1:T(8,128)(2,1)S(1)}, bf16[32,2,900]{2,0,1:T(8,128)(2,1)}, u32[]{:S(2)}, u32[]{:S(2)}) %collective-permute-start.1) | collective-permute-done | bytes 115232 | tf_op jit(solution)/shard_map/ppermute | solution.py:51
  25.2 0.9 %maximum_bitcast_fusion.1 = (bf16[2,32,40]{0,1,2:T(8,128)(2,1)S(1)}, bf16[2,32,40]{0,1,2:T(8,128)(2,1)S(1)}) fusion(bf16[32,4,900]{2,0,1:T(8,128)(2,1)S(1)} %broadcast_in_dim.91, bf16[32,2,900]{2,0,1:T(8,128)(2,1)} %collective-permute-done.1, bf16[32,32,900]{2,0,1:T(8,128)(2,1)S(1)} %copy.106, bf16[32,2,900]{2,0,1:T(8,128)(2,1)S(1)} %collective-permute-done), kind=kLoop, calls=%fused_computation.37 | loop fusion | flops 40960 | bytes 2314240 | tf_op jit(solution)/shard_map/transpose | solution.py:62
  26.2 0.5 copy.109
  26.6 0.1 reshape.451
  26.7 0.1 collective-permute-start.2
  26.8 0.5 copy.111
  27.3 0.1 reshape.453
  27.4 0.5 collective-permute-start.3
  27.9 0.6 fusion.55
  28.6 0.1 copy.113.offs_ref
  28.7 3.3 %copy.93 = bf16[2,64,32,32]{3,2,1,0:T(8,128)(2,1)} copy(bf16[2,64,32,32]{1,3,2,0:T(8,128)(2,1)} %param.13) | data formatting | bytes 524288 | tf_op args[6]
  32.0 1.2 %copy.116 = bf16[64,2,900]{2,1,0:T(2,128)(2,1)S(1)} copy(bf16[64,2,900]{2,0,1:T(8,128)(2,1)} %get-tuple-element.48) | data formatting | bytes 460800 | tf_op jit(solution)/shard_map/stack | solution.py:21
  33.2 0.9 %convert_element_type.131 = bf16[128,900]{1,0:T(8,128)(2,1)} reshape(bf16[64,2,900]{2,1,0:T(2,128)(2,1)S(1)} %copy.116) | data formatting | bytes 460800 | tf_op jit(solution)/shard_map/convert_element_type | solution.py:24
  34.2 0.1 reshape.452
  34.3 1.3 %copy.110 = bf16[2,32,40]{0,1,2:T(8,128)(2,1)} copy(bf16[2,32,40]{2,1,0:T(8,128)(2,1)S(1)} %reshape.452) | data formatting | bytes 10240 | tf_op jit(solution)/shard_map/reshape | solution.py:65
  35.6 0.1 reshape.454
  35.7 1.3 %copy.112 = bf16[2,32,40]{0,1,2:T(8,128)(2,1)} copy(bf16[2,32,40]{2,1,0:T(8,128)(2,1)S(1)} %reshape.454) | data formatting | bytes 10240 | tf_op jit(solution)/shard_map/reshape | solution.py:65
  37.1 0.2 reshape.457
  37.3 0.3 reduce_sum.9
  37.6 0.2 reshape.446
  37.8 0.3 copy.91
  38.1 0.2 reshape.447
  38.3 0.4 subtract_convert_fusion
  38.8 0.1 rev.8
  38.9 0.9 %fusion.11 = bf16[2,32,2,32]{1,3,2,0:T(8,128)(2,1)S(1)} fusion(f32[2,32]{1,0:T(2,128)S(1)} %get-tuple-element.40, pred[2]{0:T(512)(128)(4,1)} %get-tuple-element.44, bf16[2,2,32,128]{3,2,1,0:T(8,128)(2,1)S(1)} %rev.8, f32[2,128]{1,0:T(2,128)} %fusion.54, bf16[2,32,1,128]{3,2,1,0:T(2,128)(2,1)S(1)} %get-tuple-element.20, ...), kind=kOutput, calls=%fused_computation.20 | convolution fusion | flops 1220608 | bytes 124162 | tf_op jit(solution)/shard_map/mui,mpci->mupc/dot_general | solution.py:135
  39.8 0.1 copy.101
  39.9 1.2 %convolution_bitcast_fusion.1 = f32[2,32,2,32]{3,2,0,1:T(2,128)S(1)} fusion(bf16[2,32,2,32]{3,2,0,1:T(2,128)(2,1)S(1)} %copy.101, bf16[2,32,2,32,32]{4,3,2,1,0:T(8,128)(2,1)} %bitcast.146), kind=kOutput, calls=%fused_computation.13 | convolution fusion | flops 262144 | bytes 286720 | tf_op jit(solution)/shard_map/mupc,ucd->mupd/dot_general | solution.py:141
  41.0 1.2 %convolution_bitcast_fusion = f32[2,32,2,32]{3,2,0,1:T(2,128)S(1)} fusion(bf16[2,32,2,32]{3,2,0,1:T(2,128)(2,1)S(1)} %copy.101, bf16[2,32,2,32,32]{4,3,2,1,0:T(8,128)(2,1)} %bitcast.147), kind=kOutput, calls=%fused_computation.12 | convolution fusion | flops 262144 | bytes 286720 | tf_op jit(solution)/shard_map/mupc,ucd->mupd/dot_general | solution.py:144
  42.2 0.9 %fusion.12 = bf16[2,32,2,32]{1,3,2,0:T(8,128)(2,1)S(1)} fusion(f32[2,32]{1,0:T(2,128)S(1)} %get-tuple-element.39, pred[2]{0:T(512)(128)(4,1)} %get-tuple-element.43, bf16[2,2,32,128]{3,2,1,0:T(8,128)(2,1)S(1)} %rev.8, f32[2,128]{1,0:T(2,128)} %fusion.54, bf16[2,32,1,128]{3,2,1,0:T(2,128)(2,1)S(1)} %get-tuple-element.19, ...), kind=kOutput, calls=%fused_computation.21 | convolution fusion | flops 1220608 | bytes 124162 | tf_op jit(solution)/shard_map/mui,mpci->mupc/dot_general | solution.py:135
  43.1 0.1 copy.95
  43.2 1.2 %convolution_bitcast_fusion.2 = f32[2,32,2,32]{3,2,0,1:T(2,128)S(1)} fusion(bf16[2,32,2,32]{3,2,0,1:T(2,128)(2,1)S(1)} %copy.95, bf16[2,32,2,32,32]{4,3,2,1,0:T(8,128)(2,1)} %bitcast.148), kind=kOutput, calls=%fused_computation.15 | convolution fusion | flops 262144 | bytes 286720 | tf_op jit(solution)/shard_map/mupc,ucd->mupd/dot_general | solution.py:144
  44.3 1.2 %convolution_bitcast_fusion.3 = f32[2,32,2,32]{3,2,0,1:T(2,128)S(1)} fusion(bf16[2,32,2,32]{3,2,0,1:T(2,128)(2,1)S(1)} %copy.95, bf16[2,32,2,32,32]{4,3,2,1,0:T(8,128)(2,1)} %bitcast.149), kind=kOutput, calls=%fused_computation.16 | convolution fusion | flops 262144 | bytes 286720 | tf_op jit(solution)/shard_map/mupc,ucd->mupd/dot_general | solution.py:141
  45.6 0.1 pad_maximum_fusion.6
  45.7 0.2 fusion.34
  45.9 0.1 pad_maximum_fusion.7
  46.0 0.9 %subtract_multiply_fusion = (bf16[2,2,32,128]{3,2,1,0:T(8,128)(2,1)S(1)}, f32[2,2,32,128]{3,2,1,0:T(8,128)S(1)}) fusion(f32[2,128]{1,0:T(2,128)S(1)} %compare_convert_fusion, pred[2]{0:T(512)(128)(4,1)} %get-tuple-element.44, f32[2,2,32,128]{3,2,1,0:T(8,128)S(1)} %fusion.34, pred[2]{0:T(512)(128)(4,1)} %get-tuple-element.43, ...), kind=kOutput, calls=%fused_computation.67 | convolution fusion | flops 1196032 | bytes 189444 | tf_op jit(solution)/shard_map/mui,mupc->mpci/dot_general | solution.py:151
  46.9 0.1 multiply_convert_fusion.4
  47.0 0.1 concatenate.15
  47.3 0.1 concatenate.16
  47.4 0.2 maximum_bitcast_fusion.2
  47.6 0.2 broadcast_in_dim.90
  47.9 1.4 %reshape.450 = bf16[32,16,256]{2,1,0:T(8,128)(2,1)} reshape(bf16[8,4,2,2,32,32]{5,4,3,2,1,0:T(8,128)(2,1)S(1)} %broadcast_in_dim.90) | data formatting | bytes 524288 | tf_op jit(solution)/shard_map/reshape | solution.py:167
  49.3 5.6 %all-to-all-start.1 = ((bf16[32,16,256]{2,1,0:T(8,128)(2,1)}), bf16[32,16,256]{2,1,0:T(8,128)(2,1)S(1)}, u32[]{:S(2)}, u32[]{:S(2)}) async-start(bf16[32,16,256]{2,1,0:T(8,128)(2,1)} %reshape.450), calls=%async_computation.1 | async-start | bytes 524288 | tf_op jit(solution)/shard_map/all_to_all | solution.py:168
  54.9 4.5 %maximum_bitcast_fusion.rim_ref = bf16[40,32,1024]{2,1,0:T(8,128)(2,1)S(1)} fusion(bf16[32,40,2]{2,0,1:T(8,128)(2,1)} %bitcast.145, bf16[32,40,2]{2,0,1:T(8,128)(2,1)} %bitcast.144, bf16[32,4,900]{2,0,1:T(8,128)(2,1)S(1)} %broadcast_in_dim.91, bf16[32,2,900]{2,0,1:T(8,128)(2,1)} %collective-permute-done.1, bf16[32,32,900]{2,0,1:T(8,128)(2,1)S(1)} %copy.106, ...), kind=kLoop, calls=%fused_computation.10 | loop fusion | flops 18350080 | bytes 4937728 | tf_op jit(solution)/shard_map/transpose | solution.py:185
  59.5 6.9 %shard_map.73 = bf16[32,32,900]{2,1,0:T(8,128)(2,1)S(1)} custom-call(s32[9,2]{1,0:T(8,128)S(1)} %copy.113.offs_ref, bf16[40,32,1024]{2,1,0:T(8,128)(2,1)S(1)} %maximum_bitcast_fusion.rim_ref, f32[32,9]{1,0:T(8,128)S(1)} %copy.114.w_ref), custom_call_target="tpu_custom_call" | custom-call | flops 94371840 | bytes 4464640 | tf_op jit(solution)/shard_map/pallas_call | solution.py:208
  66.4 0.2 reshape.455
  66.6 0.2 copy.115
  66.8 1.8 %fusion.8 = bf16[32,32,900]{2,0,1:T(8,128)(2,1)S(1)} fusion(bf16[32,32,900]{2,0,1:T(8,128)(2,1)S(1)} %bitcast.141, bf16[128,900]{1,0:T(8,128)(2,1)S(1)} %copy-done.2, bf16[32,32,128]{2,1,0:T(8,128)(2,1)S(1)} %bitcast.151), kind=kOutput, calls=%fused_computation.9 | convolution fusion | flops 246067200 | bytes 4178944 | tf_op jit(solution)/shard_map/dot_general | solution.py:174
  68.6 2.5 %copy.123 = bf16[32,32,900]{2,1,0:T(8,128)(2,1)} copy(bf16[32,32,900]{2,0,1:T(8,128)(2,1)S(1)} %fusion.8) | data formatting | bytes 3686400 | tf_op jit(solution)/shard_map/convert_element_type | solution.py:178
  (47 shorter events, 0.9 us)
Async XLA Ops:
  0.0 2.4 %copy-start = (bf16[32,32,900]{2,1,0:T(8,128)(2,1)S(1)}, bf16[32,32,900]{2,1,0:T(8,128)(2,1)}, u32[]{:S(2)}) copy-start(bf16[32,32,900]{2,1,0:T(8,128)(2,1)} %param.7) | copy-start | bytes 5529604
  4.1 15.1 %copy-start.5 = (s32[9,2]{0,1:T(2,128)S(1)}, s32[9,2]{0,1:T(2,128)}, u32[]{:S(2)}) copy-start(s32[9,2]{0,1:T(2,128)} %param.8) | copy-start | bytes 220
  4.1 15.4 %copy-start.4 = (f32[32,9]{0,1:T(8,128)S(1)}, f32[32,9]{0,1:T(8,128)}, u32[]{:S(2)}) copy-start(f32[32,9]{0,1:T(8,128)} %param.9) | copy-start | bytes 3460
  4.1 15.6 %copy-start.3 = (bf16[2,64,128]{2,1,0:T(8,128)(2,1)S(1)}, bf16[2,64,128]{2,1,0:T(8,128)(2,1)}, u32[]{:S(2)}) copy-start(bf16[2,64,128]{2,1,0:T(8,128)(2,1)} %param.10) | copy-start | bytes 98308
  4.1 15.8 %copy-start.6 = (s32[128]{0:T(128)S(1)}, s32[128]{0:T(128)}, u32[]{:S(2)}) copy-start(s32[128]{0:T(128)} %param.12) | copy-start | bytes 1540
  4.1 15.8 %copy-start.7 = (f32[128]{0:T(128)S(1)}, f32[128]{0:T(128)}, u32[]{:S(2)}) copy-start(f32[128]{0:T(128)} %param.11) | copy-start | bytes 1540
  4.1 32.9 %all-to-all-start = ((bf16[32,16,256]{2,1,0:T(8,128)(2,1)}), bf16[32,16,256]{2,1,0:T(8,128)(2,1)S(1)}, u32[]{:S(2)}, u32[]{:S(2)}) async-start(bf16[32,16,256]{2,1,0:T(8,128)(2,1)} %convert_element_type.118), calls=%async_computation | async-start | bytes 524288 | tf_op jit(solution)/shard_map/all_to_all | solution.py:48
  14.2 7.2 %collective-permute-start = (bf16[32,2,900]{2,0,1:T(8,128)(2,1)S(1)}, bf16[32,2,900]{2,0,1:T(8,128)(2,1)S(1)}, u32[]{:S(2)}, u32[]{:S(2)}) collective-permute-start(bf16[32,2,900]{2,0,1:T(8,128)(2,1)S(1)} %get-tuple-element.11), channel_id=1, source_target_pairs={{0,4},{4,8},{8,12},{12,16},{16,20},{20,24},{24,28},{1,5},{5,9},{9,... | collective-permute-start | bytes 345608 | tf_op jit(solution)/shard_map/ppermute | solution.py:54
  17.9 7.3 %collective-permute-start.1 = (bf16[32,2,900]{2,0,1:T(8,128)(2,1)S(1)}, bf16[32,2,900]{2,0,1:T(8,128)(2,1)}, u32[]{:S(2)}, u32[]{:S(2)}) collective-permute-start(bf16[32,2,900]{2,0,1:T(8,128)(2,1)S(1)} %get-tuple-element.12), channel_id=1, source_target_pairs={{4,0},{8,4},{12,8},{16,12},{20,16},{24,20},{28,24},{5,1},{9,5},{13... | collective-permute-start | bytes 345608 | tf_op jit(solution)/shard_map/ppermute | solution.py:51
  21.4 10.6 %copy-start.1 = (bf16[32,2,900]{2,0,1:T(8,128)(2,1)}, bf16[32,2,900]{2,0,1:T(8,128)(2,1)S(1)}, u32[]{:S(2)}) copy-start(bf16[32,2,900]{2,0,1:T(8,128)(2,1)S(1)} %collective-permute-done) | copy-start | bytes 345604
  26.7 7.5 %collective-permute-start.2 = (bf16[2,1280]{1,0:T(2,128)(2,1)S(1)}, bf16[2,1280]{1,0:T(2,128)(2,1)S(1)}, u32[]{:S(2)}, u32[]{:S(2)}) collective-permute-start(bf16[2,1280]{1,0:T(2,128)(2,1)S(1)} %reshape.451), channel_id=1, source_target_pairs={{1,0},{2,1},{3,2},{0,3},{5,4},{6,5},{7,6},{4,7},{9,8},{10,9},{11,1... | collective-permute-start | bytes 15368 | tf_op jit(solution)/shard_map/ppermute | solution.py:68
  27.4 8.2 %collective-permute-start.3 = (bf16[2,1280]{1,0:T(2,128)(2,1)S(1)}, bf16[2,1280]{1,0:T(2,128)(2,1)S(1)}, u32[]{:S(2)}, u32[]{:S(2)}) collective-permute-start(bf16[2,1280]{1,0:T(2,128)(2,1)S(1)} %reshape.453), channel_id=1, source_target_pairs={{0,1},{1,2},{2,3},{3,0},{4,5},{5,6},{6,7},{7,4},{8,9},{9,10},{10,1... | collective-permute-start | bytes 15368 | tf_op jit(solution)/shard_map/ppermute | solution.py:75
  38.1 8.8 %copy-start.8 = (pred[2]{0:T(512)(128)(4,1)S(1)}, pred[2]{0:T(512)(128)(4,1)}, u32[]{:S(2)}) copy-start(pred[2]{0:T(512)(128)(4,1)} %get-tuple-element.43) | copy-start | bytes 10
  38.1 8.8 %copy-start.9 = (pred[2]{0:T(512)(128)(4,1)S(1)}, pred[2]{0:T(512)(128)(4,1)}, u32[]{:S(2)}) copy-start(pred[2]{0:T(512)(128)(4,1)} %get-tuple-element.44) | copy-start | bytes 10
  49.3 17.1 %all-to-all-start.1 = ((bf16[32,16,256]{2,1,0:T(8,128)(2,1)}), bf16[32,16,256]{2,1,0:T(8,128)(2,1)S(1)}, u32[]{:S(2)}, u32[]{:S(2)}) async-start(bf16[32,16,256]{2,1,0:T(8,128)(2,1)} %reshape.450), calls=%async_computation.1 | async-start | bytes 524288 | tf_op jit(solution)/shard_map/all_to_all | solution.py:168
  59.4 7.3 %copy-start.2 = (bf16[128,900]{1,0:T(8,128)(2,1)S(1)}, bf16[128,900]{1,0:T(8,128)(2,1)}, u32[]{:S(2)}) copy-start(bf16[128,900]{1,0:T(8,128)(2,1)} %convert_element_type.131) | copy-start | bytes 691204

commit v14 on v13

--- a/solution.py
+++ b/solution.py
@@ -124,35 +124,28 @@
     weight_q = quad_weight[None, :] * kept_mask * (1.0 / math.sqrt(half_rows))
     even_terms = (weight_q[:, None, None, :] * (north_part + south_part)).astype(jnp.bfloat16)
     odd_terms = (weight_q[:, None, None, :] * (north_part - south_part)).astype(jnp.bfloat16)
-    paired = legendre.reshape(m_dev, orders_all // 2, 2, half_rows)
-    mix_pairs = mix_weight.reshape(2, orders_all // 2, 2, channels, channels)
-    even_sum = jnp.zeros((m_dev, 2, channels, half_rows), jnp.float32)
-    odd_sum = jnp.zeros((m_dev, 2, channels, half_rows), jnp.float32)
-    for parity in range(2):
-        same_parity = ((parity + mine) % 2 == 0)[:, None, None, None]
-        operand = jnp.where(same_parity, even_terms, odd_terms)
-        degree_plane = paired[:, :, parity]
-        coeffs = jnp.einsum(
-            "mui,mpci->mupc", degree_plane, operand, preferred_element_type=jnp.float32
-        )
-        degrees = 2 * lax.iota(jnp.int32, orders_all // 2) + parity
-        triangle = (degrees[None, :] >= mine[:, None]).astype(jnp.float32)
-        coeffs = (coeffs * triangle[:, :, None, None]).astype(jnp.bfloat16)
-        with_real = jnp.einsum(
-            "mupc,ucd->mupd", coeffs, mix_pairs[0, :, parity], preferred_element_type=jnp.float32
-        )
-        with_imag = jnp.einsum(
-            "mupc,ucd->mupd", coeffs, mix_pairs[1, :, parity], preferred_element_type=jnp.float32
-        )
-        mixed = jnp.stack(
-            [with_real[:, :, 0] - with_imag[:, :, 1], with_real[:, :, 1] + with_imag[:, :, 0]],
-            axis=2,
-        ).astype(jnp.bfloat16)
-        returned = jnp.einsum(
-            "mui,mupc->mpci", degree_plane, mixed, preferred_element_type=jnp.float32
-        )
-        even_sum = even_sum + jnp.where(same_parity, returned, 0.0)
-        odd_sum = odd_sum + jnp.where(same_parity, 0.0, returned)
+    degrees = lax.iota(jnp.int32, orders_all)
+    same = ((degrees[None, :] + mine[:, None]) % 2 == 0)[:, :, None]
+    zero = jnp.zeros((), legendre.dtype)
+    leg_same = jnp.where(same, legendre, zero)
+    leg_diff = jnp.where(same, zero, legendre)
+    coeffs = jnp.einsum(
+        "mli,mpci->mlpc", leg_same, even_terms, preferred_element_type=jnp.float32
+    ) + jnp.einsum("mli,mpci->mlpc", leg_diff, odd_terms, preferred_element_type=jnp.float32)
+    triangle = (degrees[None, :] >= mine[:, None]).astype(jnp.float32)
+    coeffs = (coeffs * triangle[:, :, None, None]).astype(jnp.bfloat16)
+    with_real = jnp.einsum(
+        "mlpc,lcd->mlpd", coeffs, mix_weight[0], preferred_element_type=jnp.float32
+    )
+    with_imag = jnp.einsum(
+        "mlpc,lcd->mlpd", coeffs, mix_weight[1], preferred_element_type=jnp.float32
+    )
+    mixed = jnp.stack(
+        [with_real[:, :, 0] - with_imag[:, :, 1], with_real[:, :, 1] + with_imag[:, :, 0]],
+        axis=2,
+    ).astype(jnp.bfloat16)
+    even_sum = jnp.einsum("mli,mlpc->mpci", leg_same, mixed, preferred_element_type=jnp.float32)
+    odd_sum = jnp.einsum("mli,mlpc->mpci", leg_diff, mixed, preferred_element_type=jnp.float32)
     north_out = (even_sum + odd_sum) * kept_mask[:, None, None, :]
     south_out = (even_sum - odd_sum) * kept_mask[:, None, None, :]
     grid_spectrum = jnp.concatenate([north_out, jnp.flip(south_out, axis=3)], axis=3).astype(

time: 71.7 us -> 68.6 us (0.957)
  matrix products: 10.3 us -> 6.36 us
  local copies, waits for them, and re-layouts: 19.9 us -> 22.4 us
  other arithmetic: 10.3 us -> 9.07 us
    dot_general x8 -> x6, matrix products: 7.47 us -> 3.48 us  [the longest x1 1.32 us: per_device(): jnp.einsum('mlpc,lcd->mlpd', coeffs, mix_weight[1], preferred_element_typ...]
    unnamed x24 -> x23, local copies, waits for them, and re-layouts: 6.3 us -> 7.9 us
    slice x1, local copies, waits for them, and re-layouts: 0.05 us -> 0.84 us  [per_device(): mix_weight[0]]
    another operation x6 -> x5, other arithmetic: 1.93 us -> 1.84 us
  transfers between devices with their start and end apart: 6 -> 6, of which waited for: 2 -> 2; matrix products, arithmetic and copies ran while one was open for 28% -> 31% of each run, Pallas kernels for 10% -> 10%
where the time goes in v14:
time: 68.6 us; the launch traced here: 68.1 us
  local copies, waits for them, and re-layouts  22.4 us (33%)
  starting transfers between devices  18.5 us (27%)
  other arithmetic  9.07 us (13%)
  Pallas kernels  6.93 us (10%)
  matrix products  6.36 us (9%)
  waiting for transfers between devices  4.46 us (7%)
    unnamed x23, local copies, waits for them, and re-layouts  7.9 us
    all_to_all x1, starting transfers between devices, per_device(): lax.all_to_all(partial.astype(jnp.bfloat16), BOTH, 0, 0, tiled=True)  7.31 us
    pallas_call x1, Pallas kernels, depthwise_conv(): pl.pallas_call(body, grid_spec=pltpu.PrefetchScalarGridSpec(num_scalar_pr...  6.93 us
    all_to_all x1, starting transfers between devices, per_device(): full_rows = lax.all_to_all(outgoing, BOTH, 0, 0, tiled=True)  5.62 us
    transpose x1, other arithmetic, depthwise_conv(): by_rows = jnp.transpose(rim, (1, 0, 2))  4.5 us
    ppermute x1, waiting for transfers between devices, per_device(): lax.ppermute(field[:, :2], 'lat', [(i + 1, i) for i in range(lat_n - 1)])  3.79 us
    ppermute x1, starting transfers between devices, per_device(): lax.ppermute(field[:, lat_rows - 2:], 'lat', [(i, i + 1) for i in range(l...  3.68 us
    reshape x4, local copies, waits for them, and re-layouts, from_lanes(): return jnp.transpose(packed.reshape(2, channels, rim_rows), (1, 2, 0))  2.89 us
  transfers between devices with their start and end apart: 6, of which 2 were waited for; matrix products, arithmetic and copies ran while one was open for 31% of the time, Pallas kernels for 10%

profile of v14, /device:TPU:0, one launch (start us, length us, event | category | flops | bytes accessed | tf_op | source)
XLA Modules:
  0.0 68.1 jit_solution(14879599740172693692)
XLA Ops:
  0.0 1.2 %multiply_convert_fusion.1 = (bf16[64,1,900]{2,0,1:T(8,128)(2,1)S(1)}, bf16[64,1,900]{2,0,1:T(8,128)(2,1)S(1)}, bf16[64,1,900]{2,0,1:T(8,128)(2,1)S(1)}, bf16[64,1,900]{2,0,1:T(8,128)(2,1)S(1)}) fusion(f32[64]{0:T(128)S(1)} %fusion.58, s32[900]{0:T(1024)S(1)} %iota_add_fusion, f32[64]{0:T(128)S(1)} %fusion.61), kind=kLoop, calls=%fused_computation.43 | loop fusion | flops 979200 | bytes 464912 | tf_op jit(solution)/shard_map/convert.5
  1.2 0.8 %pad_maximum_fusion.3 = (bf16[64,2,900]{2,0,1:T(8,128)(2,1)S(1)}, bf16[64,2,900]{2,0,1:T(8,128)(2,1)}) fusion(bf16[64,1,900]{2,0,1:T(8,128)(2,1)S(1)} %get-tuple-element.31, bf16[64,1,900]{2,0,1:T(8,128)(2,1)S(1)} %get-tuple-element.32, bf16[64,1,900]{2,0,1:T(8,128)(2,1)S(1)} %get-tuple-element.30, bf16[64,1,900]{2,0,1:T(8,128)(2,1)S(1)} %get-tuple-element.29), kind=kLoop, calls=%fused_computation.37 | loop fusion | flops 230400 | bytes 921600 | tf_op jit(solution)/shard_map/stack | solution.py:21
  2.0 0.3 copy.75
  2.2 0.2 convert_element_type.99
  2.4 0.8 %convolution_convert_fusion = bf16[128,1024]{1,0:T(8,128)(2,1)S(1)} fusion(bf16[128,900]{1,0:T(8,128)(2,1)S(1)} %convert_element_type.99, bf16[1024,900]{1,0:T(8,128)(2,1)S(1)} %bitcast.108), kind=kOutput, calls=%fused_computation.11 | convolution fusion | flops 236060672 | bytes 2335744 | tf_op jit(solution)/shard_map/dot_general | solution.py:45
  3.3 0.9 %convert_element_type.101 = bf16[32,16,256]{2,1,0:T(8,128)(2,1)} reshape(bf16[128,1024]{1,0:T(8,128)(2,1)S(1)} %convolution_convert_fusion) | data formatting | bytes 524288 | tf_op jit(solution)/shard_map/convert_element_type | solution.py:48
  4.1 7.3 %all-to-all-start = ((bf16[32,16,256]{2,1,0:T(8,128)(2,1)}), bf16[32,16,256]{2,1,0:T(8,128)(2,1)S(1)}, u32[]{:S(2)}, u32[]{:S(2)}) async-start(bf16[32,16,256]{2,1,0:T(8,128)(2,1)} %convert_element_type.101), calls=%async_computation | async-start | bytes 524288 | tf_op jit(solution)/shard_map/all_to_all | solution.py:48
  11.5 2.8 %copy.84 = bf16[32,32,900]{2,0,1:T(8,128)(2,1)S(1)} copy(bf16[32,32,900]{2,1,0:T(8,128)(2,1)} %param.7) | data formatting | bytes 3686400 | tf_op args[0]
  14.3 3.7 %collective-permute-start = (bf16[32,2,900]{2,0,1:T(8,128)(2,1)S(1)}, bf16[32,2,900]{2,0,1:T(8,128)(2,1)S(1)}, u32[]{:S(2)}, u32[]{:S(2)}) collective-permute-start(bf16[32,2,900]{2,0,1:T(8,128)(2,1)S(1)} %get-tuple-element.11), channel_id=1, source_target_pairs={{0,4},{4,8},{8,12},{12,16},{16,20},{20,24},{24,28},{1,5},{5,9},{9,... | collective-permute-start | bytes 345608 | tf_op jit(solution)/shard_map/ppermute | solution.py:54
  17.9 1.3 %collective-permute-start.1 = (bf16[32,2,900]{2,0,1:T(8,128)(2,1)S(1)}, bf16[32,2,900]{2,0,1:T(8,128)(2,1)}, u32[]{:S(2)}, u32[]{:S(2)}) collective-permute-start(bf16[32,2,900]{2,0,1:T(8,128)(2,1)S(1)} %get-tuple-element.12), channel_id=1, source_target_pairs={{4,0},{8,4},{12,8},{16,12},{20,16},{24,20},{28,24},{5,1},{9,5},{13... | collective-permute-start | bytes 345608 | tf_op jit(solution)/shard_map/ppermute | solution.py:51
  19.3 0.1 fusion.60
  19.5 0.1 convolution_bitcast_fusion.2
  19.6 0.1 convolution_bitcast_fusion.3
  19.8 0.8 %fusion.71 = (bf16[1,64,32,32]{1,3,2,0:T(8,128)(2,1)}, bf16[1,64,32,32]{1,3,2,0:T(8,128)(2,1)}) fusion(bf16[2,64,32,32]{1,3,2,0:T(8,128)(2,1)S(1)} %copy-done.2), kind=kLoop, calls=%fused_computation.122 | loop fusion | bytes 524288 | tf_op jit(solution)/shard_map/slice | solution.py:138
  20.7 0.1 compare_convert_fusion.1
  20.8 0.7 collective-permute-done
  21.4 3.8 %collective-permute-done.1 = bf16[32,2,900]{2,0,1:T(8,128)(2,1)} collective-permute-done((bf16[32,2,900]{2,0,1:T(8,128)(2,1)S(1)}, bf16[32,2,900]{2,0,1:T(8,128)(2,1)}, u32[]{:S(2)}, u32[]{:S(2)}) %collective-permute-start.1) | collective-permute-done | bytes 115232 | tf_op jit(solution)/shard_map/ppermute | solution.py:51
  25.2 0.9 %maximum_bitcast_fusion.1 = (bf16[2,32,40]{0,1,2:T(8,128)(2,1)S(1)}, bf16[2,32,40]{0,1,2:T(8,128)(2,1)S(1)}) fusion(bf16[32,4,900]{2,0,1:T(8,128)(2,1)S(1)} %broadcast_in_dim.37, bf16[32,2,900]{2,0,1:T(8,128)(2,1)} %collective-permute-done.1, bf16[32,32,900]{2,0,1:T(8,128)(2,1)S(1)} %copy.84, bf16[32,2,900]{2,0,1:T(8,128)(2,1)S(1)} %collective-permute-done), kind=kLoop, calls=%fused_computation.34 | loop fusion | flops 40960 | bytes 2314240 | tf_op jit(solution)/shard_map/transpose | solution.py:62
  26.2 0.5 copy.87
  26.6 0.1 reshape.402
  26.8 0.1 collective-permute-start.2
  26.9 0.5 copy.89
  27.3 0.1 reshape.404
  27.4 0.5 collective-permute-start.3
  28.0 0.1 copy.92.w_ref
  28.1 0.1 copy.91.offs_ref
  28.2 2.5 %copy.111 = bf16[1,64,32,32]{3,2,1,0:T(8,128)(2,1)} copy(bf16[1,64,32,32]{1,3,2,0:T(8,128)(2,1)} %get-tuple-element.14) | data formatting | bytes 262144
  30.6 2.5 %copy.110 = bf16[1,64,32,32]{3,2,1,0:T(8,128)(2,1)} copy(bf16[1,64,32,32]{1,3,2,0:T(8,128)(2,1)} %get-tuple-element.13) | data formatting | bytes 262144
  33.1 1.2 %copy.94 = bf16[64,2,900]{2,1,0:T(2,128)(2,1)S(1)} copy(bf16[64,2,900]{2,0,1:T(8,128)(2,1)} %get-tuple-element.42) | data formatting | bytes 460800 | tf_op jit(solution)/shard_map/stack | solution.py:21
  34.3 0.9 %convert_element_type.110 = bf16[128,900]{1,0:T(8,128)(2,1)} reshape(bf16[64,2,900]{2,1,0:T(2,128)(2,1)S(1)} %copy.94) | data formatting | bytes 460800 | tf_op jit(solution)/shard_map/convert_element_type | solution.py:24
  35.3 0.1 reshape.403
  35.4 1.4 %copy.88 = bf16[2,32,40]{0,1,2:T(8,128)(2,1)} copy(bf16[2,32,40]{2,1,0:T(8,128)(2,1)S(1)} %reshape.403) | data formatting | bytes 10240 | tf_op jit(solution)/shard_map/reshape | solution.py:65
  36.8 0.1 reshape.405
  36.9 1.3 %copy.90 = bf16[2,32,40]{0,1,2:T(8,128)(2,1)} copy(bf16[2,32,40]{2,1,0:T(8,128)(2,1)S(1)} %reshape.405) | data formatting | bytes 10240 | tf_op jit(solution)/shard_map/reshape | solution.py:65
  38.2 0.2 reshape.408
  38.5 0.3 reduce_sum.9
  38.8 0.2 reshape.399
  39.0 0.3 copy.76
  39.3 0.2 reshape.400
  39.5 0.4 subtract_convert_fusion
  39.9 0.1 rev.8
  40.0 0.2 fusion.31
  40.2 0.2 fusion.10
  40.4 0.1 copy.78
  40.6 1.3 %convolution_bitcast_fusion = f32[2,64,2,32]{3,2,0,1:T(2,128)S(1)} fusion(bf16[2,64,2,32]{3,2,0,1:T(2,128)(2,1)S(1)} %copy.78, bf16[1,64,32,32]{3,2,1,0:T(8,128)(2,1)} %copy.111), kind=kOutput, calls=%fused_computation.12 | convolution fusion | flops 524288 | bytes 180224 | tf_op jit(solution)/shard_map/mlpc,lcd->mlpd/dot_general | solution.py:140
  41.9 1.3 %convolution_bitcast_fusion.1 = f32[2,64,2,32]{3,2,0,1:T(2,128)S(1)} fusion(bf16[2,64,2,32]{3,2,0,1:T(2,128)(2,1)S(1)} %copy.78, bf16[1,64,32,32]{3,2,1,0:T(8,128)(2,1)} %copy.110), kind=kOutput, calls=%fused_computation.13 | convolution fusion | flops 524288 | bytes 180224 | tf_op jit(solution)/shard_map/mlpc,lcd->mlpd/dot_general | solution.py:137
  43.2 0.1 fusion.28
  43.3 0.2 pad_maximum_fusion.5
  43.5 0.1 copy.81
  43.6 0.2 fusion.36
  43.8 0.2 subtract_multiply_fusion
  44.1 0.1 concatenate.15
  44.2 0.1 rev.9
  44.3 0.1 concatenate.16
  44.4 0.2 maximum_bitcast_fusion.2
  44.7 0.2 broadcast_in_dim.36
  44.9 1.4 %reshape.401 = bf16[32,16,256]{2,1,0:T(8,128)(2,1)} reshape(bf16[8,4,2,2,32,32]{5,4,3,2,1,0:T(8,128)(2,1)S(1)} %broadcast_in_dim.36) | data formatting | bytes 524288 | tf_op jit(solution)/shard_map/reshape | solution.py:160
  46.3 5.6 %all-to-all-start.1 = ((bf16[32,16,256]{2,1,0:T(8,128)(2,1)}), bf16[32,16,256]{2,1,0:T(8,128)(2,1)S(1)}, u32[]{:S(2)}, u32[]{:S(2)}) async-start(bf16[32,16,256]{2,1,0:T(8,128)(2,1)} %reshape.401), calls=%async_computation.1 | async-start | bytes 524288 | tf_op jit(solution)/shard_map/all_to_all | solution.py:161
  52.0 4.5 %maximum_bitcast_fusion.rim_ref = bf16[40,32,1024]{2,1,0:T(8,128)(2,1)S(1)} fusion(bf16[32,40,2]{2,0,1:T(8,128)(2,1)} %bitcast.111, bf16[32,40,2]{2,0,1:T(8,128)(2,1)} %bitcast.110, bf16[32,4,900]{2,0,1:T(8,128)(2,1)S(1)} %broadcast_in_dim.37, bf16[32,2,900]{2,0,1:T(8,128)(2,1)} %collective-permute-done.1, bf16[32,32,900]{2,0,1:T(8,128)(2,1)S(1)} %copy.84, ...), kind=kLoop, calls=%fused_computation.10 | loop fusion | flops 18350080 | bytes 4937728 | tf_op jit(solution)/shard_map/transpose | solution.py:178
  56.5 6.9 %shard_map.73 = bf16[32,32,900]{2,1,0:T(8,128)(2,1)S(1)} custom-call(s32[9,2]{1,0:T(8,128)S(1)} %copy.91.offs_ref, bf16[40,32,1024]{2,1,0:T(8,128)(2,1)S(1)} %maximum_bitcast_fusion.rim_ref, f32[32,9]{1,0:T(8,128)S(1)} %copy.92.w_ref), custom_call_target="tpu_custom_call" | custom-call | flops 94371840 | bytes 4464640 | tf_op jit(solution)/shard_map/pallas_call | solution.py:201
  63.4 0.2 reshape.406
  63.6 0.2 copy.93
  63.8 1.8 %fusion.8 = bf16[32,32,900]{2,0,1:T(8,128)(2,1)S(1)} fusion(bf16[32,32,900]{2,0,1:T(8,128)(2,1)S(1)} %bitcast.107, bf16[128,900]{1,0:T(8,128)(2,1)S(1)} %copy-done.3, bf16[32,32,128]{2,1,0:T(8,128)(2,1)S(1)} %bitcast.113), kind=kOutput, calls=%fused_computation.9 | convolution fusion | flops 246067200 | bytes 4178944 | tf_op jit(solution)/shard_map/dot_general | solution.py:167
  65.6 2.5 %copy.101 = bf16[32,32,900]{2,1,0:T(8,128)(2,1)} copy(bf16[32,32,900]{2,0,1:T(8,128)(2,1)S(1)} %fusion.8) | data formatting | bytes 3686400 | tf_op jit(solution)/shard_map/convert_element_type | solution.py:171
  (40 shorter events, 0.5 us)
Async XLA Ops:
  0.0 2.4 %copy-start = (bf16[32,32,900]{2,1,0:T(8,128)(2,1)S(1)}, bf16[32,32,900]{2,1,0:T(8,128)(2,1)}, u32[]{:S(2)}) copy-start(bf16[32,32,900]{2,1,0:T(8,128)(2,1)} %param.7) | copy-start | bytes 5529604
  4.1 15.1 %copy-start.6 = (s32[9,2]{0,1:T(2,128)S(1)}, s32[9,2]{0,1:T(2,128)}, u32[]{:S(2)}) copy-start(s32[9,2]{0,1:T(2,128)} %param.8) | copy-start | bytes 220
  4.1 15.4 %copy-start.5 = (f32[32,9]{0,1:T(8,128)S(1)}, f32[32,9]{0,1:T(8,128)}, u32[]{:S(2)}) copy-start(f32[32,9]{0,1:T(8,128)} %param.9) | copy-start | bytes 3460
  4.1 15.6 %copy-start.2 = (bf16[2,64,32,32]{1,3,2,0:T(8,128)(2,1)S(1)}, bf16[2,64,32,32]{1,3,2,0:T(8,128)(2,1)}, u32[]{:S(2)}) copy-start(bf16[2,64,32,32]{1,3,2,0:T(8,128)(2,1)} %param.13) | copy-start | bytes 786436
  4.1 34.1 %all-to-all-start = ((bf16[32,16,256]{2,1,0:T(8,128)(2,1)}), bf16[32,16,256]{2,1,0:T(8,128)(2,1)S(1)}, u32[]{:S(2)}, u32[]{:S(2)}) async-start(bf16[32,16,256]{2,1,0:T(8,128)(2,1)} %convert_element_type.101), calls=%async_computation | async-start | bytes 524288 | tf_op jit(solution)/shard_map/all_to_all | solution.py:48
  11.4 9.2 %copy-start.7 = (s32[128]{0:T(128)S(1)}, s32[128]{0:T(128)}, u32[]{:S(2)}) copy-start(s32[128]{0:T(128)} %param.12) | copy-start | bytes 1540
  11.5 9.2 %copy-start.8 = (f32[128]{0:T(128)S(1)}, f32[128]{0:T(128)}, u32[]{:S(2)}) copy-start(f32[128]{0:T(128)} %param.11) | copy-start | bytes 1540
  14.3 7.2 %collective-permute-start = (bf16[32,2,900]{2,0,1:T(8,128)(2,1)S(1)}, bf16[32,2,900]{2,0,1:T(8,128)(2,1)S(1)}, u32[]{:S(2)}, u32[]{:S(2)}) collective-permute-start(bf16[32,2,900]{2,0,1:T(8,128)(2,1)S(1)} %get-tuple-element.11), channel_id=1, source_target_pairs={{0,4},{4,8},{8,12},{12,16},{16,20},{20,24},{24,28},{1,5},{5,9},{9,... | collective-permute-start | bytes 345608 | tf_op jit(solution)/shard_map/ppermute | solution.py:54
  17.9 7.3 %collective-permute-start.1 = (bf16[32,2,900]{2,0,1:T(8,128)(2,1)S(1)}, bf16[32,2,900]{2,0,1:T(8,128)(2,1)}, u32[]{:S(2)}, u32[]{:S(2)}) collective-permute-start(bf16[32,2,900]{2,0,1:T(8,128)(2,1)S(1)} %get-tuple-element.12), channel_id=1, source_target_pairs={{4,0},{8,4},{12,8},{16,12},{20,16},{24,20},{28,24},{5,1},{9,5},{13... | collective-permute-start | bytes 345608 | tf_op jit(solution)/shard_map/ppermute | solution.py:51
  21.4 11.7 %copy-start.1 = (bf16[32,2,900]{2,0,1:T(8,128)(2,1)}, bf16[32,2,900]{2,0,1:T(8,128)(2,1)S(1)}, u32[]{:S(2)}) copy-start(bf16[32,2,900]{2,0,1:T(8,128)(2,1)S(1)} %collective-permute-done) | copy-start | bytes 345604
  26.8 8.6 %collective-permute-start.2 = (bf16[2,1280]{1,0:T(2,128)(2,1)S(1)}, bf16[2,1280]{1,0:T(2,128)(2,1)S(1)}, u32[]{:S(2)}, u32[]{:S(2)}) collective-permute-start(bf16[2,1280]{1,0:T(2,128)(2,1)S(1)} %reshape.402), channel_id=1, source_target_pairs={{1,0},{2,1},{3,2},{0,3},{5,4},{6,5},{7,6},{4,7},{9,8},{10,9},{11,1... | collective-permute-start | bytes 15368 | tf_op jit(solution)/shard_map/ppermute | solution.py:68
  27.4 9.3 %collective-permute-start.3 = (bf16[2,1280]{1,0:T(2,128)(2,1)S(1)}, bf16[2,1280]{1,0:T(2,128)(2,1)S(1)}, u32[]{:S(2)}, u32[]{:S(2)}) collective-permute-start(bf16[2,1280]{1,0:T(2,128)(2,1)S(1)} %reshape.404), channel_id=1, source_target_pairs={{0,1},{1,2},{2,3},{3,0},{4,5},{5,6},{6,7},{7,4},{8,9},{9,10},{10,1... | collective-permute-start | bytes 15368 | tf_op jit(solution)/shard_map/ppermute | solution.py:75
  35.2 4.8 %copy-start.4 = (bf16[2,64,128]{2,1,0:T(8,128)(2,1)S(1)}, bf16[2,64,128]{2,1,0:T(8,128)(2,1)}, u32[]{:S(2)}) copy-start(bf16[2,64,128]{2,1,0:T(8,128)(2,1)} %param.10) | copy-start | bytes 98308
  46.3 17.1 %all-to-all-start.1 = ((bf16[32,16,256]{2,1,0:T(8,128)(2,1)}), bf16[32,16,256]{2,1,0:T(8,128)(2,1)S(1)}, u32[]{:S(2)}, u32[]{:S(2)}) async-start(bf16[32,16,256]{2,1,0:T(8,128)(2,1)} %reshape.401), calls=%async_computation.1 | async-start | bytes 524288 | tf_op jit(solution)/shard_map/all_to_all | solution.py:161
  56.5 7.3 %copy-start.3 = (bf16[128,900]{1,0:T(8,128)(2,1)S(1)}, bf16[128,900]{1,0:T(8,128)(2,1)}, u32[]{:S(2)}) copy-start(bf16[128,900]{1,0:T(8,128)(2,1)} %convert_element_type.110) | copy-start | bytes 691204

commit v15 on v14

--- a/solution.py
+++ b/solution.py
@@ -58,25 +58,11 @@
         [north, field, south, jnp.zeros((channels, 4, lon_cols), field.dtype)], axis=1
     )
     rim_rows = rows_ext.shape[1]
-    def lane_dense(edge):
-        return jnp.transpose(edge, (2, 0, 1)).reshape(2, channels * rim_rows)
-
-    def from_lanes(packed):
-        return jnp.transpose(packed.reshape(2, channels, rim_rows), (1, 2, 0))
-
-    east = from_lanes(
-        lax.ppermute(
-            lane_dense(rows_ext[:, :, :2]),
-            "lon",
-            [((i + 1) % lon_count, i) for i in range(lon_count)],
-        )
-    )
-    west = from_lanes(
-        lax.ppermute(
-            lane_dense(rows_ext[:, :, lon_cols - 2 :]),
-            "lon",
-            [(i, (i + 1) % lon_count) for i in range(lon_count)],
-        )
+    east = lax.ppermute(
+        rows_ext[:, :, :2], "lon", [((i + 1) % lon_count, i) for i in range(lon_count)]
+    )
+    west = lax.ppermute(
+        rows_ext[:, :, lon_cols - 2 :], "lon", [(i, (i + 1) % lon_count) for i in range(lon_count)]
     )
     rim = jnp.concatenate(
         [
@@ -130,22 +116,19 @@
     leg_same = jnp.where(same, legendre, zero)
     leg_diff = jnp.where(same, zero, legendre)
     coeffs = jnp.einsum(
-        "mli,mpci->mlpc", leg_same, even_terms, preferred_element_type=jnp.float32
-    ) + jnp.einsum("mli,mpci->mlpc", leg_diff, odd_terms, preferred_element_type=jnp.float32)
+        "mli,mpci->mpcl", leg_same, even_terms, preferred_element_type=jnp.float32
+    ) + jnp.einsum("mli,mpci->mpcl", leg_diff, odd_terms, preferred_element_type=jnp.float32)
     triangle = (degrees[None, :] >= mine[:, None]).astype(jnp.float32)
-    coeffs = (coeffs * triangle[:, :, None, None]).astype(jnp.bfloat16)
-    with_real = jnp.einsum(
-        "mlpc,lcd->mlpd", coeffs, mix_weight[0], preferred_element_type=jnp.float32
-    )
-    with_imag = jnp.einsum(
-        "mlpc,lcd->mlpd", coeffs, mix_weight[1], preferred_element_type=jnp.float32
-    )
+    coeffs = (coeffs * triangle[:, None, None, :]).astype(jnp.bfloat16).astype(jnp.float32)
+    w_real = jnp.transpose(mix_weight[0], (1, 2, 0)).astype(jnp.float32)
+    w_imag = jnp.transpose(mix_weight[1], (1, 2, 0)).astype(jnp.float32)
+    with_real = jnp.sum(coeffs[:, :, :, None, :] * w_real[None, None], axis=2)
+    with_imag = jnp.sum(coeffs[:, :, :, None, :] * w_imag[None, None], axis=2)
     mixed = jnp.stack(
-        [with_real[:, :, 0] - with_imag[:, :, 1], with_real[:, :, 1] + with_imag[:, :, 0]],
-        axis=2,
+        [with_real[:, 0] - with_imag[:, 1], with_real[:, 1] + with_imag[:, 0]], axis=1
     ).astype(jnp.bfloat16)
-    even_sum = jnp.einsum("mli,mlpc->mpci", leg_same, mixed, preferred_element_type=jnp.float32)
-    odd_sum = jnp.einsum("mli,mlpc->mpci", leg_diff, mixed, preferred_element_type=jnp.float32)
+    even_sum = jnp.einsum("mli,mpdl->mpdi", leg_same, mixed, preferred_element_type=jnp.float32)
+    odd_sum = jnp.einsum("mli,mpdl->mpdi", leg_diff, mixed, preferred_element_type=jnp.float32)
     north_out = (even_sum + odd_sum) * kept_mask[:, None, None, :]
     south_out = (even_sum - odd_sum) * kept_mask[:, None, None, :]
     grid_spectrum = jnp.concatenate([north_out, jnp.flip(south_out, axis=3)], axis=3).astype(

time: 68.6 us -> 73.3 us (1.069)
  other arithmetic: 9.07 us -> 16.1 us
  waiting for transfers between devices: 4.46 us -> 0.02 us
  starting transfers between devices: 18.5 us -> 20.8 us
  matrix products: 6.36 us -> 5.24 us
    unnamed x23 -> x17, local copies, waits for them, and re-layouts: 7.9 us -> 2.96 us
    ppermute x1, waiting for transfers between devices: 3.79 us -> 0.01 us  [per_device(): lax.ppermute(field[:, :2], 'lat', [(i + 1, i) for i in range(lat_n - 1)])]
    reshape x6 -> x0, local copies, waits for them, and re-layouts: 3.1 us -> none  [the longest x4 2.89 us: from_lanes(): return jnp.transpose(packed.reshape(2, channels, rim_rows), (1, 2, 0))]
    transpose x1, local copies, waits for them, and re-layouts: 0.31 us -> 2.14 us  [per_device(): jnp.transpose(summed, (1, 2, 3, 0, 4))]
    slice x0 -> x1, other arithmetic: none -> 1.76 us  [per_device(): rows_ext[:, :, :2]]
    reshape x1, local copies, waits for them, and re-layouts: 0.25 us -> 1.99 us  [per_device(): summed = gathered.astype(jnp.float32).reshape(lat_count, lon_count, m_dev...]
    reshape x1, local copies, waits for them, and re-layouts: 0.17 us -> 1.87 us  [per_device(): summed = summed.reshape(lat_count, m_dev, 2, channels, lat_rows)]
    reshape x1, local copies, waits for them, and re-layouts: 0.18 us -> 1.88 us  [per_device(): jnp.transpose(summed, (1, 2, 3, 0, 4))]
  transfers between devices with their start and end apart: 6 -> 6, of which waited for: 2 -> 0; matrix products, arithmetic and copies ran while one was open for 31% -> 49% of each run, Pallas kernels for 10% -> 10%
where the time goes in v15:
time: 73.3 us; the launch traced here: 72.3 us
  local copies, waits for them, and re-layouts  22.6 us (31%)
  starting transfers between devices  20.8 us (28%)
  other arithmetic  16.1 us (22%)
  Pallas kernels  7.3 us (10%)
  matrix products  5.24 us (7%)
    all_to_all x1, starting transfers between devices, per_device(): lax.all_to_all(partial.astype(jnp.bfloat16), BOTH, 0, 0, tiled=True)  7.44 us
    pallas_call x1, Pallas kernels, depthwise_conv(): pl.pallas_call(body, grid_spec=pltpu.PrefetchScalarGridSpec(num_scalar_pr...  7.3 us
    all_to_all x1, starting transfers between devices, per_device(): full_rows = lax.all_to_all(outgoing, BOTH, 0, 0, tiled=True)  6.88 us
    transpose x1, other arithmetic, depthwise_conv(): by_rows = jnp.transpose(rim, (1, 0, 2))  4.48 us
    ppermute x1, starting transfers between devices, per_device(): lax.ppermute(field[:, lat_rows - 2:], 'lat', [(i, i + 1) for i in range(l...  4.24 us
    another operation x5, other arithmetic  3.28 us
    unnamed x17, local copies, waits for them, and re-layouts  2.96 us
    convert_element_type x1, local copies, waits for them, and re-layouts, per_device(): (conv_out.astype(jnp.float32) + jax.nn.gelu(synthesis, approximate=True))...  2.47 us
  transfers between devices with their start and end apart: 6, of which 0 were waited for; matrix products, arithmetic and copies ran while one was open for 49% of the time, Pallas kernels for 10%

profile of v15, /device:TPU:0, one launch (start us, length us, event | category | flops | bytes accessed | tf_op | source)
XLA Modules:
  0.0 72.3 jit_solution(7234244990041041292)
XLA Ops:
  0.0 1.2 %multiply_convert_fusion.1 = (bf16[64,1,900]{2,0,1:T(8,128)(2,1)S(1)}, bf16[64,1,900]{2,0,1:T(8,128)(2,1)S(1)}, bf16[64,1,900]{2,0,1:T(8,128)(2,1)S(1)}, bf16[64,1,900]{2,0,1:T(8,128)(2,1)S(1)}) fusion(f32[64]{0:T(128)S(1)} %fusion.56, s32[900]{0:T(1024)S(1)} %iota_add_fusion, f32[64]{0:T(128)S(1)} %fusion.59), kind=kLoop, calls=%fused_computation.43 | loop fusion | flops 979200 | bytes 464912 | tf_op jit(solution)/shard_map/convert.9
  1.2 0.8 %pad_maximum_fusion.4 = (bf16[64,2,900]{2,0,1:T(8,128)(2,1)S(1)}, bf16[64,2,900]{2,0,1:T(8,128)(2,1)}) fusion(bf16[64,1,900]{2,0,1:T(8,128)(2,1)S(1)} %get-tuple-element.33, bf16[64,1,900]{2,0,1:T(8,128)(2,1)S(1)} %get-tuple-element.34, bf16[64,1,900]{2,0,1:T(8,128)(2,1)S(1)} %get-tuple-element.32, bf16[64,1,900]{2,0,1:T(8,128)(2,1)S(1)} %get-tuple-element.31), kind=kLoop, calls=%fused_computation.37 | loop fusion | flops 230400 | bytes 921600 | tf_op jit(solution)/shard_map/stack | solution.py:21
  2.0 0.3 copy.64
  2.2 0.2 convert_element_type.120
  2.4 0.0 copy-done
  2.4 0.8 %convolution_convert_fusion = bf16[128,1024]{1,0:T(8,128)(2,1)S(1)} fusion(bf16[128,900]{1,0:T(8,128)(2,1)S(1)} %convert_element_type.120, bf16[1024,900]{1,0:T(8,128)(2,1)S(1)} %bitcast.92), kind=kOutput, calls=%fused_computation.13 | convolution fusion | flops 236060672 | bytes 2335744 | tf_op jit(solution)/shard_map/dot_general | solution.py:45
  3.3 0.9 %convert_element_type.122 = bf16[32,16,256]{2,1,0:T(8,128)(2,1)} reshape(bf16[128,1024]{1,0:T(8,128)(2,1)S(1)} %convolution_convert_fusion) | data formatting | bytes 524288 | tf_op jit(solution)/shard_map/convert_element_type | solution.py:48
  4.1 7.4 %all-to-all-start = ((bf16[32,16,256]{2,1,0:T(8,128)(2,1)}), bf16[32,16,256]{2,1,0:T(8,128)(2,1)}, u32[]{:S(2)}, u32[]{:S(2)}) async-start(bf16[32,16,256]{2,1,0:T(8,128)(2,1)} %convert_element_type.122), calls=%async_computation | async-start | bytes 524288 | tf_op jit(solution)/shard_map/all_to_all | solution.py:48
  11.6 2.7 %copy.67 = bf16[32,32,900]{2,0,1:T(8,128)(2,1)S(1)} copy(bf16[32,32,900]{2,1,0:T(8,128)(2,1)} %param.7) | data formatting | bytes 3686400 | tf_op args[0]
  14.3 0.0 copy-start.5
  14.3 0.0 copy-start.6
  14.3 0.7 fusion.70
  15.1 4.2 %collective-permute-start = (bf16[32,2,900]{2,0,1:T(8,128)(2,1)}, bf16[32,2,900]{2,0,1:T(8,128)(2,1)}, u32[]{:S(2)}, u32[]{:S(2)}) collective-permute-start(bf16[32,2,900]{2,0,1:T(8,128)(2,1)} %get-tuple-element.13), channel_id=1, source_target_pairs={{0,4},{4,8},{8,12},{12,16},{16,20},{20,24},{24,28},{1,5},{5,9},{9,... | collective-permute-start | bytes 345608 | tf_op jit(solution)/shard_map/ppermute | solution.py:54
  19.3 1.3 %collective-permute-start.1 = (bf16[32,2,900]{2,0,1:T(8,128)(2,1)}, bf16[32,2,900]{2,0,1:T(8,128)(2,1)}, u32[]{:S(2)}, u32[]{:S(2)}) collective-permute-start(bf16[32,2,900]{2,0,1:T(8,128)(2,1)} %get-tuple-element.14), channel_id=1, source_target_pairs={{4,0},{8,4},{12,8},{16,12},{20,16},{24,20},{28,24},{5,1},{9,5},{13... | collective-permute-start | bytes 345608 | tf_op jit(solution)/shard_map/ppermute | solution.py:51
  20.6 0.1 copy.70.offs_ref
  20.7 0.1 copy.71.w_ref
  20.8 0.1 fusion.58
  20.9 0.1 convert_bitcast_fusion.2
  21.0 0.1 convolution_bitcast_fusion.1
  21.1 0.6 fusion.71
  21.7 0.1 convolution_bitcast_fusion
  21.8 0.6 fusion.72
  22.5 1.1 %convert_bitcast_fusion = (f32[32,32,64]{2,1,0:T(8,128)S(1)}, f32[32,32,64]{2,1,0:T(8,128)S(1)}) fusion(bf16[2,64,32,32]{1,3,2,0:T(8,128)(2,1)} %param.13), kind=kLoop, calls=%fused_computation.20 | loop fusion | flops 131072 | bytes 786432 | tf_op jit(solution)/shard_map/convert_element_type | solution.py:124
  23.6 1.2 %copy.73 = bf16[64,2,900]{2,1,0:T(2,128)(2,1)S(1)} copy(bf16[64,2,900]{2,0,1:T(8,128)(2,1)} %get-tuple-element.44) | data formatting | bytes 460800 | tf_op jit(solution)/shard_map/stack | solution.py:21
  24.8 0.9 %convert_element_type.138 = bf16[128,900]{1,0:T(8,128)(2,1)} reshape(bf16[64,2,900]{2,1,0:T(2,128)(2,1)S(1)} %copy.73) | data formatting | bytes 460800 | tf_op jit(solution)/shard_map/convert_element_type | solution.py:24
  25.7 0.6 fusion.53
  26.4 0.1 pad.12.clone
  26.4 0.7 compare_convert_fusion.1
  27.1 0.1 compare_convert_fusion
  27.2 0.0 collective-permute-done
  27.2 0.0 collective-permute-done.1
  27.2 1.8 %pad_maximum_fusion.3 = (bf16[32,40,2]{2,0,1:T(8,128)(2,1)}, bf16[32,40,2]{2,0,1:T(8,128)(2,1)}) fusion(bf16[32,4,900]{2,0,1:T(8,128)(2,1)S(1)} %broadcast_in_dim.37, bf16[32,2,900]{2,0,1:T(8,128)(2,1)} %collective-permute-done.1, bf16[32,32,900]{2,0,1:T(8,128)(2,1)S(1)} %copy.67, bf16[32,2,900]{2,0,1:T(8,128)(2,1)} %collective-permute-done), kind=kLoop, calls=%fused_computation.34 | loop fusion | flops 40960 | bytes 2314240 | tf_op jit(solution)/shard_map/slice | solution.py:62
  29.0 0.9 %collective-permute-start.2 = (bf16[32,40,2]{2,0,1:T(8,128)(2,1)}, bf16[32,40,2]{2,0,1:T(8,128)(2,1)}, u32[]{:S(2)}, u32[]{:S(2)}) collective-permute-start(bf16[32,40,2]{2,0,1:T(8,128)(2,1)} %get-tuple-element.11), channel_id=1, source_target_pairs={{1,0},{2,1},{3,2},{0,3},{5,4},{6,5},{7,6},{4,7},{9,8},{10,9},{11,1... | collective-permute-start | bytes 15368 | tf_op jit(solution)/shard_map/ppermute | solution.py:61
  29.9 0.0 collective-permute-start.3
  29.9 0.0 all-to-all-done
  29.9 2.0 %reshape.396 = f32[8,4,4096]{2,1,0:T(4,128)} reshape(bf16[32,16,256]{2,1,0:T(8,128)(2,1)} %all-to-all-done) | data formatting | bytes 786432 | tf_op jit(solution)/shard_map/reshape | solution.py:80
  31.9 2.0 %reduce_sum.27 = f32[8,4096]{1,0:T(8,128)} reduce(f32[8,4,4096]{2,1,0:T(4,128)} %reshape.396, f32[]{:T(128)} %constant.34.clone.1), dimensions={1}, to_apply=%region_0.1 | reduce | flops 98304 | bytes 655364 | tf_op jit(solution)/shard_map/reduce_sum | solution.py:81
  33.9 1.9 %reshape.391 = f32[8,2,2,32,32]{4,3,2,1,0:T(8,128)} reshape(f32[8,4096]{1,0:T(8,128)} %reduce_sum.27) | data formatting | bytes 262144 | tf_op jit(solution)/shard_map/reshape | solution.py:83
  35.8 2.1 %copy.65 = f32[2,2,32,8,32]{4,3,2,1,0:T(8,128)} copy(f32[2,2,32,8,32]{4,2,1,0,3:T(8,128)} %bitcast.93) | data formatting | bytes 262144 | tf_op jit(solution)/shard_map/transpose | solution.py:84
  37.9 1.9 %reshape.392 = f32[2,2,32,256]{3,2,1,0:T(8,128)} reshape(f32[2,2,32,8,32]{4,3,2,1,0:T(8,128)} %copy.65) | data formatting | bytes 262144 | tf_op jit(solution)/shard_map/reshape | solution.py:84
  39.8 2.0 %subtract_convert_fusion = (bf16[2,1,32,256]{3,2,1,0:T(8,128)(2,1)S(1)}, bf16[2,1,32,256]{3,2,1,0:T(8,128)(2,1)S(1)}) fusion(f32[2,2,32,256]{3,2,1,0:T(8,128)} %reshape.392, f32[2,32]{1,0:T(2,128)} %bitcast.102, f32[2,32]{1,0:T(2,128)S(1)} %bitcast.97, f32[2,32]{1,0:T(2,128)} %bitcast.103, f32[2,32]{1,0:T(2,128)S(1)} %bitcast.98, f32[2,32]{1,0:T(2,128)} %bitcast.104, ...), kind=kLoop, calls=%fused_computation.63 | loop fusion | flops 655360 | bytes 335616 | tf_op jit(solution)/shard_map/convert.17
  41.8 0.6 pad_maximum_fusion.6
  42.4 1.4 %rev.8 = bf16[2,2,32,128]{3,2,1,0:T(8,128)(2,1)} reverse(bf16[2,2,32,128]{3,2,1,0:T(8,128)(2,1)} %pad_maximum_fusion.6), dimensions={3} | reverse | bytes 65536 | tf_op jit(solution)/shard_map/jit(_flip)/rev | solution.py:108
  43.9 1.0 %fusion.27 = f32[2,2,32,64]{3,2,1,0:T(8,128)S(1)} fusion(bf16[2,2,32,128]{3,2,1,0:T(8,128)(2,1)} %rev.8, f32[2,128]{1,0:T(2,128)} %fusion.53, bf16[2,64,128]{2,1,0:T(8,128)(2,1)S(1)} %copy-done.1, pred[2,64]{1,0:T(4,128)(4,1)S(1)} %get-tuple-element.40, bf16[2,1,32,256]{3,2,1,0:T(8,128)(2,1)S(1)} %get-tuple-element.17, ...), kind=kOutput, calls=%fused_computation.65 | convolution fusion | flops 2211840 | bytes 164992 | tf_op jit(solution)/shard_map/mli,mpci->mpcl/dot_general | solution.py:118
  44.8 1.0 %fusion.11 = f32[2,2,32,64]{3,2,1,0:T(8,128)S(1)} fusion(f32[2,2,32,64]{3,2,1,0:T(8,128)S(1)} %fusion.27, bf16[2,2,32,128]{3,2,1,0:T(8,128)(2,1)} %rev.8, f32[2,64]{1,0:T(2,128)} %get-tuple-element.39, f32[2,128]{1,0:T(2,128)} %fusion.53, bf16[2,64,128]{2,1,0:T(8,128)(2,1)S(1)} %copy-done.1, pred[2,64]{1,0:T(4,128)(4,1)S(1)} %get-tuple-element.40, ...), kind=kOutput, calls=%fused_computation.17 | convolution fusion | flops 2244608 | bytes 198272 | tf_op jit(solution)/shard_map/mli,mpci->mpcl/dot_general | solution.py:120
  45.8 0.4 multiply_reduce_fusion.1
  46.2 0.2 fusion.34
  46.5 0.2 subtract_multiply_fusion
  46.7 0.1 concatenate.15
  46.8 0.1 rev.9
  46.9 0.1 concatenate.16
  47.0 0.2 maximum_bitcast_fusion.1
  47.3 0.2 broadcast_in_dim.36
  47.5 1.4 %reshape.393 = bf16[32,16,256]{2,1,0:T(8,128)(2,1)} reshape(bf16[8,4,2,2,32,32]{5,4,3,2,1,0:T(8,128)(2,1)S(1)} %broadcast_in_dim.36) | data formatting | bytes 524288 | tf_op jit(solution)/shard_map/reshape | solution.py:143
  49.0 6.9 %all-to-all-start.1 = ((bf16[32,16,256]{2,1,0:T(8,128)(2,1)}), bf16[32,16,256]{2,1,0:T(8,128)(2,1)S(1)}, u32[]{:S(2)}, u32[]{:S(2)}) async-start(bf16[32,16,256]{2,1,0:T(8,128)(2,1)} %reshape.393), calls=%async_computation.1 | async-start | bytes 524288 | tf_op jit(solution)/shard_map/all_to_all | solution.py:144
  55.8 0.0 collective-permute-done.2
  55.9 0.0 collective-permute-done.3
  55.9 4.5 %maximum_bitcast_fusion.rim_ref = bf16[40,32,1024]{2,1,0:T(8,128)(2,1)S(1)} fusion(bf16[32,40,2]{2,0,1:T(8,128)(2,1)} %collective-permute-done.3, bf16[32,40,2]{2,0,1:T(8,128)(2,1)} %collective-permute-done.2, bf16[32,4,900]{2,0,1:T(8,128)(2,1)S(1)} %broadcast_in_dim.37, bf16[32,2,900]{2,0,1:T(8,128)(2,1)} %collective-permute-done.1, ...), kind=kLoop, calls=%fused_computation.10 | loop fusion | flops 18350080 | bytes 4937728 | tf_op jit(solution)/shard_map/transpose | solution.py:161
  60.4 7.3 %shard_map.73 = bf16[32,32,900]{2,1,0:T(8,128)(2,1)S(1)} custom-call(s32[9,2]{1,0:T(8,128)S(1)} %copy.70.offs_ref, bf16[40,32,1024]{2,1,0:T(8,128)(2,1)S(1)} %maximum_bitcast_fusion.rim_ref, f32[32,9]{1,0:T(8,128)S(1)} %copy.71.w_ref), custom_call_target="tpu_custom_call" | custom-call | flops 94371840 | bytes 4464640 | tf_op jit(solution)/shard_map/pallas_call | solution.py:184
  67.7 0.0 all-to-all-done.1
  67.7 0.2 reshape.394
  67.9 0.2 copy.72
  68.0 1.8 %fusion.8 = bf16[32,32,900]{2,0,1:T(8,128)(2,1)S(1)} fusion(bf16[32,32,900]{2,0,1:T(8,128)(2,1)S(1)} %bitcast.91, bf16[128,900]{1,0:T(8,128)(2,1)S(1)} %copy-done.2, bf16[32,32,128]{2,1,0:T(8,128)(2,1)S(1)} %bitcast.95), kind=kOutput, calls=%fused_computation.9 | convolution fusion | flops 246067200 | bytes 4178944 | tf_op jit(solution)/shard_map/dot_general | solution.py:150
  69.9 2.5 %copy.80 = bf16[32,32,900]{2,1,0:T(8,128)(2,1)} copy(bf16[32,32,900]{2,0,1:T(8,128)(2,1)S(1)} %fusion.8) | data formatting | bytes 3686400 | tf_op jit(solution)/shard_map/convert_element_type | solution.py:154
  (22 shorter events, 0.1 us)
Async XLA Ops:
  0.0 2.4 %copy-start = (bf16[32,32,900]{2,1,0:T(8,128)(2,1)S(1)}, bf16[32,32,900]{2,1,0:T(8,128)(2,1)}, u32[]{:S(2)}) copy-start(bf16[32,32,900]{2,1,0:T(8,128)(2,1)} %param.7) | copy-start | bytes 5529604
  4.1 16.5 %copy-start.4 = (s32[9,2]{0,1:T(2,128)S(1)}, s32[9,2]{0,1:T(2,128)}, u32[]{:S(2)}) copy-start(s32[9,2]{0,1:T(2,128)} %param.8) | copy-start | bytes 220
  4.1 16.6 %copy-start.3 = (f32[32,9]{0,1:T(8,128)S(1)}, f32[32,9]{0,1:T(8,128)}, u32[]{:S(2)}) copy-start(f32[32,9]{0,1:T(8,128)} %param.9) | copy-start | bytes 3460
  4.1 25.8 %all-to-all-start = ((bf16[32,16,256]{2,1,0:T(8,128)(2,1)}), bf16[32,16,256]{2,1,0:T(8,128)(2,1)}, u32[]{:S(2)}, u32[]{:S(2)}) async-start(bf16[32,16,256]{2,1,0:T(8,128)(2,1)} %convert_element_type.122), calls=%async_computation | async-start | bytes 524288 | tf_op jit(solution)/shard_map/all_to_all | solution.py:48
  14.3 11.4 %copy-start.5 = (s32[128]{0:T(128)S(1)}, s32[128]{0:T(128)}, u32[]{:S(2)}) copy-start(s32[128]{0:T(128)} %param.12) | copy-start | bytes 1540
  14.3 11.4 %copy-start.6 = (f32[128]{0:T(128)S(1)}, f32[128]{0:T(128)}, u32[]{:S(2)}) copy-start(f32[128]{0:T(128)} %param.11) | copy-start | bytes 1540
  15.1 12.1 %collective-permute-start = (bf16[32,2,900]{2,0,1:T(8,128)(2,1)}, bf16[32,2,900]{2,0,1:T(8,128)(2,1)}, u32[]{:S(2)}, u32[]{:S(2)}) collective-permute-start(bf16[32,2,900]{2,0,1:T(8,128)(2,1)} %get-tuple-element.13), channel_id=1, source_target_pairs={{0,4},{4,8},{8,12},{12,16},{16,20},{20,24},{24,28},{1,5},{5,9},{9,... | collective-permute-start | bytes 345608 | tf_op jit(solution)/shard_map/ppermute | solution.py:54
  19.3 7.9 %collective-permute-start.1 = (bf16[32,2,900]{2,0,1:T(8,128)(2,1)}, bf16[32,2,900]{2,0,1:T(8,128)(2,1)}, u32[]{:S(2)}, u32[]{:S(2)}) collective-permute-start(bf16[32,2,900]{2,0,1:T(8,128)(2,1)} %get-tuple-element.14), channel_id=1, source_target_pairs={{4,0},{8,4},{12,8},{16,12},{20,16},{24,20},{28,24},{5,1},{9,5},{13... | collective-permute-start | bytes 345608 | tf_op jit(solution)/shard_map/ppermute | solution.py:51
  29.0 14.9 %copy-start.1 = (bf16[2,64,128]{2,1,0:T(8,128)(2,1)S(1)}, bf16[2,64,128]{2,1,0:T(8,128)(2,1)}, u32[]{:S(2)}) copy-start(bf16[2,64,128]{2,1,0:T(8,128)(2,1)} %param.10) | copy-start | bytes 98308
  29.0 26.9 %collective-permute-start.2 = (bf16[32,40,2]{2,0,1:T(8,128)(2,1)}, bf16[32,40,2]{2,0,1:T(8,128)(2,1)}, u32[]{:S(2)}, u32[]{:S(2)}) collective-permute-start(bf16[32,40,2]{2,0,1:T(8,128)(2,1)} %get-tuple-element.11), channel_id=1, source_target_pairs={{1,0},{2,1},{3,2},{0,3},{5,4},{6,5},{7,6},{4,7},{9,8},{10,9},{11,1... | collective-permute-start | bytes 15368 | tf_op jit(solution)/shard_map/ppermute | solution.py:61
  29.9 26.0 %collective-permute-start.3 = (bf16[32,40,2]{2,0,1:T(8,128)(2,1)}, bf16[32,40,2]{2,0,1:T(8,128)(2,1)}, u32[]{:S(2)}, u32[]{:S(2)}) collective-permute-start(bf16[32,40,2]{2,0,1:T(8,128)(2,1)} %get-tuple-element.12), channel_id=1, source_target_pairs={{0,1},{1,2},{2,3},{3,0},{4,5},{5,6},{6,7},{7,4},{8,9},{9,10},{10,1... | collective-permute-start | bytes 15368 | tf_op jit(solution)/shard_map/ppermute | solution.py:64
  49.0 18.7 %all-to-all-start.1 = ((bf16[32,16,256]{2,1,0:T(8,128)(2,1)}), bf16[32,16,256]{2,1,0:T(8,128)(2,1)S(1)}, u32[]{:S(2)}, u32[]{:S(2)}) async-start(bf16[32,16,256]{2,1,0:T(8,128)(2,1)} %reshape.393), calls=%async_computation.1 | async-start | bytes 524288 | tf_op jit(solution)/shard_map/all_to_all | solution.py:144
  60.4 7.7 %copy-start.2 = (bf16[128,900]{1,0:T(8,128)(2,1)S(1)}, bf16[128,900]{1,0:T(8,128)(2,1)}, u32[]{:S(2)}) copy-start(bf16[128,900]{1,0:T(8,128)(2,1)} %convert_element_type.138) | copy-start | bytes 691204

commit v16 on v14

--- a/solution.py
+++ b/solution.py
@@ -58,25 +58,11 @@
         [north, field, south, jnp.zeros((channels, 4, lon_cols), field.dtype)], axis=1
     )
     rim_rows = rows_ext.shape[1]
-    def lane_dense(edge):
-        return jnp.transpose(edge, (2, 0, 1)).reshape(2, channels * rim_rows)
-
-    def from_lanes(packed):
-        return jnp.transpose(packed.reshape(2, channels, rim_rows), (1, 2, 0))
-
-    east = from_lanes(
-        lax.ppermute(
-            lane_dense(rows_ext[:, :, :2]),
-            "lon",
-            [((i + 1) % lon_count, i) for i in range(lon_count)],
-        )
-    )
-    west = from_lanes(
-        lax.ppermute(
-            lane_dense(rows_ext[:, :, lon_cols - 2 :]),
-            "lon",
-            [(i, (i + 1) % lon_count) for i in range(lon_count)],
-        )
+    east = lax.ppermute(
+        rows_ext[:, :, :2], "lon", [((i + 1) % lon_count, i) for i in range(lon_count)]
+    )
+    west = lax.ppermute(
+        rows_ext[:, :, lon_cols - 2 :], "lon", [(i, (i + 1) % lon_count) for i in range(lon_count)]
     )
     rim = jnp.concatenate(
         [

time: 68.6 us -> 61 us (0.89)
  local copies, waits for them, and re-layouts: 22.4 us -> 17.3 us
  waiting for transfers between devices: 4.46 us -> 0.02 us
  starting transfers between devices: 18.5 us -> 20.1 us
    ppermute x1, waiting for transfers between devices: 3.79 us -> 0.01 us  [per_device(): lax.ppermute(field[:, :2], 'lat', [(i + 1, i) for i in range(lat_n - 1)])]
    reshape x6 -> x0, local copies, waits for them, and re-layouts: 3.1 us -> none  [the longest x4 2.89 us: from_lanes(): return jnp.transpose(packed.reshape(2, channels, rim_rows), (1, 2, 0))]
    unnamed x23, local copies, waits for them, and re-layouts: 7.9 us -> 6.01 us
    all_to_all x1, starting transfers between devices: 5.62 us -> 6.89 us  [per_device(): full_rows = lax.all_to_all(outgoing, BOTH, 0, 0, tiled=True)]
    slice x0 -> x1, other arithmetic: none -> 1.02 us  [per_device(): rows_ext[:, :, :2]]
    another operation x2, local copies, waits for them, and re-layouts: 1.49 us -> 0.54 us  [wave_table(): jnp.stack([factor[:, None] * jnp.cos(angles), -factor[:, None] * jnp.sin(...]
    transpose x1 -> x0, other arithmetic: 0.93 us -> none  [lane_dense(): return jnp.transpose(edge, (2, 0, 1)).reshape(2, channels * rim_rows)]
    transpose x2 -> x0, local copies, waits for them, and re-layouts: 0.92 us -> none  [lane_dense(): return jnp.transpose(edge, (2, 0, 1)).reshape(2, channels * rim_rows)]
  transfers between devices with their start and end apart: 6 -> 6, of which waited for: 2 -> 0; matrix products, arithmetic and copies ran while one was open for 31% -> 41% of each run, Pallas kernels for 10% -> 12%
where the time goes in v16:
time: 61 us; the launch traced here: 60.5 us
  starting transfers between devices  20.1 us (33%)
  local copies, waits for them, and re-layouts  17.3 us (28%)
  other arithmetic  9.07 us (15%)
  Pallas kernels  7.3 us (12%)
  matrix products  6.35 us (10%)
    all_to_all x1, starting transfers between devices, per_device(): lax.all_to_all(partial.astype(jnp.bfloat16), BOTH, 0, 0, tiled=True)  7.3 us
    pallas_call x1, Pallas kernels, depthwise_conv(): pl.pallas_call(body, grid_spec=pltpu.PrefetchScalarGridSpec(num_scalar_pr...  7.3 us
    all_to_all x1, starting transfers between devices, per_device(): full_rows = lax.all_to_all(outgoing, BOTH, 0, 0, tiled=True)  6.89 us
    unnamed x23, local copies, waits for them, and re-layouts  6.01 us
    transpose x1, other arithmetic, depthwise_conv(): by_rows = jnp.transpose(rim, (1, 0, 2))  4.48 us
    ppermute x1, starting transfers between devices, per_device(): lax.ppermute(field[:, lat_rows - 2:], 'lat', [(i, i + 1) for i in range(l...  3.67 us
    convert_element_type x1, local copies, waits for them, and re-layouts, per_device(): (conv_out.astype(jnp.float32) + jax.nn.gelu(synthesis, approximate=True))...  2.47 us
    another operation x5, other arithmetic  1.84 us
  transfers between devices with their start and end apart: 6, of which 0 were waited for; matrix products, arithmetic and copies ran while one was open for 41% of the time, Pallas kernels for 12%

profile of v16, /device:TPU:0, one launch (start us, length us, event | category | flops | bytes accessed | tf_op | source)
XLA Modules:
  0.0 60.5 jit_solution(12504339294828933992)
XLA Ops:
  0.0 1.2 %multiply_convert_fusion.1 = (bf16[64,1,900]{2,0,1:T(8,128)(2,1)S(1)}, bf16[64,1,900]{2,0,1:T(8,128)(2,1)S(1)}, bf16[64,1,900]{2,0,1:T(8,128)(2,1)S(1)}, bf16[64,1,900]{2,0,1:T(8,128)(2,1)S(1)}) fusion(f32[64]{0:T(128)S(1)} %fusion.57, s32[900]{0:T(1024)S(1)} %iota_add_fusion, f32[64]{0:T(128)S(1)} %fusion.60), kind=kLoop, calls=%fused_computation.42 | loop fusion | flops 979200 | bytes 464912 | tf_op jit(solution)/shard_map/convert.5
  1.2 0.1 pad_maximum_fusion.4
  1.3 0.3 copy.67
  1.6 0.2 convert_element_type.99
  1.7 0.8 %convolution_convert_fusion = bf16[128,1024]{1,0:T(8,128)(2,1)S(1)} fusion(bf16[128,900]{1,0:T(8,128)(2,1)S(1)} %convert_element_type.99, bf16[1024,900]{1,0:T(8,128)(2,1)S(1)} %bitcast.102), kind=kOutput, calls=%fused_computation.11 | convolution fusion | flops 236060672 | bytes 2335744 | tf_op jit(solution)/shard_map/dot_general | solution.py:45
  2.6 0.9 %convert_element_type.101 = bf16[32,16,256]{2,1,0:T(8,128)(2,1)} reshape(bf16[128,1024]{1,0:T(8,128)(2,1)S(1)} %convolution_convert_fusion) | data formatting | bytes 524288 | tf_op jit(solution)/shard_map/convert_element_type | solution.py:48
  3.4 7.3 %all-to-all-start = ((bf16[32,16,256]{2,1,0:T(8,128)(2,1)}), bf16[32,16,256]{2,1,0:T(8,128)(2,1)S(1)}, u32[]{:S(2)}, u32[]{:S(2)}) async-start(bf16[32,16,256]{2,1,0:T(8,128)(2,1)} %convert_element_type.101), calls=%async_computation | async-start | bytes 524288 | tf_op jit(solution)/shard_map/all_to_all | solution.py:48
  10.7 2.7 %copy.76 = bf16[32,32,900]{2,0,1:T(8,128)(2,1)S(1)} copy(bf16[32,32,900]{2,1,0:T(8,128)(2,1)} %param.7) | data formatting | bytes 3686400 | tf_op args[0]
  13.5 0.0 copy-start.7
  13.5 0.0 copy-start.8
  13.5 0.7 %fusion.69 = (bf16[32,2,900]{2,0,1:T(8,128)(2,1)}, bf16[32,2,900]{2,0,1:T(8,128)(2,1)}) fusion(bf16[32,32,900]{2,0,1:T(8,128)(2,1)S(1)} %copy.76), kind=kLoop, calls=%fused_computation.120 | loop fusion | bytes 460800 | tf_op jit(solution)/shard_map/slice | solution.py:55
  14.2 3.7 %collective-permute-start = (bf16[32,2,900]{2,0,1:T(8,128)(2,1)}, bf16[32,2,900]{2,0,1:T(8,128)(2,1)S(1)}, u32[]{:S(2)}, u32[]{:S(2)}) collective-permute-start(bf16[32,2,900]{2,0,1:T(8,128)(2,1)} %get-tuple-element.11), channel_id=1, source_target_pairs={{0,4},{4,8},{8,12},{12,16},{16,20},{20,24},{24,28},{1,5},{5,9},{9,... | collective-permute-start | bytes 345608 | tf_op jit(solution)/shard_map/ppermute | solution.py:54
  17.9 1.3 %collective-permute-start.1 = (bf16[32,2,900]{2,0,1:T(8,128)(2,1)}, bf16[32,2,900]{2,0,1:T(8,128)(2,1)S(1)}, u32[]{:S(2)}, u32[]{:S(2)}) collective-permute-start(bf16[32,2,900]{2,0,1:T(8,128)(2,1)} %get-tuple-element.12), channel_id=1, source_target_pairs={{4,0},{8,4},{12,8},{16,12},{20,16},{24,20},{28,24},{5,1},{9,5},{13... | collective-permute-start | bytes 345608 | tf_op jit(solution)/shard_map/ppermute | solution.py:51
  19.2 0.1 copy.79.offs_ref
  19.3 0.1 copy.80.w_ref
  19.4 0.1 fusion.59
  19.5 0.1 convert_bitcast_fusion
  19.6 0.1 convolution_bitcast_fusion.2
  19.8 0.1 convolution_bitcast_fusion.3
  19.9 1.1 %fusion.70 = (bf16[1,64,32,32]{1,3,2,0:T(8,128)(2,1)S(1)}, bf16[1,64,32,32]{1,3,2,0:T(8,128)(2,1)S(1)}) fusion(bf16[2,64,32,32]{1,3,2,0:T(8,128)(2,1)} %param.13), kind=kLoop, calls=%fused_computation.121 | loop fusion | bytes 524288 | tf_op jit(solution)/shard_map/slice | solution.py:124
  21.0 1.5 %copy.99 = bf16[1,64,32,32]{3,2,1,0:T(8,128)(2,1)} copy(bf16[1,64,32,32]{1,3,2,0:T(8,128)(2,1)S(1)} %get-tuple-element.14) | data formatting | bytes 262144
  22.5 1.5 %copy.98 = bf16[1,64,32,32]{3,2,1,0:T(8,128)(2,1)} copy(bf16[1,64,32,32]{1,3,2,0:T(8,128)(2,1)S(1)} %get-tuple-element.13) | data formatting | bytes 262144
  24.0 0.3 copy.82
  24.3 0.9 %convert_element_type.110 = bf16[128,900]{1,0:T(8,128)(2,1)} reshape(bf16[64,2,900]{2,1,0:T(2,128)(2,1)S(1)} %copy.82) | data formatting | bytes 460800 | tf_op jit(solution)/shard_map/convert_element_type | solution.py:24
  25.1 0.1 fusion.55
  25.2 0.1 pad.12.clone
  25.3 0.1 compare_convert_fusion.1
  25.4 0.1 compare_convert_fusion
  25.5 0.0 collective-permute-done
  25.5 0.0 collective-permute-done.1
  25.5 1.0 %pad_maximum_fusion.3 = (bf16[32,40,2]{2,0,1:T(8,128)(2,1)}, bf16[32,40,2]{2,0,1:T(8,128)(2,1)}) fusion(bf16[32,4,900]{2,0,1:T(8,128)(2,1)S(1)} %broadcast_in_dim.37, bf16[32,2,900]{2,0,1:T(8,128)(2,1)S(1)} %collective-permute-done.1, bf16[32,32,900]{2,0,1:T(8,128)(2,1)S(1)} %copy.76, bf16[32,2,900]{2,0,1:T(8,128)(2,1)S(1)} %collective-permute-done), kind=kLoop, calls=%fused_computation.33 | loop fusion | flops 40960 | bytes 2314240 | tf_op jit(solution)/shard_map/slice | solution.py:62
  26.5 0.9 %collective-permute-start.2 = (bf16[32,40,2]{2,0,1:T(8,128)(2,1)}, bf16[32,40,2]{2,0,1:T(8,128)(2,1)}, u32[]{:S(2)}, u32[]{:S(2)}) collective-permute-start(bf16[32,40,2]{2,0,1:T(8,128)(2,1)} %get-tuple-element.9), channel_id=1, source_target_pairs={{1,0},{2,1},{3,2},{0,3},{5,4},{6,5},{7,6},{4,7},{9,8},{10,9},{11,1... | collective-permute-start | bytes 15368 | tf_op jit(solution)/shard_map/ppermute | solution.py:61
  27.5 0.0 collective-permute-start.3
  27.5 0.0 all-to-all-done
  27.5 0.2 reshape.392
  27.7 0.9 %reduce_sum.9 = f32[8,4096]{1,0:T(8,128)} reduce(f32[8,4,4096]{2,1,0:T(4,128)S(1)} %reshape.392, f32[]{:T(128)} %constant.40.clone.1), dimensions={1}, to_apply=%region_0.1 | reduce | flops 98304 | bytes 655364 | tf_op jit(solution)/shard_map/reduce_sum | solution.py:81
  28.7 1.1 %reshape.387 = f32[8,2,2,32,32]{4,3,2,1,0:T(8,128)S(1)} reshape(f32[8,4096]{1,0:T(8,128)} %reduce_sum.9) | data formatting | bytes 262144 | tf_op jit(solution)/shard_map/reshape | solution.py:83
  29.8 0.3 copy.68
  30.1 0.2 reshape.388
  30.3 0.4 subtract_convert_fusion
  30.7 0.1 rev.8
  30.8 0.2 fusion.30
  31.0 0.2 fusion.10
  31.3 0.1 copy.70
  31.4 1.3 %convolution_bitcast_fusion = f32[2,64,2,32]{3,2,0,1:T(2,128)S(1)} fusion(bf16[2,64,2,32]{3,2,0,1:T(2,128)(2,1)S(1)} %copy.70, bf16[1,64,32,32]{3,2,1,0:T(8,128)(2,1)} %copy.99), kind=kOutput, calls=%fused_computation.12 | convolution fusion | flops 524288 | bytes 180224 | tf_op jit(solution)/shard_map/mlpc,lcd->mlpd/dot_general | solution.py:126
  32.7 1.3 %convolution_bitcast_fusion.1 = f32[2,64,2,32]{3,2,0,1:T(2,128)S(1)} fusion(bf16[2,64,2,32]{3,2,0,1:T(2,128)(2,1)S(1)} %copy.70, bf16[1,64,32,32]{3,2,1,0:T(8,128)(2,1)} %copy.98), kind=kOutput, calls=%fused_computation.13 | convolution fusion | flops 524288 | bytes 180224 | tf_op jit(solution)/shard_map/mlpc,lcd->mlpd/dot_general | solution.py:123
  34.0 0.1 fusion.27
  34.2 0.2 pad_maximum_fusion.6
  34.4 0.1 copy.73
  34.4 0.2 fusion.35
  34.7 0.2 subtract_multiply_fusion
  34.9 0.1 concatenate.15
  35.0 0.1 rev.9
  35.1 0.1 concatenate.16
  35.2 0.2 maximum_bitcast_fusion.1
  35.5 0.2 broadcast_in_dim.36
  35.7 1.4 %reshape.389 = bf16[32,16,256]{2,1,0:T(8,128)(2,1)} reshape(bf16[8,4,2,2,32,32]{5,4,3,2,1,0:T(8,128)(2,1)S(1)} %broadcast_in_dim.36) | data formatting | bytes 524288 | tf_op jit(solution)/shard_map/reshape | solution.py:146
  37.2 6.9 %all-to-all-start.1 = ((bf16[32,16,256]{2,1,0:T(8,128)(2,1)}), bf16[32,16,256]{2,1,0:T(8,128)(2,1)S(1)}, u32[]{:S(2)}, u32[]{:S(2)}) async-start(bf16[32,16,256]{2,1,0:T(8,128)(2,1)} %reshape.389), calls=%async_computation.1 | async-start | bytes 524288 | tf_op jit(solution)/shard_map/all_to_all | solution.py:147
  44.1 4.5 %maximum_bitcast_fusion.rim_ref = bf16[40,32,1024]{2,1,0:T(8,128)(2,1)S(1)} fusion(bf16[32,40,2]{2,0,1:T(8,128)(2,1)} %collective-permute-done.3, bf16[32,40,2]{2,0,1:T(8,128)(2,1)} %collective-permute-done.2, bf16[32,4,900]{2,0,1:T(8,128)(2,1)S(1)} %broadcast_in_dim.37, bf16[32,2,900]{2,0,1:T(8,128)(2,1)} %copy-done.2, bf16[32,32,900]{2,0,1:T(8,128)(2,1)S(1)} %copy.76, ...), kind=kLoop, calls=%fused_computation.10 | loop fusion | flops 18350080 | bytes 4937728 | tf_op jit(solution)/shard_map/transpose | solution.py:164
  48.6 7.3 %shard_map.73 = bf16[32,32,900]{2,1,0:T(8,128)(2,1)S(1)} custom-call(s32[9,2]{1,0:T(8,128)S(1)} %copy.79.offs_ref, bf16[40,32,1024]{2,1,0:T(8,128)(2,1)S(1)} %maximum_bitcast_fusion.rim_ref, f32[32,9]{1,0:T(8,128)S(1)} %copy.80.w_ref), custom_call_target="tpu_custom_call" | custom-call | flops 94371840 | bytes 4464640 | tf_op jit(solution)/shard_map/pallas_call | solution.py:187
  55.9 0.2 reshape.390
  56.1 0.2 copy.81
  56.3 1.8 %fusion.8 = bf16[32,32,900]{2,0,1:T(8,128)(2,1)S(1)} fusion(bf16[32,32,900]{2,0,1:T(8,128)(2,1)S(1)} %bitcast.101, bf16[128,900]{1,0:T(8,128)(2,1)S(1)} %copy-done.3, bf16[32,32,128]{2,1,0:T(8,128)(2,1)S(1)} %bitcast.105), kind=kOutput, calls=%fused_computation.9 | convolution fusion | flops 246067200 | bytes 4178944 | tf_op jit(solution)/shard_map/dot_general | solution.py:153
  58.1 2.5 %copy.89 = bf16[32,32,900]{2,1,0:T(8,128)(2,1)} copy(bf16[32,32,900]{2,0,1:T(8,128)(2,1)S(1)} %fusion.8) | data formatting | bytes 3686400 | tf_op jit(solution)/shard_map/convert_element_type | solution.py:157
  (32 shorter events, 0.2 us)
Async XLA Ops:
  0.0 1.7 %copy-start = (bf16[32,32,900]{2,1,0:T(8,128)(2,1)S(1)}, bf16[32,32,900]{2,1,0:T(8,128)(2,1)}, u32[]{:S(2)}) copy-start(bf16[32,32,900]{2,1,0:T(8,128)(2,1)} %param.7) | copy-start | bytes 5529604
  3.4 15.8 %copy-start.6 = (s32[9,2]{0,1:T(2,128)S(1)}, s32[9,2]{0,1:T(2,128)}, u32[]{:S(2)}) copy-start(s32[9,2]{0,1:T(2,128)} %param.8) | copy-start | bytes 220
  3.4 15.9 %copy-start.5 = (f32[32,9]{0,1:T(8,128)S(1)}, f32[32,9]{0,1:T(8,128)}, u32[]{:S(2)}) copy-start(f32[32,9]{0,1:T(8,128)} %param.9) | copy-start | bytes 3460
  3.4 24.1 %all-to-all-start = ((bf16[32,16,256]{2,1,0:T(8,128)(2,1)}), bf16[32,16,256]{2,1,0:T(8,128)(2,1)S(1)}, u32[]{:S(2)}, u32[]{:S(2)}) async-start(bf16[32,16,256]{2,1,0:T(8,128)(2,1)} %convert_element_type.101), calls=%async_computation | async-start | bytes 524288 | tf_op jit(solution)/shard_map/all_to_all | solution.py:48
  13.5 11.7 %copy-start.7 = (s32[128]{0:T(128)S(1)}, s32[128]{0:T(128)}, u32[]{:S(2)}) copy-start(s32[128]{0:T(128)} %param.12) | copy-start | bytes 1540
  13.5 11.7 %copy-start.8 = (f32[128]{0:T(128)S(1)}, f32[128]{0:T(128)}, u32[]{:S(2)}) copy-start(f32[128]{0:T(128)} %param.11) | copy-start | bytes 1540
  14.2 11.2 %collective-permute-start = (bf16[32,2,900]{2,0,1:T(8,128)(2,1)}, bf16[32,2,900]{2,0,1:T(8,128)(2,1)S(1)}, u32[]{:S(2)}, u32[]{:S(2)}) collective-permute-start(bf16[32,2,900]{2,0,1:T(8,128)(2,1)} %get-tuple-element.11), channel_id=1, source_target_pairs={{0,4},{4,8},{8,12},{12,16},{16,20},{20,24},{24,28},{1,5},{5,9},{9,... | collective-permute-start | bytes 345608 | tf_op jit(solution)/shard_map/ppermute | solution.py:54
  17.9 7.6 %collective-permute-start.1 = (bf16[32,2,900]{2,0,1:T(8,128)(2,1)}, bf16[32,2,900]{2,0,1:T(8,128)(2,1)S(1)}, u32[]{:S(2)}, u32[]{:S(2)}) collective-permute-start(bf16[32,2,900]{2,0,1:T(8,128)(2,1)} %get-tuple-element.12), channel_id=1, source_target_pairs={{4,0},{8,4},{12,8},{16,12},{20,16},{24,20},{28,24},{5,1},{9,5},{13... | collective-permute-start | bytes 345608 | tf_op jit(solution)/shard_map/ppermute | solution.py:51
  25.5 4.3 %copy-start.1 = (bf16[32,2,900]{2,0,1:T(8,128)(2,1)}, bf16[32,2,900]{2,0,1:T(8,128)(2,1)S(1)}, u32[]{:S(2)}) copy-start(bf16[32,2,900]{2,0,1:T(8,128)(2,1)S(1)} %collective-permute-done) | copy-start | bytes 345604
  25.5 4.3 %copy-start.2 = (bf16[32,2,900]{2,0,1:T(8,128)(2,1)}, bf16[32,2,900]{2,0,1:T(8,128)(2,1)S(1)}, u32[]{:S(2)}) copy-start(bf16[32,2,900]{2,0,1:T(8,128)(2,1)S(1)} %collective-permute-done.1) | copy-start | bytes 345604
  26.5 4.3 %copy-start.4 = (bf16[2,64,128]{2,1,0:T(8,128)(2,1)S(1)}, bf16[2,64,128]{2,1,0:T(8,128)(2,1)}, u32[]{:S(2)}) copy-start(bf16[2,64,128]{2,1,0:T(8,128)(2,1)} %param.10) | copy-start | bytes 98308
  26.5 17.5 %collective-permute-start.2 = (bf16[32,40,2]{2,0,1:T(8,128)(2,1)}, bf16[32,40,2]{2,0,1:T(8,128)(2,1)}, u32[]{:S(2)}, u32[]{:S(2)}) collective-permute-start(bf16[32,40,2]{2,0,1:T(8,128)(2,1)} %get-tuple-element.9), channel_id=1, source_target_pairs={{1,0},{2,1},{3,2},{0,3},{5,4},{6,5},{7,6},{4,7},{9,8},{10,9},{11,1... | collective-permute-start | bytes 15368 | tf_op jit(solution)/shard_map/ppermute | solution.py:61
  27.5 16.6 %collective-permute-start.3 = (bf16[32,40,2]{2,0,1:T(8,128)(2,1)}, bf16[32,40,2]{2,0,1:T(8,128)(2,1)}, u32[]{:S(2)}, u32[]{:S(2)}) collective-permute-start(bf16[32,40,2]{2,0,1:T(8,128)(2,1)} %get-tuple-element.10), channel_id=1, source_target_pairs={{0,1},{1,2},{2,3},{3,0},{4,5},{5,6},{6,7},{7,4},{8,9},{9,10},{10,1... | collective-permute-start | bytes 15368 | tf_op jit(solution)/shard_map/ppermute | solution.py:64
  37.2 18.7 %all-to-all-start.1 = ((bf16[32,16,256]{2,1,0:T(8,128)(2,1)}), bf16[32,16,256]{2,1,0:T(8,128)(2,1)S(1)}, u32[]{:S(2)}, u32[]{:S(2)}) async-start(bf16[32,16,256]{2,1,0:T(8,128)(2,1)} %reshape.389), calls=%async_computation.1 | async-start | bytes 524288 | tf_op jit(solution)/shard_map/all_to_all | solution.py:147
  48.6 7.7 %copy-start.3 = (bf16[128,900]{1,0:T(8,128)(2,1)S(1)}, bf16[128,900]{1,0:T(8,128)(2,1)}, u32[]{:S(2)}) copy-start(bf16[128,900]{1,0:T(8,128)(2,1)} %convert_element_type.110) | copy-start | bytes 691204

commit v17 on v16

--- a/solution.py
+++ b/solution.py
@@ -120,12 +120,11 @@
     ) + jnp.einsum("mli,mpci->mlpc", leg_diff, odd_terms, preferred_element_type=jnp.float32)
     triangle = (degrees[None, :] >= mine[:, None]).astype(jnp.float32)
     coeffs = (coeffs * triangle[:, :, None, None]).astype(jnp.bfloat16)
-    with_real = jnp.einsum(
-        "mlpc,lcd->mlpd", coeffs, mix_weight[0], preferred_element_type=jnp.float32
-    )
-    with_imag = jnp.einsum(
-        "mlpc,lcd->mlpd", coeffs, mix_weight[1], preferred_element_type=jnp.float32
-    )
+    both_parts = jnp.einsum(
+        "mlpc,qlcd->qmlpd", coeffs, mix_weight, preferred_element_type=jnp.float32
+    )
+    with_real = both_parts[0]
+    with_imag = both_parts[1]
     mixed = jnp.stack(
         [with_real[:, :, 0] - with_imag[:, :, 1], with_real[:, :, 1] + with_imag[:, :, 0]],
         axis=2,

time: 61 us -> 74.7 us (1.22)
  local copies, waits for them, and re-layouts: 17.3 us -> 24.9 us
  other arithmetic: 9.07 us -> 14.3 us
    dot_general x2 -> x1, matrix products: 2.63 us -> 0.31 us  [per_device(): jnp.einsum('mlpc,qlcd->qmlpd', coeffs, mix_weight, preferred_element_type...]
    transpose x1, local copies, waits for them, and re-layouts: 0.31 us -> 2.15 us  [per_device(): jnp.transpose(summed, (1, 2, 3, 0, 4))]
    reshape x1, local copies, waits for them, and re-layouts: 0.25 us -> 1.99 us  [per_device(): summed = gathered.astype(jnp.float32).reshape(lat_count, lon_count, m_dev...]
    reshape x1, local copies, waits for them, and re-layouts: 0.18 us -> 1.88 us  [per_device(): jnp.transpose(summed, (1, 2, 3, 0, 4))]
    another operation x5, other arithmetic: 1.84 us -> 3.4 us
    dot_general x1, matrix products: 0.22 us -> 1.59 us  [per_device(): jnp.einsum('mli,mpci->mlpc', leg_diff, odd_terms, preferred_element_type=...]
    slice x1 -> x0, local copies, waits for them, and re-layouts: 1.07 us -> none  [per_device(): mix_weight[0]]
    reduce_sum x1, other arithmetic: 0.94 us -> 2 us  [per_device(): summed = gathered.astype(jnp.float32).reshape(lat_count, lon_count, m_dev...]
  transfers between devices with their start and end apart: 6 -> 6, of which waited for: 0 -> 0; matrix products, arithmetic and copies ran while one was open for 41% -> 49% of each run, Pallas kernels for 12% -> 10%
where the time goes in v17:
time: 74.7 us; the launch traced here: 73.8 us
  local copies, waits for them, and re-layouts  24.9 us (33%)
  starting transfers between devices  20.8 us (28%)
  other arithmetic  14.3 us (19%)
  Pallas kernels  7.3 us (10%)
  matrix products  6.17 us (8%)
    all_to_all x1, starting transfers between devices, per_device(): lax.all_to_all(partial.astype(jnp.bfloat16), BOTH, 0, 0, tiled=True)  7.44 us
    pallas_call x1, Pallas kernels, depthwise_conv(): pl.pallas_call(body, grid_spec=pltpu.PrefetchScalarGridSpec(num_scalar_pr...  7.3 us
    all_to_all x1, starting transfers between devices, per_device(): full_rows = lax.all_to_all(outgoing, BOTH, 0, 0, tiled=True)  6.87 us
    unnamed x20, local copies, waits for them, and re-layouts  6.16 us
    transpose x1, other arithmetic, depthwise_conv(): by_rows = jnp.transpose(rim, (1, 0, 2))  4.48 us
    ppermute x1, starting transfers between devices, per_device(): lax.ppermute(field[:, lat_rows - 2:], 'lat', [(i, i + 1) for i in range(l...  4.25 us
    another operation x5, other arithmetic  3.4 us
    convert_element_type x1, local copies, waits for them, and re-layouts, per_device(): (conv_out.astype(jnp.float32) + jax.nn.gelu(synthesis, approximate=True))...  2.47 us
  transfers between devices with their start and end apart: 6, of which 0 were waited for; matrix products, arithmetic and copies ran while one was open for 49% of the time, Pallas kernels for 10%

profile of v17, /device:TPU:0, one launch (start us, length us, event | category | flops | bytes accessed | tf_op | source)
XLA Modules:
  0.0 73.8 jit_solution(7471076299010401136)
XLA Ops:
  0.0 1.2 %multiply_convert_fusion.1 = (bf16[64,1,900]{2,0,1:T(8,128)(2,1)S(1)}, bf16[64,1,900]{2,0,1:T(8,128)(2,1)S(1)}, bf16[64,1,900]{2,0,1:T(8,128)(2,1)S(1)}, bf16[64,1,900]{2,0,1:T(8,128)(2,1)S(1)}) fusion(f32[64]{0:T(128)S(1)} %fusion.56, s32[900]{0:T(1024)S(1)} %iota_add_fusion, f32[64]{0:T(128)S(1)} %fusion.59), kind=kLoop, calls=%fused_computation.40 | loop fusion | flops 979200 | bytes 464912 | tf_op jit(solution)/shard_map/convert.5
  1.2 0.8 %pad_maximum_fusion.4 = (bf16[64,2,900]{2,0,1:T(8,128)(2,1)S(1)}, bf16[64,2,900]{2,0,1:T(8,128)(2,1)}) fusion(bf16[64,1,900]{2,0,1:T(8,128)(2,1)S(1)} %get-tuple-element.31, bf16[64,1,900]{2,0,1:T(8,128)(2,1)S(1)} %get-tuple-element.32, bf16[64,1,900]{2,0,1:T(8,128)(2,1)S(1)} %get-tuple-element.30, bf16[64,1,900]{2,0,1:T(8,128)(2,1)S(1)} %get-tuple-element.29), kind=kLoop, calls=%fused_computation.34 | loop fusion | flops 230400 | bytes 921600 | tf_op jit(solution)/shard_map/stack | solution.py:21
  2.0 0.3 copy.64
  2.2 0.2 convert_element_type.99
  2.4 0.8 %convolution_convert_fusion = bf16[128,1024]{1,0:T(8,128)(2,1)S(1)} fusion(bf16[128,900]{1,0:T(8,128)(2,1)S(1)} %convert_element_type.99, bf16[1024,900]{1,0:T(8,128)(2,1)S(1)} %bitcast.97), kind=kOutput, calls=%fused_computation.11 | convolution fusion | flops 236060672 | bytes 2335744 | tf_op jit(solution)/shard_map/dot_general | solution.py:45
  3.3 0.9 %convert_element_type.101 = bf16[32,16,256]{2,1,0:T(8,128)(2,1)} reshape(bf16[128,1024]{1,0:T(8,128)(2,1)S(1)} %convolution_convert_fusion) | data formatting | bytes 524288 | tf_op jit(solution)/shard_map/convert_element_type | solution.py:48
  4.1 7.4 %all-to-all-start = ((bf16[32,16,256]{2,1,0:T(8,128)(2,1)}), bf16[32,16,256]{2,1,0:T(8,128)(2,1)}, u32[]{:S(2)}, u32[]{:S(2)}) async-start(bf16[32,16,256]{2,1,0:T(8,128)(2,1)} %convert_element_type.101), calls=%async_computation | async-start | bytes 524288 | tf_op jit(solution)/shard_map/all_to_all | solution.py:48
  11.6 2.7 %copy.72 = bf16[32,32,900]{2,0,1:T(8,128)(2,1)S(1)} copy(bf16[32,32,900]{2,1,0:T(8,128)(2,1)} %param.7) | data formatting | bytes 3686400 | tf_op args[0]
  14.3 0.0 copy-start.6
  14.3 0.0 copy-start.7
  14.3 0.7 fusion.68
  15.0 4.3 %collective-permute-start = (bf16[32,2,900]{2,0,1:T(8,128)(2,1)}, bf16[32,2,900]{2,0,1:T(8,128)(2,1)}, u32[]{:S(2)}, u32[]{:S(2)}) collective-permute-start(bf16[32,2,900]{2,0,1:T(8,128)(2,1)} %get-tuple-element.11), channel_id=1, source_target_pairs={{0,4},{4,8},{8,12},{12,16},{16,20},{20,24},{24,28},{1,5},{5,9},{9,... | collective-permute-start | bytes 345608 | tf_op jit(solution)/shard_map/ppermute | solution.py:54
  19.3 1.3 %collective-permute-start.1 = (bf16[32,2,900]{2,0,1:T(8,128)(2,1)}, bf16[32,2,900]{2,0,1:T(8,128)(2,1)}, u32[]{:S(2)}, u32[]{:S(2)}) collective-permute-start(bf16[32,2,900]{2,0,1:T(8,128)(2,1)} %get-tuple-element.12), channel_id=1, source_target_pairs={{4,0},{8,4},{12,8},{16,12},{20,16},{24,20},{28,24},{5,1},{9,5},{13... | collective-permute-start | bytes 345608 | tf_op jit(solution)/shard_map/ppermute | solution.py:51
  20.6 0.1 copy.75.offs_ref
  20.7 0.1 copy.76.w_ref
  20.8 0.1 fusion.58
  20.9 0.1 convert_bitcast_fusion
  21.0 0.1 convolution_bitcast_fusion.1
  21.1 0.1 convolution_bitcast_fusion.2
  21.3 2.6 %copy.89 = bf16[2,64,32,32,1]{3,2,0,4,1:T(8,128)(2,1)S(1)} copy(bf16[2,64,32,32,1]{1,3,2,0,4:T(8,128)(2,1)} %bitcast.100) | data formatting | bytes 524288 | tf_op args[6]
  23.9 1.2 %copy.78 = bf16[64,2,900]{2,1,0:T(2,128)(2,1)S(1)} copy(bf16[64,2,900]{2,0,1:T(8,128)(2,1)} %get-tuple-element.42) | data formatting | bytes 460800 | tf_op jit(solution)/shard_map/stack | solution.py:21
  25.1 0.9 %convert_element_type.110 = bf16[128,900]{1,0:T(8,128)(2,1)} reshape(bf16[64,2,900]{2,1,0:T(2,128)(2,1)S(1)} %copy.78) | data formatting | bytes 460800 | tf_op jit(solution)/shard_map/convert_element_type | solution.py:24
  26.0 0.7 fusion.54
  26.6 0.1 pad.12.clone
  26.7 0.6 compare_convert_fusion.1
  27.4 0.1 compare_convert_fusion
  27.4 0.0 collective-permute-done
  27.4 0.0 collective-permute-done.1
  27.5 1.8 %pad_maximum_fusion.3 = (bf16[32,40,2]{2,0,1:T(8,128)(2,1)}, bf16[32,40,2]{2,0,1:T(8,128)(2,1)}) fusion(bf16[32,4,900]{2,0,1:T(8,128)(2,1)S(1)} %broadcast_in_dim.37, bf16[32,2,900]{2,0,1:T(8,128)(2,1)} %collective-permute-done.1, bf16[32,32,900]{2,0,1:T(8,128)(2,1)S(1)} %copy.72, bf16[32,2,900]{2,0,1:T(8,128)(2,1)} %collective-permute-done), kind=kLoop, calls=%fused_computation.31 | loop fusion | flops 40960 | bytes 2314240 | tf_op jit(solution)/shard_map/slice | solution.py:62
  29.3 0.9 %collective-permute-start.2 = (bf16[32,40,2]{2,0,1:T(8,128)(2,1)}, bf16[32,40,2]{2,0,1:T(8,128)(2,1)}, u32[]{:S(2)}, u32[]{:S(2)}) collective-permute-start(bf16[32,40,2]{2,0,1:T(8,128)(2,1)} %get-tuple-element.9), channel_id=1, source_target_pairs={{1,0},{2,1},{3,2},{0,3},{5,4},{6,5},{7,6},{4,7},{9,8},{10,9},{11,1... | collective-permute-start | bytes 15368 | tf_op jit(solution)/shard_map/ppermute | solution.py:61
  30.2 0.0 collective-permute-start.3
  30.2 2.0 %reshape.392 = f32[8,4,4096]{2,1,0:T(4,128)} reshape(bf16[32,16,256]{2,1,0:T(8,128)(2,1)} %all-to-all-done) | data formatting | bytes 786432 | tf_op jit(solution)/shard_map/reshape | solution.py:80
  32.2 2.0 %reduce_sum.9 = f32[8,4096]{1,0:T(8,128)} reduce(f32[8,4,4096]{2,1,0:T(4,128)} %reshape.392, f32[]{:T(128)} %constant.40.clone.1), dimensions={1}, to_apply=%region_0.1 | reduce | flops 98304 | bytes 655364 | tf_op jit(solution)/shard_map/reduce_sum | solution.py:81
  34.2 1.9 %reshape.387 = f32[8,2,2,32,32]{4,3,2,1,0:T(8,128)} reshape(f32[8,4096]{1,0:T(8,128)} %reduce_sum.9) | data formatting | bytes 262144 | tf_op jit(solution)/shard_map/reshape | solution.py:83
  36.1 2.1 %copy.65 = f32[2,2,32,8,32]{4,3,2,1,0:T(8,128)} copy(f32[2,2,32,8,32]{4,2,1,0,3:T(8,128)} %bitcast.98) | data formatting | bytes 262144 | tf_op jit(solution)/shard_map/transpose | solution.py:84
  38.2 1.9 %reshape.388 = f32[2,2,32,256]{3,2,1,0:T(8,128)} reshape(f32[2,2,32,8,32]{4,3,2,1,0:T(8,128)} %copy.65) | data formatting | bytes 262144 | tf_op jit(solution)/shard_map/reshape | solution.py:84
  40.1 2.0 %subtract_convert_fusion = (bf16[2,1,32,256]{3,2,1,0:T(8,128)(2,1)S(1)}, bf16[2,1,32,256]{3,2,1,0:T(8,128)(2,1)S(1)}) fusion(f32[2,2,32,256]{3,2,1,0:T(8,128)} %reshape.388, f32[2,32]{1,0:T(2,128)S(1)} %bitcast.103, f32[2,32]{1,0:T(2,128)S(1)} %bitcast.108, f32[2,32]{1,0:T(2,128)S(1)} %bitcast.104, f32[2,32]{1,0:T(2,128)S(1)} %bitcast.109, ...), kind=kLoop, calls=%fused_computation.67 | loop fusion | flops 655360 | bytes 330240 | tf_op jit(solution)/shard_map/convert.13
  42.1 0.6 copy-done.3
  42.7 0.7 rev.8
  43.4 1.0 %fusion.29 = f32[2,64,2,32]{1,3,2,0:T(8,128)S(1)} fusion(bf16[2,2,32,128]{3,2,1,0:T(8,128)(2,1)} %rev.8, f32[2,128]{1,0:T(2,128)} %fusion.54, bf16[2,64,128]{2,1,0:T(8,128)(2,1)S(1)} %copy-done.2, pred[2,64]{1,0:T(4,128)(4,1)S(1)} %get-tuple-element.38, bf16[2,1,32,256]{3,2,1,0:T(8,128)(2,1)S(1)} %get-tuple-element.17, bf16[2,1,32,256]{3,2,1,0:T(8,128)(2,1)} %copy-done.3), kind=kOutput, calls=%fused_computation.69 | convolution fusion | flops 2244608 | bytes 164992 | tf_op jit(solution)/shard_map/mli,mpci->mlpc/dot_general | solution.py:118
  44.4 1.6 %fusion.11 = bf16[2,64,2,32,1]{1,3,2,0,4:T(8,128)(2,1)} fusion(f32[2,64,2,32]{1,3,2,0:T(8,128)S(1)} %fusion.29, bf16[2,2,32,128]{3,2,1,0:T(8,128)(2,1)} %rev.8, f32[2,64]{1,0:T(2,128)} %get-tuple-element.37, f32[2,128]{1,0:T(2,128)} %fusion.54, bf16[2,64,128]{2,1,0:T(8,128)(2,1)S(1)} %copy-done.2, pred[2,64]{1,0:T(4,128)(4,1)S(1)} %get-tuple-element.38, ...), kind=kOutput, calls=%fused_computation.16 | convolution fusion | flops 2269184 | bytes 181888 | tf_op jit(solution)/shard_map/mli,mpci->mlpc/dot_general | solution.py:120
  46.0 0.9 %copy.88 = bf16[2,64,2,32,1]{3,2,4,0,1:T(2,128)(2,1)S(1)} copy(bf16[2,64,2,32,1]{1,3,2,0,4:T(8,128)(2,1)} %fusion.11) | data formatting | bytes 32768 | tf_op jit(solution)/shard_map/convert_element_type | solution.py:122
  46.8 0.3 convolution_bitcast_fusion
  47.1 0.1 slice_bitcast_fusion.1
  47.2 0.1 fusion.26
  47.4 0.2 pad_maximum_fusion.6
  47.6 0.1 copy.69
  47.7 0.2 fusion.34
  47.9 0.2 subtract_multiply_fusion
  48.1 0.1 concatenate.15
  48.2 0.1 rev.9
  48.3 0.1 concatenate.16
  48.5 0.2 maximum_bitcast_fusion.1
  48.7 0.2 broadcast_in_dim.36
  49.0 1.4 %reshape.389 = bf16[32,16,256]{2,1,0:T(8,128)(2,1)} reshape(bf16[8,4,2,2,32,32]{5,4,3,2,1,0:T(8,128)(2,1)S(1)} %broadcast_in_dim.36) | data formatting | bytes 524288 | tf_op jit(solution)/shard_map/reshape | solution.py:145
  50.4 6.9 %all-to-all-start.1 = ((bf16[32,16,256]{2,1,0:T(8,128)(2,1)}), bf16[32,16,256]{2,1,0:T(8,128)(2,1)S(1)}, u32[]{:S(2)}, u32[]{:S(2)}) async-start(bf16[32,16,256]{2,1,0:T(8,128)(2,1)} %reshape.389), calls=%async_computation.1 | async-start | bytes 524288 | tf_op jit(solution)/shard_map/all_to_all | solution.py:146
  57.3 0.0 collective-permute-done.3
  57.3 4.5 %maximum_bitcast_fusion.rim_ref = bf16[40,32,1024]{2,1,0:T(8,128)(2,1)S(1)} fusion(bf16[32,40,2]{2,0,1:T(8,128)(2,1)} %collective-permute-done.3, bf16[32,40,2]{2,0,1:T(8,128)(2,1)} %collective-permute-done.2, bf16[32,4,900]{2,0,1:T(8,128)(2,1)S(1)} %broadcast_in_dim.37, bf16[32,2,900]{2,0,1:T(8,128)(2,1)} %collective-permute-done.1, ...), kind=kLoop, calls=%fused_computation.10 | loop fusion | flops 18350080 | bytes 4937728 | tf_op jit(solution)/shard_map/transpose | solution.py:163
  61.8 7.3 %shard_map.73 = bf16[32,32,900]{2,1,0:T(8,128)(2,1)S(1)} custom-call(s32[9,2]{1,0:T(8,128)S(1)} %copy.75.offs_ref, bf16[40,32,1024]{2,1,0:T(8,128)(2,1)S(1)} %maximum_bitcast_fusion.rim_ref, f32[32,9]{1,0:T(8,128)S(1)} %copy.76.w_ref), custom_call_target="tpu_custom_call" | custom-call | flops 94371840 | bytes 4464640 | tf_op jit(solution)/shard_map/pallas_call | solution.py:186
  69.1 0.0 all-to-all-done.1
  69.1 0.2 reshape.390
  69.3 0.2 copy.77
  69.5 1.8 %fusion.8 = bf16[32,32,900]{2,0,1:T(8,128)(2,1)S(1)} fusion(bf16[32,32,900]{2,0,1:T(8,128)(2,1)S(1)} %bitcast.96, bf16[128,900]{1,0:T(8,128)(2,1)S(1)} %copy-done.1, bf16[32,32,128]{2,1,0:T(8,128)(2,1)S(1)} %bitcast.101), kind=kOutput, calls=%fused_computation.9 | convolution fusion | flops 246067200 | bytes 4178944 | tf_op jit(solution)/shard_map/dot_general | solution.py:152
  71.3 2.5 %copy.85 = bf16[32,32,900]{2,1,0:T(8,128)(2,1)} copy(bf16[32,32,900]{2,0,1:T(8,128)(2,1)S(1)} %fusion.8) | data formatting | bytes 3686400 | tf_op jit(solution)/shard_map/convert_element_type | solution.py:156
  (28 shorter events, 0.2 us)
Async XLA Ops:
  0.0 2.4 %copy-start = (bf16[32,32,900]{2,1,0:T(8,128)(2,1)S(1)}, bf16[32,32,900]{2,1,0:T(8,128)(2,1)}, u32[]{:S(2)}) copy-start(bf16[32,32,900]{2,1,0:T(8,128)(2,1)} %param.7) | copy-start | bytes 5529604
  4.1 16.5 %copy-start.5 = (s32[9,2]{0,1:T(2,128)S(1)}, s32[9,2]{0,1:T(2,128)}, u32[]{:S(2)}) copy-start(s32[9,2]{0,1:T(2,128)} %param.8) | copy-start | bytes 220
  4.1 16.6 %copy-start.4 = (f32[32,9]{0,1:T(8,128)S(1)}, f32[32,9]{0,1:T(8,128)}, u32[]{:S(2)}) copy-start(f32[32,9]{0,1:T(8,128)} %param.9) | copy-start | bytes 3460
  4.1 26.1 %all-to-all-start = ((bf16[32,16,256]{2,1,0:T(8,128)(2,1)}), bf16[32,16,256]{2,1,0:T(8,128)(2,1)}, u32[]{:S(2)}, u32[]{:S(2)}) async-start(bf16[32,16,256]{2,1,0:T(8,128)(2,1)} %convert_element_type.101), calls=%async_computation | async-start | bytes 524288 | tf_op jit(solution)/shard_map/all_to_all | solution.py:48
  14.3 11.7 %copy-start.6 = (s32[128]{0:T(128)S(1)}, s32[128]{0:T(128)}, u32[]{:S(2)}) copy-start(s32[128]{0:T(128)} %param.12) | copy-start | bytes 1540
  14.3 11.7 %copy-start.7 = (f32[128]{0:T(128)S(1)}, f32[128]{0:T(128)}, u32[]{:S(2)}) copy-start(f32[128]{0:T(128)} %param.11) | copy-start | bytes 1540
  15.0 12.4 %collective-permute-start = (bf16[32,2,900]{2,0,1:T(8,128)(2,1)}, bf16[32,2,900]{2,0,1:T(8,128)(2,1)}, u32[]{:S(2)}, u32[]{:S(2)}) collective-permute-start(bf16[32,2,900]{2,0,1:T(8,128)(2,1)} %get-tuple-element.11), channel_id=1, source_target_pairs={{0,4},{4,8},{8,12},{12,16},{16,20},{20,24},{24,28},{1,5},{5,9},{9,... | collective-permute-start | bytes 345608 | tf_op jit(solution)/shard_map/ppermute | solution.py:54
  19.3 8.1 %collective-permute-start.1 = (bf16[32,2,900]{2,0,1:T(8,128)(2,1)}, bf16[32,2,900]{2,0,1:T(8,128)(2,1)}, u32[]{:S(2)}, u32[]{:S(2)}) collective-permute-start(bf16[32,2,900]{2,0,1:T(8,128)(2,1)} %get-tuple-element.12), channel_id=1, source_target_pairs={{4,0},{8,4},{12,8},{16,12},{20,16},{24,20},{28,24},{5,1},{9,5},{13... | collective-permute-start | bytes 345608 | tf_op jit(solution)/shard_map/ppermute | solution.py:51
  29.2 14.2 %copy-start.2 = (bf16[2,64,128]{2,1,0:T(8,128)(2,1)S(1)}, bf16[2,64,128]{2,1,0:T(8,128)(2,1)}, u32[]{:S(2)}) copy-start(bf16[2,64,128]{2,1,0:T(8,128)(2,1)} %param.10) | copy-start | bytes 98308
  29.3 28.0 %collective-permute-start.2 = (bf16[32,40,2]{2,0,1:T(8,128)(2,1)}, bf16[32,40,2]{2,0,1:T(8,128)(2,1)}, u32[]{:S(2)}, u32[]{:S(2)}) collective-permute-start(bf16[32,40,2]{2,0,1:T(8,128)(2,1)} %get-tuple-element.9), channel_id=1, source_target_pairs={{1,0},{2,1},{3,2},{0,3},{5,4},{6,5},{7,6},{4,7},{9,8},{10,9},{11,1... | collective-permute-start | bytes 15368 | tf_op jit(solution)/shard_map/ppermute | solution.py:61
  30.2 27.1 %collective-permute-start.3 = (bf16[32,40,2]{2,0,1:T(8,128)(2,1)}, bf16[32,40,2]{2,0,1:T(8,128)(2,1)}, u32[]{:S(2)}, u32[]{:S(2)}) collective-permute-start(bf16[32,40,2]{2,0,1:T(8,128)(2,1)} %get-tuple-element.10), channel_id=1, source_target_pairs={{0,1},{1,2},{2,3},{3,0},{4,5},{5,6},{6,7},{7,4},{8,9},{9,10},{10,1... | collective-permute-start | bytes 15368 | tf_op jit(solution)/shard_map/ppermute | solution.py:64
  42.1 0.6 copy-start.3
  50.4 18.7 %all-to-all-start.1 = ((bf16[32,16,256]{2,1,0:T(8,128)(2,1)}), bf16[32,16,256]{2,1,0:T(8,128)(2,1)S(1)}, u32[]{:S(2)}, u32[]{:S(2)}) async-start(bf16[32,16,256]{2,1,0:T(8,128)(2,1)} %reshape.389), calls=%async_computation.1 | async-start | bytes 524288 | tf_op jit(solution)/shard_map/all_to_all | solution.py:146
  61.8 7.7 %copy-start.1 = (bf16[128,900]{1,0:T(8,128)(2,1)S(1)}, bf16[128,900]{1,0:T(8,128)(2,1)}, u32[]{:S(2)}) copy-start(bf16[128,900]{1,0:T(8,128)(2,1)} %convert_element_type.110) | copy-start | bytes 691204

commit v18 on v16

--- a/solution.py
+++ b/solution.py
@@ -55,7 +55,7 @@
         field[:, lat_rows - 2 :], "lat", [(i, (i + 1)) for i in range(lat_n - 1)]
     )
     rows_ext = jnp.concatenate(
-        [north, field, south, jnp.zeros((channels, 4, lon_cols), field.dtype)], axis=1
+        [north, field, south], axis=1
     )
     rim_rows = rows_ext.shape[1]
     east = lax.ppermute(

time: 61 us -> 68.6 us (1.12)
  waiting for transfers between devices: 0.02 us -> 9.22 us
  local copies, waits for them, and re-layouts: 17.3 us -> 19.7 us
  matrix products: 6.35 us -> 4.28 us
  other arithmetic: 9.07 us -> 7.29 us
    ppermute x1, waiting for transfers between devices: 0.01 us -> 7.74 us  [per_device(): lax.ppermute(rows_ext[:, :, :2], 'lon', [((i + 1) % lon_count, i) for i i...]
    transpose x1, other arithmetic: 4.48 us -> 2.52 us  [depthwise_conv(): by_rows = jnp.transpose(rim, (1, 0, 2))]
    ppermute x1, waiting for transfers between devices: 0.01 us -> 1.47 us  [per_device(): lax.ppermute(rows_ext[:, :, lon_cols - 2:], 'lon', [(i, (i + 1) % lon_cou...]
    unnamed x23 -> x44, local copies, waits for them, and re-layouts: 6.01 us -> 7.41 us
    dot_general x1, matrix products: 1.32 us -> 0.27 us  [per_device(): jnp.einsum('mlpc,lcd->mlpd', coeffs, mix_weight[1], preferred_element_typ...]
    dot_general x1, matrix products: 1.31 us -> 0.27 us  [per_device(): jnp.einsum('mlpc,lcd->mlpd', coeffs, mix_weight[0], preferred_element_typ...]
    slice x1 -> x0, other arithmetic: 1.02 us -> none  [per_device(): rows_ext[:, :, :2]]
    reshape x1, local copies, waits for them, and re-layouts: 1.07 us -> 0.17 us  [per_device(): summed = summed.reshape(lat_count, m_dev, 2, channels, lat_rows)]
  transfers between devices with their start and end apart: 6 -> 6, of which waited for: 0 -> 2; matrix products, arithmetic and copies ran while one was open for 41% -> 25% of each run, Pallas kernels for 12% -> 10%
where the time goes in v18:
time: 68.6 us; the launch traced here: 68.2 us
  starting transfers between devices  20.6 us (30%)
  local copies, waits for them, and re-layouts  19.7 us (29%)
  waiting for transfers between devices  9.22 us (13%)
  other arithmetic  7.29 us (11%)
  Pallas kernels  6.65 us (10%)
  matrix products  4.28 us (6%)
    ppermute x1, waiting for transfers between devices, per_device(): lax.ppermute(rows_ext[:, :, :2], 'lon', [((i + 1) % lon_count, i) for i i...  7.74 us
    unnamed x44, local copies, waits for them, and re-layouts  7.41 us
    all_to_all x1, starting transfers between devices, per_device(): lax.all_to_all(partial.astype(jnp.bfloat16), BOTH, 0, 0, tiled=True)  7.31 us
    pallas_call x1, Pallas kernels, depthwise_conv(): pl.pallas_call(body, grid_spec=pltpu.PrefetchScalarGridSpec(num_scalar_pr...  6.65 us
    all_to_all x1, starting transfers between devices, per_device(): full_rows = lax.all_to_all(outgoing, BOTH, 0, 0, tiled=True)  6.06 us
    ppermute x1, starting transfers between devices, per_device(): lax.ppermute(field[:, lat_rows - 2:], 'lat', [(i, i + 1) for i in range(l...  4.34 us
    transpose x1, other arithmetic, depthwise_conv(): by_rows = jnp.transpose(rim, (1, 0, 2))  2.52 us
    convert_element_type x1, local copies, waits for them, and re-layouts, per_device(): (conv_out.astype(jnp.float32) + jax.nn.gelu(synthesis, approximate=True))...  2.47 us
  transfers between devices with their start and end apart: 6, of which 2 were waited for; matrix products, arithmetic and copies ran while one was open for 25% of the time, Pallas kernels for 10%

profile of v18, /device:TPU:0, one launch (start us, length us, event | category | flops | bytes accessed | tf_op | source)
XLA Modules:
  0.0 68.2 jit_solution(2779242724758205633)
XLA Ops:
  0.0 1.2 %multiply_convert_fusion.1 = (bf16[64,1,900]{2,0,1:T(8,128)(2,1)S(1)}, bf16[64,1,900]{2,0,1:T(8,128)(2,1)S(1)}, bf16[64,1,900]{2,0,1:T(8,128)(2,1)S(1)}, bf16[64,1,900]{2,0,1:T(8,128)(2,1)S(1)}) fusion(f32[64]{0:T(128)S(1)} %fusion.57, s32[900]{0:T(1024)S(1)} %iota_add_fusion, f32[64]{0:T(128)S(1)} %fusion.60), kind=kLoop, calls=%fused_computation.38 | loop fusion | flops 979200 | bytes 464912 | tf_op jit(solution)/shard_map/convert.5
  1.2 0.1 pad_maximum_fusion
  1.3 0.3 copy.67
  1.6 0.2 convert_element_type.99
  1.8 0.8 %convolution_convert_fusion = bf16[128,1024]{1,0:T(8,128)(2,1)S(1)} fusion(bf16[128,900]{1,0:T(8,128)(2,1)S(1)} %convert_element_type.99, bf16[1024,900]{1,0:T(8,128)(2,1)S(1)} %bitcast.102), kind=kOutput, calls=%fused_computation.11 | convolution fusion | flops 236060672 | bytes 2335744 | tf_op jit(solution)/shard_map/dot_general | solution.py:45
  2.6 0.9 %convert_element_type.101 = bf16[32,16,256]{2,1,0:T(8,128)(2,1)} reshape(bf16[128,1024]{1,0:T(8,128)(2,1)S(1)} %convolution_convert_fusion) | data formatting | bytes 524288 | tf_op jit(solution)/shard_map/convert_element_type | solution.py:48
  3.5 7.3 %all-to-all-start = ((bf16[32,16,256]{2,1,0:T(8,128)(2,1)}), bf16[32,16,256]{2,1,0:T(8,128)(2,1)S(1)}, u32[]{:S(2)}, u32[]{:S(2)}) async-start(bf16[32,16,256]{2,1,0:T(8,128)(2,1)} %convert_element_type.101), calls=%async_computation | async-start | bytes 524288 | tf_op jit(solution)/shard_map/all_to_all | solution.py:48
  10.8 0.2 fusion.70
  11.0 4.3 %collective-permute-start = (bf16[32,2,900]{2,0,1:T(8,128)(2,1)S(1)}, bf16[32,2,900]{2,0,1:T(8,128)(2,1)}, u32[]{:S(2)}, u32[]{:S(2)}) collective-permute-start(bf16[32,2,900]{2,0,1:T(8,128)(2,1)S(1)} %copy.103), channel_id=1, source_target_pairs={{0,4},{4,8},{8,12},{12,16},{16,20},{20,24},{24,28},{1,5},{5,9},{9,... | collective-permute-start | bytes 345608 | tf_op jit(solution)/shard_map/ppermute | solution.py:54
  15.4 1.3 %collective-permute-start.1 = (bf16[32,2,900]{2,0,1:T(8,128)(2,1)S(1)}, bf16[32,2,900]{2,0,1:T(8,128)(2,1)S(1)}, u32[]{:S(2)}, u32[]{:S(2)}) collective-permute-start(bf16[32,2,900]{2,0,1:T(8,128)(2,1)S(1)} %copy.104), channel_id=1, source_target_pairs={{4,0},{8,4},{12,8},{16,12},{20,16},{24,20},{28,24},{5,1},{9,5},{13... | collective-permute-start | bytes 345608 | tf_op jit(solution)/shard_map/ppermute | solution.py:51
  16.7 0.6 compare_convert_fusion.1
  17.3 0.1 fusion.59
  17.5 0.1 convert_bitcast_fusion
  17.5 0.1 convolution_bitcast_fusion.2
  17.6 0.6 fusion.73
  18.3 0.1 convolution_bitcast_fusion.3
  18.4 0.6 fusion.72
  19.0 1.1 %fusion.71 = (bf16[1,64,32,32]{1,3,2,0:T(8,128)(2,1)S(1)}, bf16[1,64,32,32]{1,3,2,0:T(8,128)(2,1)S(1)}) fusion(bf16[2,64,32,32]{1,3,2,0:T(8,128)(2,1)} %param.13), kind=kLoop, calls=%fused_computation.121 | loop fusion | bytes 524288 | tf_op jit(solution)/shard_map/slice | solution.py:124
  20.1 1.5 %copy.99 = bf16[1,64,32,32]{3,2,1,0:T(8,128)(2,1)} copy(bf16[1,64,32,32]{1,3,2,0:T(8,128)(2,1)S(1)} %get-tuple-element.14) | data formatting | bytes 262144
  21.6 1.5 %copy.98 = bf16[1,64,32,32]{3,2,1,0:T(8,128)(2,1)} copy(bf16[1,64,32,32]{1,3,2,0:T(8,128)(2,1)S(1)} %get-tuple-element.13) | data formatting | bytes 262144
  23.1 0.7 %fusion.55 = f32[2,128]{1,0:T(2,128)S(1)} fusion(f32[128]{0:T(128)} %param.11, s32[128]{0:T(128)} %param.12, s32[2]{0:T(128)S(1)} %iota_add_fusion.2), kind=kLoop, calls=%fused_computation.105 | loop fusion | flops 768 | bytes 2056 | tf_op jit(solution)/shard_map/mul | solution.py:110
  23.8 0.7 %compare_convert_fusion = f32[2,128]{1,0:T(2,128)S(1)} fusion(s32[128]{0:T(128)} %param.12, s32[2]{0:T(128)S(1)} %iota_add_fusion.2), kind=kLoop, calls=%fused_computation.94 | loop fusion | flops 512 | bytes 1544 | tf_op jit(solution)/shard_map/convert_element_type | solution.py:109
  24.6 1.6 %constant_dynamic-update-slice_fusion.2 = bf16[32,36,900]{2,0,1:T(8,128)(2,1)} fusion(bf16[32,2,900]{2,0,1:T(8,128)(2,1)} %collective-permute-done), kind=kLoop, calls=%fused_computation.83 | loop fusion | bytes 246272
  26.1 2.5 %constant_dynamic-update-slice_fusion.1 = bf16[32,36,900]{2,0,1:T(8,128)(2,1)} fusion(bf16[32,36,900]{2,0,1:T(8,128)(2,1)} %constant_dynamic-update-slice_fusion.2, bf16[32,32,900]{2,1,0:T(8,128)(2,1)S(1)} %copy-done), kind=kLoop, calls=%fused_computation.82 | loop fusion | bytes 3940352
  28.7 0.7 constant_dynamic-update-slice_fusion
  29.4 0.2 reshape.392
  29.7 0.3 reduce_sum.9
  30.0 0.2 reshape.387
  30.2 0.3 copy.68
  30.5 0.2 reshape.388
  30.8 0.4 subtract_convert_fusion
  31.2 0.1 rev.8
  31.3 0.2 fusion.30
  31.5 0.2 fusion.10
  31.8 0.1 copy.70
  31.9 0.3 convolution_bitcast_fusion
  32.2 0.3 convolution_bitcast_fusion.1
  32.4 0.1 fusion.27
  32.6 0.2 pad_maximum_fusion.2
  32.8 0.1 copy.73
  32.9 0.2 fusion.35
  33.1 0.2 subtract_multiply_fusion
  33.3 0.1 concatenate.15
  33.4 0.1 rev.9
  33.5 0.1 concatenate.16
  33.7 0.2 maximum_bitcast_fusion.1
  33.9 0.2 broadcast_in_dim.34
  34.2 1.4 %reshape.389 = bf16[32,16,256]{2,1,0:T(8,128)(2,1)} reshape(bf16[8,4,2,2,32,32]{5,4,3,2,1,0:T(8,128)(2,1)S(1)} %broadcast_in_dim.34) | data formatting | bytes 524288 | tf_op jit(solution)/shard_map/reshape | solution.py:146
  35.6 6.1 %all-to-all-start.1 = ((bf16[32,16,256]{2,1,0:T(8,128)(2,1)}), bf16[32,16,256]{2,1,0:T(8,128)(2,1)S(1)}, u32[]{:S(2)}, u32[]{:S(2)}) async-start(bf16[32,16,256]{2,1,0:T(8,128)(2,1)} %reshape.389), calls=%async_computation.1 | async-start | bytes 524288 | tf_op jit(solution)/shard_map/all_to_all | solution.py:147
  41.7 1.2 %fusion.69 = (bf16[32,36,2]{2,0,1:T(8,128)(2,1)S(1)}, bf16[32,36,2]{2,0,1:T(8,128)(2,1)S(1)}) fusion(bf16[32,36,900]{2,0,1:T(8,128)(2,1)} %constant_dynamic-update-slice_fusion), kind=kLoop, calls=%fused_computation.119 | loop fusion | bytes 18432 | tf_op jit(solution)/shard_map/slice | solution.py:62
  42.9 1.6 %collective-permute-start.2 = (bf16[32,36,2]{2,0,1:T(8,128)(2,1)S(1)}, bf16[32,36,2]{2,0,1:T(8,128)(2,1)S(1)}, u32[]{:S(2)}, u32[]{:S(2)}) collective-permute-start(bf16[32,36,2]{2,0,1:T(8,128)(2,1)S(1)} %get-tuple-element.9), channel_id=1, source_target_pairs={{1,0},{2,1},{3,2},{0,3},{5,4},{6,5},{7,6},{4,7},{9,8},{10,9},{11,1... | collective-permute-start | bytes 13832 | tf_op jit(solution)/shard_map/ppermute | solution.py:61
  44.5 0.1 copy.80.w_ref
  44.5 0.1 copy.79.offs_ref
  44.6 0.3 copy.82
  44.9 0.2 convert_element_type.110
  45.1 0.1 pad.9.clone
  45.2 7.7 %collective-permute-done.2 = bf16[32,36,2]{2,0,1:T(8,128)(2,1)S(1)} collective-permute-done((bf16[32,36,2]{2,0,1:T(8,128)(2,1)S(1)}, bf16[32,36,2]{2,0,1:T(8,128)(2,1)S(1)}, u32[]{:S(2)}, u32[]{:S(2)}) %collective-permute-start.2) | collective-permute-done | bytes 4640 | tf_op jit(solution)/shard_map/ppermute | solution.py:61
  52.9 1.5 %collective-permute-done.3 = bf16[32,36,2]{2,0,1:T(8,128)(2,1)S(1)} collective-permute-done((bf16[32,36,2]{2,0,1:T(8,128)(2,1)S(1)}, bf16[32,36,2]{2,0,1:T(8,128)(2,1)S(1)}, u32[]{:S(2)}, u32[]{:S(2)}) %collective-permute-start.3) | collective-permute-done | bytes 4640 | tf_op jit(solution)/shard_map/ppermute | solution.py:64
  54.4 2.5 %maximum_bitcast_fusion.rim_ref = bf16[36,32,1024]{2,1,0:T(8,128)(2,1)S(1)} fusion(bf16[32,36,2]{2,0,1:T(8,128)(2,1)S(1)} %collective-permute-done.3, bf16[32,36,2]{2,0,1:T(8,128)(2,1)S(1)} %collective-permute-done.2, bf16[32,36,900]{2,0,1:T(8,128)(2,1)} %constant_dynamic-update-slice_fusion, bf16[1024]{0:T(1024)(128)(2,1)S(1)} %pad.9.clone), kind=kLoop, calls=%fused_computation.10 | loop fusion | flops 9437184 | bytes 4444160 | tf_op jit(solution)/shard_map/transpose | solution.py:164
  56.9 6.6 %shard_map.73 = bf16[32,32,900]{2,1,0:T(8,128)(2,1)S(1)} custom-call(s32[9,2]{1,0:T(8,128)S(1)} %copy.79.offs_ref, bf16[36,32,1024]{2,1,0:T(8,128)(2,1)S(1)} %maximum_bitcast_fusion.rim_ref, f32[32,9]{1,0:T(8,128)S(1)} %copy.80.w_ref), custom_call_target="tpu_custom_call" | custom-call | flops 84934656 | bytes 4202496 | tf_op jit(solution)/shard_map/pallas_call | solution.py:187
  63.6 0.2 reshape.390
  63.7 0.2 copy.81
  63.9 1.8 %fusion.8 = bf16[32,32,900]{2,0,1:T(8,128)(2,1)S(1)} fusion(bf16[32,32,900]{2,0,1:T(8,128)(2,1)S(1)} %bitcast.101, bf16[128,900]{1,0:T(8,128)(2,1)S(1)} %convert_element_type.110, bf16[32,32,128]{2,1,0:T(8,128)(2,1)S(1)} %bitcast.105), kind=kOutput, calls=%fused_computation.9 | convolution fusion | flops 246067200 | bytes 4178944 | tf_op jit(solution)/shard_map/dot_general | solution.py:153
  65.7 2.5 %copy.89 = bf16[32,32,900]{2,1,0:T(8,128)(2,1)} copy(bf16[32,32,900]{2,0,1:T(8,128)(2,1)S(1)} %fusion.8) | data formatting | bytes 3686400 | tf_op jit(solution)/shard_map/convert_element_type | solution.py:157
  (53 shorter events, 0.2 us)
Async XLA Ops:
  0.0 1.7 %copy-start = (bf16[32,32,900]{2,1,0:T(8,128)(2,1)S(1)}, bf16[32,32,900]{2,1,0:T(8,128)(2,1)}, u32[]{:S(2)}) copy-start(bf16[32,32,900]{2,1,0:T(8,128)(2,1)} %param.7) | copy-start | bytes 5529604
  1.7 15.0 %copy-start.15 = (s32[9,2]{0,1:T(2,128)S(1)}, s32[9,2]{0,1:T(2,128)}, u32[]{:S(2)}) copy-start(s32[9,2]{0,1:T(2,128)} %param.8) | copy-start | bytes 220
  1.8 15.8 %copy-start.4 = (f32[32,9]{0,1:T(8,128)S(1)}, f32[32,9]{0,1:T(8,128)}, u32[]{:S(2)}) copy-start(f32[32,9]{0,1:T(8,128)} %param.9) | copy-start | bytes 3460
  3.5 25.9 %all-to-all-start = ((bf16[32,16,256]{2,1,0:T(8,128)(2,1)}), bf16[32,16,256]{2,1,0:T(8,128)(2,1)S(1)}, u32[]{:S(2)}, u32[]{:S(2)}) async-start(bf16[32,16,256]{2,1,0:T(8,128)(2,1)} %convert_element_type.101), calls=%async_computation | async-start | bytes 524288 | tf_op jit(solution)/shard_map/all_to_all | solution.py:48
  11.0 13.5 %collective-permute-start = (bf16[32,2,900]{2,0,1:T(8,128)(2,1)S(1)}, bf16[32,2,900]{2,0,1:T(8,128)(2,1)}, u32[]{:S(2)}, u32[]{:S(2)}) collective-permute-start(bf16[32,2,900]{2,0,1:T(8,128)(2,1)S(1)} %copy.103), channel_id=1, source_target_pairs={{0,4},{4,8},{8,12},{12,16},{16,20},{20,24},{24,28},{1,5},{5,9},{9,... | collective-permute-start | bytes 345608 | tf_op jit(solution)/shard_map/ppermute | solution.py:54
  15.4 13.3 %collective-permute-start.1 = (bf16[32,2,900]{2,0,1:T(8,128)(2,1)S(1)}, bf16[32,2,900]{2,0,1:T(8,128)(2,1)S(1)}, u32[]{:S(2)}, u32[]{:S(2)}) collective-permute-start(bf16[32,2,900]{2,0,1:T(8,128)(2,1)S(1)} %copy.104), channel_id=1, source_target_pairs={{4,0},{8,4},{12,8},{16,12},{20,16},{24,20},{28,24},{5,1},{9,5},{13... | collective-permute-start | bytes 345608 | tf_op jit(solution)/shard_map/ppermute | solution.py:51
  28.6 2.0 %copy-start.5 = (f32[1,2,32]{2,0,1:T(1,128)S(1)}, f32[1,2,32]{2,0,1:T(1,128)}, u32[]{:S(2)}) copy-start(f32[1,2,32]{2,0,1:T(1,128)} %get-tuple-element.24) | copy-start | bytes 772
  28.6 2.0 %copy-start.6 = (f32[1,2,32]{2,0,1:T(1,128)S(1)}, f32[1,2,32]{2,0,1:T(1,128)}, u32[]{:S(2)}) copy-start(f32[1,2,32]{2,0,1:T(1,128)} %get-tuple-element.25) | copy-start | bytes 772
  28.6 2.0 %copy-start.7 = (f32[1,2,32]{2,0,1:T(1,128)S(1)}, f32[1,2,32]{2,0,1:T(1,128)}, u32[]{:S(2)}) copy-start(f32[1,2,32]{2,0,1:T(1,128)} %get-tuple-element.26) | copy-start | bytes 772
  28.6 2.0 %copy-start.8 = (f32[1,2,32]{2,0,1:T(1,128)S(1)}, f32[1,2,32]{2,0,1:T(1,128)}, u32[]{:S(2)}) copy-start(f32[1,2,32]{2,0,1:T(1,128)} %get-tuple-element.27) | copy-start | bytes 772
  28.7 2.0 %copy-start.9 = (f32[1,2,32]{2,0,1:T(1,128)S(1)}, f32[1,2,32]{2,0,1:T(1,128)}, u32[]{:S(2)}) copy-start(f32[1,2,32]{2,0,1:T(1,128)} %get-tuple-element.28) | copy-start | bytes 772
  28.7 2.0 %copy-start.10 = (f32[1,2,32]{2,0,1:T(1,128)S(1)}, f32[1,2,32]{2,0,1:T(1,128)}, u32[]{:S(2)}) copy-start(f32[1,2,32]{2,0,1:T(1,128)} %get-tuple-element.19) | copy-start | bytes 772
  28.7 2.0 %copy-start.11 = (f32[1,2,32]{2,0,1:T(1,128)S(1)}, f32[1,2,32]{2,0,1:T(1,128)}, u32[]{:S(2)}) copy-start(f32[1,2,32]{2,0,1:T(1,128)} %get-tuple-element.20) | copy-start | bytes 772
  28.7 2.0 %copy-start.12 = (f32[1,2,32]{2,0,1:T(1,128)S(1)}, f32[1,2,32]{2,0,1:T(1,128)}, u32[]{:S(2)}) copy-start(f32[1,2,32]{2,0,1:T(1,128)} %get-tuple-element.21) | copy-start | bytes 772
  28.7 2.0 %copy-start.13 = (f32[1,2,32]{2,0,1:T(1,128)S(1)}, f32[1,2,32]{2,0,1:T(1,128)}, u32[]{:S(2)}) copy-start(f32[1,2,32]{2,0,1:T(1,128)} %get-tuple-element.22) | copy-start | bytes 772
  28.7 2.0 %copy-start.14 = (f32[1,2,32]{2,0,1:T(1,128)S(1)}, f32[1,2,32]{2,0,1:T(1,128)}, u32[]{:S(2)}) copy-start(f32[1,2,32]{2,0,1:T(1,128)} %get-tuple-element.23) | copy-start | bytes 772
  28.7 2.6 %copy-start.3 = (bf16[2,64,128]{2,1,0:T(8,128)(2,1)S(1)}, bf16[2,64,128]{2,1,0:T(8,128)(2,1)}, u32[]{:S(2)}) copy-start(bf16[2,64,128]{2,1,0:T(8,128)(2,1)} %param.10) | copy-start | bytes 98308
  28.7 2.8 %copy-start.17 = (f32[2,64]{1,0:T(2,128)S(1)}, f32[2,64]{1,0:T(2,128)}, u32[]{:S(2)}) copy-start(f32[2,64]{1,0:T(2,128)} %get-tuple-element.37) | copy-start | bytes 1540
  29.4 2.5 %copy-start.1 = (bf16[1,64,32,32]{3,2,1,0:T(8,128)(2,1)S(1)}, bf16[1,64,32,32]{3,2,1,0:T(8,128)(2,1)}, u32[]{:S(2)}) copy-start(bf16[1,64,32,32]{3,2,1,0:T(8,128)(2,1)} %copy.99) | copy-start | bytes 393220
  29.7 2.5 %copy-start.2 = (bf16[1,64,32,32]{3,2,1,0:T(8,128)(2,1)S(1)}, bf16[1,64,32,32]{3,2,1,0:T(8,128)(2,1)}, u32[]{:S(2)}) copy-start(bf16[1,64,32,32]{3,2,1,0:T(8,128)(2,1)} %copy.98) | copy-start | bytes 393220
  33.8 10.7 %copy-start.16 = (s32[9,2]{0,1:T(2,128)S(1)}, s32[9,2]{0,1:T(2,128)}, u32[]{:S(2)}) copy-start(s32[9,2]{0,1:T(2,128)} %param.8) | copy-start | bytes 220
  35.6 28.0 %all-to-all-start.1 = ((bf16[32,16,256]{2,1,0:T(8,128)(2,1)}), bf16[32,16,256]{2,1,0:T(8,128)(2,1)S(1)}, u32[]{:S(2)}, u32[]{:S(2)}) async-start(bf16[32,16,256]{2,1,0:T(8,128)(2,1)} %reshape.389), calls=%async_computation.1 | async-start | bytes 524288 | tf_op jit(solution)/shard_map/all_to_all | solution.py:147
  42.9 10.0 %collective-permute-start.2 = (bf16[32,36,2]{2,0,1:T(8,128)(2,1)S(1)}, bf16[32,36,2]{2,0,1:T(8,128)(2,1)S(1)}, u32[]{:S(2)}, u32[]{:S(2)}) collective-permute-start(bf16[32,36,2]{2,0,1:T(8,128)(2,1)S(1)} %get-tuple-element.9), channel_id=1, source_target_pairs={{1,0},{2,1},{3,2},{0,3},{5,4},{6,5},{7,6},{4,7},{9,8},{10,9},{11,1... | collective-permute-start | bytes 13832 | tf_op jit(solution)/shard_map/ppermute | solution.py:61
  44.5 9.9 %collective-permute-start.3 = (bf16[32,36,2]{2,0,1:T(8,128)(2,1)S(1)}, bf16[32,36,2]{2,0,1:T(8,128)(2,1)S(1)}, u32[]{:S(2)}, u32[]{:S(2)}) collective-permute-start(bf16[32,36,2]{2,0,1:T(8,128)(2,1)S(1)} %get-tuple-element.10), channel_id=1, source_target_pairs={{0,1},{1,2},{2,3},{3,0},{4,5},{5,6},{6,7},{7,4},{8,9},{9,10},{10,1... | collective-permute-start | bytes 13832 | tf_op jit(solution)/shard_map/ppermute | solution.py:64

commit v19 on v16

--- a/solution.py
+++ b/solution.py
@@ -163,7 +163,7 @@
     channels, rim_rows, rim_cols = rim.shape
     by_rows = jnp.transpose(rim, (1, 0, 2))
     block_c = 16
-    chunk = 2
+    chunk = 1
 
     def body(offs_ref, rim_ref, w_ref, out_ref, shifted):
         for row in range(rim_rows):

time: 61 us -> 61 us (level)
  no operation moved by 1% of the time
where the time goes in v19:
time: 61 us; the launch traced here: 60.5 us
  starting transfers between devices  20.1 us (33%)
  local copies, waits for them, and re-layouts  17.3 us (28%)
  other arithmetic  9.07 us (15%)
  Pallas kernels  7.25 us (12%)
  matrix products  6.34 us (10%)
    all_to_all x1, starting transfers between devices, per_device(): lax.all_to_all(partial.astype(jnp.bfloat16), BOTH, 0, 0, tiled=True)  7.3 us
    pallas_call x1, Pallas kernels, depthwise_conv(): pl.pallas_call(body, grid_spec=pltpu.PrefetchScalarGridSpec(num_scalar_pr...  7.25 us
    all_to_all x1, starting transfers between devices, per_device(): full_rows = lax.all_to_all(outgoing, BOTH, 0, 0, tiled=True)  6.89 us
    unnamed x23, local copies, waits for them, and re-layouts  6.01 us
    transpose x1, other arithmetic, depthwise_conv(): by_rows = jnp.transpose(rim, (1, 0, 2))  4.48 us
    ppermute x1, starting transfers between devices, per_device(): lax.ppermute(field[:, lat_rows - 2:], 'lat', [(i, i + 1) for i in range(l...  3.67 us
    convert_element_type x1, local copies, waits for them, and re-layouts, per_device(): (conv_out.astype(jnp.float32) + jax.nn.gelu(synthesis, approximate=True))...  2.47 us
    another operation x5, other arithmetic  1.84 us
  transfers between devices with their start and end apart: 6, of which 0 were waited for; matrix products, arithmetic and copies ran while one was open for 41% of the time, Pallas kernels for 12%

profile of v19, /device:TPU:0, one launch (start us, length us, event | category | flops | bytes accessed | tf_op | source)
XLA Modules:
  0.0 60.5 jit_solution(17217377339411727868)
XLA Ops:
  0.0 1.2 %multiply_convert_fusion.1 = (bf16[64,1,900]{2,0,1:T(8,128)(2,1)S(1)}, bf16[64,1,900]{2,0,1:T(8,128)(2,1)S(1)}, bf16[64,1,900]{2,0,1:T(8,128)(2,1)S(1)}, bf16[64,1,900]{2,0,1:T(8,128)(2,1)S(1)}) fusion(f32[64]{0:T(128)S(1)} %fusion.57, s32[900]{0:T(1024)S(1)} %iota_add_fusion, f32[64]{0:T(128)S(1)} %fusion.60), kind=kLoop, calls=%fused_computation.42 | loop fusion | flops 979200 | bytes 464912 | tf_op jit(solution)/shard_map/convert.5
  1.2 0.1 pad_maximum_fusion.4
  1.3 0.3 copy.67
  1.6 0.2 convert_element_type.99
  1.7 0.8 %convolution_convert_fusion = bf16[128,1024]{1,0:T(8,128)(2,1)S(1)} fusion(bf16[128,900]{1,0:T(8,128)(2,1)S(1)} %convert_element_type.99, bf16[1024,900]{1,0:T(8,128)(2,1)S(1)} %bitcast.102), kind=kOutput, calls=%fused_computation.11 | convolution fusion | flops 236060672 | bytes 2335744 | tf_op jit(solution)/shard_map/dot_general | solution.py:45
  2.6 0.9 %convert_element_type.101 = bf16[32,16,256]{2,1,0:T(8,128)(2,1)} reshape(bf16[128,1024]{1,0:T(8,128)(2,1)S(1)} %convolution_convert_fusion) | data formatting | bytes 524288 | tf_op jit(solution)/shard_map/convert_element_type | solution.py:48
  3.4 7.3 %all-to-all-start = ((bf16[32,16,256]{2,1,0:T(8,128)(2,1)}), bf16[32,16,256]{2,1,0:T(8,128)(2,1)S(1)}, u32[]{:S(2)}, u32[]{:S(2)}) async-start(bf16[32,16,256]{2,1,0:T(8,128)(2,1)} %convert_element_type.101), calls=%async_computation | async-start | bytes 524288 | tf_op jit(solution)/shard_map/all_to_all | solution.py:48
  10.7 2.7 %copy.76 = bf16[32,32,900]{2,0,1:T(8,128)(2,1)S(1)} copy(bf16[32,32,900]{2,1,0:T(8,128)(2,1)} %param.7) | data formatting | bytes 3686400 | tf_op args[0]
  13.5 0.0 copy-start.7
  13.5 0.0 copy-start.8
  13.5 0.7 %fusion.69 = (bf16[32,2,900]{2,0,1:T(8,128)(2,1)}, bf16[32,2,900]{2,0,1:T(8,128)(2,1)}) fusion(bf16[32,32,900]{2,0,1:T(8,128)(2,1)S(1)} %copy.76), kind=kLoop, calls=%fused_computation.120 | loop fusion | bytes 460800 | tf_op jit(solution)/shard_map/slice | solution.py:55
  14.2 3.7 %collective-permute-start = (bf16[32,2,900]{2,0,1:T(8,128)(2,1)}, bf16[32,2,900]{2,0,1:T(8,128)(2,1)S(1)}, u32[]{:S(2)}, u32[]{:S(2)}) collective-permute-start(bf16[32,2,900]{2,0,1:T(8,128)(2,1)} %get-tuple-element.11), channel_id=1, source_target_pairs={{0,4},{4,8},{8,12},{12,16},{16,20},{20,24},{24,28},{1,5},{5,9},{9,... | collective-permute-start | bytes 345608 | tf_op jit(solution)/shard_map/ppermute | solution.py:54
  17.9 1.3 %collective-permute-start.1 = (bf16[32,2,900]{2,0,1:T(8,128)(2,1)}, bf16[32,2,900]{2,0,1:T(8,128)(2,1)S(1)}, u32[]{:S(2)}, u32[]{:S(2)}) collective-permute-start(bf16[32,2,900]{2,0,1:T(8,128)(2,1)} %get-tuple-element.12), channel_id=1, source_target_pairs={{4,0},{8,4},{12,8},{16,12},{20,16},{24,20},{28,24},{5,1},{9,5},{13... | collective-permute-start | bytes 345608 | tf_op jit(solution)/shard_map/ppermute | solution.py:51
  19.2 0.1 copy.79.offs_ref
  19.3 0.1 copy.80.w_ref
  19.4 0.1 fusion.59
  19.5 0.1 convert_bitcast_fusion
  19.6 0.1 convolution_bitcast_fusion.2
  19.8 0.1 convolution_bitcast_fusion.3
  19.9 1.1 %fusion.70 = (bf16[1,64,32,32]{1,3,2,0:T(8,128)(2,1)S(1)}, bf16[1,64,32,32]{1,3,2,0:T(8,128)(2,1)S(1)}) fusion(bf16[2,64,32,32]{1,3,2,0:T(8,128)(2,1)} %param.13), kind=kLoop, calls=%fused_computation.121 | loop fusion | bytes 524288 | tf_op jit(solution)/shard_map/slice | solution.py:124
  21.0 1.5 %copy.99 = bf16[1,64,32,32]{3,2,1,0:T(8,128)(2,1)} copy(bf16[1,64,32,32]{1,3,2,0:T(8,128)(2,1)S(1)} %get-tuple-element.14) | data formatting | bytes 262144
  22.5 1.5 %copy.98 = bf16[1,64,32,32]{3,2,1,0:T(8,128)(2,1)} copy(bf16[1,64,32,32]{1,3,2,0:T(8,128)(2,1)S(1)} %get-tuple-element.13) | data formatting | bytes 262144
  24.0 0.3 copy.82
  24.3 0.9 %convert_element_type.110 = bf16[128,900]{1,0:T(8,128)(2,1)} reshape(bf16[64,2,900]{2,1,0:T(2,128)(2,1)S(1)} %copy.82) | data formatting | bytes 460800 | tf_op jit(solution)/shard_map/convert_element_type | solution.py:24
  25.1 0.1 fusion.55
  25.2 0.1 pad.12.clone
  25.3 0.1 compare_convert_fusion.1
  25.4 0.1 compare_convert_fusion
  25.5 0.0 collective-permute-done.1
  25.5 1.0 %pad_maximum_fusion.3 = (bf16[32,40,2]{2,0,1:T(8,128)(2,1)}, bf16[32,40,2]{2,0,1:T(8,128)(2,1)}) fusion(bf16[32,4,900]{2,0,1:T(8,128)(2,1)S(1)} %broadcast_in_dim.37, bf16[32,2,900]{2,0,1:T(8,128)(2,1)S(1)} %collective-permute-done.1, bf16[32,32,900]{2,0,1:T(8,128)(2,1)S(1)} %copy.76, bf16[32,2,900]{2,0,1:T(8,128)(2,1)S(1)} %collective-permute-done), kind=kLoop, calls=%fused_computation.33 | loop fusion | flops 40960 | bytes 2314240 | tf_op jit(solution)/shard_map/slice | solution.py:62
  26.5 0.9 %collective-permute-start.2 = (bf16[32,40,2]{2,0,1:T(8,128)(2,1)}, bf16[32,40,2]{2,0,1:T(8,128)(2,1)}, u32[]{:S(2)}, u32[]{:S(2)}) collective-permute-start(bf16[32,40,2]{2,0,1:T(8,128)(2,1)} %get-tuple-element.9), channel_id=1, source_target_pairs={{1,0},{2,1},{3,2},{0,3},{5,4},{6,5},{7,6},{4,7},{9,8},{10,9},{11,1... | collective-permute-start | bytes 15368 | tf_op jit(solution)/shard_map/ppermute | solution.py:61
  27.5 0.0 collective-permute-start.3
  27.5 0.0 all-to-all-done
  27.5 0.2 reshape.392
  27.7 0.9 %reduce_sum.9 = f32[8,4096]{1,0:T(8,128)} reduce(f32[8,4,4096]{2,1,0:T(4,128)S(1)} %reshape.392, f32[]{:T(128)} %constant.40.clone.1), dimensions={1}, to_apply=%region_0.1 | reduce | flops 98304 | bytes 655364 | tf_op jit(solution)/shard_map/reduce_sum | solution.py:81
  28.7 1.1 %reshape.387 = f32[8,2,2,32,32]{4,3,2,1,0:T(8,128)S(1)} reshape(f32[8,4096]{1,0:T(8,128)} %reduce_sum.9) | data formatting | bytes 262144 | tf_op jit(solution)/shard_map/reshape | solution.py:83
  29.8 0.3 copy.68
  30.1 0.2 reshape.388
  30.3 0.4 subtract_convert_fusion
  30.7 0.1 rev.8
  30.8 0.2 fusion.30
  31.0 0.2 fusion.10
  31.3 0.1 copy.70
  31.4 1.3 %convolution_bitcast_fusion = f32[2,64,2,32]{3,2,0,1:T(2,128)S(1)} fusion(bf16[2,64,2,32]{3,2,0,1:T(2,128)(2,1)S(1)} %copy.70, bf16[1,64,32,32]{3,2,1,0:T(8,128)(2,1)} %copy.99), kind=kOutput, calls=%fused_computation.12 | convolution fusion | flops 524288 | bytes 180224 | tf_op jit(solution)/shard_map/mlpc,lcd->mlpd/dot_general | solution.py:126
  32.7 1.3 %convolution_bitcast_fusion.1 = f32[2,64,2,32]{3,2,0,1:T(2,128)S(1)} fusion(bf16[2,64,2,32]{3,2,0,1:T(2,128)(2,1)S(1)} %copy.70, bf16[1,64,32,32]{3,2,1,0:T(8,128)(2,1)} %copy.98), kind=kOutput, calls=%fused_computation.13 | convolution fusion | flops 524288 | bytes 180224 | tf_op jit(solution)/shard_map/mlpc,lcd->mlpd/dot_general | solution.py:123
  34.0 0.1 fusion.27
  34.2 0.2 pad_maximum_fusion.6
  34.4 0.1 copy.73
  34.4 0.2 fusion.35
  34.7 0.2 subtract_multiply_fusion
  34.9 0.1 concatenate.15
  35.0 0.1 rev.9
  35.1 0.1 concatenate.16
  35.2 0.2 maximum_bitcast_fusion.1
  35.5 0.2 broadcast_in_dim.36
  35.7 1.4 %reshape.389 = bf16[32,16,256]{2,1,0:T(8,128)(2,1)} reshape(bf16[8,4,2,2,32,32]{5,4,3,2,1,0:T(8,128)(2,1)S(1)} %broadcast_in_dim.36) | data formatting | bytes 524288 | tf_op jit(solution)/shard_map/reshape | solution.py:146
  37.2 6.9 %all-to-all-start.1 = ((bf16[32,16,256]{2,1,0:T(8,128)(2,1)}), bf16[32,16,256]{2,1,0:T(8,128)(2,1)S(1)}, u32[]{:S(2)}, u32[]{:S(2)}) async-start(bf16[32,16,256]{2,1,0:T(8,128)(2,1)} %reshape.389), calls=%async_computation.1 | async-start | bytes 524288 | tf_op jit(solution)/shard_map/all_to_all | solution.py:147
  44.1 0.0 collective-permute-done.2
  44.1 4.5 %maximum_bitcast_fusion.rim_ref = bf16[40,32,1024]{2,1,0:T(8,128)(2,1)S(1)} fusion(bf16[32,40,2]{2,0,1:T(8,128)(2,1)} %collective-permute-done.3, bf16[32,40,2]{2,0,1:T(8,128)(2,1)} %collective-permute-done.2, bf16[32,4,900]{2,0,1:T(8,128)(2,1)S(1)} %broadcast_in_dim.37, bf16[32,2,900]{2,0,1:T(8,128)(2,1)} %copy-done.2, bf16[32,32,900]{2,0,1:T(8,128)(2,1)S(1)} %copy.76, ...), kind=kLoop, calls=%fused_computation.10 | loop fusion | flops 18350080 | bytes 4937728 | tf_op jit(solution)/shard_map/transpose | solution.py:164
  48.6 7.3 %shard_map.73 = bf16[32,32,900]{2,1,0:T(8,128)(2,1)S(1)} custom-call(s32[9,2]{1,0:T(8,128)S(1)} %copy.79.offs_ref, bf16[40,32,1024]{2,1,0:T(8,128)(2,1)S(1)} %maximum_bitcast_fusion.rim_ref, f32[32,9]{1,0:T(8,128)S(1)} %copy.80.w_ref), custom_call_target="tpu_custom_call" | custom-call | flops 94371840 | bytes 4464640 | tf_op jit(solution)/shard_map/pallas_call | solution.py:187
  55.8 0.2 reshape.390
  56.0 0.2 copy.81
  56.2 1.8 %fusion.8 = bf16[32,32,900]{2,0,1:T(8,128)(2,1)S(1)} fusion(bf16[32,32,900]{2,0,1:T(8,128)(2,1)S(1)} %bitcast.101, bf16[128,900]{1,0:T(8,128)(2,1)S(1)} %copy-done.3, bf16[32,32,128]{2,1,0:T(8,128)(2,1)S(1)} %bitcast.105), kind=kOutput, calls=%fused_computation.9 | convolution fusion | flops 246067200 | bytes 4178944 | tf_op jit(solution)/shard_map/dot_general | solution.py:153
  58.0 2.5 %copy.89 = bf16[32,32,900]{2,1,0:T(8,128)(2,1)} copy(bf16[32,32,900]{2,0,1:T(8,128)(2,1)S(1)} %fusion.8) | data formatting | bytes 3686400 | tf_op jit(solution)/shard_map/convert_element_type | solution.py:157
  (32 shorter events, 0.2 us)
Async XLA Ops:
  0.0 1.7 %copy-start = (bf16[32,32,900]{2,1,0:T(8,128)(2,1)S(1)}, bf16[32,32,900]{2,1,0:T(8,128)(2,1)}, u32[]{:S(2)}) copy-start(bf16[32,32,900]{2,1,0:T(8,128)(2,1)} %param.7) | copy-start | bytes 5529604
  3.4 15.8 %copy-start.6 = (s32[9,2]{0,1:T(2,128)S(1)}, s32[9,2]{0,1:T(2,128)}, u32[]{:S(2)}) copy-start(s32[9,2]{0,1:T(2,128)} %param.8) | copy-start | bytes 220
  3.4 15.9 %copy-start.5 = (f32[32,9]{0,1:T(8,128)S(1)}, f32[32,9]{0,1:T(8,128)}, u32[]{:S(2)}) copy-start(f32[32,9]{0,1:T(8,128)} %param.9) | copy-start | bytes 3460
  3.4 24.1 %all-to-all-start = ((bf16[32,16,256]{2,1,0:T(8,128)(2,1)}), bf16[32,16,256]{2,1,0:T(8,128)(2,1)S(1)}, u32[]{:S(2)}, u32[]{:S(2)}) async-start(bf16[32,16,256]{2,1,0:T(8,128)(2,1)} %convert_element_type.101), calls=%async_computation | async-start | bytes 524288 | tf_op jit(solution)/shard_map/all_to_all | solution.py:48
  13.5 11.7 %copy-start.7 = (s32[128]{0:T(128)S(1)}, s32[128]{0:T(128)}, u32[]{:S(2)}) copy-start(s32[128]{0:T(128)} %param.12) | copy-start | bytes 1540
  13.5 11.7 %copy-start.8 = (f32[128]{0:T(128)S(1)}, f32[128]{0:T(128)}, u32[]{:S(2)}) copy-start(f32[128]{0:T(128)} %param.11) | copy-start | bytes 1540
  14.2 11.2 %collective-permute-start = (bf16[32,2,900]{2,0,1:T(8,128)(2,1)}, bf16[32,2,900]{2,0,1:T(8,128)(2,1)S(1)}, u32[]{:S(2)}, u32[]{:S(2)}) collective-permute-start(bf16[32,2,900]{2,0,1:T(8,128)(2,1)} %get-tuple-element.11), channel_id=1, source_target_pairs={{0,4},{4,8},{8,12},{12,16},{16,20},{20,24},{24,28},{1,5},{5,9},{9,... | collective-permute-start | bytes 345608 | tf_op jit(solution)/shard_map/ppermute | solution.py:54
  17.9 7.6 %collective-permute-start.1 = (bf16[32,2,900]{2,0,1:T(8,128)(2,1)}, bf16[32,2,900]{2,0,1:T(8,128)(2,1)S(1)}, u32[]{:S(2)}, u32[]{:S(2)}) collective-permute-start(bf16[32,2,900]{2,0,1:T(8,128)(2,1)} %get-tuple-element.12), channel_id=1, source_target_pairs={{4,0},{8,4},{12,8},{16,12},{20,16},{24,20},{28,24},{5,1},{9,5},{13... | collective-permute-start | bytes 345608 | tf_op jit(solution)/shard_map/ppermute | solution.py:51
  25.5 4.3 %copy-start.1 = (bf16[32,2,900]{2,0,1:T(8,128)(2,1)}, bf16[32,2,900]{2,0,1:T(8,128)(2,1)S(1)}, u32[]{:S(2)}) copy-start(bf16[32,2,900]{2,0,1:T(8,128)(2,1)S(1)} %collective-permute-done) | copy-start | bytes 345604
  25.5 4.3 %copy-start.2 = (bf16[32,2,900]{2,0,1:T(8,128)(2,1)}, bf16[32,2,900]{2,0,1:T(8,128)(2,1)S(1)}, u32[]{:S(2)}) copy-start(bf16[32,2,900]{2,0,1:T(8,128)(2,1)S(1)} %collective-permute-done.1) | copy-start | bytes 345604
  26.5 4.3 %copy-start.4 = (bf16[2,64,128]{2,1,0:T(8,128)(2,1)S(1)}, bf16[2,64,128]{2,1,0:T(8,128)(2,1)}, u32[]{:S(2)}) copy-start(bf16[2,64,128]{2,1,0:T(8,128)(2,1)} %param.10) | copy-start | bytes 98308
  26.5 17.5 %collective-permute-start.2 = (bf16[32,40,2]{2,0,1:T(8,128)(2,1)}, bf16[32,40,2]{2,0,1:T(8,128)(2,1)}, u32[]{:S(2)}, u32[]{:S(2)}) collective-permute-start(bf16[32,40,2]{2,0,1:T(8,128)(2,1)} %get-tuple-element.9), channel_id=1, source_target_pairs={{1,0},{2,1},{3,2},{0,3},{5,4},{6,5},{7,6},{4,7},{9,8},{10,9},{11,1... | collective-permute-start | bytes 15368 | tf_op jit(solution)/shard_map/ppermute | solution.py:61
  27.5 16.6 %collective-permute-start.3 = (bf16[32,40,2]{2,0,1:T(8,128)(2,1)}, bf16[32,40,2]{2,0,1:T(8,128)(2,1)}, u32[]{:S(2)}, u32[]{:S(2)}) collective-permute-start(bf16[32,40,2]{2,0,1:T(8,128)(2,1)} %get-tuple-element.10), channel_id=1, source_target_pairs={{0,1},{1,2},{2,3},{3,0},{4,5},{5,6},{6,7},{7,4},{8,9},{9,10},{10,1... | collective-permute-start | bytes 15368 | tf_op jit(solution)/shard_map/ppermute | solution.py:64
  37.2 18.7 %all-to-all-start.1 = ((bf16[32,16,256]{2,1,0:T(8,128)(2,1)}), bf16[32,16,256]{2,1,0:T(8,128)(2,1)S(1)}, u32[]{:S(2)}, u32[]{:S(2)}) async-start(bf16[32,16,256]{2,1,0:T(8,128)(2,1)} %reshape.389), calls=%async_computation.1 | async-start | bytes 524288 | tf_op jit(solution)/shard_map/all_to_all | solution.py:147
  48.6 7.6 %copy-start.3 = (bf16[128,900]{1,0:T(8,128)(2,1)S(1)}, bf16[128,900]{1,0:T(8,128)(2,1)}, u32[]{:S(2)}) copy-start(bf16[128,900]{1,0:T(8,128)(2,1)} %convert_element_type.110) | copy-start | bytes 691204
